TPU v7x, 32 devices: a whole 2x2x4 slice. The times are simulated.
32 devices in a mesh: height: 2 (over y), chan: 4 (over x, core), batch: 4 (over z).
Axes of the slice: x: 2, y: 2, z: 4, core: 2. Of those that a mesh axis runs over, the one named last changes fastest.
Arguments:
- block_input: bfloat16 [64, 16, 16, 2048], P('batch', 'height', None, 'chan'), may hold values from -6 to 6
- w_reduce: bfloat16 [2048, 1024], P(None, 'chan'), may hold values from -0.125 to 0.125
- w_group: bfloat16 [3, 3, 32, 1024], P(None, None, None, 'chan'), may hold values from -0.375 to 0.375
- w_expand: bfloat16 [1024, 2048], P('chan'), may hold values from -0.1875 to 0.1875
- gain_one: bfloat16 [1024], P('chan'), may hold values from 0.5 to 1.5
- bias_one: bfloat16 [1024], P('chan'), may hold values from -3 to 3
- gain_two: bfloat16 [1024], P('chan'), may hold values from 0.5 to 1.5
- bias_two: bfloat16 [1024], P('chan'), may hold values from -3 to 3
- gain_three: bfloat16 [2048], P('chan'), may hold values from 0.5 to 1.5
- bias_three: bfloat16 [2048], P('chan'), may hold values from -3 to 3
- image_counts: int32 [4], replicated, may hold values from 1 to 16, as said below
- grad_output: bfloat16 [64, 16, 16, 2048], P('batch', 'height', None, 'chan'), may hold values from -6 to 6
Outputs:
- output: bfloat16 [64, 16, 16, 2048], P('batch', 'height', None, 'chan')
- grad_input: bfloat16 [64, 16, 16, 2048], P('batch', 'height', None, 'chan')
- grad_reduce: float32 [2048, 1024], P(None, 'chan')
- grad_group: float32 [3, 3, 32, 1024], P(None, None, None, 'chan')
- grad_expand: float32 [1024, 2048], P('chan')
- grad_gain_one: float32 [1024], P('chan')
- grad_bias_one: float32 [1024], P('chan')
- grad_gain_two: float32 [1024], P('chan')
- grad_bias_two: float32 [1024], P('chan')
- grad_gain_three: float32 [2048], P('chan')
- grad_bias_three: float32 [2048], P('chan')
Inputs may be any that keep to these rules, and one draw needn't show every extreme that they name: image_counts[s] real images fill the first slots of batch shard s of 16 slots; the other slots are padding; some shard is full.
All inputs are finite; a program needn't handle non-finite values.
Results may differ from a plain program's by a relative error of at most 0.018.
Values may be sent and summed in bfloat16 or wider, within the bound.
No kernel may reach another device: no remote copies, remote signals or barrier semaphores. Data moves between devices by JAX's collectives and lax.ppermute only.
A program may use at most 192 MiB of HBM per device.

v0:
```python
import jax
import jax.numpy as jnp
from jax import lax
from jax.sharding import PartitionSpec as P

EPSILON = 1e-05
LAYOUT_DIMS = ("NHWC", "HWIO", "NHWC")


def extended(cells, sides, width):
    for axis, dim in sides:
        count = lax.axis_size(axis)
        ends = count - 1
        head = lax.slice_in_dim(cells, 0, width, axis=dim)
        tail = lax.slice_in_dim(cells, cells.shape[dim] - width, cells.shape[dim], axis=dim)
        cells = jnp.concatenate(
            [
                lax.ppermute(tail, axis, [(i, (i + 1) % count) for i in range(ends)]),
                cells,
                lax.ppermute(head, axis, [((i + 1) % count, i) for i in range(ends)]),
            ],
            axis=dim,
        )
    return cells


def smooth_slope(values):
    logistic = jax.nn.sigmoid(values)
    return logistic * (1.0 + values * (1.0 - logistic))


def spread_out(vector, offset, width_all):
    return lax.dynamic_update_slice(jnp.zeros((width_all,), jnp.float32), vector, (offset,))


def batch_sums(first_sum, second_sum, offset, width_all):
    total_one, total_two = lax.psum(
        (spread_out(first_sum, offset, width_all), spread_out(second_sum, offset, width_all)),
        ("height", "chan", "batch"),
    )
    length = first_sum.shape[0]
    return (
        lax.dynamic_slice_in_dim(total_one, offset, length),
        lax.dynamic_slice_in_dim(total_two, offset, length),
    )


def grad_sums(first_sum, second_sum, offset, width_all):
    total_one, total_two = lax.psum(
        (spread_out(first_sum, offset, width_all), spread_out(second_sum, offset, width_all)),
        ("height", "chan", "batch"),
    )
    length = first_sum.shape[0]
    return (
        lax.dynamic_slice_in_dim(total_one, offset, length),
        lax.dynamic_slice_in_dim(total_two, offset, length),
    )


def norm_forward(values, gain_vec, bias_vec, pixel_mask, valid_total, offset, width_all):
    masked = pixel_mask * values
    sum_one, sum_two = batch_sums(
        jnp.sum(masked, 0), jnp.sum(masked * values, 0), offset, width_all
    )
    average = sum_one / valid_total
    inv_std = lax.rsqrt(sum_two / valid_total - average * average + EPSILON)
    normalized = (values - average) * inv_std
    return (
        normalized,
        inv_std,
        normalized * gain_vec.astype(jnp.float32) + bias_vec.astype(jnp.float32),
    )


def norm_backward(
    upstream, normalized, inv_std, gain_vec, pixel_mask, valid_total, offset, width_all
):
    sum_bias, sum_gain = grad_sums(
        jnp.sum(upstream, 0), jnp.sum(upstream * normalized, 0), offset, width_all
    )
    grad_in = (
        pixel_mask
        * inv_std
        * gain_vec.astype(jnp.float32)
        * (upstream - (sum_bias + normalized * sum_gain) / valid_total)
    )
    return (grad_in, sum_gain, sum_bias)


def height_rows(field_in):
    padded = extended(field_in, (("height", 1),), 1)
    return jnp.pad(padded, ((0, 0), (0, 0), (1, 1), (0, 0)))


def grad_rows_of(field_in):
    padded = extended(field_in, (("height", 1),), 1)
    return jnp.pad(padded, ((0, 0), (0, 0), (1, 1), (0, 0)))


def group_conv(padded, kernel):
    return lax.conv_general_dilated(
        padded,
        kernel,
        (1, 1),
        "VALID",
        dimension_numbers=LAYOUT_DIMS,
        feature_group_count=kernel.shape[3] // kernel.shape[2],
        preferred_element_type=jnp.float32,
    )


def flipped(kernel):
    group_width = kernel.shape[2]
    groups_here = kernel.shape[3] // group_width
    turned = kernel[::-1, ::-1].reshape(3, 3, group_width, groups_here, group_width)
    return jnp.transpose(turned, (0, 1, 4, 3, 2)).reshape(
        3, 3, group_width, groups_here * group_width
    )


def kernel_grad(padded, grad_low, group_width):
    images, row_count, col_count, chan_count = grad_low.shape
    groups_here = chan_count // group_width
    pixels = images * row_count * col_count
    grad_grouped = grad_low.reshape(pixels, groups_here, group_width)
    tap_list = []
    for row_tap in range(3):
        for col_tap in range(3):
            window = padded[
                :, row_tap : row_tap + row_count, col_tap : col_tap + col_count, :
            ].reshape(pixels, groups_here, group_width)
            product = lax.dot_general(
                window,
                grad_grouped,
                (((0,), (0,)), ((1,), (1,))),
                preferred_element_type=jnp.float32,
            )
            tap_list.append(jnp.transpose(product, (1, 0, 2)).reshape(group_width, chan_count))
    return jnp.stack(tap_list).reshape(3, 3, group_width, chan_count)


def project_scatter(acts, cols_local):
    return (
        lax.psum_scatter(
            lax.dot_general(
                cols_local, acts, (((0,), (1,)), ((), ())), preferred_element_type=jnp.float32
            ).astype(jnp.bfloat16),
            "chan",
            scatter_dimension=0,
            tiled=True,
        )
        .astype(jnp.float32)
        .T
    )


def middle_forward(
    reduced, kernel, norm_params, pixel_mask, valid_total, offset, width_all, shape_four
):
    norm_one, inv_one, pre_one = norm_forward(
        reduced, norm_params[0], norm_params[1], pixel_mask, valid_total, offset, width_all
    )
    act_one = (pixel_mask * jax.nn.silu(pre_one)).astype(jnp.bfloat16)
    padded = height_rows(act_one.reshape(shape_four))
    grouped = group_conv(padded, kernel).reshape(reduced.shape)
    norm_two, inv_two, pre_two = norm_forward(
        grouped, norm_params[2], norm_params[3], pixel_mask, valid_total, offset, width_all
    )
    act_two = (pixel_mask * jax.nn.silu(pre_two)).astype(jnp.bfloat16)
    return (act_two, (norm_one, inv_one, pre_one, padded, norm_two, inv_two, pre_two))


def middle_backward(
    grad_act_two, saved, kernel, norm_params, pixel_mask, valid_total, offset, width_all, shape_four
):
    norm_one, inv_one, pre_one, padded, norm_two, inv_two, pre_two = saved
    grad_pre_two = pixel_mask * grad_act_two * smooth_slope(pre_two)
    grad_grouped, gain_two_sum, bias_two_sum = norm_backward(
        grad_pre_two, norm_two, inv_two, norm_params[2], pixel_mask, valid_total, offset, width_all
    )
    grad_low = grad_grouped.astype(jnp.bfloat16).reshape(shape_four)
    grad_act_one = group_conv(grad_rows_of(grad_low), flipped(kernel)).reshape(grad_pre_two.shape)
    grad_kernel = kernel_grad(padded, grad_low, kernel.shape[2])
    grad_pre_one = pixel_mask * grad_act_one * smooth_slope(pre_one)
    grad_reduced, gain_one_sum, bias_one_sum = norm_backward(
        grad_pre_one, norm_one, inv_one, norm_params[0], pixel_mask, valid_total, offset, width_all
    )
    return (
        grad_reduced.astype(jnp.bfloat16),
        grad_kernel,
        (gain_one_sum, bias_one_sum, gain_two_sum, bias_two_sum),
    )


def pixel_weights(image_total, own_count, per_image):
    flags = (jnp.arange(image_total) < own_count).astype(jnp.float32)
    return jnp.broadcast_to(flags[:, None], (image_total, per_image)).reshape(
        image_total * per_image, 1
    )


def shards(
    block_input,
    w_reduce,
    w_group,
    w_expand,
    gain_one,
    bias_one,
    gain_two,
    bias_two,
    gain_three,
    bias_three,
    image_counts,
    grad_output,
):
    chan_size = lax.axis_size("chan")
    chan_index = lax.axis_index("chan")
    images, row_count, col_count, out_part = block_input.shape
    mid_part = w_group.shape[3]
    mid_width = mid_part * chan_size
    out_width = out_part * chan_size
    own_count = jnp.sum(
        jnp.where(jnp.arange(image_counts.shape[0]) == lax.axis_index("batch"), image_counts, 0)
    )
    valid_total = jnp.sum(image_counts).astype(jnp.float32) * (
        row_count * lax.axis_size("height") * col_count
    )
    mid_offset = chan_index * mid_part
    out_offset = chan_index * out_part
    pixels = images * row_count * col_count
    pixel_mask = pixel_weights(images, own_count, row_count * col_count)
    pixels_in = block_input.reshape(pixels, out_part)
    reduce_turned = w_reduce.T
    gathered = lax.all_gather(pixels_in, "chan", axis=1, tiled=True)
    reduced = jnp.dot(gathered, w_reduce, preferred_element_type=jnp.float32)
    norm_params = (gain_one, bias_one, gain_two, bias_two)
    shape_four = (images, row_count, col_count, mid_part)
    act_two, saved = middle_forward(
        reduced, w_group, norm_params, pixel_mask, valid_total, mid_offset, mid_width, shape_four
    )
    expanded = project_scatter(act_two, w_expand)
    norm_three, inv_three, pre_three = norm_forward(
        expanded, gain_three, bias_three, pixel_mask, valid_total, out_offset, out_width
    )
    summed = pre_three + pixels_in.astype(jnp.float32)
    output = (pixel_mask * jax.nn.silu(summed)).astype(jnp.bfloat16).reshape(block_input.shape)
    grad_summed = (
        pixel_mask
        * grad_output.reshape(pixels, out_part).astype(jnp.float32)
        * smooth_slope(summed)
    )
    grad_expanded, grad_gain_three, grad_bias_three = norm_backward(
        grad_summed,
        norm_three,
        inv_three,
        gain_three,
        pixel_mask,
        valid_total,
        out_offset,
        out_width,
    )
    expanded_low = grad_expanded.astype(jnp.bfloat16)
    shard_piece = lax.all_gather(expanded_low, "chan", axis=1, tiled=True)
    first_row = jnp.int32(0)
    grad_mid = jnp.zeros((pixels, mid_part), jnp.float32)
    grad_weight = jnp.zeros((mid_part, out_width), jnp.float32)
    rows_here = lax.dynamic_slice_in_dim(w_expand, first_row, shard_piece.shape[1], 1)
    grad_mid = grad_mid + lax.dot_general(
        shard_piece, rows_here, (((1,), (1,)), ((), ())), preferred_element_type=jnp.float32
    )
    weight_block = lax.dot_general(
        act_two, shard_piece, (((0,), (0,)), ((), ())), preferred_element_type=jnp.float32
    )
    grad_expand = lax.dynamic_update_slice(grad_weight, weight_block, (0, first_row))
    reduced_low, grad_group, norm_grads = middle_backward(
        grad_mid,
        saved,
        w_group,
        norm_params,
        pixel_mask,
        valid_total,
        mid_offset,
        mid_width,
        shape_four,
    )
    grad_reduce = lax.dot_general(
        gathered, reduced_low, (((0,), (0,)), ((), ())), preferred_element_type=jnp.float32
    )
    back_in = project_scatter(reduced_low, reduce_turned)
    grad_input = (grad_summed + back_in).astype(jnp.bfloat16).reshape(block_input.shape)
    grad_reduce, grad_group, grad_expand = (
        lax.psum(grad_reduce.astype(jnp.bfloat16), ("height", "batch")).astype(jnp.float32),
        lax.psum(grad_group.astype(jnp.bfloat16), ("height", "batch")).astype(jnp.float32),
        lax.psum(grad_expand.astype(jnp.bfloat16), ("height", "batch")).astype(jnp.float32),
    )
    return (
        output,
        grad_input,
        grad_reduce,
        grad_group,
        grad_expand,
        norm_grads[0],
        norm_grads[1],
        norm_grads[2],
        norm_grads[3],
        grad_gain_three,
        grad_bias_three,
    )


def solution(mesh):
    placed = (
        P("batch", "height", None, "chan"),
        P(None, "chan"),
        P(None, None, None, "chan"),
        P("chan", None),
        P("chan"),
        P("chan"),
        P("chan"),
        P("chan"),
        P("chan"),
        P("chan"),
        P(),
        P("batch", "height", None, "chan"),
    )
    return jax.shard_map(
        shards,
        mesh=mesh,
        in_specs=placed,
        out_specs=(
            P("batch", "height", None, "chan"),
            P("batch", "height", None, "chan"),
            P(None, "chan"),
            P(None, None, None, "chan"),
            P("chan", None),
            P("chan"),
            P("chan"),
            P("chan"),
            P("chan"),
            P("chan"),
            P("chan"),
        ),
        check_vma=False,
    )
```

profile of v0, /device:TPU:0, one launch (start us, length us, event | category | flops | bytes accessed | tf_op | source)
XLA Modules:
  0.0 820.9 jit_solution(2283540890738680934)
XLA Ops:
  10.1 60.5 %all-gather.3.cloned.1.call-done = bf16[2048,2048]{1,0:T(8,128)(2,1)} async-done(((bf16[2048,512]{1,0:T(8,128)(2,1)}), bf16[2048,2048]{1,0:T(8,128)(2,1)}) %all-gather.3.cloned.1.call-update) | async-done | bytes 8388624 | tf_op jit(solution)/shard_map/all_gather | solution.py:234
  70.6 6.1 fusion.43
  77.2 39.4 %all-reduce.7 = (f32[1024]{0:T(1024)S(1)}, f32[1024]{0:T(1024)S(1)}) all-reduce(f32[1024]{0:T(1024)S(1)} %dynamic_update_slice.36, f32[1024]{0:T(1024)S(1)} %dynamic_update_slice.37), channel_id=1, replica_groups=mesh['height'=2,'chan'=4,'batch'=4] {'height','chan','batch'}, use_global_device_ids=true, to_apply=%region_2.3 | all-reduce | flops 2048 | bytes 16384 | tf_op jit(solution)/shard_map/psum | solution.py:37
  132.9 4.9 reshape.144
  137.8 13.0 %fusion = (f32[8,32]{1,0:T(8,128)S(1)}, f32[8,32]{1,0:T(8,128)S(1)}, f32[16,8,16,8,32]{4,0,3,2,1:T(8,128)}) fusion(f32[16]{0:T(128)S(1)} %copy-done.48, bf16[3,3,32,8,32]{4,3,2,1,0:T(8,128)(2,1)} %shard_map.205, bf16[16,10,18,8,32]{4,3,2,1,0:T(8,128)(2,1)} %reshape.144), kind=kOutput, calls=%fused_computation.2 | convolution fusion | flops 304086528 | bytes 3721280 | tf_op jit(solution)/shard_map/conv_general_dilated | solution.py:101
  151.0 9.3 %copy.49 = f32[16,8,16,8,32]{4,3,2,1,0:T(8,128)} copy(f32[16,8,16,8,32]{4,0,3,2,1:T(8,128)} %get-tuple-element.84) | data formatting | bytes 4194304 | tf_op jit(solution)/shard_map/conv_general_dilated | solution.py:101
  160.4 7.1 reshape.128
  168.3 39.3 %all-reduce.6 = (f32[1024]{0:T(1024)S(1)}, f32[1024]{0:T(1024)S(1)}) all-reduce(f32[1024]{0:T(1024)S(1)} %dynamic_update_slice.38, f32[1024]{0:T(1024)S(1)} %dynamic_update_slice.39), channel_id=1, replica_groups=mesh['height'=2,'chan'=4,'batch'=4] {'height','chan','batch'}, use_global_device_ids=true, to_apply=%region_7.8 | all-reduce | flops 2048 | bytes 16384 | tf_op jit(solution)/shard_map/psum | solution.py:37
  207.7 7.4 convert_bitcast_fusion.1
  215.8 72.0 %reduce-scatter.3.cloned.1.call-done = bf16[512,2048]{0,1:T(8,128)(2,1)} async-done(((bf16[2048,2048]{0,1:T(8,128)(2,1)}), bf16[512,2048]{0,1:T(8,128)(2,1)}) %reduce-scatter.3.cloned.1.call-update) | async-done | bytes 2097168 | tf_op jit(solution)/shard_map/reduce_scatter | solution.py:144
  290.7 39.4 %all-reduce.5 = (f32[2048]{0:T(1024)S(1)}, f32[2048]{0:T(1024)S(1)}) all-reduce(f32[2048]{0:T(1024)S(1)} %dynamic_update_slice.41, f32[2048]{0:T(1024)S(1)} %dynamic_update_slice.40), channel_id=1, replica_groups=mesh['height'=2,'chan'=4,'batch'=4] {'height','chan','batch'}, use_global_device_ids=true, to_apply=%region_14.15 | all-reduce | flops 4096 | bytes 32768 | tf_op jit(solution)/shard_map/psum | solution.py:37
  330.2 6.8 fusion.103
  337.5 41.2 %all-reduce.4 = (f32[2048]{0:T(1024)S(1)}, f32[2048]{0:T(1024)S(1)}) all-reduce(f32[2048]{0:T(1024)S(1)} %dynamic_update_slice.43, f32[2048]{0:T(1024)S(1)} %dynamic_update_slice.42), channel_id=1, replica_groups=mesh['height'=2,'chan'=4,'batch'=4] {'height','chan','batch'}, use_global_device_ids=true, to_apply=%region_18.19 | all-reduce | flops 4096 | bytes 32768 | tf_op jit(solution)/shard_map/psum | solution.py:49
  378.9 4.5 fusion.35
  390.1 5.9 reshape.135
  399.4 5.8 reshape.134
  422.0 5.9 reshape.142
  427.9 13.8 %all-gather.5.cloned.1.call-done = bf16[2048,2048]{1,0:T(8,128)(2,1)} async-done(((bf16[2048,512]{1,0:T(8,128)(2,1)}), bf16[2048,2048]{1,0:T(8,128)(2,1)}) %all-gather.5.cloned.1.call-update) | async-done | bytes 8388624 | tf_op jit(solution)/shard_map/all_gather | solution.py:263
  441.7 8.0 fusion.105
  450.1 39.4 %all-reduce.3 = (f32[1024]{0:T(1024)S(1)}, f32[1024]{0:T(1024)S(1)}) all-reduce(f32[1024]{0:T(1024)S(1)} %dynamic_update_slice.45, f32[1024]{0:T(1024)S(1)} %dynamic_update_slice.44), channel_id=1, replica_groups=mesh['height'=2,'chan'=4,'batch'=4] {'height','chan','batch'}, use_global_device_ids=true, to_apply=%region_22.23 | all-reduce | flops 2048 | bytes 16384 | tf_op jit(solution)/shard_map/psum | solution.py:49
  529.7 4.2 collective-permute-start.2
  535.5 6.9 convolution_convert_fusion
  543.7 4.6 pad.14
  548.3 12.4 %fusion.3 = f32[16,8,16,8,32]{4,0,3,2,1:T(8,128)S(1)} fusion(bf16[16,10,18,8,32]{4,3,0,2,1:T(8,128)(2,1)} %pad.14, bf16[3,3,32,8,32]{4,3,2,1,0:T(8,128)(2,1)S(1)} %copy-done.15), kind=kOutput, calls=%fused_computation.11 | convolution fusion | flops 301989888 | bytes 3719168 | tf_op jit(solution)/shard_map/conv_general_dilated | solution.py:101
  560.7 5.8 copy.55
  566.5 7.2 reshape.132
  577.5 42.3 %all-reduce.2 = (f32[1024]{0:T(1024)S(1)}, f32[1024]{0:T(1024)S(1)}) all-reduce(f32[1024]{0:T(1024)S(1)} %dynamic_update_slice.47, f32[1024]{0:T(1024)S(1)} %dynamic_update_slice.46), channel_id=1, replica_groups=mesh['height'=2,'chan'=4,'batch'=4] {'height','chan','batch'}, use_global_device_ids=true, to_apply=%region_26.27 | all-reduce | flops 2048 | bytes 16384 | tf_op jit(solution)/shard_map/psum | solution.py:49
  622.2 6.7 fusion.39
  630.2 5.7 convert_bitcast_fusion
  635.9 100.1 %all-reduce.11.cloned.1.call-done = (bf16[2048,256]{0,1:T(8,128)(2,1)}, bf16[3,3,32,256]{3,2,1,0:T(8,128)(2,1)}, bf16[256,2048]{1,0:T(8,128)(2,1)}) async-done(((bf16[2048,256]{0,1:T(8,128)(2,1)}, bf16[3,3,32,256]{3,2,1,0:T(8,128)(2,1)}, bf16[256,2048]{1,0:T(8,128)(2,1)}), (bf16[2048,256]{0,1:T(8,128)(2,1)}, bf16[3,3,32,256]{3,2,1,0:T(8,128)(2,1)}, ...) | async-done | bytes 2244624 | tf_op jit(solution)/shard_map/psum | solution.py:292
  741.2 67.9 %reduce-scatter.5.cloned.1.call-done = bf16[512,2048]{0,1:T(8,128)(2,1)} async-done(((bf16[2048,2048]{0,1:T(8,128)(2,1)}), bf16[512,2048]{0,1:T(8,128)(2,1)}) %reduce-scatter.5.cloned.1.call-update) | async-done | bytes 2097168 | tf_op jit(solution)/shard_map/reduce_scatter | solution.py:144
  809.2 5.0 fusion.7
  (232 shorter events, 106.8 us)
Async XLA Ops:
  7.2 200.5 %copy-start = (bf16[256,2048]{1,0:T(8,128)(2,1)S(1)}, bf16[256,2048]{1,0:T(8,128)(2,1)}, u32[]{:S(2)}) copy-start(bf16[256,2048]{1,0:T(8,128)(2,1)} %param.15) | copy-start | bytes 3145732
  7.2 63.4 %all-gather.3.cloned.1.call-start = ((), (), s32[]{:S(2)}) async-start(), calls=%async_computation.2 | async-start | bytes 10485760 | tf_op jit(solution)/shard_map/all_gather | solution.py:234
  8.0 279.8 %reduce-scatter.3.cloned.1.call-start = ((), (), s32[]{:S(2)}) async-start(), calls=%async_computation.3 | async-start | bytes 10485760 | tf_op jit(solution)/shard_map/reduce_scatter | solution.py:144
  9.3 107.4 %copy-start.29 = (f32[256]{0:T(256)}, f32[256]{0:T(256)S(1)}, u32[]{:S(2)}) copy-start(f32[256]{0:T(256)S(1)} %convert_element_type.102) | copy-start | bytes 3076
  9.4 107.4 %copy-start.33 = (f32[256]{0:T(256)}, f32[256]{0:T(256)S(1)}, u32[]{:S(2)}) copy-start(f32[256]{0:T(256)S(1)} %convert_element_type.103) | copy-start | bytes 3076
  10.0 66.7 %copy-start.47 = (f32[16]{0:T(128)}, f32[16]{0:T(128)S(1)}, u32[]{:S(2)}) copy-start(f32[16]{0:T(128)S(1)} %compare_convert_fusion) | copy-start | bytes 196
  10.1 106.6 %copy-start.21 = (f32[2048]{0:T(1024)}, f32[2048]{0:T(1024)S(1)}, u32[]{:S(2)}) copy-start(f32[2048]{0:T(1024)S(1)} %broadcast_bitcast_fusion) | copy-start | bytes 24580
  76.7 49.1 %copy-start.3 = (f32[2048,256]{1,0:T(8,128)}, f32[2048,256]{1,0:T(8,128)S(1)}, u32[]{:S(2)}) copy-start(f32[2048,256]{1,0:T(8,128)S(1)} %get-tuple-element.83) | copy-start | bytes 6291460
  76.7 48.0 %copy-start.16 = (bf16[3,3,32,256]{3,2,1,0:T(8,128)(2,1)S(1)}, bf16[3,3,32,256]{3,2,1,0:T(8,128)(2,1)}, u32[]{:S(2)}) copy-start(bf16[3,3,32,256]{3,2,1,0:T(8,128)(2,1)} %param.14) | copy-start | bytes 442372
  119.3 8.5 %collective-permute-start = (bf16[16,1,16,256]{3,2,1,0:T(8,128)(2,1)}, bf16[16,1,16,256]{3,2,1,0:T(8,128)(2,1)S(1)}, u32[]{:S(2)}, u32[]{:S(2)}) collective-permute-start(bf16[16,1,16,256]{3,2,1,0:T(8,128)(2,1)} %get-tuple-element.79), channel_id=1, source_target_pairs={{0,16},{1,17},{2,18},{3,19},{4,20},{5,21},{6,22},{7,23},{8,24},{9,... | collective-permute-start | bytes 393224 | tf_op jit(solution)/shard_map/ppermute | solution.py:18
  123.5 7.1 collective-permute-start.1
  127.7 79.9 %copy-start.52 = (f32[256]{0:T(256)}, f32[256]{0:T(256)S(1)}, u32[]{:S(2)}) copy-start(f32[256]{0:T(256)S(1)} %convert_element_type.106) | copy-start | bytes 3076
  127.8 10.1 %copy-start.17 = (bf16[16,1,16,256]{3,2,1,0:T(8,128)(2,1)}, bf16[16,1,16,256]{3,2,1,0:T(8,128)(2,1)S(1)}, u32[]{:S(2)}) copy-start(bf16[16,1,16,256]{3,2,1,0:T(8,128)(2,1)S(1)} %collective-permute-done) | copy-start | bytes 393220
  130.6 7.3 copy-start.19
  160.4 47.3 %copy-start.22 = (f32[2048]{0:T(1024)S(1)}, f32[2048]{0:T(1024)}, u32[]{:S(2)}) copy-start(f32[2048]{0:T(1024)} %copy-done.21) | copy-start | bytes 24580
  160.4 47.3 %copy-start.45 = (f32[256]{0:T(256)S(1)}, f32[256]{0:T(256)}, u32[]{:S(2)}) copy-start(f32[256]{0:T(256)} %convert_element_type.105) | copy-start | bytes 3076
  207.7 282.0 %copy-start.35 = (f32[256]{0:T(256)}, f32[256]{0:T(256)S(1)}, u32[]{:S(2)}) copy-start(f32[256]{0:T(256)S(1)} %get-tuple-element.64) | copy-start | bytes 3076
  207.7 282.0 %copy-start.37 = (f32[256]{0:T(256)}, f32[256]{0:T(256)S(1)}, u32[]{:S(2)}) copy-start(f32[256]{0:T(256)S(1)} %get-tuple-element.65) | copy-start | bytes 3076
  215.2 226.5 %all-gather.5.cloned.1.call-start = ((), (), s32[]{:S(2)}) async-start(), calls=%async_computation.4 | async-start | bytes 10485760 | tf_op jit(solution)/shard_map/all_gather | solution.py:263
  383.4 352.6 %all-reduce.11.cloned.1.call-start = ((), (), s32[]{:S(2)}) async-start(), calls=%async_computation.6 | async-start | bytes 4489216 | tf_op jit(solution)/shard_map/psum | solution.py:292
  422.0 19.7 %copy-start.5 = (f32[2048,256]{1,0:T(8,128)S(1)}, f32[2048,256]{1,0:T(8,128)}, u32[]{:S(2)}) copy-start(f32[2048,256]{1,0:T(8,128)} %reshape.128) | copy-start | bytes 6291460
  422.0 19.7 %copy-start.53 = (f32[256]{0:T(256)S(1)}, f32[256]{0:T(256)}, u32[]{:S(2)}) copy-start(f32[256]{0:T(256)} %copy-done.52) | copy-start | bytes 3076
  527.4 8.1 copy-start.36
  527.4 8.1 copy-start.38
  527.4 8.1 copy-start.46
  527.4 8.1 copy-start.54
  529.7 12.9 %collective-permute-start.2 = (bf16[16,1,16,256]{3,0,2,1:T(8,128)(2,1)}, bf16[16,1,16,256]{3,0,2,1:T(8,128)(2,1)S(1)}, u32[]{:S(2)}, u32[]{:S(2)}) collective-permute-start(bf16[16,1,16,256]{3,0,2,1:T(8,128)(2,1)} %get-tuple-element.77), channel_id=1, source_target_pairs={{0,16},{1,17},{2,18},{3,19},{4,20},{5,21},{6,22},{7,23},{8,24},{9,... | collective-permute-start | bytes 393224 | tf_op jit(solution)/shard_map/ppermute | solution.py:18
  533.9 8.7 %collective-permute-start.3 = (bf16[16,1,16,256]{3,0,2,1:T(8,128)(2,1)}, bf16[16,1,16,256]{3,0,2,1:T(8,128)(2,1)}, u32[]{:S(2)}, u32[]{:S(2)}) collective-permute-start(bf16[16,1,16,256]{3,0,2,1:T(8,128)(2,1)} %get-tuple-element.78), channel_id=1, source_target_pairs={{16,0},{17,1},{18,2},{19,3},{20,4},{21,5},{22,6},{23,7},{24,8},{25... | collective-permute-start | bytes 393224 | tf_op jit(solution)/shard_map/ppermute | solution.py:20
  566.5 7.2 copy-start.28
  566.5 7.2 copy-start.30
  566.5 7.2 copy-start.34
  629.0 180.2 %reduce-scatter.5.cloned.1.call-start = ((), (), s32[]{:S(2)}) async-start(), calls=%async_computation.5 | async-start | bytes 10485760 | tf_op jit(solution)/shard_map/reduce_scatter | solution.py:144
  (32 other events, 114.3 us)
Sparse Core Ops, SparseCore 0:
  9.6 60.9 all-gather.2
  215.3 72.4 reduce-scatter.2
  383.5 58.1 all-gather.4
  629.1 106.8 all-reduce.10
  738.4 70.7 reduce-scatter.4
where the time goes:
time: 827 us; the launch traced here: 821 us
  waiting for transfers between devices  318 us (38%)
  blocking collectives  241 us (29%)
  matrix products  98.7 us (12%)
  local copies, waits for them, and re-layouts  95.8 us (12%)
  other arithmetic  40.8 us (5%)
  between operations  15.4 us (2%)
  starting transfers between devices  11.3 us (1%)
    reduce_scatter x2, waiting for transfers between devices, project_scatter(): lax.psum_scatter(lax.dot_general(cols_local, acts, (((0,), (1,)), ((), ()...  140 us
    psum x3, blocking collectives, grad_sums(): lax.psum((spread_out(first_sum, offset, width_all), spread_out(second_sum...  123 us
    psum x3, blocking collectives, batch_sums(): lax.psum((spread_out(first_sum, offset, width_all), spread_out(second_sum...  118 us
    psum x1, waiting for transfers between devices, shards(): lax.psum(grad_reduce.astype(jnp.bfloat16), ('height', 'batch'))  100 us
    all_gather x1, waiting for transfers between devices, shards(): gathered = lax.all_gather(pixels_in, 'chan', axis=1, tiled=True)  60.5 us
    reshape x8, local copies, waits for them, and re-layouts, kernel_grad(): window = padded[:, row_tap:row_tap + row_count, col_tap:col_tap + col_cou...  34.4 us
    dot_general x9, matrix products, kernel_grad(): lax.dot_general(window, grad_grouped, (((0,), (0,)), ((1,), (1,))), prefe...  32.4 us
    conv_general_dilated x2, matrix products, group_conv(): lax.conv_general_dilated(padded, kernel, (1, 1), 'VALID', dimension_numbe...  25.4 us
  transfers between devices with their start and end apart: 9, of which 6 were waited for; matrix products, arithmetic and copies ran while one was open for 8% of the time, Pallas kernels for 0%

commit v1 on v0

v1 whole, which is shorter than its diff:
```python
import functools

import jax
import jax.numpy as jnp
from jax import lax
from jax.experimental import pallas as pl
from jax.experimental.pallas import tpu as pltpu
from jax.sharding import PartitionSpec as P

EPSILON = 1e-05
F32, BF16 = jnp.float32, jnp.bfloat16
REDUCE_AXES = ("height", "batch")
STEP_IMAGES = 4


def dot(a, b, contract):
    return lax.dot_general(a, b, (contract, ((), ())), preferred_element_type=F32)


def swap(value, distance):
    count = lax.axis_size("chan")
    return lax.ppermute(value, "chan", [(i, i ^ distance) for i in range(count)])


def gather_pieces(value):
    count = lax.axis_size("chan")
    pieces = [None] * count
    pieces[0] = value
    pieces[1] = swap(value, 1)
    for k in range(2, count, 2):
        pieces[k] = swap(value, k)
    for k in range(2, count, 2):
        pieces[k + 1] = swap(pieces[k], 1)
    return pieces


def scatter_pieces(parts):
    count = len(parts)
    low = [swap(parts[k + 1].astype(BF16), 1) for k in range(0, count, 2)]
    sums = [parts[k] + low[k // 2].astype(F32) for k in range(0, count, 2)]
    total = sums[0]
    arrived = [swap(sums[k // 2].astype(BF16), k) for k in range(2, count, 2)]
    for value in arrived:
        total = total + value.astype(F32)
    return total


def total_sums(*vectors):
    stacked = jnp.stack(vectors)
    count = lax.axis_size(REDUCE_AXES)
    sent = jnp.broadcast_to(stacked[None], (count,) + stacked.shape)
    return jnp.sum(lax.all_to_all(sent, REDUCE_AXES, 0, 0), 0)


def smooth_slope(values):
    logistic = jax.nn.sigmoid(values)
    return logistic * (1.0 + values * (1.0 - logistic))


def edge_rows(field):
    count = lax.axis_size("height")
    first, last = field[:, 0], field[:, -1]
    if count == 2:
        mine = jnp.where(lax.axis_index("height") == 0, last, first)
        other = lax.ppermute(mine, "height", [(0, 1), (1, 0)])
        return other, other
    above = lax.ppermute(last, "height", [(i, i + 1) for i in range(count - 1)])
    below = lax.ppermute(first, "height", [(i + 1, i) for i in range(count - 1)])
    return above, below


def fold_rows(values):
    rows, chans = values.shape
    return jnp.sum(values.reshape(rows // 8, 8, chans), 0)


def shifted(value, cols):
    rows = value.shape[0]
    place = lax.broadcasted_iota(jnp.int32, value.shape, 0) % cols
    left = jnp.where(place == 0, 0.0, pltpu.roll(value, 1, 0))
    right = jnp.where(place == cols - 1, 0.0, pltpu.roll(value, rows - 1, 0))
    return left, right


def fill_windows(window_ref, slot, value, cols):
    left, right = shifted(value, cols)
    window_ref[0, slot] = left.astype(BF16)
    window_ref[1, slot] = value.astype(BF16)
    window_ref[2, slot] = right.astype(BF16)


def conv_forward_kernel(
    images, rows, cols, flags_ref, red_ref, above_ref, below_ref, vec_ref, mat_ref,
    act_ref, out_ref, sums_ref, window_ref,
):
    step = pl.program_id(0)
    count = flags_ref[0]
    average, scale, bias = vec_ref[0:1, :], vec_ref[1:2, :], vec_ref[2:3, :]
    pixels = rows * cols
    chans = red_ref.shape[2]

    def activate(v, keep):
        pre = (v - average) * scale + bias
        return jnp.where(keep, pre / (1.0 + jnp.exp(-pre)), 0.0)

    for image in range(images):
        real = step * images + image < count
        own = activate(red_ref[image], real)
        above = activate(above_ref[image], jnp.logical_and(real, flags_ref[1] > 0))
        below = activate(below_ref[image], jnp.logical_and(real, flags_ref[2] > 0))
        act_ref[image] = own.astype(BF16)
        fill_windows(window_ref, image, jnp.concatenate([above, own, below], 0), cols)
    total = jnp.zeros((images * pixels, chans), F32)
    for i in range(3):
        for j in range(3):
            piece = window_ref[j, :, i * cols : i * cols + pixels, :].reshape(images * pixels, chans)
            total = total + dot(piece, mat_ref[3 * i + j], ((1,), (0,)))
    out_ref[...] = total.reshape(images, pixels, chans)

    @pl.when(step == 0)
    def _():
        sums_ref[...] = jnp.zeros_like(sums_ref)

    sums_ref[0] += fold_rows(total)
    sums_ref[1] += fold_rows(total * total)


def conv_forward(reduced, above, below, vectors, matrices, flags, rows, cols):
    image_count, pixels, chans = reduced.shape
    images = STEP_IMAGES
    block = lambda shape: pl.BlockSpec((images,) + shape, lambda s: (s, 0, 0))
    whole = lambda shape: pl.BlockSpec(shape, lambda s: (0,) * len(shape))
    return pl.pallas_call(
        functools.partial(conv_forward_kernel, images, rows, cols),
        grid=(image_count // images,),
        in_specs=[
            pl.BlockSpec(memory_space=pltpu.SMEM),
            block((pixels, chans)),
            block((cols, chans)),
            block((cols, chans)),
            whole((8, chans)),
            whole((9, chans, chans)),
        ],
        out_specs=[block((pixels, chans)), block((pixels, chans)), whole((2, 8, chans))],
        out_shape=[
            jax.ShapeDtypeStruct((image_count, pixels, chans), BF16),
            jax.ShapeDtypeStruct((image_count, pixels, chans), F32),
            jax.ShapeDtypeStruct((2, 8, chans), F32),
        ],
        scratch_shapes=[pltpu.VMEM((3, images, pixels + 2 * cols, chans), BF16)],
        compiler_params=pltpu.CompilerParams(
            dimension_semantics=("arbitrary",), vmem_limit_bytes=40 << 20
        ),
        cost_estimate=pl.CostEstimate(
            flops=18 * image_count * pixels * chans * chans,
            bytes_accessed=image_count * pixels * chans * 10,
            transcendentals=image_count * pixels * chans,
        ),
        name="conv_forward",
    )(flags, reduced, above, below, vectors, matrices)


def conv_backward_kernel(
    images, rows, cols, group, flags_ref, d_ref, d_above_ref, d_below_ref, grp_ref, g_above_ref, g_below_ref,
    red_ref, act_ref, vec_ref, mat_ref, out_ref, sums_ref, kernel_ref, window_ref, total_ref,
):
    step = pl.program_id(0)
    count = flags_ref[0]
    pixels = rows * cols
    chans = d_ref.shape[2]
    avg_two, inv_two, scale_two = vec_ref[0:1, :], vec_ref[1:2, :], vec_ref[2:3, :]
    bias_part, gain_part = vec_ref[3:4, :], vec_ref[4:5, :]
    avg_one, inv_one, gain_one, bias_one = (
        vec_ref[5:6, :], vec_ref[6:7, :], vec_ref[7:8, :], vec_ref[8:9, :],
    )

    def input_grad(d, grouped, keep):
        normalized = (grouped - avg_two) * inv_two
        return jnp.where(keep, scale_two * (d - (bias_part + normalized * gain_part)), 0.0)

    @pl.when(step == 0)
    def _():
        sums_ref[...] = jnp.zeros_like(sums_ref)
        total_ref[...] = jnp.zeros_like(total_ref)

    for image in range(images):
        real = step * images + image < count
        own = input_grad(d_ref[image], grp_ref[image], real)
        above = input_grad(d_above_ref[image], g_above_ref[image], jnp.logical_and(real, flags_ref[1] > 0))
        below = input_grad(d_below_ref[image], g_below_ref[image], jnp.logical_and(real, flags_ref[2] > 0))
        fill_windows(window_ref, image, jnp.concatenate([above, own, below], 0), cols)
    grad = jnp.zeros((images * pixels, chans), F32)
    acts = act_ref[...].reshape(images * pixels, chans)
    for i in range(3):
        for j in range(3):
            piece = window_ref[2 - j, :, (2 - i) * cols : (2 - i) * cols + pixels, :].reshape(images * pixels, chans)
            grad = grad + dot(piece, mat_ref[3 * i + j], ((1,), (0,)))
            total_ref[3 * i + j] += dot(acts, piece, ((0,), (0,)))
    for image in range(images):
        real = step * images + image < count
        normalized = (red_ref[image] - avg_one) * inv_one
        pre = normalized * gain_one + bias_one
        logistic = 1.0 / (1.0 + jnp.exp(-pre))
        slope = logistic * (1.0 + pre * (1.0 - logistic))
        d_one = jnp.where(real, grad[image * pixels : (image + 1) * pixels] * slope, 0.0)
        out_ref[image] = d_one
        sums_ref[0] += fold_rows(d_one)
        sums_ref[1] += fold_rows(d_one * normalized)

    @pl.when(step == pl.num_programs(0) - 1)
    def _():
        row_group = lax.broadcasted_iota(jnp.int32, (chans, chans), 0) // group
        col_group = lax.broadcasted_iota(jnp.int32, (chans, chans), 1) // group
        for tap in range(9):
            own = jnp.where(row_group == col_group, total_ref[tap], 0.0)
            kernel_ref[tap] = jnp.sum(own.reshape(chans // group, group, chans), 0)


def conv_backward(d_two, d_edges, grouped, g_edges, reduced, acts, vectors, matrices, flags, rows, cols, group):
    image_count, pixels, chans = reduced.shape
    images = STEP_IMAGES
    block = lambda shape: pl.BlockSpec((images,) + shape, lambda s: (s, 0, 0))
    whole = lambda shape: pl.BlockSpec(shape, lambda s: (0,) * len(shape))
    field, edge = block((pixels, chans)), block((cols, chans))
    return pl.pallas_call(
        functools.partial(conv_backward_kernel, images, rows, cols, group),
        grid=(image_count // images,),
        in_specs=[
            pl.BlockSpec(memory_space=pltpu.SMEM),
            field, edge, edge, field, edge, edge, field, field,
            whole((16, chans)),
            whole((9, chans, chans)),
        ],
        out_specs=[field, whole((2, 8, chans)), whole((9, group, chans))],
        out_shape=[
            jax.ShapeDtypeStruct((image_count, pixels, chans), F32),
            jax.ShapeDtypeStruct((2, 8, chans), F32),
            jax.ShapeDtypeStruct((9, group, chans), F32),
        ],
        scratch_shapes=[
            pltpu.VMEM((3, images, pixels + 2 * cols, chans), BF16),
            pltpu.VMEM((9, chans, chans), F32),
        ],
        compiler_params=pltpu.CompilerParams(
            dimension_semantics=("arbitrary",), vmem_limit_bytes=40 << 20
        ),
        cost_estimate=pl.CostEstimate(
            flops=36 * image_count * pixels * chans * chans,
            bytes_accessed=image_count * pixels * chans * 18,
            transcendentals=image_count * pixels * chans,
        ),
        name="conv_backward",
    )(flags, d_two, *d_edges, grouped, *g_edges, reduced, acts, vectors, matrices)


def norm_vectors(sums, valid_total):
    average = sums[0] / valid_total
    inv_std = lax.rsqrt(sums[1] / valid_total - average * average + EPSILON)
    return average, inv_std


def block_matrices(kernel):
    group, chans = kernel.shape[2], kernel.shape[3]
    taps = kernel.reshape(9, group, chans)
    same = jnp.arange(chans)[:, None] // group == jnp.arange(chans)[None, :] // group
    spread = jnp.where(same[None], jnp.tile(taps, (1, chans // group, 1)), jnp.zeros((), kernel.dtype))
    return spread, jnp.transpose(spread, (0, 2, 1))


def padded_rows(vectors, count):
    stacked = jnp.stack(vectors)
    return jnp.pad(stacked, ((0, count - stacked.shape[0]), (0, 0)))


def shards(
    block_input, w_reduce, w_group, w_expand, gain_one, bias_one, gain_two, bias_two,
    gain_three, bias_three, image_counts, grad_output,
):
    chan_size = lax.axis_size("chan")
    me = lax.axis_index("chan")
    images, rows, cols, out_part = block_input.shape
    mid_part = w_group.shape[3]
    group = w_group.shape[2]
    out_width = out_part * chan_size
    pixels = images * rows * cols
    own_count = jnp.sum(
        jnp.where(jnp.arange(image_counts.shape[0]) == lax.axis_index("batch"), image_counts, 0)
    )
    valid_total = jnp.sum(image_counts).astype(F32) * (rows * lax.axis_size("height") * cols)
    mask = jnp.repeat((jnp.arange(images) < own_count).astype(F32), rows * cols)[:, None]
    height_at = lax.axis_index("height")
    flags = jnp.stack(
        [own_count, (height_at > 0).astype(jnp.int32), (height_at < lax.axis_size("height") - 1).astype(jnp.int32)]
    ).astype(jnp.int32)
    params = [v.astype(F32) for v in (gain_one, bias_one, gain_two, bias_two, gain_three, bias_three)]
    gain_one, bias_one, gain_two, bias_two, gain_three, bias_three = params
    matrices, matrices_back = block_matrices(w_group)

    reduce_rows = [
        lax.dynamic_slice_in_dim(w_reduce, (me ^ k) * out_part, out_part, 0) for k in range(chan_size)
    ]
    reduce_back = [reduce_rows[0]] + [swap(reduce_rows[k], k) for k in range(1, chan_size)]
    expand_cols = [
        lax.dynamic_slice_in_dim(w_expand, (me ^ k) * out_part, out_part, 1) for k in range(chan_size)
    ]
    expand_here = [expand_cols[0]] + [swap(expand_cols[k], k) for k in range(1, chan_size)]

    field = block_input.reshape(pixels, out_part)
    inputs = gather_pieces(field)
    reduced = dot(inputs[0], reduce_rows[0], ((1,), (0,)))
    for k in range(1, chan_size):
        reduced = reduced + dot(inputs[k], reduce_rows[k], ((1,), (0,)))
    masked = reduced * mask
    sums_one = total_sums(jnp.sum(masked, 0), jnp.sum(masked * reduced, 0))
    reduced = reduced.reshape(images, rows * cols, mid_part)
    red_edges = edge_rows(reduced.reshape(images, rows, cols, mid_part))
    avg_one, inv_one = norm_vectors(sums_one, valid_total)

    acts_one, grouped, part = conv_forward(
        reduced, *red_edges, padded_rows([avg_one, inv_one * gain_one, bias_one], 8), matrices, flags, rows, cols
    )
    part = jnp.sum(part, 1)
    sums_two = total_sums(part[0], part[1])
    grp_edges = edge_rows(grouped.reshape(images, rows, cols, mid_part))
    avg_two, inv_two = norm_vectors(sums_two, valid_total)
    normal_two = (grouped.reshape(pixels, mid_part) - avg_two) * inv_two
    pre_two = normal_two * gain_two + bias_two
    act_two = (mask * jax.nn.silu(pre_two)).astype(BF16)

    acts_two = gather_pieces(act_two)
    expanded = dot(acts_two[0], expand_here[0], ((1,), (0,)))
    for k in range(1, chan_size):
        expanded = expanded + dot(acts_two[k], expand_here[k], ((1,), (0,)))
    masked = expanded * mask
    sums_three = total_sums(jnp.sum(masked, 0), jnp.sum(masked * expanded, 0))
    avg_three, inv_three = norm_vectors(sums_three, valid_total)
    normal_three = (expanded - avg_three) * inv_three
    summed = normal_three * gain_three + bias_three + field.astype(F32)
    output = (mask * jax.nn.silu(summed)).astype(BF16).reshape(block_input.shape)
    grad_summed = mask * grad_output.reshape(pixels, out_part).astype(F32) * smooth_slope(summed)
    grads_three = total_sums(jnp.sum(grad_summed, 0), jnp.sum(grad_summed * normal_three, 0))
    grad_expanded = (
        mask * inv_three * gain_three
        * (grad_summed - (grads_three[0] + normal_three * grads_three[1]) / valid_total)
    ).astype(BF16)

    grad_mid = scatter_pieces([dot(grad_expanded, expand_here[k], ((1,), (1,))) for k in range(chan_size)])
    expand_grads = [
        dot(acts_two[k], grad_expanded, ((0,), (0,))).astype(BF16) for k in range(chan_size)
    ]
    expand_grads = [expand_grads[0]] + [swap(expand_grads[k], k) for k in range(1, chan_size)]
    d_two = mask * grad_mid * smooth_slope(pre_two)
    grads_two = total_sums(jnp.sum(d_two, 0), jnp.sum(d_two * normal_two, 0))
    d_two = d_two.reshape(images, rows * cols, mid_part)
    d_edges = edge_rows(d_two.reshape(images, rows, cols, mid_part))
    vectors = padded_rows(
        [avg_two, inv_two, inv_two * gain_two, grads_two[0] / valid_total, grads_two[1] / valid_total,
         avg_one, inv_one, gain_one, bias_one],
        16,
    )
    d_one, part, grad_group = conv_backward(
        d_two, d_edges, grouped, grp_edges, reduced, acts_one, vectors, matrices_back, flags, rows, cols, group
    )
    part = jnp.sum(part, 1)
    grads_one = total_sums(part[0], part[1])
    normal_one = (reduced.reshape(pixels, mid_part) - avg_one) * inv_one
    grad_reduced = (
        mask * inv_one * gain_one
        * (d_one.reshape(pixels, mid_part) - (grads_one[0] + normal_one * grads_one[1]) / valid_total)
    ).astype(BF16)

    reduce_grads = [dot(inputs[k], grad_reduced, ((0,), (0,))).astype(BF16) for k in range(chan_size)]
    pieces = gather_pieces(grad_reduced)
    back = dot(pieces[0], reduce_back[0], ((1,), (1,)))
    for k in range(1, chan_size):
        back = back + dot(pieces[k], reduce_back[k], ((1,), (1,)))
    grad_input = (grad_summed + back).astype(BF16).reshape(block_input.shape)

    grad_reduce = jnp.zeros((out_width, mid_part), BF16)
    grad_expand = jnp.zeros((mid_part, out_width), BF16)
    for k in range(chan_size):
        grad_reduce = lax.dynamic_update_slice(grad_reduce, reduce_grads[k], ((me ^ k) * out_part, 0))
        grad_expand = lax.dynamic_update_slice(grad_expand, expand_grads[k], (0, (me ^ k) * out_part))
    grad_reduce, grad_group, grad_expand = (
        lax.psum(value, REDUCE_AXES).astype(F32)
        for value in (grad_reduce, grad_group.astype(BF16).reshape(w_group.shape), grad_expand)
    )
    return (
        output, grad_input, grad_reduce, grad_group, grad_expand,
        grads_one[1], grads_one[0], grads_two[1], grads_two[0], grads_three[1], grads_three[0],
    )


def solution(mesh):
    split = P("batch", "height", None, "chan")
    vector = P("chan")
    return jax.shard_map(
        shards,
        mesh=mesh,
        in_specs=(
            split, P(None, "chan"), P(None, None, None, "chan"), P("chan", None),
            vector, vector, vector, vector, vector, vector, P(), split,
        ),
        out_specs=(
            split, split, P(None, "chan"), P(None, None, None, "chan"), P("chan", None),
            vector, vector, vector, vector, vector, vector,
        ),
        check_vma=False,
    )
```

time: 827 us -> 413 us (0.50)
  blocking collectives: 241 us -> 0 us
  waiting for transfers between devices: 318 us -> 199 us
  matrix products: 98.7 us -> 39.2 us
  local copies, waits for them, and re-layouts: 95.8 us -> 45.8 us
  starting transfers between devices: 11.3 us -> 49.1 us
  Pallas kernels: 0 us -> 13 us
  other arithmetic: 40.8 us -> 49.4 us
    psum x6 -> x0, blocking collectives: 241 us -> none  [the longest x3 123 us: grad_sums(): lax.psum((spread_out(first_sum, offset, width_all), spread_out(second_sum...]
    reduce_scatter x2 -> x0, waiting for transfers between devices: 140 us -> none  [project_scatter(): lax.psum_scatter(lax.dot_general(cols_local, acts, (((0,), (1,)), ((), ()...]
    ppermute x4 -> x24, waiting for transfers between devices: 2.82 us -> 101 us  [the longest x21 99.5 us: swap(): lax.ppermute(value, 'chan', [(i, i ^ distance) for i in range(count)])]
    all_gather x2 -> x0, waiting for transfers between devices: 74.3 us -> none  [the longest x1 60.5 us: shards(): gathered = lax.all_gather(pixels_in, 'chan', axis=1, tiled=True)]
    reshape x12 -> x2, local copies, waits for them, and re-layouts: 50.3 us -> 5.92 us  [the longest x1 3.04 us: shards(): d_one.reshape(pixels, mid_part)]
    dot_general x15 -> x24, matrix products: 73.2 us -> 39.2 us  [dot(): lax.dot_general(a, b, (contract, ((), ())), preferred_element_type=F32)]
    all_to_all x0 -> x6, starting transfers between devices: none -> 28.6 us  [total_sums(): return jnp.sum(lax.all_to_all(sent, REDUCE_AXES, 0, 0), 0)]
    conv_general_dilated x2 -> x0, matrix products: 25.4 us -> none  [group_conv(): lax.conv_general_dilated(padded, kernel, (1, 1), 'VALID', dimension_numbe...]
  transfers between devices with their start and end apart: 9 -> 31, of which waited for: 6 -> 14; matrix products, arithmetic and copies ran while one was open for 8% -> 22% of each run, Pallas kernels for 0% -> 2%
where the time goes in v1:
time: 413 us; the launch traced here: 411 us
  waiting for transfers between devices  199 us (48%)
  other arithmetic  49.4 us (12%)
  starting transfers between devices  49.1 us (12%)
  local copies, waits for them, and re-layouts  45.8 us (11%)
  matrix products  39.2 us (9%)
  between operations  15.7 us (4%)
  Pallas kernels  13 us (3%)
    ppermute x21, waiting for transfers between devices, swap(): lax.ppermute(value, 'chan', [(i, i ^ distance) for i in range(count)])  99.5 us
    psum x1, waiting for transfers between devices, shards(): lax.psum(value, REDUCE_AXES).astype(F32)  85.9 us
    dot_general x24, matrix products, dot(): lax.dot_general(a, b, (contract, ((), ())), preferred_element_type=F32)  39.2 us
    all_to_all x6, starting transfers between devices, total_sums(): return jnp.sum(lax.all_to_all(sent, REDUCE_AXES, 0, 0), 0)  28.6 us
    ppermute x21, starting transfers between devices, swap(): lax.ppermute(value, 'chan', [(i, i ^ distance) for i in range(count)])  14.2 us
    unnamed x112, local copies, waits for them, and re-layouts  11.9 us
    all_to_all x6, waiting for transfers between devices, total_sums(): return jnp.sum(lax.all_to_all(sent, REDUCE_AXES, 0, 0), 0)  11.9 us
  transfers between devices with their start and end apart: 31, of which 14 were waited for; matrix products, arithmetic and copies ran while one was open for 22% of the time, Pallas kernels for 2%

profile of v1, /device:TPU:0, one launch (start us, length us, event | category | flops | bytes accessed | tf_op | source)
XLA Modules:
  0.0 411.4 jit_solution(15169272758499601661)
XLA Ops:
  7.2 3.0 collective-permute-start.1
  15.2 41.0 %collective-permute-done.1 = bf16[2048,512]{1,0:T(8,128)(2,1)} collective-permute-done((bf16[2048,512]{1,0:T(8,128)(2,1)}, bf16[2048,512]{1,0:T(8,128)(2,1)}, u32[]{:S(2)}, u32[]{:S(2)}) %collective-permute-start.1) | collective-permute-done | bytes 2097184 | tf_op jit(solution)/shard_map/ppermute | solution.py:22
  69.7 3.8 multiply_reduce_fusion.2
  74.1 6.1 %all-to-all-start = ((f32[8,2,256]{2,1,0:T(2,128)}), f32[8,2,256]{2,1,0:T(2,128)}, u32[]{:S(2)}, u32[]{:S(2)}) async-start(f32[8,2,256]{2,1,0:T(2,128)} %broadcast_in_dim.38), calls=%async_computation | async-start | bytes 32768 | tf_op jit(solution)/shard_map/all_to_all | solution.py:52
  84.2 2.7 all-to-all-done
  90.9 5.1 %conv_forward.1 = (bf16[16,128,256]{2,1,0:T(8,128)(2,1)S(1)}, f32[16,128,256]{2,1,0:T(8,128)S(1)}, f32[2,8,256]{2,1,0:T(8,128)S(1)}) custom-call(s32[3]{0:T(128)S(1)} %pad_add_fusion.flags_ref, f32[16,128,256]{2,1,0:T(8,128)S(1)} %bitcast.142, f32[16,16,256]{2,1,0:T(8,128)} %collective-permute-done.3.above_ref.below_ref, ...), custom_call_target="tpu_custom_call" | custom-call | flops 2415919104 | bytes 5242880 | tf_op jit(solution)/shard_map/conv_forward/pallas_call | solution.py:133
  98.9 5.6 %all-to-all-start.1 = ((f32[8,2,256]{2,1,0:T(2,128)}), f32[8,2,256]{2,1,0:T(2,128)S(1)}, u32[]{:S(2)}, u32[]{:S(2)}) async-start(f32[8,2,256]{2,1,0:T(2,128)} %broadcast_in_dim.41), calls=%async_computation.1 | async-start | bytes 32768 | tf_op jit(solution)/shard_map/all_to_all | solution.py:52
  104.6 2.9 copy.89
  107.5 3.6 all-to-all-done.1
  111.2 3.1 multiply_convert_fusion.3
  118.0 22.5 %collective-permute-done.6 = bf16[2048,256]{0,1:T(8,128)(2,1)S(1)} collective-permute-done((bf16[2048,256]{0,1:T(8,128)(2,1)S(1)}, bf16[2048,256]{0,1:T(8,128)(2,1)S(1)}, u32[]{:S(2)}, u32[]{:S(2)}) %collective-permute-start.6) | collective-permute-done | bytes 1048608 | tf_op jit(solution)/shard_map/ppermute | solution.py:22
  141.3 4.3 %collective-permute-done.7 = bf16[256,512]{1,0:T(8,128)(2,1)S(1)} collective-permute-done((bf16[256,512]{1,0:T(8,128)(2,1)S(1)}, bf16[256,512]{1,0:T(8,128)(2,1)S(1)}, u32[]{:S(2)}, u32[]{:S(2)}) %collective-permute-start.7) | collective-permute-done | bytes 262176 | tf_op jit(solution)/shard_map/ppermute | solution.py:22
  147.4 2.9 multiply_reduce_fusion
  151.0 4.1 %all-to-all-start.2 = ((f32[8,2,512]{2,1,0:T(2,128)}), f32[8,2,512]{2,1,0:T(2,128)}, u32[]{:S(2)}, u32[]{:S(2)}) async-start(f32[8,2,512]{2,1,0:T(2,128)} %broadcast_in_dim.42), calls=%async_computation.2 | async-start | bytes 65536 | tf_op jit(solution)/shard_map/all_to_all | solution.py:52
  164.0 7.1 %fusion.29 = (f32[512]{0:T(512)S(1)}, f32[512]{0:T(512)S(1)}, f32[2048,512]{1,0:T(8,128)}, bf16[2048,512]{1,0:T(8,128)(2,1)}) fusion(f32[512]{0:T(512)S(1)} %bitcast.161, f32[2048,512]{1,0:T(8,128)} %get-tuple-element.60, f32[512]{0:T(512)S(1)} %bitcast.163, bf16[16,8,16,512]{3,2,1,0:T(8,128)(2,1)} %param.12, f32[512]{0:T(512)} %convert_element_type.125, ...), kind=kLoop, calls=%fused_computation.112 | loop fusion | flops 23067648 | bytes 14700544 | tf_op jit(solution)/shard_map/reduce_sum | solution.py:341
  171.7 4.2 %all-to-all-start.3 = ((f32[8,2,512]{2,1,0:T(2,128)}), f32[8,2,512]{2,1,0:T(2,128)}, u32[]{:S(2)}, u32[]{:S(2)}) async-start(f32[8,2,512]{2,1,0:T(2,128)} %broadcast_in_dim.43), calls=%async_computation.3 | async-start | bytes 65536 | tf_op jit(solution)/shard_map/all_to_all | solution.py:52
  179.8 3.1 all-to-all-done.3
  185.0 4.2 %multiply_convert_fusion = bf16[2048,512]{1,0:T(8,128)(2,1)S(1)} fusion(f32[2048,512]{1,0:T(8,128)} %get-tuple-element.37, f32[2048,512]{1,0:T(8,128)} %get-tuple-element.60, f32[]{:T(128)S(6)} %mul.240, f32[512]{0:T(512)S(1)} %bitcast.172, f32[512]{0:T(512)S(1)} %bitcast.170, f32[512]{0:T(512)} %convert_element_type.124, f32[512]{0:T(512)} %bitcast.162, ...), kind=kLoop, calls=%fused_computation.6 | loop fusion | flops 10485760 | bytes 10504196 | tf_op jit(solution)/shard_map/convert_element_type | solution.py:345
  205.2 20.1 %collective-permute-done.12 = bf16[2048,256]{0,1:T(8,128)(2,1)S(1)} collective-permute-done((bf16[2048,256]{0,1:T(8,128)(2,1)S(1)}, bf16[2048,256]{0,1:T(8,128)(2,1)S(1)}, u32[]{:S(2)}, u32[]{:S(2)}) %collective-permute-start.12) | collective-permute-done | bytes 1048608 | tf_op jit(solution)/shard_map/ppermute | solution.py:22
  225.4 2.7 fusion.30
  228.7 3.9 all-to-all-start.4
  232.7 2.9 copy.96
  243.0 2.6 stack.106
  250.8 7.9 %conv_backward.1 = (f32[16,128,256]{2,1,0:T(8,128)S(1)}, f32[2,8,256]{2,1,0:T(8,128)S(1)}, f32[9,32,256]{2,1,0:T(8,128)S(1)}) custom-call(s32[3]{0:T(128)S(1)} %pad_add_fusion.flags_ref, f32[16,128,256]{2,1,0:T(8,128)S(1)} %bitcast.147, f32[16,16,256]{2,1,0:T(8,128)} %collective-permute-done.13.d_above_ref.d_below_ref, ...), custom_call_target="tpu_custom_call" | custom-call | flops 4831838208 | bytes 9437184 | tf_op jit(solution)/shard_map/conv_backward/pallas_call | solution.py:225
  261.4 4.6 %all-to-all-start.5 = ((f32[8,2,256]{2,1,0:T(2,128)}), f32[8,2,256]{2,1,0:T(2,128)S(1)}, u32[]{:S(2)}, u32[]{:S(2)}) async-start(f32[8,2,256]{2,1,0:T(2,128)} %broadcast_in_dim.46), calls=%async_computation.5 | async-start | bytes 32768 | tf_op jit(solution)/shard_map/all_to_all | solution.py:52
  267.9 3.0 copy.104
  272.6 4.3 %multiply_convert_fusion.2 = bf16[2048,256]{0,1:T(8,128)(2,1)S(1)} fusion(f32[2048,256]{0,1:T(8,128)} %copy.104, f32[2048,256]{0,1:T(8,128)S(1)} %copy-done.9, f32[]{:T(128)S(6)} %mul.240, f32[256]{0:T(256)S(1)} %bitcast.189, f32[256]{0:T(256)S(1)} %bitcast.169, f32[256]{0:T(256)S(1)} %bitcast.187, f32[256]{0:T(256)S(1)} %copy-done.50, f32[256]{0:T(256)S(1)} %bitcast.168, ...), kind=kLoop, calls=%fused_computation.24 | loop fusion | flops 5242880 | bytes 5256196 | tf_op jit(solution)/shard_map/convert_element_type | solution.py:370
  294.8 7.7 %collective-permute-done.17 = bf16[2048,256]{0,1:T(8,128)(2,1)S(1)} collective-permute-done((bf16[2048,256]{0,1:T(8,128)(2,1)S(1)}, bf16[2048,256]{0,1:T(8,128)(2,1)S(1)}, u32[]{:S(2)}, u32[]{:S(2)}) %collective-permute-start.17) | collective-permute-done | bytes 1048608 | tf_op jit(solution)/shard_map/ppermute | solution.py:22
  304.3 3.5 collective-permute-done.18
  310.8 2.7 add_convert_fusion
  313.5 85.9 %all-reduce.5.cloned.1.call-done = (bf16[2048,256]{1,0:T(8,128)(2,1)}, bf16[3,3,32,256]{3,2,1,0:T(8,128)(2,1)}, bf16[256,2048]{1,0:T(8,128)(2,1)}) async-done(((bf16[2048,256]{1,0:T(8,128)(2,1)}, bf16[3,3,32,256]{3,2,1,0:T(8,128)(2,1)}, bf16[256,2048]{1,0:T(8,128)(2,1)}), (bf16[2048,256]{1,0:T(8,128)(2,1)}, bf16[3,3,32,256]{3,2,1,0:T(8,128)(2,1)}, bf16[256,2048]{1,0:T(8,128)(2,1)})) %all-reduce.5.cloned.1.call-update) | async-done | bytes 2244624 | tf_op jit(solution)/shard_map/psum | solution.py:385
  399.4 2.8 convert_element_type.147
  (246 shorter events, 111.2 us)
Async XLA Ops:
  7.2 49.0 %collective-permute-start.1 = (bf16[2048,512]{1,0:T(8,128)(2,1)}, bf16[2048,512]{1,0:T(8,128)(2,1)}, u32[]{:S(2)}, u32[]{:S(2)}) collective-permute-start(bf16[2048,512]{1,0:T(8,128)(2,1)} %bitcast.149), channel_id=1, source_target_pairs={{0,8},{4,12},{8,0},{12,4},{1,9},{5,13},{9,1},{13,5},{2,10},{6,14},... | collective-permute-start | bytes 6291464 | tf_op jit(solution)/shard_map/ppermute | solution.py:22
  10.2 54.7 %collective-permute-start = (bf16[2048,512]{1,0:T(8,128)(2,1)}, bf16[2048,512]{1,0:T(8,128)(2,1)}, u32[]{:S(2)}, u32[]{:S(2)}) collective-permute-start(bf16[2048,512]{1,0:T(8,128)(2,1)} %bitcast.150), channel_id=1, source_target_pairs={{0,4},{4,0},{8,12},{12,8},{1,5},{5,1},{9,13},{13,9},{2,6},{6,2},{1... | collective-permute-start | bytes 6291464 | tf_op jit(solution)/shard_map/ppermute | solution.py:22
  15.1 44.4 %copy-start.11 = (bf16[9,256,256]{1,2,0:T(8,128)(2,1)}, bf16[9,256,256]{1,2,0:T(8,128)(2,1)S(1)}, u32[]{:S(2)}) copy-start(bf16[9,256,256]{1,2,0:T(8,128)(2,1)S(1)} %copy.86) | copy-start | bytes 3538948
  56.1 13.5 %collective-permute-start.2 = (bf16[2048,512]{1,0:T(8,128)(2,1)}, bf16[2048,512]{1,0:T(8,128)(2,1)}, u32[]{:S(2)}, u32[]{:S(2)}) collective-permute-start(bf16[2048,512]{1,0:T(8,128)(2,1)} %collective-permute-done.1), channel_id=1, source_target_pairs={{0,4},{4,0},{8,12},{12,8},{1,5},{5,1},{9,13},{13,9},{2,6},{6,2},{1... | collective-permute-start | bytes 6291464 | tf_op jit(solution)/shard_map/ppermute | solution.py:22
  74.1 12.9 %all-to-all-start = ((f32[8,2,256]{2,1,0:T(2,128)}), f32[8,2,256]{2,1,0:T(2,128)}, u32[]{:S(2)}, u32[]{:S(2)}) async-start(f32[8,2,256]{2,1,0:T(2,128)} %broadcast_in_dim.38), calls=%async_computation | async-start | bytes 32768 | tf_op jit(solution)/shard_map/all_to_all | solution.py:52
  82.1 8.7 %collective-permute-start.3 = (f32[16,16,256]{2,1,0:T(8,128)S(1)}, f32[16,16,256]{2,1,0:T(8,128)}, u32[]{:S(2)}, u32[]{:S(2)}) collective-permute-start(f32[16,16,256]{2,1,0:T(8,128)S(1)} %fusion.15), channel_id=1, source_target_pairs={{0,16},{16,0},{1,17},{17,1},{2,18},{18,2},{3,19},{19,3},{4,20},{20... | collective-permute-start | bytes 786440 | tf_op jit(solution)/shard_map/ppermute | solution.py:65
  98.9 12.2 %all-to-all-start.1 = ((f32[8,2,256]{2,1,0:T(2,128)}), f32[8,2,256]{2,1,0:T(2,128)S(1)}, u32[]{:S(2)}, u32[]{:S(2)}) async-start(f32[8,2,256]{2,1,0:T(2,128)} %broadcast_in_dim.41), calls=%async_computation.1 | async-start | bytes 32768 | tf_op jit(solution)/shard_map/all_to_all | solution.py:52
  114.4 26.2 %collective-permute-start.6 = (bf16[2048,256]{0,1:T(8,128)(2,1)S(1)}, bf16[2048,256]{0,1:T(8,128)(2,1)S(1)}, u32[]{:S(2)}, u32[]{:S(2)}) collective-permute-start(bf16[2048,256]{0,1:T(8,128)(2,1)S(1)} %multiply_convert_fusion.3), channel_id=1, source_target_pairs={{0,8},{4,12},{8,0},{12,4},{1,9},{5,13},{9,1},{13,5},{2,10},{6,14},... | collective-permute-start | bytes 3145736 | tf_op jit(solution)/shard_map/ppermute | solution.py:22
  115.9 30.4 %collective-permute-start.4 = (bf16[2048,256]{0,1:T(8,128)(2,1)S(1)}, bf16[2048,256]{0,1:T(8,128)(2,1)S(1)}, u32[]{:S(2)}, u32[]{:S(2)}) collective-permute-start(bf16[2048,256]{0,1:T(8,128)(2,1)S(1)} %multiply_convert_fusion.3), channel_id=1, source_target_pairs={{0,4},{4,0},{8,12},{12,8},{1,5},{5,1},{9,13},{13,9},{2,6},{6,2},{1... | collective-permute-start | bytes 3145736 | tf_op jit(solution)/shard_map/ppermute | solution.py:22
  116.0 30.3 %collective-permute-start.5 = (bf16[256,512]{1,0:T(8,128)(2,1)S(1)}, bf16[256,512]{1,0:T(8,128)(2,1)S(1)}, u32[]{:S(2)}, u32[]{:S(2)}) collective-permute-start(bf16[256,512]{1,0:T(8,128)(2,1)S(1)} %get-tuple-element.46), channel_id=1, source_target_pairs={{0,4},{4,0},{8,12},{12,8},{1,5},{5,1},{9,13},{13,9},{2,6},{6,2},{1... | collective-permute-start | bytes 786440 | tf_op jit(solution)/shard_map/ppermute | solution.py:22
  116.6 29.0 %collective-permute-start.7 = (bf16[256,512]{1,0:T(8,128)(2,1)S(1)}, bf16[256,512]{1,0:T(8,128)(2,1)S(1)}, u32[]{:S(2)}, u32[]{:S(2)}) collective-permute-start(bf16[256,512]{1,0:T(8,128)(2,1)S(1)} %get-tuple-element.47), channel_id=1, source_target_pairs={{0,8},{4,12},{8,0},{12,4},{1,9},{5,13},{9,1},{13,5},{2,10},{6,14},... | collective-permute-start | bytes 786440 | tf_op jit(solution)/shard_map/ppermute | solution.py:22
  117.1 30.3 %collective-permute-start.9 = (bf16[256,512]{1,0:T(8,128)(2,1)S(1)}, bf16[256,512]{1,0:T(8,128)(2,1)S(1)}, u32[]{:S(2)}, u32[]{:S(2)}) collective-permute-start(bf16[256,512]{1,0:T(8,128)(2,1)S(1)} %get-tuple-element.45), channel_id=1, source_target_pairs={{0,12},{4,8},{8,4},{12,0},{1,13},{5,9},{9,5},{13,1},{2,14},{6,10},... | collective-permute-start | bytes 786440 | tf_op jit(solution)/shard_map/ppermute | solution.py:22
  140.6 6.9 %collective-permute-start.8 = (bf16[2048,256]{0,1:T(8,128)(2,1)S(1)}, bf16[2048,256]{0,1:T(8,128)(2,1)S(1)}, u32[]{:S(2)}, u32[]{:S(2)}) collective-permute-start(bf16[2048,256]{0,1:T(8,128)(2,1)S(1)} %collective-permute-done.6), channel_id=1, source_target_pairs={{0,4},{4,0},{8,12},{12,8},{1,5},{5,1},{9,13},{13,9},{2,6},{6,2},{1... | collective-permute-start | bytes 3145736 | tf_op jit(solution)/shard_map/ppermute | solution.py:22
  151.0 10.8 %all-to-all-start.2 = ((f32[8,2,512]{2,1,0:T(2,128)}), f32[8,2,512]{2,1,0:T(2,128)}, u32[]{:S(2)}, u32[]{:S(2)}) async-start(f32[8,2,512]{2,1,0:T(2,128)} %broadcast_in_dim.42), calls=%async_computation.2 | async-start | bytes 65536 | tf_op jit(solution)/shard_map/all_to_all | solution.py:52
  171.7 11.2 %all-to-all-start.3 = ((f32[8,2,512]{2,1,0:T(2,128)}), f32[8,2,512]{2,1,0:T(2,128)}, u32[]{:S(2)}, u32[]{:S(2)}) async-start(f32[8,2,512]{2,1,0:T(2,128)} %broadcast_in_dim.43), calls=%async_computation.3 | async-start | bytes 65536 | tf_op jit(solution)/shard_map/all_to_all | solution.py:52
  177.7 68.6 %collective-permute-start.14 = (f32[16,16,256]{2,1,0:T(8,128)}, f32[16,16,256]{2,1,0:T(8,128)}, u32[]{:S(2)}, u32[]{:S(2)}) collective-permute-start(f32[16,16,256]{2,1,0:T(8,128)} %fusion.11), channel_id=1, source_target_pairs={{0,16},{16,0},{1,17},{17,1},{2,18},{18,2},{3,19},{19,3},{4,20},{20... | collective-permute-start | bytes 786440 | tf_op jit(solution)/shard_map/ppermute | solution.py:65
  190.1 5.8 %collective-permute-start.11 = (bf16[2048,256]{0,1:T(8,128)(2,1)S(1)}, bf16[2048,256]{0,1:T(8,128)(2,1)S(1)}, u32[]{:S(2)}, u32[]{:S(2)}) collective-permute-start(bf16[2048,256]{0,1:T(8,128)(2,1)S(1)} %convolution_convert_fusion), channel_id=1, source_target_pairs={{0,4},{4,0},{8,12},{12,8},{1,5},{5,1},{9,13},{13,9},{2,6},{6,2},{1... | collective-permute-start | bytes 3145736 | tf_op jit(solution)/shard_map/ppermute | solution.py:22
  191.5 11.7 %collective-permute-start.21 = (bf16[256,512]{1,0:T(8,128)(2,1)S(1)}, bf16[256,512]{1,0:T(8,128)(2,1)S(1)}, u32[]{:S(2)}, u32[]{:S(2)}) collective-permute-start(bf16[256,512]{1,0:T(8,128)(2,1)S(1)} %convolution_convert_fusion.4), channel_id=1, source_target_pairs={{0,4},{4,0},{8,12},{12,8},{1,5},{5,1},{9,13},{13,9},{2,6},{6,2},{1... | collective-permute-start | bytes 786440 | tf_op jit(solution)/shard_map/ppermute | solution.py:22
  193.5 45.1 %collective-permute-start.22 = (bf16[256,512]{1,0:T(8,128)(2,1)}, bf16[256,512]{1,0:T(8,128)(2,1)}, u32[]{:S(2)}, u32[]{:S(2)}) collective-permute-start(bf16[256,512]{1,0:T(8,128)(2,1)} %convolution_convert_fusion.3), channel_id=1, source_target_pairs={{0,8},{4,12},{8,0},{12,4},{1,9},{5,13},{9,1},{13,5},{2,10},{6,14},... | collective-permute-start | bytes 786440 | tf_op jit(solution)/shard_map/ppermute | solution.py:22
  195.8 9.4 %collective-permute-start.10 = (bf16[2048,256]{0,1:T(8,128)(2,1)S(1)}, bf16[2048,256]{0,1:T(8,128)(2,1)S(1)}, u32[]{:S(2)}, u32[]{:S(2)}) collective-permute-start(bf16[2048,256]{0,1:T(8,128)(2,1)S(1)} %convolution_convert_fusion.1), channel_id=1, source_target_pairs={{0,4},{4,0},{8,12},{12,8},{1,5},{5,1},{9,13},{13,9},{2,6},{6,2},{1... | collective-permute-start | bytes 3145736 | tf_op jit(solution)/shard_map/ppermute | solution.py:22
  196.7 28.7 %collective-permute-start.12 = (bf16[2048,256]{0,1:T(8,128)(2,1)S(1)}, bf16[2048,256]{0,1:T(8,128)(2,1)S(1)}, u32[]{:S(2)}, u32[]{:S(2)}) collective-permute-start(bf16[2048,256]{0,1:T(8,128)(2,1)S(1)} %fusion.3), channel_id=1, source_target_pairs={{0,8},{4,12},{8,0},{12,4},{1,9},{5,13},{9,1},{13,5},{2,10},{6,14},... | collective-permute-start | bytes 3145736 | tf_op jit(solution)/shard_map/ppermute | solution.py:22
  203.2 63.0 %collective-permute-start.23 = (bf16[256,512]{1,0:T(8,128)(2,1)}, bf16[256,512]{1,0:T(8,128)(2,1)}, u32[]{:S(2)}, u32[]{:S(2)}) collective-permute-start(bf16[256,512]{1,0:T(8,128)(2,1)} %convolution_convert_fusion.2), channel_id=1, source_target_pairs={{0,12},{4,8},{8,4},{12,0},{1,13},{5,9},{9,5},{13,1},{2,14},{6,10},... | collective-permute-start | bytes 786440 | tf_op jit(solution)/shard_map/ppermute | solution.py:22
  228.7 11.6 %all-to-all-start.4 = ((f32[8,2,256]{2,1,0:T(2,128)}), f32[8,2,256]{2,1,0:T(2,128)}, u32[]{:S(2)}, u32[]{:S(2)}) async-start(f32[8,2,256]{2,1,0:T(2,128)} %broadcast_in_dim.44), calls=%async_computation.4 | async-start | bytes 32768 | tf_op jit(solution)/shard_map/all_to_all | solution.py:52
  236.7 9.7 %collective-permute-start.13 = (f32[16,16,256]{2,1,0:T(8,128)S(1)}, f32[16,16,256]{2,1,0:T(8,128)}, u32[]{:S(2)}, u32[]{:S(2)}) collective-permute-start(f32[16,16,256]{2,1,0:T(8,128)S(1)} %fusion.13), channel_id=1, source_target_pairs={{0,16},{16,0},{1,17},{17,1},{2,18},{18,2},{3,19},{19,3},{4,20},{20... | collective-permute-start | bytes 786440 | tf_op jit(solution)/shard_map/ppermute | solution.py:65
  261.4 11.2 %all-to-all-start.5 = ((f32[8,2,256]{2,1,0:T(2,128)}), f32[8,2,256]{2,1,0:T(2,128)S(1)}, u32[]{:S(2)}, u32[]{:S(2)}) async-start(f32[8,2,256]{2,1,0:T(2,128)} %broadcast_in_dim.46), calls=%async_computation.5 | async-start | bytes 32768 | tf_op jit(solution)/shard_map/all_to_all | solution.py:52
  265.9 133.5 %all-reduce.5.cloned.1.call-start = ((), (), s32[]{:S(2)}) async-start(), calls=%async_computation.6 | async-start | bytes 4489216 | tf_op jit(solution)/shard_map/psum | solution.py:385
  277.7 24.8 %collective-permute-start.17 = (bf16[2048,256]{0,1:T(8,128)(2,1)S(1)}, bf16[2048,256]{0,1:T(8,128)(2,1)S(1)}, u32[]{:S(2)}, u32[]{:S(2)}) collective-permute-start(bf16[2048,256]{0,1:T(8,128)(2,1)S(1)} %multiply_convert_fusion.2), channel_id=1, source_target_pairs={{0,8},{4,12},{8,0},{12,4},{1,9},{5,13},{9,1},{13,5},{2,10},{6,14},... | collective-permute-start | bytes 3145736 | tf_op jit(solution)/shard_map/ppermute | solution.py:22
  292.8 15.8 %collective-permute-start.15 = (bf16[2048,256]{0,1:T(8,128)(2,1)S(1)}, bf16[2048,256]{0,1:T(8,128)(2,1)S(1)}, u32[]{:S(2)}, u32[]{:S(2)}) collective-permute-start(bf16[2048,256]{0,1:T(8,128)(2,1)S(1)} %multiply_convert_fusion.2), channel_id=1, source_target_pairs={{0,4},{4,0},{8,12},{12,8},{1,5},{5,1},{9,13},{13,9},{2,6},{6,2},{1... | collective-permute-start | bytes 3145736 | tf_op jit(solution)/shard_map/ppermute | solution.py:22
  292.9 15.7 %collective-permute-start.16 = (bf16[512,256]{1,0:T(8,128)(2,1)}, bf16[512,256]{1,0:T(8,128)(2,1)S(1)}, u32[]{:S(2)}, u32[]{:S(2)}) collective-permute-start(bf16[512,256]{1,0:T(8,128)(2,1)} %copy-done.26), channel_id=1, source_target_pairs={{0,4},{4,0},{8,12},{12,8},{1,5},{5,1},{9,13},{13,9},{2,6},{6,2},{1... | collective-permute-start | bytes 786440 | tf_op jit(solution)/shard_map/ppermute | solution.py:22
  293.4 14.4 %collective-permute-start.18 = (bf16[512,256]{1,0:T(8,128)(2,1)}, bf16[512,256]{1,0:T(8,128)(2,1)S(1)}, u32[]{:S(2)}, u32[]{:S(2)}) collective-permute-start(bf16[512,256]{1,0:T(8,128)(2,1)} %copy-done.27), channel_id=1, source_target_pairs={{0,8},{4,12},{8,0},{12,4},{1,9},{5,13},{9,1},{13,5},{2,10},{6,14},... | collective-permute-start | bytes 786440 | tf_op jit(solution)/shard_map/ppermute | solution.py:22
  293.9 15.8 %collective-permute-start.20 = (bf16[512,256]{1,0:T(8,128)(2,1)S(1)}, bf16[512,256]{1,0:T(8,128)(2,1)S(1)}, u32[]{:S(2)}, u32[]{:S(2)}) collective-permute-start(bf16[512,256]{1,0:T(8,128)(2,1)S(1)} %copy-done.25), channel_id=1, source_target_pairs={{0,12},{4,8},{8,4},{12,0},{1,13},{5,9},{9,5},{13,1},{2,14},{6,10},... | collective-permute-start | bytes 786440 | tf_op jit(solution)/shard_map/ppermute | solution.py:22
  302.5 7.2 %collective-permute-start.19 = (bf16[2048,256]{0,1:T(8,128)(2,1)S(1)}, bf16[2048,256]{0,1:T(8,128)(2,1)S(1)}, u32[]{:S(2)}, u32[]{:S(2)}) collective-permute-start(bf16[2048,256]{0,1:T(8,128)(2,1)S(1)} %collective-permute-done.17), channel_id=1, source_target_pairs={{0,4},{4,0},{8,12},{12,8},{1,5},{5,1},{9,13},{13,9},{2,6},{6,2},{1... | collective-permute-start | bytes 3145736 | tf_op jit(solution)/shard_map/ppermute | solution.py:22
  (55 other events, 309.7 us)
Sparse Core Ops, SparseCore 0:
  292.9 106.4 all-reduce.4

commit v2 on v1

v2 whole, which is shorter than its diff:
```python
import functools

import jax
import jax.numpy as jnp
from jax import lax
from jax.experimental import pallas as pl
from jax.experimental.pallas import tpu as pltpu
from jax.sharding import PartitionSpec as P

EPSILON = 1e-05
F32, BF16 = jnp.float32, jnp.bfloat16
REDUCE_AXES = ("height", "batch")
CHUNKS = 4
OWN_COUNT, TOTAL_COUNT, HEIGHT_AT, CHAN_AT, EDGE_ROW = range(5)


def dot(a, b, left, right):
    return lax.dot_general(a, b, (((left,), (right,)), ((), ())), preferred_element_type=F32)


def whole(shape):
    return pl.BlockSpec(shape, lambda s: (0,) * len(shape))


def rows_at(shape, offset=0):
    return pl.BlockSpec(shape, lambda s: (s + offset,) + (0,) * (len(shape) - 1))


SCALARS = pl.BlockSpec(memory_space=pltpu.SMEM)
KEPT = pl.BlockSpec(memory_space=pl.ANY)


def kernel_call(body, name, steps, ins, outs, scratch=(), alias=None, flops=0, heavy=0):
    arrays = [a for a, _ in ins]
    moved = sum(a.size * a.dtype.itemsize for a, s in ins if s is not KEPT)
    return pl.pallas_call(
        body,
        grid=(steps,),
        in_specs=[s for _, s in ins],
        out_specs=[s for _, _, s in outs],
        out_shape=[jax.ShapeDtypeStruct(shape, dtype) for shape, dtype, _ in outs],
        scratch_shapes=list(scratch),
        input_output_aliases=alias or {},
        compiler_params=pltpu.CompilerParams(
            dimension_semantics=("arbitrary",), vmem_limit_bytes=48 << 20
        ),
        cost_estimate=pl.CostEstimate(flops=flops, bytes_accessed=moved, transcendentals=heavy),
        name=name,
    )(*arrays)


def permute(value, axis, distance):
    count = lax.axis_size(axis)
    return lax.ppermute(value, axis, [(i, i ^ distance) for i in range(count)])


def swap(value, distance):
    return permute(value, "chan", distance)


def spread_sums(sent):
    return lax.all_to_all(sent, REDUCE_AXES, 0, 0)


def part_of(value, index, count):
    size = value.shape[0] // count
    return lax.dynamic_slice_in_dim(value, index * size, size, 0)


def scatter_over(value, axis):
    count, at = lax.axis_size(axis), lax.axis_index(axis)
    arrived = [permute(part_of(value, at ^ k, count), axis, k) for k in range(1, count)]
    total = part_of(value, at, count).astype(F32)
    for piece in arrived:
        total = total + piece.astype(F32)
    return total.astype(value.dtype)


def gather_over(value, axis):
    count, at = lax.axis_size(axis), lax.axis_index(axis)
    size = value.shape[0]
    pieces = [value] + [permute(value, axis, k) for k in range(1, count)]
    out = jnp.zeros((count * size,) + value.shape[1:], value.dtype)
    for k, piece in enumerate(pieces):
        out = lax.dynamic_update_slice_in_dim(out, piece, (at ^ k) * size, 0)
    return out


def norm_of(sums_ref, total):
    sums = jnp.sum(sums_ref[...], 0)
    average = sums[0:1] / total
    return average, lax.rsqrt(sums[1:2] / total - average * average + EPSILON)


def silu(v):
    return v / (1.0 + jnp.exp(-v))


def silu_slope(v):
    logistic = 1.0 / (1.0 + jnp.exp(-v))
    return logistic * (1.0 + v * (1.0 - logistic))


def fold(values):
    rows, chans = values.shape
    return jnp.sum(values.reshape(rows // 8, 8, chans), 0)


def share(out_ref, acc):
    both = jnp.concatenate([jnp.sum(acc[0], 0, keepdims=True), jnp.sum(acc[1], 0, keepdims=True)], 0)
    out_ref[...] = jnp.broadcast_to(both[None], out_ref.shape)


def start_sums(acc_ref, before_ref):
    @pl.when(pl.program_id(0) == 0)
    def _():
        acc_ref[...] = jnp.zeros_like(acc_ref) if before_ref is None else before_ref[...]


def end_sums(acc_ref, out_ref, last):
    @pl.when(pl.program_id(0) == pl.num_programs(0) - 1)
    def _():
        if last:
            share(out_ref, acc_ref[...])
        else:
            out_ref[...] = acc_ref[...]


def sums_out(last, chans):
    if last:
        shape = (lax.axis_size(REDUCE_AXES), 2, chans)
    else:
        shape = (2, 8, chans)
    return (shape, F32, whole(shape))


def block_matrices_kernel(group, taps_ref, fwd_ref, back_ref):
    chans = taps_ref.shape[2]
    same = (
        lax.broadcasted_iota(jnp.int32, (chans, chans), 0) // group
        == lax.broadcasted_iota(jnp.int32, (chans, chans), 1) // group
    )
    for tap in range(9):
        wide = jnp.concatenate([taps_ref[tap].astype(F32)] * (chans // group), 0)
        wide = jnp.where(same, wide, 0.0)
        fwd_ref[tap] = wide.astype(BF16)
        back_ref[tap] = wide.T.astype(BF16)


def block_matrices(kernel):
    group, chans = kernel.shape[2], kernel.shape[3]
    taps = kernel.reshape(9, group, chans)
    shape = (9, chans, chans)
    return kernel_call(
        functools.partial(block_matrices_kernel, group), "block_matrices", 1,
        [(taps, whole(taps.shape))], [(shape, BF16, whole(shape))] * 2,
    )


def reduce_kernel(offset, images, count, last, chained, info_ref, *refs):
    pieces, w_ref, refs = refs[:count], refs[count], refs[count + 1 :]
    before_ref = None
    if chained:
        before_ref, refs = refs[0], refs[3:]
    red_ref, edge_ref, sums_ref, acc_ref = refs
    start_sums(acc_ref, before_ref)
    me = info_ref[CHAN_AT]
    part = pieces[0].shape[1]
    total = None
    for k in range(count):
        rows = w_ref[pl.ds(pl.multiple_of((me ^ k) * part, part), part), :]
        term = dot(pieces[k][...], rows, 1, 0)
        total = term if total is None else total + term
    red_ref[...] = total.reshape(red_ref.shape)
    keep_edges(info_ref, red_ref, edge_ref, images)
    add_images(info_ref, acc_ref, offset, images, total, None)
    end_sums(acc_ref, sums_ref, last)


def keep_edges(info_ref, field_ref, edge_ref, images):
    rows = pl.ds(pl.multiple_of(info_ref[EDGE_ROW], 16), edge_ref.shape[1])
    for image in range(images):
        edge_ref[image] = field_ref[image, rows, :]


def add_images(info_ref, acc_ref, offset, images, values, others):
    pixels = values.shape[0] // images
    for image in range(images):
        real = offset + pl.program_id(0) * images + image < info_ref[OWN_COUNT]
        at = slice(image * pixels, (image + 1) * pixels)
        value = jnp.where(real, values[at], 0.0)
        other = value if others is None else others[at]
        acc_ref[0] += fold(value)
        acc_ref[1] += fold(value * other)


def reduce_chunk(info, inputs, chunk, w_reduce, state, plan):
    images, pixels, cols, step_images, per_chunk = plan
    count = len(inputs)
    part, mid = inputs[0].shape[1], w_reduce.shape[1]
    steps = per_chunk // step_images
    block = step_images * pixels
    ins = [(info, SCALARS)]
    for k, piece in enumerate(inputs):
        if k < 2:
            ins.append((piece, rows_at((block, part), chunk * steps)))
        else:
            ins.append((piece[chunk], rows_at((block, part))))
    ins.append((w_reduce, whole(w_reduce.shape)))
    alias = {}
    if state is not None:
        red, edge, acc = state
        ins += [(acc, whole(acc.shape)), (red, KEPT), (edge, KEPT)]
        alias = {len(ins) - 2: 0, len(ins) - 1: 1}
    last = (chunk + 1) * per_chunk == images
    return kernel_call(
        functools.partial(reduce_kernel, chunk * per_chunk, step_images, count, last, state is not None),
        "reduce", steps, ins,
        [
            ((images, pixels, mid), F32, rows_at((step_images, pixels, mid), chunk * steps)),
            ((images, cols, mid), F32, rows_at((step_images, cols, mid), chunk * steps)),
            sums_out(last, mid),
        ],
        [pltpu.VMEM((2, 8, mid), F32)], alias, 2 * per_chunk * pixels * part * count * mid,
    )


def fill_windows(window_ref, slot, value, cols):
    rows = value.shape[0]
    place = lax.broadcasted_iota(jnp.int32, value.shape, 0) % cols
    left = jnp.where(place == 0, 0.0, pltpu.roll(value, 1, 0))
    right = jnp.where(place == cols - 1, 0.0, pltpu.roll(value, rows - 1, 0))
    window_ref[0, slot] = left.astype(BF16)
    window_ref[1, slot] = value.astype(BF16)
    window_ref[2, slot] = right.astype(BF16)


def with_edges(info_ref, own, edge):
    above = jnp.where(info_ref[HEIGHT_AT] > 0, edge, 0.0)
    below = jnp.where(info_ref[HEIGHT_AT] > 0, 0.0, edge)
    return jnp.concatenate([above, own, below], 0)


def conv_forward_kernel(
    images, per_image, info_ref, red_ref, edge_ref, sums_one_ref, par_ref, mat_ref,
    act_ref, out_ref, out_edge_ref, sums_ref, window_ref, acc_ref,
):
    step = pl.program_id(0)
    pixels, chans = red_ref.shape[1:]
    cols = edge_ref.shape[1]
    start_sums(acc_ref, None)
    average, inv_std = norm_of(sums_one_ref, info_ref[TOTAL_COUNT].astype(F32) * per_image)
    scale, bias = inv_std * par_ref[0:1, :], par_ref[1:2, :]
    for image in range(images):
        real = step * images + image < info_ref[OWN_COUNT]
        own = jnp.where(real, silu((red_ref[image] - average) * scale + bias), 0.0)
        edge = jnp.where(real, silu((edge_ref[image] - average) * scale + bias), 0.0)
        act_ref[image] = own.astype(BF16)
        fill_windows(window_ref, image, with_edges(info_ref, own, edge), cols)
    total = jnp.zeros((images * pixels, chans), F32)
    for i in range(3):
        for j in range(3):
            piece = window_ref[j, :, i * cols : i * cols + pixels, :].reshape(images * pixels, chans)
            total = total + dot(piece, mat_ref[3 * i + j], 1, 0)
    out_ref[...] = total.reshape(images, pixels, chans)
    keep_edges(info_ref, out_ref, out_edge_ref, images)
    add_images(info_ref, acc_ref, 0, images, total, None)
    end_sums(acc_ref, sums_ref, True)


def conv_forward(info, reduced, edge, sums_one, params, matrices, per_image):
    image_count, pixels, chans = reduced.shape
    cols = edge.shape[1]
    images = 4
    field, edges = rows_at((images, pixels, chans)), rows_at((images, cols, chans))
    return kernel_call(
        functools.partial(conv_forward_kernel, images, per_image), "conv_forward", image_count // images,
        [
            (info, SCALARS), (reduced, field), (edge, edges), (sums_one, whole(sums_one.shape)),
            (params, whole(params.shape)), (matrices, whole(matrices.shape)),
        ],
        [
            (reduced.shape, BF16, field), (reduced.shape, F32, field), (edge.shape, F32, edges),
            sums_out(True, chans),
        ],
        [pltpu.VMEM((3, images, pixels + 2 * cols, chans), BF16), pltpu.VMEM((2, 8, chans), F32)],
        flops=18 * image_count * pixels * chans * chans, heavy=image_count * pixels * chans,
    )


def act_two_kernel(offset, images, per_image, info_ref, grp_ref, sums_ref, par_ref, out_ref):
    pixels = grp_ref.shape[1]
    average, inv_std = norm_of(sums_ref, info_ref[TOTAL_COUNT].astype(F32) * per_image)
    scale, bias = inv_std * par_ref[2:3, :], par_ref[3:4, :]
    for image in range(images):
        real = offset + pl.program_id(0) * images + image < info_ref[OWN_COUNT]
        act = jnp.where(real, silu((grp_ref[image] - average) * scale + bias), 0.0)
        out_ref[image * pixels : (image + 1) * pixels] = act.astype(BF16)


def act_two_chunk(info, grouped, sums_two, params, chunk, plan, per_image):
    images, pixels, cols, step_images, per_chunk = plan
    mid = grouped.shape[2]
    steps = per_chunk // step_images
    return kernel_call(
        functools.partial(act_two_kernel, chunk * per_chunk, step_images, per_image), "act_two", steps,
        [
            (info, SCALARS), (grouped, rows_at((step_images, pixels, mid), chunk * steps)),
            (sums_two, whole(sums_two.shape)), (params, whole(params.shape)),
        ],
        [((per_chunk * pixels, mid), BF16, rows_at((step_images * pixels, mid)))],
        heavy=per_chunk * pixels * mid,
    )[0]


def expand_kernel(offset, images, count, last, chained, info_ref, *refs):
    acts, weights, refs = refs[:count], refs[count : 2 * count], refs[2 * count :]
    before_ref = None
    if chained:
        before_ref, refs = refs[0], refs[2:]
    out_ref, sums_ref, acc_ref = refs
    start_sums(acc_ref, before_ref)
    total = None
    for a_ref, w_ref in zip(acts, weights):
        term = dot(a_ref[...], w_ref[...], 1, 0)
        total = term if total is None else total + term
    out_ref[...] = total
    add_images(info_ref, acc_ref, offset, images, total, None)
    end_sums(acc_ref, sums_ref, last)


def expand_chunk(info, acts, weights, chunk, state, plan):
    images, pixels, cols, step_images, per_chunk = plan
    count, mid, out = len(acts), acts[0].shape[1], weights[0].shape[1]
    steps = per_chunk // step_images
    block = step_images * pixels
    ins = [(info, SCALARS)]
    ins += [(a, rows_at((block, mid))) for a in acts]
    ins += [(w, whole(w.shape)) for w in weights]
    alias = {}
    if state is not None:
        buffer, acc = state
        ins += [(acc, whole(acc.shape)), (buffer, KEPT)]
        alias = {len(ins) - 1: 0}
    last = (chunk + 1) * per_chunk == images
    return kernel_call(
        functools.partial(expand_kernel, chunk * per_chunk, step_images, count, last, state is not None),
        "expand", steps, ins,
        [((images * pixels, out), F32, rows_at((block, out), chunk * steps)), sums_out(last, out)],
        [pltpu.VMEM((2, 8, out), F32)], alias, 2 * per_chunk * pixels * mid * count * out,
    )


def output_kernel(images, per_image, info_ref, exp_ref, in_ref, go_ref, sums_three_ref, par_ref,
                  out_ref, grad_ref, sums_ref, acc_ref):
    start_sums(acc_ref, None)
    average, inv_std = norm_of(sums_three_ref, info_ref[TOTAL_COUNT].astype(F32) * per_image)
    pixels = exp_ref.shape[0] // images
    for image in range(images):
        real = pl.program_id(0) * images + image < info_ref[OWN_COUNT]
        at = slice(image * pixels, (image + 1) * pixels)
        normalized = (exp_ref[at] - average) * inv_std
        summed = normalized * par_ref[0:1, :] + par_ref[1:2, :] + in_ref[at].astype(F32)
        logistic = 1.0 / (1.0 + jnp.exp(-summed))
        out_ref[at] = jnp.where(real, summed * logistic, 0.0).astype(BF16)
        slope = logistic * (1.0 + summed * (1.0 - logistic))
        grad = jnp.where(real, go_ref[at].astype(F32) * slope, 0.0)
        grad_ref[at] = grad
        acc_ref[0] += fold(grad)
        acc_ref[1] += fold(grad * normalized)
    end_sums(acc_ref, sums_ref, True)


def output_pass(info, expanded, field, grad_output, sums_three, params, plan, per_image):
    images, pixels, cols, step_images, per_chunk = plan
    out = expanded.shape[1]
    spec = rows_at((step_images * pixels, out))
    return kernel_call(
        functools.partial(output_kernel, step_images, per_image), "output", images // step_images,
        [
            (info, SCALARS), (expanded, spec), (field, spec), (grad_output, spec),
            (sums_three, whole(sums_three.shape)), (params, whole(params.shape)),
        ],
        [(expanded.shape, BF16, spec), (expanded.shape, F32, spec), sums_out(True, out)],
        [pltpu.VMEM((2, 8, out), F32)], heavy=expanded.size,
    )


def back_expand_kernel(offset, images, count, per_image, chained, info_ref, grad_ref, exp_ref, sums_three_ref,
                       grads_ref, par_ref, *refs):
    weights, refs = refs[:count], refs[count:]
    if chained:
        refs = refs[1:]
    out_ref, near_ref, far_ref = refs
    total = info_ref[TOTAL_COUNT].astype(F32) * per_image
    average, inv_std = norm_of(sums_three_ref, total)
    grads = jnp.sum(grads_ref[...], 0)
    bias_part, gain_part = grads[0:1] / total, grads[1:2] / total
    scale = inv_std * par_ref[0:1, :]
    pixels = grad_ref.shape[0] // images
    for image in range(images):
        real = offset + pl.program_id(0) * images + image < info_ref[OWN_COUNT]
        at = slice(image * pixels, (image + 1) * pixels)
        normalized = (exp_ref[at] - average) * inv_std
        value = scale * (grad_ref[at] - (bias_part + normalized * gain_part))
        out_ref[at] = jnp.where(real, value, 0.0).astype(BF16)
    grad = out_ref[...]
    mid = weights[0].shape[0]
    for k in range(count):
        term = dot(grad, weights[k][...], 1, 1)
        to = slice((k // 2) * mid, (k // 2 + 1) * mid)
        if k % 2 == 0:
            near_ref[:, to] = term
        else:
            far_ref[:, to] = term.astype(BF16)


def back_expand_chunk(info, grad_summed, expanded, sums_three, grads_three, params, weights, chunk, state, plan, per_image):
    images, pixels, cols, step_images, per_chunk = plan
    count, mid, out = len(weights), weights[0].shape[0], expanded.shape[1]
    steps = per_chunk // step_images
    block = step_images * pixels
    spec = rows_at((block, out), chunk * steps)
    ins = [
        (info, SCALARS), (grad_summed, spec), (expanded, spec), (sums_three, whole(sums_three.shape)),
        (grads_three, whole(grads_three.shape)), (params, whole(params.shape)),
    ]
    ins += [(w, whole(w.shape)) for w in weights]
    alias = {}
    if state is not None:
        ins.append((state, KEPT))
        alias = {len(ins) - 1: 0}
    half = count // 2 * mid
    return kernel_call(
        functools.partial(back_expand_kernel, chunk * per_chunk, step_images, count, per_image, state is not None),
        "back_expand", steps, ins,
        [
            (expanded.shape, BF16, spec),
            ((per_chunk * pixels, half), F32, rows_at((block, half))),
            ((per_chunk * pixels, half), BF16, rows_at((block, half))),
        ],
        alias=alias, flops=2 * per_chunk * pixels * mid * count * out,
    )


def pair_sum_kernel(near_ref, far_ref, own_ref, *send_refs):
    mid = own_ref.shape[1]
    for k, ref in enumerate((own_ref,) + send_refs):
        at = slice(k * mid, (k + 1) * mid)
        ref[...] = (near_ref[:, at] + far_ref[:, at].astype(F32)).astype(ref.dtype)


def pair_sum(near, far, mid):
    rows, half = near.shape
    spec = whole((rows, half))
    return kernel_call(
        pair_sum_kernel, "pair_sum", 1, [(near, spec), (far, spec)],
        [((rows, mid), F32 if k == 0 else BF16, whole((rows, mid))) for k in range(half // mid)],
    )


def slope_two_kernel(offset, images, count, per_image, last, chained, info_ref, own_ref, *refs):
    arrived, refs = refs[:count], refs[count:]
    grp_ref, sums_two_ref, par_ref, refs = refs[0], refs[1], refs[2], refs[3:]
    before_ref = None
    if chained:
        before_ref, refs = refs[0], refs[3:]
    out_ref, edge_ref, sums_ref, acc_ref = refs
    start_sums(acc_ref, before_ref)
    average, inv_std = norm_of(sums_two_ref, info_ref[TOTAL_COUNT].astype(F32) * per_image)
    gain, bias = par_ref[2:3, :], par_ref[3:4, :]
    pixels = grp_ref.shape[1]
    for image in range(images):
        real = offset + pl.program_id(0) * images + image < info_ref[OWN_COUNT]
        at = slice(image * pixels, (image + 1) * pixels)
        grad = own_ref[at]
        for ref in arrived:
            grad = grad + ref[at].astype(F32)
        normalized = (grp_ref[image] - average) * inv_std
        grad = jnp.where(real, grad * silu_slope(normalized * gain + bias), 0.0)
        out_ref[image] = grad
        acc_ref[0] += fold(grad)
        acc_ref[1] += fold(grad * normalized)
    keep_edges(info_ref, out_ref, edge_ref, images)
    end_sums(acc_ref, sums_ref, last)


def slope_two_chunk(info, own, arrived, grouped, sums_two, params, chunk, state, plan, per_image):
    images, pixels, cols, step_images, per_chunk = plan
    mid = grouped.shape[2]
    steps = per_chunk // step_images
    local = rows_at((step_images * pixels, mid))
    field = rows_at((step_images, pixels, mid), chunk * steps)
    ins = [(info, SCALARS), (own, local)] + [(a, local) for a in arrived]
    ins += [(grouped, field), (sums_two, whole(sums_two.shape)), (params, whole(params.shape))]
    alias = {}
    if state is not None:
        buffer, edge, acc = state
        ins += [(acc, whole(acc.shape)), (buffer, KEPT), (edge, KEPT)]
        alias = {len(ins) - 2: 0, len(ins) - 1: 1}
    last = (chunk + 1) * per_chunk == images
    return kernel_call(
        functools.partial(
            slope_two_kernel, chunk * per_chunk, step_images, len(arrived), per_image, last, state is not None
        ),
        "slope_two", steps, ins,
        [
            (grouped.shape, F32, field),
            ((images, cols, mid), F32, rows_at((step_images, cols, mid), chunk * steps)),
            sums_out(last, mid),
        ],
        [pltpu.VMEM((2, 8, mid), F32)], alias, heavy=per_chunk * pixels * mid,
    )


def expand_grad_kernel(count, chunks, parts, *refs):
    acts, grad_ref, out_ref = refs[: count * chunks], refs[-2], refs[-1]
    rows = grad_ref.shape[0] // chunks
    mid = acts[0].shape[1]
    size = mid // parts
    for k in range(count):
        total = None
        for c in range(chunks):
            term = dot(acts[k * chunks + c][...], grad_ref[c * rows : (c + 1) * rows, :], 0, 0)
            total = term if total is None else total + term
        out_ref[:, k] = total.reshape(parts, size, total.shape[1]).astype(BF16)


def expand_grad(acts, grad_expanded, parts):
    count, chunks = len(acts), len(acts[0])
    mid, out = acts[0][0].shape[1], grad_expanded.shape[1]
    shape = (parts, count, mid // parts, out)
    return kernel_call(
        functools.partial(expand_grad_kernel, count, chunks, parts), "expand_grad", 1,
        [(a, whole(a.shape)) for piece in acts for a in piece] + [(grad_expanded, whole(grad_expanded.shape))],
        [(shape, BF16, whole(shape))],
        flops=2 * grad_expanded.shape[0] * mid * count * out,
    )[0]


def conv_backward_kernel(
    images, per_image, group, info_ref, d_ref, d_edge_ref, grp_ref, g_edge_ref, red_ref, act_ref,
    sums_two_ref, grads_two_ref, sums_one_ref, par_ref, mat_ref,
    out_ref, sums_ref, kernel_ref, window_ref, total_ref, acc_ref,
):
    step = pl.program_id(0)
    pixels, chans = d_ref.shape[1:]
    cols = d_edge_ref.shape[1]
    total_pixels = info_ref[TOTAL_COUNT].astype(F32) * per_image
    avg_two, inv_two = norm_of(sums_two_ref, total_pixels)
    grads = jnp.sum(grads_two_ref[...], 0)
    bias_part, gain_part = grads[0:1] / total_pixels, grads[1:2] / total_pixels
    scale_two = inv_two * par_ref[2:3, :]
    avg_one, inv_one = norm_of(sums_one_ref, total_pixels)
    gain_one, bias_one = par_ref[0:1, :], par_ref[1:2, :]

    def input_grad(d, grouped, keep):
        normalized = (grouped - avg_two) * inv_two
        return jnp.where(keep, scale_two * (d - (bias_part + normalized * gain_part)), 0.0)

    start_sums(acc_ref, None)

    @pl.when(step == 0)
    def _():
        total_ref[...] = jnp.zeros_like(total_ref)

    for image in range(images):
        real = step * images + image < info_ref[OWN_COUNT]
        own = input_grad(d_ref[image], grp_ref[image], real)
        edge = input_grad(d_edge_ref[image], g_edge_ref[image], real)
        fill_windows(window_ref, image, with_edges(info_ref, own, edge), cols)
    grad = jnp.zeros((images * pixels, chans), F32)
    acts = act_ref[...].reshape(images * pixels, chans)
    for i in range(3):
        for j in range(3):
            at = (2 - i) * cols
            piece = window_ref[2 - j, :, at : at + pixels, :].reshape(images * pixels, chans)
            grad = grad + dot(piece, mat_ref[3 * i + j], 1, 0)
            total_ref[3 * i + j] += dot(acts, piece, 0, 0)
    for image in range(images):
        real = step * images + image < info_ref[OWN_COUNT]
        normalized = (red_ref[image] - avg_one) * inv_one
        slope = silu_slope(normalized * gain_one + bias_one)
        d_one = jnp.where(real, grad[image * pixels : (image + 1) * pixels] * slope, 0.0)
        out_ref[image] = d_one
        acc_ref[0] += fold(d_one)
        acc_ref[1] += fold(d_one * normalized)
    end_sums(acc_ref, sums_ref, True)

    @pl.when(step == pl.num_programs(0) - 1)
    def _():
        same = (
            lax.broadcasted_iota(jnp.int32, (chans, chans), 0) // group
            == lax.broadcasted_iota(jnp.int32, (chans, chans), 1) // group
        )
        for tap in range(9):
            own = jnp.where(same, total_ref[tap], 0.0)
            kernel_ref[tap] = jnp.sum(own.reshape(chans // group, group, chans), 0).astype(kernel_ref.dtype)


def conv_backward(info, d_two, d_edge, grouped, g_edge, reduced, acts, sums_two, grads_two, sums_one, params, matrices,
                  group, per_image):
    image_count, pixels, chans = reduced.shape
    cols = d_edge.shape[1]
    images = 4
    field, edges = rows_at((images, pixels, chans)), rows_at((images, cols, chans))
    small = [(v, whole(v.shape)) for v in (sums_two, grads_two, sums_one, params, matrices)]
    return kernel_call(
        functools.partial(conv_backward_kernel, images, per_image, group), "conv_backward", image_count // images,
        [
            (info, SCALARS), (d_two, field), (d_edge, edges), (grouped, field), (g_edge, edges),
            (reduced, field), (acts, field),
        ] + small,
        [
            (reduced.shape, F32, field), sums_out(True, chans),
            ((9, group, chans), BF16, whole((9, group, chans))),
        ],
        [
            pltpu.VMEM((3, images, pixels + 2 * cols, chans), BF16),
            pltpu.VMEM((9, chans, chans), F32),
            pltpu.VMEM((2, 8, chans), F32),
        ],
        flops=36 * image_count * pixels * chans * chans, heavy=image_count * pixels * chans,
    )


def grad_reduced_kernel(offset, images, per_image, info_ref, d_ref, red_ref, sums_one_ref, grads_ref, par_ref, out_ref):
    total = info_ref[TOTAL_COUNT].astype(F32) * per_image
    average, inv_std = norm_of(sums_one_ref, total)
    grads = jnp.sum(grads_ref[...], 0)
    bias_part, gain_part = grads[0:1] / total, grads[1:2] / total
    scale = inv_std * par_ref[0:1, :]
    pixels = d_ref.shape[1]
    for image in range(images):
        real = offset + pl.program_id(0) * images + image < info_ref[OWN_COUNT]
        normalized = (red_ref[image] - average) * inv_std
        value = scale * (d_ref[image] - (bias_part + normalized * gain_part))
        out_ref[image * pixels : (image + 1) * pixels] = jnp.where(real, value, 0.0).astype(BF16)


def grad_reduced_chunk(info, d_one, reduced, sums_one, grads_one, params, chunk, plan, per_image):
    images, pixels, cols, step_images, per_chunk = plan
    mid = reduced.shape[2]
    steps = per_chunk // step_images
    field = rows_at((step_images, pixels, mid), chunk * steps)
    return kernel_call(
        functools.partial(grad_reduced_kernel, chunk * per_chunk, step_images, per_image), "grad_reduced", steps,
        [
            (info, SCALARS), (d_one, field), (reduced, field), (sums_one, whole(sums_one.shape)),
            (grads_one, whole(grads_one.shape)), (params, whole(params.shape)),
        ],
        [((per_chunk * pixels, mid), BF16, rows_at((step_images * pixels, mid)))],
    )[0]


def reduce_grad_kernel(counts, chunks, *refs):
    grads, out_ref = refs[-1 - chunks : -1], refs[-1]
    rows = grads[0].shape[0]
    at = 0
    for k, pieces in enumerate(counts):
        total = None
        for c in range(chunks):
            ref = refs[at] if pieces == 1 else refs[at + c]
            value = ref[c * rows : (c + 1) * rows, :] if pieces == 1 else ref[...]
            term = dot(value, grads[c][...], 0, 0)
            total = term if total is None else total + term
        at += pieces
        part = total.shape[0]
        out_ref[k * part : (k + 1) * part, :] = total.astype(BF16)


def reduce_grad(inputs, grads):
    flat, counts = [], []
    for piece in inputs:
        piece = piece if isinstance(piece, (list, tuple)) else [piece]
        flat += piece
        counts.append(len(piece))
    part, mid = flat[0].shape[1], grads[0].shape[1]
    shape = (len(inputs) * part, mid)
    return kernel_call(
        functools.partial(reduce_grad_kernel, tuple(counts), len(grads)), "reduce_grad", 1,
        [(v, whole(v.shape)) for v in flat + list(grads)],
        [(shape, BF16, whole(shape))],
        flops=2 * len(grads) * grads[0].shape[0] * shape[0] * mid,
    )[0]


def input_grad_kernel(count, chained, grad_ref, *refs):
    pieces, weights, out_ref = refs[:count], refs[count : 2 * count], refs[-1]
    total = grad_ref[...]
    for p_ref, w_ref in zip(pieces, weights):
        total = total + dot(p_ref[...], w_ref[...], 1, 1)
    out_ref[...] = total.astype(BF16)


def input_grad_chunk(grad_summed, pieces, weights, chunk, state, plan):
    images, pixels, cols, step_images, per_chunk = plan
    count, mid, out = len(pieces), pieces[0].shape[1], grad_summed.shape[1]
    steps = per_chunk // step_images
    block = step_images * pixels
    spec = rows_at((block, out), chunk * steps)
    ins = [(grad_summed, spec)] + [(p, rows_at((block, mid))) for p in pieces]
    ins += [(w, whole(w.shape)) for w in weights]
    alias = {}
    if state is not None:
        ins.append((state, KEPT))
        alias = {len(ins) - 1: 0}
    return kernel_call(
        functools.partial(input_grad_kernel, count, state is not None), "input_grad", steps, ins,
        [(grad_summed.shape, BF16, spec)], alias=alias, flops=2 * per_chunk * pixels * mid * count * out,
    )[0]


def widen_kernel(at_ref, in_ref, out_ref):
    out_ref[...] = in_ref[...].reshape(out_ref.shape).astype(F32)


def place(at, value, block, out_shape, out_block, in_map, out_map, grid):
    return pl.pallas_call(
        widen_kernel,
        grid_spec=pltpu.PrefetchScalarGridSpec(
            num_scalar_prefetch=1, grid=grid,
            in_specs=[pl.BlockSpec(block, in_map)], out_specs=pl.BlockSpec(out_block, out_map),
        ),
        out_shape=jax.ShapeDtypeStruct(out_shape, F32),
        compiler_params=pltpu.CompilerParams(vmem_limit_bytes=48 << 20),
        name="place",
    )(at, value)


def shards(
    block_input, w_reduce, w_group, w_expand, gain_one, bias_one, gain_two, bias_two,
    gain_three, bias_three, image_counts, grad_output,
):
    chan_size = lax.axis_size("chan")
    me = lax.axis_index("chan")
    height_at = lax.axis_index("height")
    images, rows, cols, out_part = block_input.shape
    mid_part, group = w_group.shape[3], w_group.shape[2]
    pixels = rows * cols
    per_image = float(pixels * lax.axis_size("height"))
    per_chunk = images // CHUNKS
    plan = (images, pixels, cols, 2, per_chunk)
    chunk_rows = per_chunk * pixels
    own_count = jnp.sum(
        jnp.where(jnp.arange(image_counts.shape[0]) == lax.axis_index("batch"), image_counts, 0)
    )
    info = jnp.stack(
        [own_count, jnp.sum(image_counts), height_at, me, jnp.where(height_at == 0, pixels - cols, 0)]
    ).astype(jnp.int32)
    mid_params = jnp.stack([gain_one, bias_one, gain_two, bias_two]).astype(F32)
    out_params = jnp.stack([gain_three, bias_three]).astype(F32)
    chunks = range(CHUNKS)
    distances = range(2, chan_size, 2)

    def edge_swap(edge):
        return permute(edge, "height", 1)

    field = block_input.reshape(images * pixels, out_part)
    grad_field = grad_output.reshape(images * pixels, out_part)
    pieces = [lax.slice_in_dim(field, c * chunk_rows, (c + 1) * chunk_rows) for c in chunks]
    inputs = [field, swap(field, 1)] + [[] for _ in range(2, chan_size)]
    for c in chunks:
        for k in distances:
            inputs[k].append(swap(pieces[c], k))
    matrices, matrices_back = block_matrices(w_group)
    state = None
    for c in chunks:
        for k in distances:
            inputs[k + 1].append(swap(inputs[k][c], 1))
        state = reduce_chunk(info, inputs, c, w_reduce, state, plan)
    reduced, red_edge, sums = state
    sums_one = spread_sums(sums)
    red_edge = edge_swap(red_edge)

    reduced, w_expand, w_reduce = lax.optimization_barrier((reduced, w_expand, w_reduce))
    expand_here = [lax.dynamic_slice_in_dim(w_expand, (me ^ k) * out_part, out_part, 1) for k in range(chan_size)]
    expand_here = expand_here[:1] + [swap(expand_here[k], k) for k in range(1, chan_size)]
    reduce_back = [lax.dynamic_slice_in_dim(w_reduce, (me ^ k) * out_part, out_part, 0) for k in range(chan_size)]
    reduce_back = reduce_back[:1] + [swap(reduce_back[k], k) for k in range(1, chan_size)]

    acts_one, grouped, grp_edge, sums = conv_forward(
        info, reduced, red_edge, sums_one, mid_params, matrices, per_image
    )
    sums_two = spread_sums(sums)
    grp_edge = edge_swap(grp_edge)

    acts = [[] for _ in range(chan_size)]
    for c in chunks:
        acts[0].append(act_two_chunk(info, grouped, sums_two, mid_params, c, plan, per_image))
        for k in distances:
            acts[k].append(swap(acts[0][c], k))
        acts[1].append(swap(acts[0][c], 1))
    state = None
    for c in chunks:
        for k in distances:
            acts[k + 1].append(swap(acts[k][c], 1))
        state = expand_chunk(info, [piece[c] for piece in acts], expand_here, c, state, plan)
    expanded, sums = state
    sums_three = spread_sums(sums)
    output, grad_summed, sums = output_pass(
        info, expanded, field, grad_field, sums_three, out_params, plan, per_image
    )
    grads_three = spread_sums(sums)

    own, sent = [], []
    grad_expanded = None
    for c in chunks:
        grad_expanded, near, far = back_expand_chunk(
            info, grad_summed, expanded, sums_three, grads_three, out_params, expand_here, c, grad_expanded, plan, per_image
        )
        summed = pair_sum(near, swap(far, 1), mid_part)
        own.append(summed[0])
        sent.append([swap(value, k) for value, k in zip(summed[1:], distances)])
    state = None
    for c in chunks:
        state = slope_two_chunk(
            info, own[c], sent[c], grouped, sums_two, mid_params, c, state, plan, per_image
        )
    d_two, d_edge, sums = state
    grads_two = spread_sums(sums)
    d_edge = edge_swap(d_edge)

    parts = lax.axis_size(REDUCE_AXES)
    expand_part = expand_grad(acts, grad_expanded, parts)
    expand_part = scatter_over(scatter_over(expand_part, "height"), "batch")

    d_one, sums, grad_group = conv_backward(
        info, d_two, d_edge, grouped, grp_edge, reduced, acts_one, sums_two, grads_two, sums_one, mid_params,
        matrices_back, group, per_image,
    )
    grads_one = spread_sums(sums)
    grad_group = lax.psum(grad_group, REDUCE_AXES).astype(F32).reshape(w_group.shape)

    grads = [[] for _ in range(chan_size)]
    for c in chunks:
        grads[0].append(grad_reduced_chunk(info, d_one, reduced, sums_one, grads_one, mid_params, c, plan, per_image))
        for k in distances:
            grads[k].append(swap(grads[0][c], k))
        grads[1].append(swap(grads[0][c], 1))
    half = chan_size // 2
    reduce_parts = [reduce_grad(inputs[i * half : (i + 1) * half], grads[0]) for i in range(2)]
    reduce_parts = [scatter_over(v, "height") for v in reduce_parts]
    reduce_parts = [scatter_over(v, "batch") for v in reduce_parts]
    reduce_parts = [gather_over(v, "batch") for v in reduce_parts]
    reduce_parts = [gather_over(v, "height") for v in reduce_parts]
    grad_input = None
    for c in chunks:
        for k in distances:
            grads[k + 1].append(swap(grads[k][c], 1))
        grad_input = input_grad_chunk(
            grad_summed, [piece[c] for piece in grads], reduce_back, c, grad_input, plan
        )

    expand_part = [expand_part[:, k] for k in range(chan_size)]
    expand_part = expand_part[:1] + [swap(expand_part[k], k) for k in range(1, chan_size)]
    expand_all = gather_over(gather_over(jnp.stack(expand_part, 1), "batch"), "height")
    at = info[CHAN_AT : CHAN_AT + 1]
    size = mid_part // parts
    grad_expand = place(
        at, expand_all, (parts, None, size, out_part), (mid_part, out_part * chan_size), (mid_part, out_part),
        lambda k, at: (0, k, 0, 0), lambda k, at: (0, at[0] ^ k), (chan_size,),
    )
    grad_reduce = place(
        at, jnp.concatenate(reduce_parts, 0), (out_part, mid_part), (out_part * chan_size, mid_part), (out_part, mid_part),
        lambda k, at: (k, 0), lambda k, at: (at[0] ^ k, 0), (chan_size,),
    )
    vectors = [jnp.sum(v, 0) for v in (grads_one, grads_two, grads_three)]
    return (
        output.reshape(block_input.shape), grad_input.reshape(block_input.shape), grad_reduce, grad_group, grad_expand,
        vectors[0][1], vectors[0][0], vectors[1][1], vectors[1][0], vectors[2][1], vectors[2][0],
    )


def solution(mesh):
    split = P("batch", "height", None, "chan")
    vector = P("chan")
    return jax.shard_map(
        shards,
        mesh=mesh,
        in_specs=(
            split, P(None, "chan"), P(None, None, None, "chan"), P("chan", None),
            vector, vector, vector, vector, vector, vector, P(), split,
        ),
        out_specs=(
            split, split, P(None, "chan"), P(None, None, None, "chan"), P("chan", None),
            vector, vector, vector, vector, vector, vector,
        ),
        check_vma=False,
    )
```

time: 413 us -> 454 us (1.099)
  Pallas kernels: 13 us -> 102 us
  other arithmetic: 49.4 us -> 6.62 us
  matrix products: 39.2 us -> 0 us
  starting transfers between devices: 49.1 us -> 80.8 us
  blocking collectives: 0 us -> 8.95 us
    pallas_call x2 -> x41, Pallas kernels: 13 us -> 102 us  [the longest x39 96.9 us: kernel_call(): pl.pallas_call(body, grid=(steps,), in_specs=[s for _, s in ins], out_spe...]
    ppermute x24 -> x77, starting transfers between devices: 20.3 us -> 61.7 us  [permute(): return lax.ppermute(value, axis, [(i, i ^ distance) for i in range(count)])]
    dot_general x24 -> x0, matrix products: 39.2 us -> none  [dot(): lax.dot_general(a, b, (contract, ((), ())), preferred_element_type=F32)]
    psum x1, waiting for transfers between devices: 85.9 us -> 56 us  [shards(): lax.psum(grad_group, REDUCE_AXES).astype(F32).reshape(w_group.shape)]
    convert_element_type x13 -> x6, other arithmetic: 21.9 us -> 2.67 us  [the longest x4 2.65 us: scatter_over(): return total.astype(value.dtype)]
    ppermute x24 -> x77, waiting for transfers between devices: 101 us -> 120 us  [permute(): return lax.ppermute(value, axis, [(i, i ^ distance) for i in range(count)])]
    reduce_sum x11 -> x4, other arithmetic: 16 us -> 0.7 us  [the longest x1 0.64 us: shards(): jnp.sum(image_counts)]
    unnamed x112 -> x160, local copies, waits for them, and re-layouts: 11.9 us -> 25.2 us
  transfers between devices with their start and end apart: 31 -> 83, of which waited for: 14 -> 28; matrix products, arithmetic and copies ran while one was open for 22% -> 5% of each run, Pallas kernels for 2% -> 15%
where the time goes in v2:
time: 454 us; the launch traced here: 452 us
  waiting for transfers between devices  196 us (43%)
  Pallas kernels  102 us (22%)
  starting transfers between devices  80.8 us (18%)
  local copies, waits for them, and re-layouts  42.4 us (9%)
  between operations  15.3 us (3%)
  blocking collectives  8.95 us (2%)
  other arithmetic  6.62 us (1%)
    ppermute x77, waiting for transfers between devices, permute(): return lax.ppermute(value, axis, [(i, i ^ distance) for i in range(count)])  120 us
    pallas_call x39, Pallas kernels, kernel_call(): pl.pallas_call(body, grid=(steps,), in_specs=[s for _, s in ins], out_spe...  96.9 us
    ppermute x77, starting transfers between devices, permute(): return lax.ppermute(value, axis, [(i, i ^ distance) for i in range(count)])  61.7 us
    psum x1, waiting for transfers between devices, shards(): lax.psum(grad_group, REDUCE_AXES).astype(F32).reshape(w_group.shape)  56 us
    unnamed x160, local copies, waits for them, and re-layouts  25.2 us
    all_to_all x5, waiting for transfers between devices, spread_sums(): return lax.all_to_all(sent, REDUCE_AXES, 0, 0)  20.3 us
    all_to_all x5, starting transfers between devices, spread_sums(): return lax.all_to_all(sent, REDUCE_AXES, 0, 0)  18.8 us
  transfers between devices with their start and end apart: 83, of which 28 were waited for; matrix products, arithmetic and copies ran while one was open for 5% of the time, Pallas kernels for 15%

profile of v2, /device:TPU:0, one launch (start us, length us, event | category | flops | bytes accessed | tf_op | source)
XLA Modules:
  0.0 452.4 jit_solution(2853560953272876108)
XLA Ops:
  14.2 10.8 %collective-permute-done.7.refs_2_.refs_0_ = bf16[512,512]{1,0:T(8,128)(2,1)} collective-permute-done((bf16[512,512]{1,0:T(8,128)(2,1)S(1)}, bf16[512,512]{1,0:T(8,128)(2,1)}, u32[]{:S(2)}, u32[]{:S(2)}) %collective-permute-start.7) | collective-permute-done | bytes 524320 | tf_op jit(solution)/shard_map/ppermute | solution.py:54
  25.0 11.2 %collective-permute-done.5.refs_2_.refs_1_ = bf16[512,512]{1,0:T(8,128)(2,1)} collective-permute-done((bf16[512,512]{1,0:T(8,128)(2,1)S(1)}, bf16[512,512]{1,0:T(8,128)(2,1)}, u32[]{:S(2)}, u32[]{:S(2)}) %collective-permute-start.5) | collective-permute-done | bytes 524320 | tf_op jit(solution)/shard_map/ppermute | solution.py:54
  36.2 11.2 %collective-permute-done.3.refs_2_ = bf16[512,512]{1,0:T(8,128)(2,1)} collective-permute-done((bf16[512,512]{1,0:T(8,128)(2,1)S(1)}, bf16[512,512]{1,0:T(8,128)(2,1)}, u32[]{:S(2)}, u32[]{:S(2)}) %collective-permute-start.3) | collective-permute-done | bytes 524320 | tf_op jit(solution)/shard_map/ppermute | solution.py:54
  47.4 11.0 %collective-permute-done.1.refs_2_.refs_3_ = bf16[512,512]{1,0:T(8,128)(2,1)} collective-permute-done((bf16[512,512]{1,0:T(8,128)(2,1)S(1)}, bf16[512,512]{1,0:T(8,128)(2,1)}, u32[]{:S(2)}, u32[]{:S(2)}) %collective-permute-start.1) | collective-permute-done | bytes 524320 | tf_op jit(solution)/shard_map/ppermute | solution.py:54
  78.8 4.9 %all-to-all-start = ((f32[8,2,256]{2,1,0:T(2,128)}), f32[8,2,256]{2,1,0:T(2,128)S(1)}, u32[]{:S(2)}, u32[]{:S(2)}) async-start(f32[8,2,256]{2,1,0:T(2,128)} %get-tuple-element.90), calls=%async_computation | async-start | bytes 32768 | tf_op jit(solution)/shard_map/all_to_all | solution.py:62
  86.5 3.8 all-to-all-done.sums_one_ref
  93.2 5.7 %conv_forward.1 = (bf16[16,128,256]{2,1,0:T(8,128)(2,1)S(1)}, f32[16,128,256]{2,1,0:T(8,128)S(1)}, f32[16,16,256]{2,1,0:T(8,128)}, f32[8,2,256]{2,1,0:T(2,128)S(1)}) custom-call(s32[5]{0:T(128)S(1)} %stack.59.info_ref, f32[16,128,256]{2,1,0:T(8,128)} %copy-done.3, f32[16,16,256]{2,1,0:T(8,128)S(1)} %copy-done.67, ...), custom_call_target="tpu_custom_call" | custom-call | flops 2415919104 | bytes 3559444 | tf_op jit(solution)/shard_map/conv_forward/pallas_call | solution.py:36
  99.9 9.0 %all_to_all.30.sums_ref.refs_2_.sums_two_ref = f32[8,2,256]{2,1,0:T(2,128)S(1)} all-to-all(f32[8,2,256]{2,1,0:T(2,128)S(1)} %get-tuple-element.93), channel_id=1, replica_groups=mesh['height'=2,'chan'=4,'batch'=4] {'height','batch'}, dimensions={0} | all-to-all | bytes 32768 | tf_op jit(solution)/shard_map/all_to_all | solution.py:62
  119.0 5.6 %collective-permute-done.23.refs_2_.refs_8_ = bf16[512,256]{1,0:T(8,128)(2,1)S(1)} collective-permute-done((bf16[512,256]{1,0:T(8,128)(2,1)S(1)}, bf16[512,256]{1,0:T(8,128)(2,1)S(1)}, u32[]{:S(2)}, u32[]{:S(2)}) %collective-permute-start.23) | collective-permute-done | bytes 262176 | tf_op jit(solution)/shard_map/ppermute | solution.py:54
  124.6 5.6 %collective-permute-done.20.refs_2_.refs_9_ = bf16[512,256]{1,0:T(8,128)(2,1)S(1)} collective-permute-done((bf16[512,256]{1,0:T(8,128)(2,1)S(1)}, bf16[512,256]{1,0:T(8,128)(2,1)S(1)}, u32[]{:S(2)}, u32[]{:S(2)}) %collective-permute-start.20) | collective-permute-done | bytes 262176 | tf_op jit(solution)/shard_map/ppermute | solution.py:54
  146.5 3.3 all-to-all-start.2
  149.9 6.6 %all-to-all-done.2.sums_three_ref = f32[8,2,512]{2,1,0:T(2,128)S(1)} async-done(((f32[8,2,512]{2,1,0:T(2,128)}), f32[8,2,512]{2,1,0:T(2,128)S(1)}, u32[]{:S(2)}, u32[]{:S(2)}) %all-to-all-start.2) | async-done | bytes 32800 | tf_op jit(solution)/shard_map/all_to_all | solution.py:62
  159.7 9.1 %output.1 = (bf16[2048,512]{1,0:T(8,128)(2,1)}, f32[2048,512]{1,0:T(8,128)}, f32[8,2,512]{2,1,0:T(2,128)}) custom-call(s32[5]{0:T(128)S(1)} %stack.59.info_ref, f32[2048,512]{1,0:T(8,128)} %get-tuple-element.101.exp_ref, bf16[2048,512]{1,0:T(8,128)(2,1)S(1)} %bitcast.35, bf16[2048,512]{1,0:T(8,128)(2,1)S(1)} %bitcast.37, ...), custom_call_target="tpu_custom_call" | custom-call | bytes 8425492 | tf_op jit(solution)/shard_map/output/pallas_call | solution.py:36
  168.8 3.5 all-to-all-start.3
  172.3 6.5 %all-to-all-done.3.grads_ref = f32[8,2,512]{2,1,0:T(2,128)S(1)} async-done(((f32[8,2,512]{2,1,0:T(2,128)}), f32[8,2,512]{2,1,0:T(2,128)S(1)}, u32[]{:S(2)}, u32[]{:S(2)}) %all-to-all-start.3) | async-done | bytes 32800 | tf_op jit(solution)/shard_map/all_to_all | solution.py:62
  182.0 3.6 back_expand.5
  185.6 3.6 back_expand.6
  189.3 3.7 back_expand.7
  195.5 3.9 expand_grad.1
  202.9 10.5 %collective-permute-done.66 = bf16[4,4,32,512]{3,2,1,0:T(8,128)(2,1)} collective-permute-done((bf16[4,4,32,512]{3,2,1,0:T(8,128)(2,1)}, bf16[4,4,32,512]{3,2,1,0:T(8,128)(2,1)}, u32[]{:S(2)}, u32[]{:S(2)}) %collective-permute-start.66) | collective-permute-done | bytes 524320 | tf_op jit(solution)/shard_map/ppermute | solution.py:54
  234.3 10.8 %collective-permute-done.30.refs_0_ = bf16[512,256]{1,0:T(8,128)(2,1)S(1)} collective-permute-done((bf16[512,256]{1,0:T(8,128)(2,1)S(1)}, bf16[512,256]{1,0:T(8,128)(2,1)S(1)}, u32[]{:S(2)}, u32[]{:S(2)}) %collective-permute-start.30) | collective-permute-done | bytes 262176 | tf_op jit(solution)/shard_map/ppermute | solution.py:54
  255.6 3.3 all-to-all-start.4
  270.4 5.4 %collective-permute-done.74 = bf16[1,4,32,512]{3,2,1,0:T(8,128)(2,1)S(1)} collective-permute-done((bf16[1,4,32,512]{3,2,1,0:T(8,128)(2,1)S(1)}, bf16[1,4,32,512]{3,2,1,0:T(8,128)(2,1)S(1)}, u32[]{:S(2)}, u32[]{:S(2)}) %collective-permute-start.74) | collective-permute-done | bytes 131104 | tf_op jit(solution)/shard_map/ppermute | solution.py:54
  282.6 9.0 %conv_backward.1 = (f32[16,128,256]{2,1,0:T(8,128)S(1)}, f32[8,2,256]{2,1,0:T(2,128)}, bf16[9,32,256]{2,1,0:T(8,128)(2,1)S(1)}) custom-call(s32[5]{0:T(128)S(1)} %stack.59.info_ref, f32[16,128,256]{2,1,0:T(8,128)} %copy-done.10, f32[16,16,256]{2,1,0:T(8,128)S(1)} %collective-permute-done.33.d_edge_ref, f32[16,128,256]{2,1,0:T(8,128)} %copy-done, ...), custom_call_target="tpu_custom_call" | custom-call | flops 4831838208 | bytes 9097236 | tf_op jit(solution)/shard_map/conv_backward/pallas_call | solution.py:36
  293.6 3.7 all-to-all-start.5
  308.7 3.6 reduce_grad.3
  316.4 56.0 %all-reduce.2.cloned.1.call-done = bf16[3,3,32,256]{3,2,1,0:T(8,128)(2,1)} async-done(((bf16[3,3,32,256]{3,2,1,0:T(8,128)(2,1)}), bf16[3,3,32,256]{3,2,1,0:T(8,128)(2,1)}) %all-reduce.2.cloned.1.call-update) | async-done | bytes 147472 | tf_op jit(solution)/shard_map/psum | solution.py:833
  380.8 3.7 place.3
  406.1 4.3 collective-permute-done.42.refs_2_
  410.5 5.5 %collective-permute-done.48.refs_2_ = bf16[512,256]{1,0:T(8,128)(2,1)S(1)} collective-permute-done((bf16[512,256]{1,0:T(8,128)(2,1)S(1)}, bf16[512,256]{1,0:T(8,128)(2,1)S(1)}, u32[]{:S(2)}, u32[]{:S(2)}) %collective-permute-start.48) | collective-permute-done | bytes 262176 | tf_op jit(solution)/shard_map/ppermute | solution.py:54
  416.5 6.0 %collective-permute-done.55 = bf16[128,256]{1,0:T(8,128)(2,1)S(1)} collective-permute-done((bf16[128,256]{1,0:T(8,128)(2,1)S(1)}, bf16[128,256]{1,0:T(8,128)(2,1)S(1)}, u32[]{:S(2)}, u32[]{:S(2)}) %collective-permute-start.55) | collective-permute-done | bytes 65568 | tf_op jit(solution)/shard_map/ppermute | solution.py:54
  424.3 4.3 collective-permute-done.56
  (393 shorter events, 188.2 us)
Async XLA Ops:
  7.2 53.2 %collective-permute-start = (bf16[2048,512]{1,0:T(8,128)(2,1)}, bf16[2048,512]{1,0:T(8,128)(2,1)S(1)}, u32[]{:S(2)}, u32[]{:S(2)}) collective-permute-start(bf16[2048,512]{1,0:T(8,128)(2,1)} %bitcast.30), channel_id=1, source_target_pairs={{0,4},{4,0},{8,12},{12,8},{1,5},{5,1},{9,13},{13,9},{2,6},{6,2},{1... | collective-permute-start | bytes 6291464 | tf_op jit(solution)/shard_map/ppermute | solution.py:54
  12.1 24.1 %collective-permute-start.5 = (bf16[512,512]{1,0:T(8,128)(2,1)S(1)}, bf16[512,512]{1,0:T(8,128)(2,1)}, u32[]{:S(2)}, u32[]{:S(2)}) collective-permute-start(bf16[512,512]{1,0:T(8,128)(2,1)S(1)} %bitcast.43), channel_id=1, source_target_pairs={{0,8},{4,12},{8,0},{12,4},{1,9},{5,13},{9,1},{13,5},{2,10},{6,14},... | collective-permute-start | bytes 1572872 | tf_op jit(solution)/shard_map/ppermute | solution.py:54
  12.1 35.3 %collective-permute-start.3 = (bf16[512,512]{1,0:T(8,128)(2,1)S(1)}, bf16[512,512]{1,0:T(8,128)(2,1)}, u32[]{:S(2)}, u32[]{:S(2)}) collective-permute-start(bf16[512,512]{1,0:T(8,128)(2,1)S(1)} %bitcast.42), channel_id=1, source_target_pairs={{0,8},{4,12},{8,0},{12,4},{1,9},{5,13},{9,1},{13,5},{2,10},{6,14},... | collective-permute-start | bytes 1572872 | tf_op jit(solution)/shard_map/ppermute | solution.py:54
  14.1 44.3 %collective-permute-start.1 = (bf16[512,512]{1,0:T(8,128)(2,1)S(1)}, bf16[512,512]{1,0:T(8,128)(2,1)}, u32[]{:S(2)}, u32[]{:S(2)}) collective-permute-start(bf16[512,512]{1,0:T(8,128)(2,1)S(1)} %bitcast.41), channel_id=1, source_target_pairs={{0,8},{4,12},{8,0},{12,4},{1,9},{5,13},{9,1},{13,5},{2,10},{6,14},... | collective-permute-start | bytes 1572872 | tf_op jit(solution)/shard_map/ppermute | solution.py:54
  24.9 35.5 %collective-permute-start.8 = (bf16[512,512]{1,0:T(8,128)(2,1)}, bf16[512,512]{1,0:T(8,128)(2,1)}, u32[]{:S(2)}, u32[]{:S(2)}) collective-permute-start(bf16[512,512]{1,0:T(8,128)(2,1)} %collective-permute-done.7.refs_2_.refs_0_), channel_id=1, source_target_pairs={{0,4},{4,0},{8,12},{12,8},{1,5},{5,1},{9,13},{13,9},{2,6},{6,2},{1... | collective-permute-start | bytes 1572872 | tf_op jit(solution)/shard_map/ppermute | solution.py:54
  36.2 28.3 %collective-permute-start.6 = (bf16[512,512]{1,0:T(8,128)(2,1)}, bf16[512,512]{1,0:T(8,128)(2,1)}, u32[]{:S(2)}, u32[]{:S(2)}) collective-permute-start(bf16[512,512]{1,0:T(8,128)(2,1)} %collective-permute-done.5.refs_2_.refs_1_), channel_id=1, source_target_pairs={{0,4},{4,0},{8,12},{12,8},{1,5},{5,1},{9,13},{13,9},{2,6},{6,2},{1... | collective-permute-start | bytes 1572872 | tf_op jit(solution)/shard_map/ppermute | solution.py:54
  47.4 19.9 %collective-permute-start.4 = (bf16[512,512]{1,0:T(8,128)(2,1)}, bf16[512,512]{1,0:T(8,128)(2,1)}, u32[]{:S(2)}, u32[]{:S(2)}) collective-permute-start(bf16[512,512]{1,0:T(8,128)(2,1)} %collective-permute-done.3.refs_2_), channel_id=1, source_target_pairs={{0,4},{4,0},{8,12},{12,8},{1,5},{5,1},{9,13},{13,9},{2,6},{6,2},{1... | collective-permute-start | bytes 1572872 | tf_op jit(solution)/shard_map/ppermute | solution.py:54
  74.4 15.9 %collective-permute-start.9 = (f32[16,16,256]{2,1,0:T(8,128)}, f32[16,16,256]{2,1,0:T(8,128)S(1)}, u32[]{:S(2)}, u32[]{:S(2)}) collective-permute-start(f32[16,16,256]{2,1,0:T(8,128)} %get-tuple-element.89), channel_id=1, source_target_pairs={{0,16},{16,0},{1,17},{17,1},{2,18},{18,2},{3,19},{19,3},{4,20},{20... | collective-permute-start | bytes 786440 | tf_op jit(solution)/shard_map/ppermute | solution.py:54
  84.6 28.9 %collective-permute-start.13 = (bf16[256,512]{1,0:T(8,128)(2,1)}, bf16[256,512]{1,0:T(8,128)(2,1)}, u32[]{:S(2)}, u32[]{:S(2)}) collective-permute-start(bf16[256,512]{1,0:T(8,128)(2,1)} %get-tuple-element.161), channel_id=1, source_target_pairs={{0,4},{4,0},{8,12},{12,8},{1,5},{5,1},{9,13},{13,9},{2,6},{6,2},{1... | collective-permute-start | bytes 786440 | tf_op jit(solution)/shard_map/ppermute | solution.py:54
  84.6 31.3 %collective-permute-start.14 = (bf16[256,512]{1,0:T(8,128)(2,1)}, bf16[256,512]{1,0:T(8,128)(2,1)}, u32[]{:S(2)}, u32[]{:S(2)}) collective-permute-start(bf16[256,512]{1,0:T(8,128)(2,1)} %get-tuple-element.160), channel_id=1, source_target_pairs={{0,8},{4,12},{8,0},{12,4},{1,9},{5,13},{9,1},{13,5},{2,10},{6,14},... | collective-permute-start | bytes 786440 | tf_op jit(solution)/shard_map/ppermute | solution.py:54
  86.1 30.4 %collective-permute-start.15 = (bf16[256,512]{1,0:T(8,128)(2,1)}, bf16[256,512]{1,0:T(8,128)(2,1)}, u32[]{:S(2)}, u32[]{:S(2)}) collective-permute-start(bf16[256,512]{1,0:T(8,128)(2,1)} %get-tuple-element.159), channel_id=1, source_target_pairs={{0,12},{4,8},{8,4},{12,0},{1,13},{5,9},{9,5},{13,1},{2,14},{6,10},... | collective-permute-start | bytes 786440 | tf_op jit(solution)/shard_map/ppermute | solution.py:54
  113.5 16.7 %collective-permute-start.20 = (bf16[512,256]{1,0:T(8,128)(2,1)S(1)}, bf16[512,256]{1,0:T(8,128)(2,1)S(1)}, u32[]{:S(2)}, u32[]{:S(2)}) collective-permute-start(bf16[512,256]{1,0:T(8,128)(2,1)S(1)} %act_two.6.refs_0_.refs_1_), channel_id=1, source_target_pairs={{0,8},{4,12},{8,0},{12,4},{1,9},{5,13},{9,1},{13,5},{2,10},{6,14},... | collective-permute-start | bytes 786440 | tf_op jit(solution)/shard_map/ppermute | solution.py:54
  115.9 17.3 %collective-permute-start.17 = (bf16[512,256]{1,0:T(8,128)(2,1)S(1)}, bf16[512,256]{1,0:T(8,128)(2,1)S(1)}, u32[]{:S(2)}, u32[]{:S(2)}) collective-permute-start(bf16[512,256]{1,0:T(8,128)(2,1)S(1)} %act_two.5.refs_0_.refs_2_), channel_id=1, source_target_pairs={{0,8},{4,12},{8,0},{12,4},{1,9},{5,13},{9,1},{13,5},{2,10},{6,14},... | collective-permute-start | bytes 786440 | tf_op jit(solution)/shard_map/ppermute | solution.py:54
  116.6 16.7 %collective-permute-start.19 = (bf16[512,256]{1,0:T(8,128)(2,1)S(1)}, bf16[512,256]{1,0:T(8,128)(2,1)S(1)}, u32[]{:S(2)}, u32[]{:S(2)}) collective-permute-start(bf16[512,256]{1,0:T(8,128)(2,1)S(1)} %act_two.6.refs_0_.refs_1_), channel_id=1, source_target_pairs={{0,4},{4,0},{8,12},{12,8},{1,5},{5,1},{9,13},{13,9},{2,6},{6,2},{1... | collective-permute-start | bytes 786440 | tf_op jit(solution)/shard_map/ppermute | solution.py:54
  201.8 15.6 %collective-permute-start.27 = (bf16[512,512]{1,0:T(8,128)(2,1)}, bf16[512,512]{1,0:T(8,128)(2,1)}, u32[]{:S(2)}, u32[]{:S(2)}) collective-permute-start(bf16[512,512]{1,0:T(8,128)(2,1)} %get-tuple-element.114), channel_id=1, source_target_pairs={{0,4},{4,0},{8,12},{12,8},{1,5},{5,1},{9,13},{13,9},{2,6},{6,2},{1... | collective-permute-start | bytes 1572872 | tf_op jit(solution)/shard_map/ppermute | solution.py:54
  202.3 23.5 %collective-permute-start.29 = (bf16[512,512]{1,0:T(8,128)(2,1)}, bf16[512,512]{1,0:T(8,128)(2,1)}, u32[]{:S(2)}, u32[]{:S(2)}) collective-permute-start(bf16[512,512]{1,0:T(8,128)(2,1)} %get-tuple-element.118), channel_id=1, source_target_pairs={{0,4},{4,0},{8,12},{12,8},{1,5},{5,1},{9,13},{13,9},{2,6},{6,2},{1... | collective-permute-start | bytes 1572872 | tf_op jit(solution)/shard_map/ppermute | solution.py:54
  202.3 26.2 %collective-permute-start.31 = (bf16[512,512]{1,0:T(8,128)(2,1)}, bf16[512,512]{1,0:T(8,128)(2,1)}, u32[]{:S(2)}, u32[]{:S(2)}) collective-permute-start(bf16[512,512]{1,0:T(8,128)(2,1)} %get-tuple-element.122), channel_id=1, source_target_pairs={{0,4},{4,0},{8,12},{12,8},{1,5},{5,1},{9,13},{13,9},{2,6},{6,2},{1... | collective-permute-start | bytes 1572872 | tf_op jit(solution)/shard_map/ppermute | solution.py:54
  216.1 15.8 %collective-permute-start.68 = (bf16[1,4,32,512]{3,2,1,0:T(8,128)(2,1)}, bf16[1,4,32,512]{3,2,1,0:T(8,128)(2,1)}, u32[]{:S(2)}, u32[]{:S(2)}) collective-permute-start(bf16[1,4,32,512]{3,2,1,0:T(8,128)(2,1)} %get-tuple-element.165), channel_id=1, source_target_pairs={{0,2},{1,3},{2,0},{3,1},{4,6},{5,7},{6,4},{7,5},{8,10},{9,11},{10,... | collective-permute-start | bytes 393224 | tf_op jit(solution)/shard_map/ppermute | solution.py:54
  225.8 26.2 %collective-permute-start.26 = (bf16[512,256]{1,0:T(8,128)(2,1)S(1)}, bf16[512,256]{1,0:T(8,128)(2,1)S(1)}, u32[]{:S(2)}, u32[]{:S(2)}) collective-permute-start(bf16[512,256]{1,0:T(8,128)(2,1)S(1)} %get-tuple-element.112), channel_id=1, source_target_pairs={{0,8},{4,12},{8,0},{12,4},{1,9},{5,13},{9,1},{13,5},{2,10},{6,14},... | collective-permute-start | bytes 786440 | tf_op jit(solution)/shard_map/ppermute | solution.py:54
  228.6 21.9 %collective-permute-start.28 = (bf16[512,256]{1,0:T(8,128)(2,1)S(1)}, bf16[512,256]{1,0:T(8,128)(2,1)S(1)}, u32[]{:S(2)}, u32[]{:S(2)}) collective-permute-start(bf16[512,256]{1,0:T(8,128)(2,1)S(1)} %get-tuple-element.116), channel_id=1, source_target_pairs={{0,8},{4,12},{8,0},{12,4},{1,9},{5,13},{9,1},{13,5},{2,10},{6,14},... | collective-permute-start | bytes 786440 | tf_op jit(solution)/shard_map/ppermute | solution.py:54
  231.9 15.9 %collective-permute-start.32 = (bf16[512,256]{1,0:T(8,128)(2,1)S(1)}, bf16[512,256]{1,0:T(8,128)(2,1)S(1)}, u32[]{:S(2)}, u32[]{:S(2)}) collective-permute-start(bf16[512,256]{1,0:T(8,128)(2,1)S(1)} %get-tuple-element.124), channel_id=1, source_target_pairs={{0,8},{4,12},{8,0},{12,4},{1,9},{5,13},{9,1},{13,5},{2,10},{6,14},... | collective-permute-start | bytes 786440 | tf_op jit(solution)/shard_map/ppermute | solution.py:54
  234.2 24.7 %collective-permute-start.72 = (bf16[1,32,512]{2,1,0:T(8,128)(2,1)}, bf16[1,32,512]{2,1,0:T(8,128)(2,1)S(1)}, u32[]{:S(2)}, u32[]{:S(2)}) collective-permute-start(bf16[1,32,512]{2,1,0:T(8,128)(2,1)} %get-tuple-element.175), channel_id=1, source_target_pairs={{0,12},{4,8},{8,4},{12,0},{1,13},{5,9},{9,5},{13,1},{2,14},{6,10},... | collective-permute-start | bytes 98312 | tf_op jit(solution)/shard_map/ppermute | solution.py:54
  250.5 143.0 %collective-permute-start.38 = (bf16[512,256]{1,0:T(8,128)(2,1)}, bf16[512,256]{1,0:T(8,128)(2,1)S(1)}, u32[]{:S(2)}, u32[]{:S(2)}) collective-permute-start(bf16[512,256]{1,0:T(8,128)(2,1)} %get-tuple-element.157), channel_id=1, source_target_pairs={{0,4},{4,0},{8,12},{12,8},{1,5},{5,1},{9,13},{13,9},{2,6},{6,2},{1... | collective-permute-start | bytes 786440 | tf_op jit(solution)/shard_map/ppermute | solution.py:54
  252.1 28.1 %collective-permute-start.34 = (f32[16,16,256]{2,1,0:T(8,128)}, f32[16,16,256]{2,1,0:T(8,128)}, u32[]{:S(2)}, u32[]{:S(2)}) collective-permute-start(f32[16,16,256]{2,1,0:T(8,128)} %get-tuple-element.136), channel_id=1, source_target_pairs={{0,16},{16,0},{1,17},{17,1},{2,18},{18,2},{3,19},{19,3},{4,20},{20... | collective-permute-start | bytes 786440 | tf_op jit(solution)/shard_map/ppermute | solution.py:54
  275.8 124.2 %collective-permute-start.39 = (bf16[512,256]{1,0:T(8,128)(2,1)}, bf16[512,256]{1,0:T(8,128)(2,1)S(1)}, u32[]{:S(2)}, u32[]{:S(2)}) collective-permute-start(bf16[512,256]{1,0:T(8,128)(2,1)} %get-tuple-element.156), channel_id=1, source_target_pairs={{0,8},{4,12},{8,0},{12,4},{1,9},{5,13},{9,1},{13,5},{2,10},{6,14},... | collective-permute-start | bytes 786440 | tf_op jit(solution)/shard_map/ppermute | solution.py:54
  278.7 98.1 %collective-permute-start.76 = (bf16[4,4,32,512]{3,2,1,0:T(8,128)(2,1)}, bf16[4,4,32,512]{3,2,1,0:T(8,128)(2,1)}, u32[]{:S(2)}, u32[]{:S(2)}) collective-permute-start(bf16[4,4,32,512]{3,2,1,0:T(8,128)(2,1)} %constant_dynamic-update-slice_fusion.2), channel_id=1, source_target_pairs={{0,16},{16,0},{1,17},{17,1},{2,18},{18,2},{3,19},{19,3},{4,20},{20... | collective-permute-start | bytes 1572872 | tf_op jit(solution)/shard_map/ppermute | solution.py:54
  297.4 75.1 %all-reduce.2.cloned.1.call-start = ((), (), s32[]{:S(2)}) async-start(), calls=%async_computation.6 | async-start | bytes 294912 | tf_op jit(solution)/shard_map/psum | solution.py:833
  312.3 61.8 %collective-permute-start.58 = (bf16[512,256]{1,0:T(8,128)(2,1)S(1)}, bf16[512,256]{1,0:T(8,128)(2,1)S(1)}, u32[]{:S(2)}, u32[]{:S(2)}) collective-permute-start(bf16[512,256]{1,0:T(8,128)(2,1)S(1)} %constant_dynamic-slice_fusion.7), channel_id=1, source_target_pairs={{0,16},{16,0},{1,17},{17,1},{2,18},{18,2},{3,19},{19,3},{4,20},{20... | collective-permute-start | bytes 786440 | tf_op jit(solution)/shard_map/ppermute | solution.py:54
  314.3 62.3 %collective-permute-start.50 = (bf16[512,256]{1,0:T(8,128)(2,1)S(1)}, bf16[512,256]{1,0:T(8,128)(2,1)S(1)}, u32[]{:S(2)}, u32[]{:S(2)}) collective-permute-start(bf16[512,256]{1,0:T(8,128)(2,1)S(1)} %constant_dynamic-slice_fusion.11), channel_id=1, source_target_pairs={{0,16},{16,0},{1,17},{17,1},{2,18},{18,2},{3,19},{19,3},{4,20},{20... | collective-permute-start | bytes 786440 | tf_op jit(solution)/shard_map/ppermute | solution.py:54
  405.0 19.2 %collective-permute-start.45 = (bf16[512,256]{1,0:T(8,128)(2,1)S(1)}, bf16[512,256]{1,0:T(8,128)(2,1)S(1)}, u32[]{:S(2)}, u32[]{:S(2)}) collective-permute-start(bf16[512,256]{1,0:T(8,128)(2,1)S(1)} %copy-done.15), channel_id=1, source_target_pairs={{0,8},{4,12},{8,0},{12,4},{1,9},{5,13},{9,1},{13,5},{2,10},{6,14},... | collective-permute-start | bytes 786440 | tf_op jit(solution)/shard_map/ppermute | solution.py:54
  406.0 22.6 %collective-permute-start.44 = (bf16[512,256]{1,0:T(8,128)(2,1)S(1)}, bf16[512,256]{1,0:T(8,128)(2,1)S(1)}, u32[]{:S(2)}, u32[]{:S(2)}) collective-permute-start(bf16[512,256]{1,0:T(8,128)(2,1)S(1)} %copy-done.15), channel_id=1, source_target_pairs={{0,4},{4,0},{8,12},{12,8},{1,5},{5,1},{9,13},{13,9},{2,6},{6,2},{1... | collective-permute-start | bytes 786440 | tf_op jit(solution)/shard_map/ppermute | solution.py:54
  410.4 18.8 %collective-permute-start.47 = (bf16[512,256]{1,0:T(8,128)(2,1)S(1)}, bf16[512,256]{1,0:T(8,128)(2,1)S(1)}, u32[]{:S(2)}, u32[]{:S(2)}) collective-permute-start(bf16[512,256]{1,0:T(8,128)(2,1)S(1)} %copy-done.17), channel_id=1, source_target_pairs={{0,4},{4,0},{8,12},{12,8},{1,5},{5,1},{9,13},{13,9},{2,6},{6,2},{1... | collective-permute-start | bytes 786440 | tf_op jit(solution)/shard_map/ppermute | solution.py:54
  (131 other events, 1324.5 us)
Sparse Core Ops, SparseCore 0:
  302.1 70.3 all-reduce.1

commit v3 on v0

v3 whole, which is shorter than its diff:
```python
import functools

import jax
import jax.numpy as jnp
from jax import lax
from jax.experimental import pallas as pl
from jax.experimental.pallas import tpu as pltpu
from jax.sharding import PartitionSpec as P

EPSILON = 1e-05
F32, BF16 = jnp.float32, jnp.bfloat16
REDUCE_AXES = ("height", "batch")
REDUCE_CHUNKS, EXPAND_CHUNKS, BACK_CHUNKS = (12, 4), (8, 8), (4, 8, 4)
OWN_COUNT, TOTAL_COUNT, HEIGHT_AT, CHAN_AT, EDGE_ROW, BATCH_AT = range(6)
VMEM = pl.BlockSpec(memory_space=pltpu.VMEM)
SMEM = pl.BlockSpec(memory_space=pltpu.SMEM)


def dot(a, b, left, right):
    return lax.dot_general(a, b, (((left,), (right,)), ((), ())), preferred_element_type=F32)


def kernel_call(body, name, ins, outs, scratch=(), alias=None, flops=0, heavy=0, room=16):
    moved = sum(a.size * a.dtype.itemsize for a in ins)
    return pl.pallas_call(
        body,
        in_specs=[SMEM if a.dtype == jnp.int32 else VMEM for a in ins],
        out_specs=[VMEM] * len(outs),
        out_shape=[jax.ShapeDtypeStruct(shape, dtype) for shape, dtype in outs],
        scratch_shapes=list(scratch),
        input_output_aliases=alias or {},
        compiler_params=pltpu.CompilerParams(vmem_limit_bytes=room << 20),
        cost_estimate=pl.CostEstimate(flops=flops, bytes_accessed=moved, transcendentals=heavy),
        name=name,
    )(*ins)


def after(value, *others):
    return lax.optimization_barrier((value,) + others)[0]


def permute(value, axis, distance):
    count = lax.axis_size(axis)
    return lax.ppermute(value, axis, [(i, i ^ distance) for i in range(count)])


def swap(value, distance):
    return permute(value, "chan", distance)


def spread_sums(sent):
    return lax.all_to_all(sent, REDUCE_AXES, 0, 0)


def norm_of(sums_ref, total):
    sums = jnp.sum(sums_ref[...], 0)
    average = sums[0:1] / total
    return average, lax.rsqrt(sums[1:2] / total - average * average + EPSILON)


def pixel_count(info_ref, per_image):
    return info_ref[TOTAL_COUNT].astype(F32) * per_image


def sigmoid(v):
    return 0.5 * jnp.tanh(0.5 * v) + 0.5


def silu_slope(v):
    logistic = sigmoid(v)
    return logistic * (1.0 + v * (1.0 - logistic))


def fold(values):
    rows, chans = values.shape
    return jnp.sum(values.reshape(rows // 8, 8, chans), 0)


def put_sums(out_ref, one, two):
    if out_ref.shape[1] == 8:
        out_ref[0] = one
        out_ref[1] = two
    else:
        both = jnp.concatenate([jnp.sum(one, 0, keepdims=True), jnp.sum(two, 0, keepdims=True)], 0)
        out_ref[...] = jnp.broadcast_to(both[None], out_ref.shape)


def sums_out(last, chans):
    return ((lax.axis_size(REDUCE_AXES), 2, chans) if last else (2, 8, chans), F32)


def before_sums(before_ref, chans):
    if before_ref is None:
        zero = jnp.zeros((8, chans), F32)
        return zero, zero
    return before_ref[0], before_ref[1]


def edge_rows(info_ref, ref, image, cols):
    return ref[image, pl.ds(pl.multiple_of(info_ref[EDGE_ROW], 16), cols), :]


def prepare_kernel(group, info_ref, taps_ref, mid_a, mid_b, mid_c, mid_d, out_a, out_b, fwd_ref, back_ref, mid_ref, out_ref):
    chans = taps_ref.shape[2]
    same = (
        lax.broadcasted_iota(jnp.int32, (chans, chans), 0) // group
        == lax.broadcasted_iota(jnp.int32, (chans, chans), 1) // group
    )
    for i in range(3):
        for j in range(3):
            wide = jnp.concatenate([taps_ref[3 * i + j].astype(F32)] * (chans // group), 0)
            wide = jnp.where(same, wide, 0.0)
            fwd_ref[i, j * chans : (j + 1) * chans, :] = wide.astype(BF16)
            back_ref[2 - i, (2 - j) * chans : (3 - j) * chans, :] = wide.T.astype(BF16)
    for row, ref in enumerate((mid_a, mid_b, mid_c, mid_d)):
        mid_ref[row : row + 1, :] = ref[...].astype(F32)
    for row, ref in enumerate((out_a, out_b)):
        out_ref[row : row + 1, :] = ref[...].astype(F32)


def prepare(info, kernel, mid_vectors, out_vectors):
    group, chans = kernel.shape[2], kernel.shape[3]
    wide = (3, 3 * chans, chans)
    rows = [v.reshape(1, -1) for v in list(mid_vectors) + list(out_vectors)]
    return kernel_call(
        functools.partial(prepare_kernel, group), "prepare", [info, kernel.reshape(9, group, chans)] + rows,
        [(wide, BF16), (wide, BF16), ((4, chans), F32), ((2, rows[-1].shape[1]), F32)],
    )


def cut_images(shares):
    return [(sum(shares[:i]), share) for i, share in enumerate(shares)]


def reduce_kernel(first, plan, count, info_ref, *refs):
    pixels, cols = plan
    pieces, w_ref, before_ref = refs[:count], refs[count], None if len(refs) == count + 4 else refs[count + 1]
    red_ref, edge_ref, sums_ref = refs[-3:]
    me = info_ref[CHAN_AT]
    part, images = pieces[0].shape[1], red_ref.shape[0]
    one, two = before_sums(before_ref, w_ref.shape[1])
    step = min(4, images)
    for start in range(0, images, step):
        total = None
        for k in range(count):
            rows = w_ref[pl.ds(pl.multiple_of((me ^ k) * part, part), part), :]
            term = dot(pieces[k][start * pixels : (start + step) * pixels, :], rows, 1, 0)
            total = term if total is None else total + term
        for i in range(start, start + step):
            value = total[(i - start) * pixels : (i - start + 1) * pixels]
            red_ref[i] = value
            edge_ref[i] = edge_rows(info_ref, red_ref, i, cols).astype(BF16)
            value = value * (first + i < info_ref[OWN_COUNT]).astype(F32)
            one, two = one + fold(value), two + fold(value * value)
    put_sums(sums_ref, one, two)


def reduce_chunk(info, pieces, chunk, w_reduce, before, images, plan):
    pixels, cols = plan
    first, share = chunk
    count, mid = len(pieces), w_reduce.shape[1]
    ins = [info] + list(pieces) + [w_reduce] + ([] if before is None else [before])
    return kernel_call(
        functools.partial(reduce_kernel, first, plan, count), "reduce", ins,
        [((share, pixels, mid), F32), ((share, cols, mid), BF16), sums_out(first + share == images, mid)],
        flops=2 * pieces[0].size * count * mid,
    )


def each_image(chunks, body, carry, step=1):
    first = 0
    for refs in chunks:
        count = refs[0].shape[0]
        start = first
        carry = lax.fori_loop(
            0, count // step, lambda i, c, refs=refs, start=start: body(refs, i * step, start + i * step, c), carry
        )
        first += count
    return carry


def fill_windows(window_ref, slot, value, cols):
    rows, chans = value.shape
    place = lax.broadcasted_iota(jnp.int32, value.shape, 0) % cols
    left = jnp.where(place == 0, 0.0, pltpu.roll(value, 1, 0))
    right = jnp.where(place == cols - 1, 0.0, pltpu.roll(value, rows - 1, 0))
    window_ref[slot, :, 0:chans] = left.astype(BF16)
    window_ref[slot, :, chans : 2 * chans] = value.astype(BF16)
    window_ref[slot, :, 2 * chans : 3 * chans] = right.astype(BF16)


def with_edges(info_ref, own, edge):
    low = (info_ref[HEIGHT_AT] > 0).astype(F32)
    return jnp.concatenate([edge * low, own, edge * (1.0 - low)], 0)


def conv_forward_kernel(
    per_image, group_images, count, info_ref, *refs
):
    fields = list(zip(refs[:count], refs[count : 2 * count]))
    sums_one_ref, par_ref, mat_ref, act_ref, out_ref, out_edge_ref, sums_ref, window_ref = refs[2 * count :]
    images, pixels, chans = act_ref.shape
    cols = out_edge_ref.shape[1]
    average, inv_std = norm_of(sums_one_ref, pixel_count(info_ref, per_image))
    scale, bias = inv_std * par_ref[0:1, :], par_ref[1:2, :]

    def activate(v, keep):
        pre = (v - average) * scale + bias
        return pre * sigmoid(pre) * keep

    def fill(refs, at, image, nothing):
        keep = (image < info_ref[OWN_COUNT]).astype(F32)
        own = activate(refs[0][at], keep)
        edge = activate(refs[1][at].astype(F32), keep)
        act_ref[image] = own.astype(BF16)
        fill_windows(window_ref, image, with_edges(info_ref, own, edge), cols)
        return nothing

    def convolve(step, sums):
        first = step * group_images
        total = None
        for i in range(3):
            piece = window_ref[pl.ds(first, group_images), i * cols : i * cols + pixels, :]
            term = dot(piece.reshape(group_images * pixels, 3 * chans), mat_ref[i], 1, 0)
            total = term if total is None else total + term
        out_ref[pl.ds(first, group_images)] = total.reshape(group_images, pixels, chans)
        for i in range(group_images):
            out_edge_ref[first + i] = edge_rows(info_ref, out_ref, first + i, cols).astype(BF16)
        return sums[0] + fold(total), sums[1] + fold(total * total)

    each_image(fields, fill, 0)
    zero = jnp.zeros((8, chans), F32)
    put_sums(sums_ref, *lax.fori_loop(0, images // group_images, convolve, (zero, zero)))


def conv_forward(info, reduced, edges, sums_one, params, matrices, per_image):
    images = sum(v.shape[0] for v in reduced)
    pixels, chans = reduced[0].shape[1:]
    cols = edges[0].shape[1]
    shape = (images, pixels, chans)
    return kernel_call(
        functools.partial(conv_forward_kernel, per_image, 4, len(reduced)), "conv_forward",
        [info, *reduced, *edges, sums_one, params, matrices],
        [(shape, BF16), (shape, F32), ((images, cols, chans), BF16), sums_out(True, chans)],
        [pltpu.VMEM((images, pixels + 2 * cols, 3 * chans), BF16)],
        flops=18 * images * pixels * chans * chans, heavy=images * pixels * chans,
    )


def act_two_kernel(chunk, plan, per_image, info_ref, grp_ref, sums_ref, par_ref, out_ref):
    pixels, cols = plan
    first, images = chunk
    average, inv_std = norm_of(sums_ref, pixel_count(info_ref, per_image))
    scale, bias = inv_std * par_ref[2:3, :], par_ref[3:4, :]
    for i in range(images):
        image = first + i
        pre = (grp_ref[image] - average) * scale + bias
        act = pre * sigmoid(pre) * (image < info_ref[OWN_COUNT]).astype(F32)
        out_ref[i * pixels : (i + 1) * pixels] = act.astype(BF16)


def act_two_chunk(info, grouped, sums_two, params, chunk, plan, per_image):
    pixels, cols = plan
    shape = (chunk[1] * pixels, grouped.shape[2])
    return kernel_call(
        functools.partial(act_two_kernel, chunk, plan, per_image), "act_two",
        [info, grouped, sums_two, params], [(shape, BF16)], heavy=shape[0] * shape[1],
    )[0]


def expand_kernel(first, plan, count, mid, info_ref, *refs):
    pixels, cols = plan
    acts, weights = refs[:count], refs[count : 2 * count]
    before_ref = None if len(refs) == 2 * count + 2 else refs[2 * count]
    out_ref, sums_ref = refs[-2:]
    images = out_ref.shape[0]
    one, two = before_sums(before_ref, out_ref.shape[2])
    step = min(4, images)
    for start in range(0, images, step):
        total = None
        for a_ref, w_ref in zip(acts, weights):
            term = dot(a_ref[start * pixels : (start + step) * pixels, :], w_ref[0:mid, :], 1, 0)
            total = term if total is None else total + term
        out_ref[start : start + step] = total.reshape(step, pixels, total.shape[1])
        for i in range(step):
            keep = (first + start + i < info_ref[OWN_COUNT]).astype(F32)
            value = total[i * pixels : (i + 1) * pixels] * keep
            one, two = one + fold(value), two + fold(value * value)
    put_sums(sums_ref, one, two)


def expand_chunk(info, acts, weights, chunk, before, images, plan):
    pixels, cols = plan
    first, share = chunk
    count, mid, out = len(acts), acts[0].shape[1], weights[0].shape[1]
    ins = [info] + list(acts) + list(weights) + ([] if before is None else [before])
    return kernel_call(
        functools.partial(expand_kernel, first, plan, count, mid), "expand", ins,
        [((share, pixels, out), F32), sums_out(first + share == images, out)],
        flops=2 * acts[0].size * count * out,
    )


def output_kernel(per_image, count, info_ref, *refs):
    expanded = [[v] for v in refs[:count]]
    in_ref, go_ref, sums_three_ref, par_ref, out_ref, grad_ref, sums_ref = refs[count:]
    average, inv_std = norm_of(sums_three_ref, pixel_count(info_ref, per_image))
    gain, bias = par_ref[0:1, :], par_ref[1:2, :]
    chans = out_ref.shape[2]

    def body(refs, at, image, sums):
        keep = (image < info_ref[OWN_COUNT]).astype(F32)
        normalized = (refs[0][at] - average) * inv_std
        summed = normalized * gain + bias + in_ref[image].astype(F32)
        logistic = sigmoid(summed)
        out_ref[image] = (summed * logistic * keep).astype(BF16)
        slope = logistic * (1.0 + summed * (1.0 - logistic))
        grad = go_ref[image].astype(F32) * (slope * keep)
        grad_ref[image] = grad
        return sums[0] + fold(grad), sums[1] + fold(grad * normalized)

    zero = jnp.zeros((8, chans), F32)
    put_sums(sums_ref, *each_image(expanded, body, (zero, zero)))


def output_pass(info, expanded, field, grad_output, sums_three, params, per_image):
    return kernel_call(
        functools.partial(output_kernel, per_image, len(expanded)), "output",
        [info, *expanded, field, grad_output, sums_three, params],
        [(field.shape, BF16), (field.shape, F32), sums_out(True, field.shape[2])],
        heavy=field.size,
    )


def at_image(refs, image):
    for ref in refs:
        if image < ref.shape[0]:
            return ref[image]
        image -= ref.shape[0]


def back_expand_kernel(first, plan, count, mid, fields, per_image, info_ref, *refs):
    pixels, cols = plan
    expanded, refs = refs[:fields], refs[fields:]
    grad_ref, sums_three_ref, grads_ref, par_ref = refs[:4]
    weights = refs[4 : 4 + count]
    out_ref, near_ref, far_ref = refs[-3:]
    total = pixel_count(info_ref, per_image)
    average, inv_std = norm_of(sums_three_ref, total)
    grads = jnp.sum(grads_ref[...], 0)
    scale = inv_std * par_ref[0:1, :]
    bias_part, gain_part = grads[0:1] / total, grads[1:2] / total * inv_std
    for i in range(out_ref.shape[0] // pixels):
        image = first + i
        value = grad_ref[image] - (bias_part + (at_image(expanded, image) - average) * gain_part)
        value = value * (scale * (image < info_ref[OWN_COUNT]).astype(F32))
        out_ref[i * pixels : (i + 1) * pixels, :] = value.astype(BF16)
    for k in range(count):
        term = dot(out_ref[...], weights[k][0:mid, :], 1, 1)
        to = slice((k // 2) * mid, (k // 2 + 1) * mid)
        if k % 2 == 0:
            near_ref[:, to] = term
        else:
            far_ref[:, to] = term.astype(BF16)


def back_expand_chunk(info, grad_summed, expanded, sums_three, grads_three, params, weights, chunk, mid, plan, per_image):
    pixels, cols = plan
    count, out = len(weights), grad_summed.shape[2]
    block, half = chunk[1] * pixels, count // 2 * mid
    return kernel_call(
        functools.partial(back_expand_kernel, chunk[0], plan, count, mid, len(expanded), per_image), "back_expand",
        [info, *expanded, grad_summed, sums_three, grads_three, params, *weights],
        [((block, out), BF16), ((block, half), F32), ((block, half), BF16)],
        flops=2 * block * mid * count * out,
    )


def pair_sum_kernel(near_ref, far_ref, own_ref, *send_refs):
    mid = own_ref.shape[1]
    for k, ref in enumerate((own_ref,) + send_refs):
        at = slice(k * mid, (k + 1) * mid)
        ref[...] = (near_ref[:, at] + far_ref[:, at].astype(F32)).astype(ref.dtype)


def pair_sum(near, far, mid):
    rows, half = near.shape
    return kernel_call(
        pair_sum_kernel, "pair_sum", [near, far],
        [((rows, mid), F32 if k == 0 else BF16) for k in range(half // mid)],
    )


def slope_two_kernel(first, plan, count, per_image, info_ref, own_ref, *refs):
    pixels, cols = plan
    arrived, refs = refs[:count], refs[count:]
    grp_ref, sums_two_ref, par_ref = refs[:3]
    before_ref = None if len(refs) == 6 else refs[3]
    out_ref, edge_ref, sums_ref = refs[-3:]
    average, inv_std = norm_of(sums_two_ref, pixel_count(info_ref, per_image))
    gain, bias = par_ref[2:3, :], par_ref[3:4, :]
    one, two = before_sums(before_ref, grp_ref.shape[2])
    for i in range(out_ref.shape[0]):
        image = first + i
        at = slice(i * pixels, (i + 1) * pixels)
        grad = own_ref[at, :]
        for ref in arrived:
            grad = grad + ref[at, :].astype(F32)
        normalized = (grp_ref[image] - average) * inv_std
        keep = (image < info_ref[OWN_COUNT]).astype(F32)
        grad = grad * (silu_slope(normalized * gain + bias) * keep)
        out_ref[i] = grad
        edge_ref[i] = edge_rows(info_ref, out_ref, i, cols).astype(BF16)
        one, two = one + fold(grad), two + fold(grad * normalized)
    put_sums(sums_ref, one, two)


def slope_two_chunk(info, own, arrived, grouped, sums_two, params, chunk, before, plan, per_image):
    pixels, cols = plan
    first, share = chunk
    images, mid = grouped.shape[0], grouped.shape[2]
    ins = [info, own] + list(arrived) + [grouped, sums_two, params] + ([] if before is None else [before])
    return kernel_call(
        functools.partial(slope_two_kernel, first, plan, len(arrived), per_image), "slope_two", ins,
        [((share, pixels, mid), F32), ((share, cols, mid), BF16), sums_out(first + share == images, mid)],
        heavy=own.size,
    )


def conv_backward_kernel(
    per_image, group_images, group, d_count, red_count, info_ref, *refs
):
    d_fields, refs = list(zip(refs[:d_count], refs[d_count : 2 * d_count])), refs[2 * d_count :]
    reduced, refs = [[v] for v in refs[:red_count]], refs[red_count:]
    grp_ref, g_edge_ref, act_ref, sums_two_ref, grads_two_ref, sums_one_ref, par_ref, mat_ref = refs[:8]
    out_ref, sums_ref, kernel_ref, window_ref, turned_ref = refs[8:]
    images, pixels, chans = act_ref.shape
    cols = g_edge_ref.shape[1]
    total_pixels = pixel_count(info_ref, per_image)
    avg_two, inv_two = norm_of(sums_two_ref, total_pixels)
    grads = jnp.sum(grads_two_ref[...], 0)
    bias_part, gain_part = grads[0:1] / total_pixels, grads[1:2] / total_pixels * inv_two
    scale_two = inv_two * par_ref[2:3, :]
    avg_one, inv_one = norm_of(sums_one_ref, total_pixels)
    gain_one, bias_one = par_ref[0:1, :], par_ref[1:2, :]

    def input_grad(d, grouped, keep):
        return (d - (bias_part + (grouped - avg_two) * gain_part)) * (scale_two * keep)

    def fill(refs, at, image, nothing):
        keep = (image < info_ref[OWN_COUNT]).astype(F32)
        own = input_grad(refs[0][at], grp_ref[image], keep)
        edge = input_grad(refs[1][at].astype(F32), g_edge_ref[image].astype(F32), keep)
        fill_windows(window_ref, image, with_edges(info_ref, own, edge), cols)
        turned_ref[:, pl.ds(pl.multiple_of(image * pixels, pixels), pixels)] = act_ref[image].T
        return nothing

    def convolve(refs, at, first, sums):
        grad = None
        for i in range(3):
            piece = window_ref[pl.ds(first, group_images), i * cols : i * cols + pixels, :]
            term = dot(piece.reshape(group_images * pixels, 3 * chans), mat_ref[i], 1, 0)
            grad = term if grad is None else grad + term
        one, two = sums
        for i in range(group_images):
            image = first + i
            keep = (image < info_ref[OWN_COUNT]).astype(F32)
            normalized = (refs[0][at + i] - avg_one) * inv_one
            slope = silu_slope(normalized * gain_one + bias_one)
            d_one = grad[i * pixels : (i + 1) * pixels] * (slope * keep)
            out_ref[image] = d_one
            one, two = one + fold(d_one), two + fold(d_one * normalized)
        return one, two

    each_image(d_fields, fill, 0)
    zero = jnp.zeros((8, chans), F32)
    put_sums(sums_ref, *each_image(reduced, convolve, (zero, zero), group_images))
    same = (
        lax.broadcasted_iota(jnp.int32, (chans, 3 * chans), 0) // group
        == lax.broadcasted_iota(jnp.int32, (chans, 3 * chans), 1) % chans // group
    )
    for i in range(3):
        total = None
        for first in range(0, images, group_images):
            piece = window_ref[first : first + group_images, i * cols : i * cols + pixels, :]
            turned = turned_ref[:, first * pixels : (first + group_images) * pixels]
            term = dot(turned, piece.reshape(group_images * pixels, 3 * chans), 1, 0)
            total = term if total is None else total + term
        total = jnp.sum(jnp.where(same, total, 0.0).reshape(chans // group, group, 3 * chans), 0)
        for j in range(3):
            kernel_ref[3 * (2 - i) + 2 - j] = total[:, j * chans : (j + 1) * chans].astype(kernel_ref.dtype)


def conv_backward(info, d_two, d_edges, grouped, g_edge, reduced, acts, sums_two, grads_two, sums_one, params, matrices,
                  group, per_image):
    images, pixels, chans = grouped.shape
    cols = g_edge.shape[1]
    return kernel_call(
        functools.partial(conv_backward_kernel, per_image, 4, group, len(d_two), len(reduced)), "conv_backward",
        [info, *d_two, *d_edges, *reduced, grouped, g_edge, acts, sums_two, grads_two, sums_one, params, matrices],
        [(grouped.shape, F32), sums_out(True, chans), ((9, group, chans), F32)],
        [
            pltpu.VMEM((images, pixels + 2 * cols, 3 * chans), BF16),
            pltpu.VMEM((chans, images * pixels), BF16),
        ],
        flops=36 * images * pixels * chans * chans, heavy=images * pixels * chans,
    )


def grad_reduced_kernel(per_image, count, info_ref, *refs):
    reduced = [[v] for v in refs[:count]]
    d_ref, sums_one_ref, grads_ref, par_ref, out_ref = refs[count:]
    pixels = d_ref.shape[1]
    total = pixel_count(info_ref, per_image)
    average, inv_std = norm_of(sums_one_ref, total)
    grads = jnp.sum(grads_ref[...], 0)
    bias_part, gain_part = grads[0:1] / total, grads[1:2] / total * inv_std
    scale = inv_std * par_ref[0:1, :]

    def body(refs, at, image, nothing):
        value = d_ref[image] - (bias_part + (refs[0][at] - average) * gain_part)
        value = value * (scale * (image < info_ref[OWN_COUNT]).astype(F32))
        out_ref[pl.ds(pl.multiple_of(image * pixels, pixels), pixels), :] = value.astype(BF16)
        return nothing

    each_image(reduced, body, 0)


def grad_reduced(info, d_one, reduced, sums_one, grads_one, params, per_image):
    images, pixels, mid = d_one.shape
    return kernel_call(
        functools.partial(grad_reduced_kernel, per_image, len(reduced)), "grad_reduced",
        [info, *reduced, d_one, sums_one, grads_one, params], [((images * pixels, mid), BF16)],
    )[0]


def input_grad_kernel(count, mid, grad_ref, *refs):
    pieces, weights, out_ref = refs[:count], refs[count : 2 * count], refs[-1]
    rows = 512

    def body(step, nothing):
        at = pl.ds(pl.multiple_of(step * rows, rows), rows)
        total = grad_ref[at, :]
        for p_ref, w_ref in zip(pieces, weights):
            total = total + dot(p_ref[at, :], w_ref[mid : 2 * mid, :], 1, 0)
        out_ref[at, :] = total.astype(BF16)
        return nothing

    lax.fori_loop(0, grad_ref.shape[0] // rows, body, 0)


def input_grad(grad_summed, pieces, weights):
    count, mid = len(pieces), pieces[0].shape[1]
    return kernel_call(
        functools.partial(input_grad_kernel, count, mid), "input_grad", [grad_summed] + list(pieces) + list(weights),
        [(grad_summed.shape, BF16)], flops=2 * pieces[0].size * count * grad_summed.shape[1],
    )[0]


def cut_weights_kernel(count, info_ref, reduce_ref, expand_ref, *refs):
    me = info_ref[CHAN_AT]
    mid = expand_ref.shape[0]
    for k, ref in enumerate(refs):
        part = ref.shape[1]
        at = pl.ds(pl.multiple_of((me ^ k) * part, part), part)
        ref[0:mid, :] = expand_ref[:, at]
        ref[mid : 2 * mid, :] = reduce_ref[at, :].T


def cut_weights(info, w_reduce, w_expand, count):
    part, mid = w_reduce.shape[0] // count, w_reduce.shape[1]
    return kernel_call(
        functools.partial(cut_weights_kernel, count), "cut_weights", [info, w_reduce, w_expand],
        [((2 * mid, part), BF16)] * count,
    )


def sum_vectors_kernel(*refs):
    half = len(refs) // 3
    for ref, out_one, out_two in zip(refs[:half], refs[half::2], refs[half + 1 :: 2]):
        sums = jnp.sum(ref[...], 0)
        out_one[...] = sums[0:1]
        out_two[...] = sums[1:2]


def sum_vectors(values):
    outs = [((1, v.shape[2]), F32) for v in values for _ in range(2)]
    return [v.reshape(-1) for v in kernel_call(sum_vectors_kernel, "sum_vectors", list(values), outs)]


def split(at, keep_ref, send_ref, all_ref, arrived_ref):
    half = keep_ref.shape[0]
    for to, ref in ((at, keep_ref), (1 - at, send_ref)):
        value = all_ref[pl.ds(to * half, half)]
        if arrived_ref is not None:
            value = value + arrived_ref[pl.ds(to * half, half)].astype(F32)
        ref[...] = value.astype(ref.dtype)


def split_first_kernel(make, info_ref, *refs):
    keep_ref, send_ref, all_ref = refs[-3:]
    make(refs[:-3], all_ref)
    split(info_ref[HEIGHT_AT], keep_ref, send_ref, all_ref, None)


def split_first(info, make, name, ins, shape, flops):
    half = (shape[0] // 2,) + shape[1:]
    return kernel_call(
        functools.partial(split_first_kernel, make), name, [info] + ins, [(half, F32), (half, BF16)],
        [pltpu.VMEM(shape, F32)], flops=flops,
    )


def split_next_kernel(bit, info_ref, keep_ref, arrived_ref, out_ref, send_ref):
    split((info_ref[BATCH_AT] >> bit) & 1, out_ref, send_ref, keep_ref, arrived_ref)


def split_next(info, bit, keep, arrived):
    half = (keep.shape[0] // 2,) + keep.shape[1:]
    return kernel_call(
        functools.partial(split_next_kernel, bit), "split_next", [info, keep, arrived], [(half, F32), (half, BF16)]
    )


def add_kernel(first_ref, second_ref, out_ref):
    out_ref[...] = (first_ref[...] + second_ref[...].astype(F32)).astype(BF16)


def add_last(keep, arrived):
    return kernel_call(add_kernel, "add_last", [keep, arrived], [(keep.shape, BF16)])[0]


def join_kernel(*refs):
    size = refs[0].shape[0]
    for k, ref in enumerate(refs[:-1]):
        refs[-1][k * size : (k + 1) * size] = ref[...]


def join(*values):
    shape = (values[0].shape[0] * len(values),) + values[0].shape[1:]
    return kernel_call(join_kernel, "join", list(values), [(shape, BF16)])[0]


def batch_distance(bit):
    return lax.axis_size("batch") >> (bit + 1)


def scatter_height(pair):
    return pair[0], permute(pair[1], "height", 1)


def scatter_batch(info, pair):
    for bit in reversed(range(lax.axis_size("batch").bit_length() - 1)):
        keep, send = split_next(info, bit, *pair)
        pair = keep, permute(send, "batch", batch_distance(bit))
    return add_last(*pair)


def gather_batch(value):
    for bit in range(lax.axis_size("batch").bit_length() - 1):
        value = join(value, permute(value, "batch", batch_distance(bit)))
    return value


def gather_height(value):
    return value, permute(value, "height", 1)


def reduce_grad_make(places, spans, extra, refs, all_ref):
    grad_ref = refs[places * len(spans)]
    parts = all_ref.shape[0]
    per = parts // places
    for k in range(places):
        total = None
        for c, (first, end) in enumerate(spans):
            term = dot(refs[k * len(spans) + c][...], grad_ref[first:end, :], 0, 0)
            total = term if total is None else total + term
        size = total.shape[0] // per
        all_ref[k * per : (k + 1) * per, 0:size, :] = total.reshape(per, size, total.shape[1])
    if extra:
        more = refs[-1][...]
        more = more.reshape(-1, more.shape[2])
        room = parts * extra - more.shape[0]
        more = jnp.concatenate([more, jnp.zeros((room, more.shape[1]), F32)], 0)
        all_ref[:, size : size + extra, :] = more.reshape(parts, extra, more.shape[1])


def reduce_grad(info, inputs, grad, parts, more):
    spans = spans_of(inputs[0])
    rows, mid = len(inputs) * inputs[0][0].shape[1], grad.shape[1]
    extra = 0 if more is None else -(-more.shape[0] * more.shape[1] // (8 * parts)) * 8
    ins = [v for piece in inputs for v in piece] + [grad] + ([] if more is None else [more])
    return split_first(
        info, functools.partial(reduce_grad_make, len(inputs), tuple(spans), extra), "reduce_grad", ins,
        (parts, rows // parts + extra, mid), 2 * grad.size * rows,
    )


def spans_of(values):
    spans, at = [], 0
    for value in values:
        spans.append((at, at + value.shape[0]))
        at += value.shape[0]
    return spans


def expand_grad_make(count, chunks, refs, all_ref):
    acts, grads = refs[: count * chunks], refs[count * chunks :]
    parts, wide, out = all_ref.shape
    size = wide // count
    for k in range(count):
        total = None
        own = acts[k * chunks : (k + 1) * chunks]
        for a_ref, (a_first, a_end) in zip(own, spans_of(own)):
            for g_ref, (g_first, g_end) in zip(grads, spans_of(grads)):
                first, end = max(a_first, g_first), min(a_end, g_end)
                if first < end:
                    term = dot(a_ref[first - a_first : end - a_first, :], g_ref[first - g_first : end - g_first, :], 0, 0)
                    total = term if total is None else total + term
        all_ref[:, k * size : (k + 1) * size, :] = total.reshape(parts, size, out)


def expand_grad(info, acts, grads, parts):
    count, mid, out = len(acts), acts[0][0].shape[1], grads[0].shape[1]
    return split_first(
        info, functools.partial(expand_grad_make, count, len(acts[0])), "expand_grad",
        [a for piece in acts for a in piece] + list(grads),
        (parts, count * mid // parts, out), 2 * sum(g.size for g in grads) * mid * count,
    )


def cut_places_kernel(in_ref, *refs):
    size = refs[0].shape[0]
    for k, ref in enumerate(refs):
        ref[...] = in_ref[0, k * size : (k + 1) * size, :]


def cut_places(value, count):
    rows, out = value.shape[1:]
    return kernel_call(cut_places_kernel, "cut_places", [value], [((rows // count, out), BF16)] * count)


def part_rows(info_ref, other, k, batches):
    return (info_ref[HEIGHT_AT] ^ other) * batches + (info_ref[BATCH_AT] ^ k)


def place_reduce_kernel(count, info_ref, *refs):
    out_ref, more_ref = refs[4:]
    me = info_ref[CHAN_AT]
    part = out_ref.shape[0] // count
    batches = refs[0].shape[0]
    size = refs[2].shape[1]
    extra = refs[0].shape[1] - size
    for half in range(2):
        for other in range(2):
            ref = refs[2 * half + other]
            for k in range(batches):
                at = part_rows(info_ref, other, k, batches)
                row = at * size
                to = (me ^ (half * (count // 2) + row // part)) * part + row % part
                out_ref[pl.ds(pl.multiple_of(to, size), size), :] = ref[k, 0:size, :].astype(F32)
                if half == 0:
                    more_ref[pl.ds(pl.multiple_of(at * extra, 8), extra), :] = ref[k, size:, :].astype(F32)


def place_reduce(info, halves, count, part):
    batches, rows, mid = halves[0][0].shape
    extra = rows - halves[1][0].shape[1]
    return kernel_call(
        functools.partial(place_reduce_kernel, count), "place_reduce", [info] + [v for pair in halves for v in pair],
        [((part * count, mid), F32), ((2 * batches * extra, mid), F32)],
    )


def place_expand_kernel(count, info_ref, own_ref, arrived_ref, out_ref):
    me = info_ref[CHAN_AT]
    batches, rows, out = own_ref.shape
    size = rows // count
    for other, ref in enumerate((own_ref, arrived_ref)):
        for k in range(batches):
            row = part_rows(info_ref, other, k, batches) * size
            for place in range(count):
                to = pl.ds(pl.multiple_of((me ^ place) * out, out), out)
                out_ref[pl.ds(pl.multiple_of(row, size), size), to] = ref[k, place * size : (place + 1) * size, :].astype(F32)


def place_expand(info, pair, count, mid):
    out = pair[0].shape[2]
    return kernel_call(
        functools.partial(place_expand_kernel, count), "place_expand", [info] + list(pair), [((mid, out * count), F32)]
    )[0]


def plain_weight_grads(inputs, grad, acts, grad_expanded, grad_group):
    count, me = len(inputs), lax.axis_index("chan")
    part, mid = inputs[0][0].shape[1], grad.shape[1]
    grad_reduce = jnp.zeros((part * count, mid), BF16)
    grad_expand = jnp.zeros((mid, part * count), BF16)
    for k in range(count):
        block = dot(jnp.concatenate(inputs[k], 0), grad, 0, 0).astype(BF16)
        grad_reduce = lax.dynamic_update_slice(grad_reduce, block, ((me ^ k) * part, 0))
        block = dot(jnp.concatenate(acts[k], 0), jnp.concatenate(grad_expanded, 0), 0, 0).astype(BF16)
        block = swap(block, k) if k else block
        grad_expand = lax.dynamic_update_slice(grad_expand, block, (0, (me ^ k) * part))
    return [lax.psum(v, REDUCE_AXES).astype(F32) for v in (grad_reduce, grad_expand, grad_group.astype(BF16))]


def shards(
    block_input, w_reduce, w_group, w_expand, gain_one, bias_one, gain_two, bias_two,
    gain_three, bias_three, image_counts, grad_output,
):
    chan_size = lax.axis_size("chan")
    me = lax.axis_index("chan")
    height_at = lax.axis_index("height")
    images, rows, cols, out_part = block_input.shape
    mid_part, group = w_group.shape[3], w_group.shape[2]
    pixels = rows * cols
    per_image = float(pixels * lax.axis_size("height"))
    plan = (pixels, cols)
    distances = range(2, chan_size, 2)
    own_count = jnp.sum(
        jnp.where(jnp.arange(image_counts.shape[0]) == lax.axis_index("batch"), image_counts, 0)
    )
    batch_at, bits = lax.axis_index("batch"), lax.axis_size("batch").bit_length() - 1
    turned = sum(((batch_at >> bit) & 1) << (bits - 1 - bit) for bit in range(bits))
    info = jnp.stack(
        [own_count, jnp.sum(image_counts), height_at, me, jnp.where(height_at == 0, pixels - cols, 0), turned]
    ).astype(jnp.int32)
    parts = lax.axis_size(REDUCE_AXES)
    staged = lax.axis_size("batch") == 4

    def edge_swap(edge):
        return permute(edge, "height", 1)

    def far_swaps(value, pieces):
        for k in distances:
            pieces[k].append(swap(value, k))

    def core_swaps(pieces, *waits):
        for k in distances:
            pieces[k + 1].append(swap(after(pieces[k][-1], *waits) if waits else pieces[k][-1], 1))

    field = block_input.reshape(images * pixels, out_part)
    matrices, matrices_back, mid_params, out_params = prepare(
        info, w_group, (gain_one, bias_one, gain_two, bias_two), (gain_three, bias_three)
    )
    inputs = [[] for _ in range(chan_size)]
    reduced, red_edges, sums = [], [], None
    for first, share in cut_images(REDUCE_CHUNKS):
        source = after(field, inputs[0][0]) if first else field
        piece = lax.slice_in_dim(source, first * pixels, (first + share) * pixels)
        inputs[0].append(piece)
        far_swaps(piece, inputs)
        inputs[1].append(swap(piece, 1))
        core_swaps(inputs, *(() if sums is None else (sums,)))
        red, edge, sums = reduce_chunk(info, [p[-1] for p in inputs], (first, share), w_reduce, sums, images, plan)
        reduced.append(red)
        red_edges.append(edge_swap(edge))
    sums_one = spread_sums(sums)

    w_expand, w_reduce = after((w_expand, w_reduce), sums)
    weights = cut_weights(info, w_reduce, w_expand, chan_size)
    weights = [v if k == 0 else swap(v, k) for k, v in enumerate(weights)]

    acts_one, grouped, grp_edge, sums = conv_forward(
        info, reduced, red_edges, sums_one, mid_params, matrices, per_image
    )
    sums_two = spread_sums(sums)

    acts = [[] for _ in range(chan_size)]
    for chunk in cut_images(EXPAND_CHUNKS):
        acts[0].append(act_two_chunk(info, grouped, sums_two, mid_params, chunk, plan, per_image))
        far_swaps(acts[0][-1], acts)
    expanded, sums = [], None
    for c, chunk in enumerate(cut_images(EXPAND_CHUNKS)):
        acts[1].append(swap(acts[0][c], 1))
        for k in distances:
            acts[k + 1].append(swap(acts[k][c] if sums is None else after(acts[k][c], sums), 1))
        out, sums = expand_chunk(info, [piece[c] for piece in acts], weights, chunk, sums, images, plan)
        expanded.append(out)
    sums_three = spread_sums(sums)
    grp_edge = edge_swap(after(grp_edge, sums_three))
    output, grad_summed, sums = output_pass(
        info, expanded, field.reshape(images, pixels, out_part), grad_output.reshape(images, pixels, out_part), sums_three,
        out_params, per_image,
    )
    grads_three = spread_sums(sums)

    own, sent = [], [[] for _ in range(chan_size)]
    grad_expanded = []
    for chunk in cut_images(BACK_CHUNKS):
        grad_here = after(grad_summed, own[-2]) if len(own) > 1 else grad_summed
        grad, near, far = back_expand_chunk(
            info, grad_here, expanded, sums_three, grads_three, out_params, weights, chunk, mid_part, plan, per_image
        )
        grad_expanded.append(grad)
        summed = pair_sum(near, swap(far, 1), mid_part)
        own.append(summed[0])
        for value, k in zip(summed[1:], distances):
            sent[k].append(swap(value, k))
    if staged:
        expand_part = scatter_height(expand_grad(info, acts, after(grad_expanded, own[-1]), parts))
    d_two, d_edges, sums = [], [], None
    for c, chunk in enumerate(cut_images(BACK_CHUNKS)):
        grad, edge, sums = slope_two_chunk(
            info, own[c], [sent[k][c] for k in distances], grouped, sums_two, mid_params, chunk, sums, plan, per_image
        )
        d_two.append(grad)
        d_edges.append(edge)
    if staged:
        sums = after(sums, expand_part[1])
    grads_two = spread_sums(sums)
    d_edges = [edge_swap(edge) for edge in d_edges]
    if staged:
        expand_part = scatter_batch(info, (expand_part[0], after(expand_part[1], grads_two)))

    d_one, sums, grad_group = conv_backward(
        info, d_two, d_edges, grouped, grp_edge, reduced, acts_one, sums_two, grads_two, sums_one, mid_params,
        matrices_back, group, per_image,
    )
    grads_one = spread_sums(sums)

    grads = [[] for _ in range(chan_size)]
    grads[0].append(grad_reduced(info, d_one, reduced, sums_one, grads_one, mid_params, per_image))
    far_swaps(grads[0][0], grads)
    grads[1].append(swap(grads[0][0], 1))
    core_swaps(grads)
    half = chan_size // 2
    if staged:
        halves = [
            scatter_height(reduce_grad(info, inputs[i * half : (i + 1) * half], grads[0][0], parts, None if i else grad_group))
            for i in range(2)
        ]
        halves = [gather_height(gather_batch(scatter_batch(info, pair))) for pair in halves]
        grad_reduce, grad_group = place_reduce(info, halves, chan_size, out_part)
        grad_group = grad_group[: 9 * group]
        places = cut_places(expand_part, chan_size)
        places = [v if k == 0 else swap(v, k) for k, v in enumerate(places)]
        expand_part = after(join(*places), grads_one)
        expand_part = gather_height(gather_batch(expand_part.reshape((1,) + expand_part.shape)))
        grad_expand = place_expand(info, expand_part, chan_size, mid_part)
    else:
        grad_reduce, grad_expand, grad_group = plain_weight_grads(inputs, grads[0][0], acts, grad_expanded, grad_group)
    grad_input = input_grad(grad_summed.reshape(images * pixels, out_part), [piece[0] for piece in grads], weights)
    vectors = sum_vectors([grads_one, grads_two, grads_three])
    return (
        output.reshape(block_input.shape), grad_input.reshape(block_input.shape), grad_reduce,
        grad_group.reshape(w_group.shape), grad_expand,
        vectors[1], vectors[0], vectors[3], vectors[2], vectors[5], vectors[4],
    )


def solution(mesh):
    split = P("batch", "height", None, "chan")
    vector = P("chan")
    return jax.shard_map(
        shards,
        mesh=mesh,
        in_specs=(
            split, P(None, "chan"), P(None, None, None, "chan"), P("chan", None),
            vector, vector, vector, vector, vector, vector, P(), split,
        ),
        out_specs=(
            split, split, P(None, "chan"), P(None, None, None, "chan"), P("chan", None),
            vector, vector, vector, vector, vector, vector,
        ),
        check_vma=False,
    )
```

time: 827 us -> 326 us (0.39)
  blocking collectives: 241 us -> 36.4 us
  waiting for transfers between devices: 318 us -> 149 us
  matrix products: 98.7 us -> 0 us
  local copies, waits for them, and re-layouts: 95.8 us -> 22.5 us
  Pallas kernels: 0 us -> 66.7 us
  other arithmetic: 40.8 us -> 0.63 us
  starting transfers between devices: 11.3 us -> 48.7 us
  between operations: 15.4 us -> 1.3 us
    psum x6 -> x0, blocking collectives: 241 us -> none  [the longest x3 123 us: grad_sums(): lax.psum((spread_out(first_sum, offset, width_all), spread_out(second_sum...]
    reduce_scatter x2 -> x0, waiting for transfers between devices: 140 us -> none  [project_scatter(): lax.psum_scatter(lax.dot_general(cols_local, acts, (((0,), (1,)), ((), ()...]
    ppermute x4 -> x51, waiting for transfers between devices: 2.82 us -> 139 us  [permute(): return lax.ppermute(value, axis, [(i, i ^ distance) for i in range(count)])]
    psum x1 -> x0, waiting for transfers between devices: 100 us -> none  [shards(): lax.psum(grad_reduce.astype(jnp.bfloat16), ('height', 'batch'))]
    all_gather x2 -> x0, waiting for transfers between devices: 74.3 us -> none  [the longest x1 60.5 us: shards(): gathered = lax.all_gather(pixels_in, 'chan', axis=1, tiled=True)]
    dot_general x15 -> x0, matrix products: 73.2 us -> none  [the longest x9 32.4 us: kernel_grad(): lax.dot_general(window, grad_grouped, (((0,), (0,)), ((1,), (1,))), prefe...]
    pallas_call x0 -> x45, Pallas kernels: none -> 66.7 us  [kernel_call(): pl.pallas_call(body, in_specs=[SMEM if a.dtype == jnp.int32 else VMEM for...]
    reshape x12 -> x6, local copies, waits for them, and re-layouts: 50.3 us -> 0.03 us  [prepare(): rows = [v.reshape(1, -1) for v in list(mid_vectors) + list(out_vectors)]]
  transfers between devices with their start and end apart: 9 -> 53, of which waited for: 6 -> 23; matrix products, arithmetic and copies ran while one was open for 8% -> 1% of each run, Pallas kernels for 0% -> 12%
where the time goes in v3:
time: 326 us; the launch traced here: 325 us
  waiting for transfers between devices  149 us (46%)
  Pallas kernels  66.7 us (20%)
  starting transfers between devices  48.7 us (15%)
  blocking collectives  36.4 us (11%)
  local copies, waits for them, and re-layouts  22.5 us (7%)
    ppermute x51, waiting for transfers between devices, permute(): return lax.ppermute(value, axis, [(i, i ^ distance) for i in range(count)])  139 us
    pallas_call x45, Pallas kernels, kernel_call(): pl.pallas_call(body, in_specs=[SMEM if a.dtype == jnp.int32 else VMEM for...  66.7 us
    ppermute x51, starting transfers between devices, permute(): return lax.ppermute(value, axis, [(i, i ^ distance) for i in range(count)])  40.5 us
    all_to_all x4, blocking collectives, spread_sums(): return lax.all_to_all(sent, REDUCE_AXES, 0, 0)  36.4 us
    unnamed x94, local copies, waits for them, and re-layouts  17.6 us
    all_to_all x2, waiting for transfers between devices, spread_sums(): return lax.all_to_all(sent, REDUCE_AXES, 0, 0)  9.96 us
    all_to_all x2, starting transfers between devices, spread_sums(): return lax.all_to_all(sent, REDUCE_AXES, 0, 0)  8.21 us
  transfers between devices with their start and end apart: 53, of which 23 were waited for; matrix products, arithmetic and copies ran while one was open for 1% of the time, Pallas kernels for 12%

profile of v3, /device:TPU:0, one launch (start us, length us, event | category | flops | bytes accessed | tf_op | source)
XLA Modules:
  0.0 325.1 jit_solution(15235978278766159787)
XLA Ops:
  2.4 3.0 collective-permute-start.1
  5.4 34.5 %collective-permute-done.1.refs_2_.refs_0_ = bf16[1536,512]{1,0:T(8,128)(2,1)} collective-permute-done((bf16[1536,512]{1,0:T(8,128)(2,1)S(1)}, bf16[1536,512]{1,0:T(8,128)(2,1)}, u32[]{:S(2)}, u32[]{:S(2)}) %collective-permute-start.1) | collective-permute-done | bytes 1572896 | tf_op jit(solution)/shard_map/ppermute | solution.py:44
  45.0 4.9 %reduce.2 = (f32[12,128,256]{2,1,0:T(8,128)S(1)}, bf16[12,16,256]{2,1,0:T(8,128)(2,1)}, f32[2,8,256]{2,1,0:T(8,128)S(1)}) custom-call(s32[6]{0:T(128)S(1)} %stack.27.info_ref, bf16[1536,512]{1,0:T(8,128)(2,1)S(1)} %bitcast.25, bf16[1536,512]{1,0:T(8,128)(2,1)} %collective-permute-done.refs_1_.refs_2_, ...), custom_call_target="tpu_custom_call" | custom-call | flops 1610612736 | bytes 7340056 | tf_op jit(solution)/shard_map/reduce/pallas_call | solution.py:25
  51.1 4.4 %collective-permute-done.4.refs_2_.refs_1_ = bf16[512,512]{1,0:T(8,128)(2,1)} collective-permute-done((bf16[512,512]{1,0:T(8,128)(2,1)S(1)}, bf16[512,512]{1,0:T(8,128)(2,1)}, u32[]{:S(2)}, u32[]{:S(2)}) %collective-permute-start.4) | collective-permute-done | bytes 524320 | tf_op jit(solution)/shard_map/ppermute | solution.py:44
  62.9 4.9 %all-to-all-start = ((f32[8,2,256]{2,1,0:T(2,128)}), f32[8,2,256]{2,1,0:T(2,128)S(1)}, u32[]{:S(2)}, u32[]{:S(2)}) async-start(f32[8,2,256]{2,1,0:T(2,128)} %get-tuple-element.113), calls=%async_computation | async-start | bytes 32768 | tf_op jit(solution)/shard_map/all_to_all | solution.py:52
  70.9 3.4 %all-to-all-done.refs_4_.refs_13_.refs_3_ = f32[8,2,256]{2,1,0:T(2,128)S(1)} async-done(((f32[8,2,256]{2,1,0:T(2,128)}), f32[8,2,256]{2,1,0:T(2,128)S(1)}, u32[]{:S(2)}, u32[]{:S(2)}) %all-to-all-start) | async-done | bytes 16416 | tf_op jit(solution)/shard_map/all_to_all | solution.py:52
  78.1 5.2 %conv_forward.1 = (bf16[16,128,256]{2,1,0:T(8,128)(2,1)S(1)}, f32[16,128,256]{2,1,0:T(8,128)S(1)}, bf16[16,16,256]{2,1,0:T(8,128)(2,1)S(1)}, f32[8,2,256]{2,1,0:T(2,128)S(1)}) custom-call(s32[6]{0:T(128)S(1)} %stack.27.info_ref, f32[12,128,256]{2,1,0:T(8,128)S(1)} %copy-done.17, f32[4,128,256]{2,1,0:T(8,128)S(1)} %copy-done.23, ...), custom_call_target="tpu_custom_call" | custom-call | flops 2415919104 | bytes 3428376 | tf_op jit(solution)/shard_map/conv_forward/pallas_call | solution.py:25
  83.3 9.2 %all_to_all.30.sums_ref.refs_2_.refs_11_ = f32[8,2,256]{2,1,0:T(2,128)S(1)} all-to-all(f32[8,2,256]{2,1,0:T(2,128)S(1)} %get-tuple-element.117), channel_id=1, replica_groups=mesh['height'=2,'chan'=4,'batch'=4] {'height','batch'}, dimensions={0} | all-to-all | bytes 32768 | tf_op jit(solution)/shard_map/all_to_all | solution.py:52
  98.2 10.2 %collective-permute-done.9.refs_2_.refs_4_ = bf16[1024,256]{1,0:T(8,128)(2,1)S(1)} collective-permute-done((bf16[1024,256]{1,0:T(8,128)(2,1)S(1)}, bf16[1024,256]{1,0:T(8,128)(2,1)S(1)}, u32[]{:S(2)}, u32[]{:S(2)}) %collective-permute-start.9) | collective-permute-done | bytes 524320 | tf_op jit(solution)/shard_map/ppermute | solution.py:44
  110.9 8.8 %collective-permute-done.12.refs_6_.refs_8_ = bf16[512,512]{1,0:T(8,128)(2,1)S(1)} collective-permute-done((bf16[512,512]{1,0:T(8,128)(2,1)S(1)}, bf16[512,512]{1,0:T(8,128)(2,1)S(1)}, u32[]{:S(2)}, u32[]{:S(2)}) %collective-permute-start.12) | collective-permute-done | bytes 524320 | tf_op jit(solution)/shard_map/ppermute | solution.py:44
  119.6 10.2 %collective-permute-done.13.refs_7_.refs_9_ = bf16[512,512]{1,0:T(8,128)(2,1)S(1)} collective-permute-done((bf16[512,512]{1,0:T(8,128)(2,1)S(1)}, bf16[512,512]{1,0:T(8,128)(2,1)S(1)}, u32[]{:S(2)}, u32[]{:S(2)}) %collective-permute-start.13) | collective-permute-done | bytes 524320 | tf_op jit(solution)/shard_map/ppermute | solution.py:44
  131.7 7.2 %collective-permute-done.15.refs_2_.refs_5_ = bf16[1024,256]{1,0:T(8,128)(2,1)S(1)} collective-permute-done((bf16[1024,256]{1,0:T(8,128)(2,1)S(1)}, bf16[1024,256]{1,0:T(8,128)(2,1)S(1)}, u32[]{:S(2)}, u32[]{:S(2)}) %collective-permute-start.15) | collective-permute-done | bytes 524320 | tf_op jit(solution)/shard_map/ppermute | solution.py:44
  142.7 9.1 %all_to_all.31.refs_4_.refs_3_ = f32[8,2,512]{2,1,0:T(2,128)S(1)} all-to-all(f32[8,2,512]{2,1,0:T(2,128)S(1)} %get-tuple-element.128), channel_id=1, replica_groups=mesh['height'=2,'chan'=4,'batch'=4] {'height','batch'}, dimensions={0} | all-to-all | bytes 65536 | tf_op jit(solution)/shard_map/all_to_all | solution.py:52
  151.8 5.1 %output.1 = (bf16[16,128,512]{2,1,0:T(8,128)(2,1)}, f32[16,128,512]{2,1,0:T(8,128)S(1)}, f32[8,2,512]{2,1,0:T(2,128)S(1)}) custom-call(s32[6]{0:T(128)S(1)} %stack.27.info_ref, f32[8,128,512]{2,1,0:T(8,128)S(1)} %get-tuple-element.124.refs_0_, f32[8,128,512]{2,1,0:T(8,128)S(1)} %get-tuple-element.127.refs_1_, bf16[16,128,512]{2,1,0:T(8,128)(2,1)S(1)} %bitcast.28, ...), custom_call_target="tpu_custom_call" | custom-call | bytes 8425496 | tf_op jit(solution)/shard_map/output/pallas_call | solution.py:25
  156.8 9.1 %all_to_all.32.refs_4_.refs_2_ = f32[8,2,512]{2,1,0:T(2,128)S(1)} all-to-all(f32[8,2,512]{2,1,0:T(2,128)S(1)} %get-tuple-element.132), channel_id=1, replica_groups=mesh['height'=2,'chan'=4,'batch'=4] {'height','batch'}, dimensions={0} | all-to-all | bytes 65536 | tf_op jit(solution)/shard_map/all_to_all | solution.py:52
  175.1 3.0 expand_grad.1
  182.2 11.7 %collective-permute-done.18.refs_0_ = bf16[512,256]{1,0:T(8,128)(2,1)S(1)} collective-permute-done((bf16[512,256]{1,0:T(8,128)(2,1)S(1)}, bf16[512,256]{1,0:T(8,128)(2,1)S(1)}, u32[]{:S(2)}, u32[]{:S(2)}) %collective-permute-start.18) | collective-permute-done | bytes 262176 | tf_op jit(solution)/shard_map/ppermute | solution.py:44
  203.2 3.3 %all-to-all-start.4 = ((f32[8,2,256]{2,1,0:T(2,128)}), f32[8,2,256]{2,1,0:T(2,128)S(1)}, u32[]{:S(2)}, u32[]{:S(2)}) async-start(f32[8,2,256]{2,1,0:T(2,128)} %get-tuple-element.165), calls=%async_computation.4 | async-start | bytes 32768 | tf_op jit(solution)/shard_map/all_to_all | solution.py:52
  206.5 6.5 %all-to-all-done.4.refs_12_.refs_1_ = f32[8,2,256]{2,1,0:T(2,128)S(1)} async-done(((f32[8,2,256]{2,1,0:T(2,128)}), f32[8,2,256]{2,1,0:T(2,128)S(1)}, u32[]{:S(2)}, u32[]{:S(2)}) %all-to-all-start.4) | async-done | bytes 16416 | tf_op jit(solution)/shard_map/all_to_all | solution.py:52
  221.3 8.5 %conv_backward.1 = (f32[16,128,256]{2,1,0:T(8,128)S(1)}, f32[8,2,256]{2,1,0:T(2,128)S(1)}, f32[9,32,256]{2,1,0:T(8,128)S(1)}) custom-call(s32[6]{0:T(128)S(1)} %stack.27.info_ref, f32[4,128,256]{2,1,0:T(8,128)S(1)} %copy-done.35, f32[8,128,256]{2,1,0:T(8,128)S(1)} %copy-done.33, f32[4,128,256]{2,1,0:T(8,128)S(1)} %copy-done.37, ...), custom_call_target="tpu_custom_call" | custom-call | flops 4831838208 | bytes 8835096 | tf_op jit(solution)/shard_map/conv_backward/pallas_call | solution.py:25
  229.8 9.0 %all_to_all.33.refs_4_.refs_0_ = f32[8,2,256]{2,1,0:T(2,128)S(1)} all-to-all(f32[8,2,256]{2,1,0:T(2,128)S(1)} %get-tuple-element.168), channel_id=1, replica_groups=mesh['height'=2,'chan'=4,'batch'=4] {'height','batch'}, dimensions={0} | all-to-all | bytes 32768 | tf_op jit(solution)/shard_map/all_to_all | solution.py:52
  246.2 3.5 %collective-permute-done.43.arrived_ref = bf16[2,128,512]{2,1,0:T(8,128)(2,1)S(1)} collective-permute-done((bf16[2,128,512]{2,1,0:T(8,128)(2,1)S(1)}, bf16[2,128,512]{2,1,0:T(8,128)(2,1)S(1)}, u32[]{:S(2)}, u32[]{:S(2)}) %collective-permute-start.43) | collective-permute-done | bytes 262176 | tf_op jit(solution)/shard_map/ppermute | solution.py:44
  250.7 6.9 %collective-permute-done.44.second_ref = bf16[1,128,512]{2,1,0:T(8,128)(2,1)S(1)} collective-permute-done((bf16[1,128,512]{2,1,0:T(8,128)(2,1)S(1)}, bf16[1,128,512]{2,1,0:T(8,128)(2,1)S(1)}, u32[]{:S(2)}, u32[]{:S(2)}) %collective-permute-start.44) | collective-permute-done | bytes 131104 | tf_op jit(solution)/shard_map/ppermute | solution.py:44
  262.9 3.4 %reduce_grad.3 = (f32[4,128,256]{2,1,0:T(8,128)S(1)}, bf16[4,128,256]{2,1,0:T(8,128)(2,1)S(1)}) custom-call(s32[6]{0:T(128)S(1)} %stack.27.info_ref, bf16[1536,512]{1,0:T(8,128)(2,1)} %collective-permute-done.1.refs_2_.refs_0_, bf16[512,512]{1,0:T(8,128)(2,1)} %collective-permute-done.4.refs_2_.refs_1_, ...), custom_call_target="tpu_custom_call" | custom-call | flops 1073741824 | bytes 5242904 | tf_op jit(solution)/shard_map/reduce_grad/pallas_call | solution.py:25
  268.9 7.4 %collective-permute-done.48.refs_1_ = bf16[1,128,512]{2,1,0:T(8,128)(2,1)S(1)} collective-permute-done((bf16[1,128,512]{2,1,0:T(8,128)(2,1)S(1)}, bf16[1,128,512]{2,1,0:T(8,128)(2,1)S(1)}, u32[]{:S(2)}, u32[]{:S(2)}) %collective-permute-start.48) | collective-permute-done | bytes 131104 | tf_op jit(solution)/shard_map/ppermute | solution.py:44
  280.4 4.4 %collective-permute-done.33.second_ref = bf16[1,168,256]{2,1,0:T(8,128)(2,1)S(1)} collective-permute-done((bf16[1,168,256]{2,1,0:T(8,128)(2,1)S(1)}, bf16[1,168,256]{2,1,0:T(8,128)(2,1)S(1)}, u32[]{:S(2)}, u32[]{:S(2)}) %collective-permute-start.33) | collective-permute-done | bytes 86048 | tf_op jit(solution)/shard_map/ppermute | solution.py:44
  284.8 3.5 %collective-permute-start.34 = (bf16[1,168,256]{2,1,0:T(8,128)(2,1)S(1)}, bf16[1,168,256]{2,1,0:T(8,128)(2,1)S(1)}, u32[]{:S(2)}, u32[]{:S(2)}) collective-permute-start(bf16[1,168,256]{2,1,0:T(8,128)(2,1)S(1)} %add_last.3.refs_0_), channel_id=1, source_target_pairs={{0,2},{1,3},{2,0},{3,1},{4,6},{5,7},{6,4},{7,5},{8,10},{9,11},{10,... | collective-permute-start | bytes 258056 | tf_op jit(solution)/shard_map/ppermute | solution.py:44
  293.3 3.5 %collective-permute-done.39.second_ref = bf16[1,128,256]{2,1,0:T(8,128)(2,1)S(1)} collective-permute-done((bf16[1,128,256]{2,1,0:T(8,128)(2,1)S(1)}, bf16[1,128,256]{2,1,0:T(8,128)(2,1)S(1)}, u32[]{:S(2)}, u32[]{:S(2)}) %collective-permute-start.39) | collective-permute-done | bytes 65568 | tf_op jit(solution)/shard_map/ppermute | solution.py:44
  297.0 5.5 %collective-permute-done.40.refs_1_ = bf16[1,128,256]{2,1,0:T(8,128)(2,1)S(1)} collective-permute-done((bf16[1,128,256]{2,1,0:T(8,128)(2,1)S(1)}, bf16[1,128,256]{2,1,0:T(8,128)(2,1)S(1)}, u32[]{:S(2)}, u32[]{:S(2)}) %collective-permute-start.40) | collective-permute-done | bytes 65568 | tf_op jit(solution)/shard_map/ppermute | solution.py:44
  303.9 3.7 %collective-permute-done.41.refs_1_ = bf16[2,128,256]{2,1,0:T(8,128)(2,1)S(1)} collective-permute-done((bf16[2,128,256]{2,1,0:T(8,128)(2,1)S(1)}, bf16[2,128,256]{2,1,0:T(8,128)(2,1)S(1)}, u32[]{:S(2)}, u32[]{:S(2)}) %collective-permute-start.41) | collective-permute-done | bytes 131104 | tf_op jit(solution)/shard_map/ppermute | solution.py:44
  309.5 6.6 %collective-permute-done.42.refs_3_ = bf16[4,128,256]{2,1,0:T(8,128)(2,1)S(1)} collective-permute-done((bf16[4,128,256]{2,1,0:T(8,128)(2,1)S(1)}, bf16[4,128,256]{2,1,0:T(8,128)(2,1)S(1)}, u32[]{:S(2)}, u32[]{:S(2)}) %collective-permute-start.42) | collective-permute-done | bytes 262176 | tf_op jit(solution)/shard_map/ppermute | solution.py:44
  320.9 4.2 %input_grad.1 = bf16[2048,512]{1,0:T(8,128)(2,1)} custom-call(f32[2048,512]{1,0:T(8,128)S(1)} %bitcast.22, bf16[2048,256]{1,0:T(8,128)(2,1)S(1)} %grad_reduced.1.refs_0_.refs_4_, bf16[2048,256]{1,0:T(8,128)(2,1)S(1)} %collective-permute-done.28.refs_1_, bf16[2048,256]{1,0:T(8,128)(2,1)S(1)} %collective-permute-done.29.refs_2_, ...), custom_call_target="tpu_custom_call" | custom-call | flops 2147483648 | bytes 10485760 | tf_op jit(solution)/shard_map/input_grad/pallas_call | solution.py:25
  (228 shorter events, 100.1 us)
Async XLA Ops:
  2.4 37.5 %collective-permute-start.1 = (bf16[1536,512]{1,0:T(8,128)(2,1)S(1)}, bf16[1536,512]{1,0:T(8,128)(2,1)}, u32[]{:S(2)}, u32[]{:S(2)}) collective-permute-start(bf16[1536,512]{1,0:T(8,128)(2,1)S(1)} %bitcast.23), channel_id=1, source_target_pairs={{0,8},{4,12},{8,0},{12,4},{1,9},{5,13},{9,1},{13,5},{2,10},{6,14},... | collective-permute-start | bytes 4718600 | tf_op jit(solution)/shard_map/ppermute | solution.py:44
  5.4 39.6 %collective-permute-start = (bf16[1536,512]{1,0:T(8,128)(2,1)S(1)}, bf16[1536,512]{1,0:T(8,128)(2,1)}, u32[]{:S(2)}, u32[]{:S(2)}) collective-permute-start(bf16[1536,512]{1,0:T(8,128)(2,1)S(1)} %bitcast.24), channel_id=1, source_target_pairs={{0,4},{4,0},{8,12},{12,8},{1,5},{5,1},{9,13},{13,9},{2,6},{6,2},{1... | collective-permute-start | bytes 4718600 | tf_op jit(solution)/shard_map/ppermute | solution.py:44
  41.0 14.5 %collective-permute-start.4 = (bf16[512,512]{1,0:T(8,128)(2,1)S(1)}, bf16[512,512]{1,0:T(8,128)(2,1)}, u32[]{:S(2)}, u32[]{:S(2)}) collective-permute-start(bf16[512,512]{1,0:T(8,128)(2,1)S(1)} %slice.14.refs_0_.refs_1_), channel_id=1, source_target_pairs={{0,8},{4,12},{8,0},{12,4},{1,9},{5,13},{9,1},{13,5},{2,10},{6,14},... | collective-permute-start | bytes 1572872 | tf_op jit(solution)/shard_map/ppermute | solution.py:44
  42.8 14.5 %collective-permute-start.3 = (bf16[512,512]{1,0:T(8,128)(2,1)S(1)}, bf16[512,512]{1,0:T(8,128)(2,1)}, u32[]{:S(2)}, u32[]{:S(2)}) collective-permute-start(bf16[512,512]{1,0:T(8,128)(2,1)S(1)} %slice.14.refs_0_.refs_1_), channel_id=1, source_target_pairs={{0,4},{4,0},{8,12},{12,8},{1,5},{5,1},{9,13},{13,9},{2,6},{6,2},{1... | collective-permute-start | bytes 1572872 | tf_op jit(solution)/shard_map/ppermute | solution.py:44
  55.5 15.4 %collective-permute-start.6 = (bf16[12,16,256]{2,1,0:T(8,128)(2,1)}, bf16[12,16,256]{2,1,0:T(8,128)(2,1)S(1)}, u32[]{:S(2)}, u32[]{:S(2)}) collective-permute-start(bf16[12,16,256]{2,1,0:T(8,128)(2,1)} %get-tuple-element.111), channel_id=1, source_target_pairs={{0,16},{16,0},{1,17},{17,1},{2,18},{18,2},{3,19},{19,3},{4,20},{20... | collective-permute-start | bytes 294920 | tf_op jit(solution)/shard_map/ppermute | solution.py:44
  61.1 13.2 %collective-permute-start.7 = (bf16[4,16,256]{2,1,0:T(8,128)(2,1)S(1)}, bf16[4,16,256]{2,1,0:T(8,128)(2,1)S(1)}, u32[]{:S(2)}, u32[]{:S(2)}) collective-permute-start(bf16[4,16,256]{2,1,0:T(8,128)(2,1)S(1)} %get-tuple-element.112), channel_id=1, source_target_pairs={{0,16},{16,0},{1,17},{17,1},{2,18},{18,2},{3,19},{19,3},{4,20},{20... | collective-permute-start | bytes 98312 | tf_op jit(solution)/shard_map/ppermute | solution.py:44
  62.9 11.5 %all-to-all-start = ((f32[8,2,256]{2,1,0:T(2,128)}), f32[8,2,256]{2,1,0:T(2,128)S(1)}, u32[]{:S(2)}, u32[]{:S(2)}) async-start(f32[8,2,256]{2,1,0:T(2,128)} %get-tuple-element.113), calls=%async_computation | async-start | bytes 32768 | tf_op jit(solution)/shard_map/all_to_all | solution.py:52
  93.5 14.9 %collective-permute-start.9 = (bf16[1024,256]{1,0:T(8,128)(2,1)S(1)}, bf16[1024,256]{1,0:T(8,128)(2,1)S(1)}, u32[]{:S(2)}, u32[]{:S(2)}) collective-permute-start(bf16[1024,256]{1,0:T(8,128)(2,1)S(1)} %act_two.2.refs_0_), channel_id=1, source_target_pairs={{0,8},{4,12},{8,0},{12,4},{1,9},{5,13},{9,1},{13,5},{2,10},{6,14},... | collective-permute-start | bytes 1572872 | tf_op jit(solution)/shard_map/ppermute | solution.py:44
  95.9 13.4 %collective-permute-start.11 = (bf16[512,512]{1,0:T(8,128)(2,1)S(1)}, bf16[512,512]{1,0:T(8,128)(2,1)S(1)}, u32[]{:S(2)}, u32[]{:S(2)}) collective-permute-start(bf16[512,512]{1,0:T(8,128)(2,1)S(1)} %get-tuple-element.121), channel_id=1, source_target_pairs={{0,4},{4,0},{8,12},{12,8},{1,5},{5,1},{9,13},{13,9},{2,6},{6,2},{1... | collective-permute-start | bytes 1572872 | tf_op jit(solution)/shard_map/ppermute | solution.py:44
  96.0 23.6 %collective-permute-start.12 = (bf16[512,512]{1,0:T(8,128)(2,1)S(1)}, bf16[512,512]{1,0:T(8,128)(2,1)S(1)}, u32[]{:S(2)}, u32[]{:S(2)}) collective-permute-start(bf16[512,512]{1,0:T(8,128)(2,1)S(1)} %get-tuple-element.122), channel_id=1, source_target_pairs={{0,8},{4,12},{8,0},{12,4},{1,9},{5,13},{9,1},{13,5},{2,10},{6,14},... | collective-permute-start | bytes 1572872 | tf_op jit(solution)/shard_map/ppermute | solution.py:44
  96.6 33.3 %collective-permute-start.13 = (bf16[512,512]{1,0:T(8,128)(2,1)S(1)}, bf16[512,512]{1,0:T(8,128)(2,1)S(1)}, u32[]{:S(2)}, u32[]{:S(2)}) collective-permute-start(bf16[512,512]{1,0:T(8,128)(2,1)S(1)} %get-tuple-element.123), channel_id=1, source_target_pairs={{0,12},{4,8},{8,4},{12,0},{1,13},{5,9},{9,5},{13,1},{2,14},{6,10},... | collective-permute-start | bytes 1572872 | tf_op jit(solution)/shard_map/ppermute | solution.py:44
  97.9 32.0 %collective-permute-start.8 = (bf16[1024,256]{1,0:T(8,128)(2,1)S(1)}, bf16[1024,256]{1,0:T(8,128)(2,1)S(1)}, u32[]{:S(2)}, u32[]{:S(2)}) collective-permute-start(bf16[1024,256]{1,0:T(8,128)(2,1)S(1)} %act_two.2.refs_0_), channel_id=1, source_target_pairs={{0,4},{4,0},{8,12},{12,8},{1,5},{5,1},{9,13},{13,9},{2,6},{6,2},{1... | collective-permute-start | bytes 1572872 | tf_op jit(solution)/shard_map/ppermute | solution.py:44
  108.4 21.5 %collective-permute-start.10 = (bf16[1024,256]{1,0:T(8,128)(2,1)S(1)}, bf16[1024,256]{1,0:T(8,128)(2,1)S(1)}, u32[]{:S(2)}, u32[]{:S(2)}) collective-permute-start(bf16[1024,256]{1,0:T(8,128)(2,1)S(1)} %collective-permute-done.9.refs_2_.refs_4_), channel_id=1, source_target_pairs={{0,4},{4,0},{8,12},{12,8},{1,5},{5,1},{9,13},{13,9},{2,6},{6,2},{1... | collective-permute-start | bytes 1572872 | tf_op jit(solution)/shard_map/ppermute | solution.py:44
  109.3 29.6 %collective-permute-start.15 = (bf16[1024,256]{1,0:T(8,128)(2,1)S(1)}, bf16[1024,256]{1,0:T(8,128)(2,1)S(1)}, u32[]{:S(2)}, u32[]{:S(2)}) collective-permute-start(bf16[1024,256]{1,0:T(8,128)(2,1)S(1)} %act_two.3.refs_0_.refs_1_), channel_id=1, source_target_pairs={{0,8},{4,12},{8,0},{12,4},{1,9},{5,13},{9,1},{13,5},{2,10},{6,14},... | collective-permute-start | bytes 1572872 | tf_op jit(solution)/shard_map/ppermute | solution.py:44
  119.6 19.3 %collective-permute-start.14 = (bf16[1024,256]{1,0:T(8,128)(2,1)S(1)}, bf16[1024,256]{1,0:T(8,128)(2,1)S(1)}, u32[]{:S(2)}, u32[]{:S(2)}) collective-permute-start(bf16[1024,256]{1,0:T(8,128)(2,1)S(1)} %act_two.3.refs_0_.refs_1_), channel_id=1, source_target_pairs={{0,4},{4,0},{8,12},{12,8},{1,5},{5,1},{9,13},{13,9},{2,6},{6,2},{1... | collective-permute-start | bytes 1572872 | tf_op jit(solution)/shard_map/ppermute | solution.py:44
  173.5 22.0 %collective-permute-start.20 = (bf16[1024,256]{1,0:T(8,128)(2,1)S(1)}, bf16[1024,256]{1,0:T(8,128)(2,1)S(1)}, u32[]{:S(2)}, u32[]{:S(2)}) collective-permute-start(bf16[1024,256]{1,0:T(8,128)(2,1)S(1)} %get-tuple-element.141), channel_id=1, source_target_pairs={{0,8},{4,12},{8,0},{12,4},{1,9},{5,13},{9,1},{13,5},{2,10},{6,14},... | collective-permute-start | bytes 1572872 | tf_op jit(solution)/shard_map/ppermute | solution.py:44
  178.1 24.3 %collective-permute-start.27 = (bf16[4,128,512]{2,1,0:T(8,128)(2,1)S(1)}, bf16[4,128,512]{2,1,0:T(8,128)(2,1)S(1)}, u32[]{:S(2)}, u32[]{:S(2)}) collective-permute-start(bf16[4,128,512]{2,1,0:T(8,128)(2,1)S(1)} %get-tuple-element.164), channel_id=1, source_target_pairs={{0,16},{16,0},{1,17},{17,1},{2,18},{18,2},{3,19},{19,3},{4,20},{20... | collective-permute-start | bytes 1572872 | tf_op jit(solution)/shard_map/ppermute | solution.py:44
  178.7 15.3 %collective-permute-start.18 = (bf16[512,256]{1,0:T(8,128)(2,1)S(1)}, bf16[512,256]{1,0:T(8,128)(2,1)S(1)}, u32[]{:S(2)}, u32[]{:S(2)}) collective-permute-start(bf16[512,256]{1,0:T(8,128)(2,1)S(1)} %get-tuple-element.136), channel_id=1, source_target_pairs={{0,8},{4,12},{8,0},{12,4},{1,9},{5,13},{9,1},{13,5},{2,10},{6,14},... | collective-permute-start | bytes 786440 | tf_op jit(solution)/shard_map/ppermute | solution.py:44
  179.3 20.2 %collective-permute-start.22 = (bf16[512,256]{1,0:T(8,128)(2,1)S(1)}, bf16[512,256]{1,0:T(8,128)(2,1)S(1)}, u32[]{:S(2)}, u32[]{:S(2)}) collective-permute-start(bf16[512,256]{1,0:T(8,128)(2,1)S(1)} %get-tuple-element.148), channel_id=1, source_target_pairs={{0,8},{4,12},{8,0},{12,4},{1,9},{5,13},{9,1},{13,5},{2,10},{6,14},... | collective-permute-start | bytes 786440 | tf_op jit(solution)/shard_map/ppermute | solution.py:44
  180.7 25.8 %collective-permute-start.26 = (bf16[16,16,256]{2,1,0:T(8,128)(2,1)S(1)}, bf16[16,16,256]{2,1,0:T(8,128)(2,1)S(1)}, u32[]{:S(2)}, u32[]{:S(2)}) collective-permute-start(bf16[16,16,256]{2,1,0:T(8,128)(2,1)S(1)} %get-tuple-element.155), channel_id=1, source_target_pairs={{0,16},{16,0},{1,17},{17,1},{2,18},{18,2},{3,19},{19,3},{4,20},{20... | collective-permute-start | bytes 393224 | tf_op jit(solution)/shard_map/ppermute | solution.py:44
  197.5 15.6 %collective-permute-start.24 = (bf16[8,16,256]{2,1,0:T(8,128)(2,1)}, bf16[8,16,256]{2,1,0:T(8,128)(2,1)}, u32[]{:S(2)}, u32[]{:S(2)}) collective-permute-start(bf16[8,16,256]{2,1,0:T(8,128)(2,1)} %get-tuple-element.152), channel_id=1, source_target_pairs={{0,16},{16,0},{1,17},{17,1},{2,18},{18,2},{3,19},{19,3},{4,20},{20... | collective-permute-start | bytes 196616 | tf_op jit(solution)/shard_map/ppermute | solution.py:44
  201.8 11.2 %collective-permute-start.25 = (bf16[4,16,256]{2,1,0:T(8,128)(2,1)}, bf16[4,16,256]{2,1,0:T(8,128)(2,1)}, u32[]{:S(2)}, u32[]{:S(2)}) collective-permute-start(bf16[4,16,256]{2,1,0:T(8,128)(2,1)} %get-tuple-element.153), channel_id=1, source_target_pairs={{0,16},{16,0},{1,17},{17,1},{2,18},{18,2},{3,19},{19,3},{4,20},{20... | collective-permute-start | bytes 98312 | tf_op jit(solution)/shard_map/ppermute | solution.py:44
  203.2 9.9 %all-to-all-start.4 = ((f32[8,2,256]{2,1,0:T(2,128)}), f32[8,2,256]{2,1,0:T(2,128)S(1)}, u32[]{:S(2)}, u32[]{:S(2)}) async-start(f32[8,2,256]{2,1,0:T(2,128)} %get-tuple-element.165), calls=%async_computation.4 | async-start | bytes 32768 | tf_op jit(solution)/shard_map/all_to_all | solution.py:52
  239.9 21.2 %collective-permute-start.29 = (bf16[2048,256]{1,0:T(8,128)(2,1)S(1)}, bf16[2048,256]{1,0:T(8,128)(2,1)S(1)}, u32[]{:S(2)}, u32[]{:S(2)}) collective-permute-start(bf16[2048,256]{1,0:T(8,128)(2,1)S(1)} %grad_reduced.1.refs_0_.refs_4_), channel_id=1, source_target_pairs={{0,8},{4,12},{8,0},{12,4},{1,9},{5,13},{9,1},{13,5},{2,10},{6,14},... | collective-permute-start | bytes 3145736 | tf_op jit(solution)/shard_map/ppermute | solution.py:44
  245.6 21.9 %collective-permute-start.31 = (bf16[4,168,256]{2,1,0:T(8,128)(2,1)S(1)}, bf16[4,168,256]{2,1,0:T(8,128)(2,1)S(1)}, u32[]{:S(2)}, u32[]{:S(2)}) collective-permute-start(bf16[4,168,256]{2,1,0:T(8,128)(2,1)S(1)} %get-tuple-element.171), channel_id=1, source_target_pairs={{0,16},{16,0},{1,17},{17,1},{2,18},{18,2},{3,19},{19,3},{4,20},{20... | collective-permute-start | bytes 1032200 | tf_op jit(solution)/shard_map/ppermute | solution.py:44
  257.8 63.1 %collective-permute-start.28 = (bf16[2048,256]{1,0:T(8,128)(2,1)S(1)}, bf16[2048,256]{1,0:T(8,128)(2,1)S(1)}, u32[]{:S(2)}, u32[]{:S(2)}) collective-permute-start(bf16[2048,256]{1,0:T(8,128)(2,1)S(1)} %grad_reduced.1.refs_0_.refs_4_), channel_id=1, source_target_pairs={{0,4},{4,0},{8,12},{12,8},{1,5},{5,1},{9,13},{13,9},{2,6},{6,2},{1... | collective-permute-start | bytes 3145736 | tf_op jit(solution)/shard_map/ppermute | solution.py:44
  261.0 59.9 %collective-permute-start.30 = (bf16[2048,256]{1,0:T(8,128)(2,1)S(1)}, bf16[2048,256]{1,0:T(8,128)(2,1)S(1)}, u32[]{:S(2)}, u32[]{:S(2)}) collective-permute-start(bf16[2048,256]{1,0:T(8,128)(2,1)S(1)} %collective-permute-done.29.refs_2_), channel_id=1, source_target_pairs={{0,4},{4,0},{8,12},{12,8},{1,5},{5,1},{9,13},{13,9},{2,6},{6,2},{1... | collective-permute-start | bytes 3145736 | tf_op jit(solution)/shard_map/ppermute | solution.py:44
  266.3 11.9 %collective-permute-start.37 = (bf16[4,128,256]{2,1,0:T(8,128)(2,1)S(1)}, bf16[4,128,256]{2,1,0:T(8,128)(2,1)S(1)}, u32[]{:S(2)}, u32[]{:S(2)}) collective-permute-start(bf16[4,128,256]{2,1,0:T(8,128)(2,1)S(1)} %get-tuple-element.177), channel_id=1, source_target_pairs={{0,16},{16,0},{1,17},{17,1},{2,18},{18,2},{3,19},{19,3},{4,20},{20... | collective-permute-start | bytes 786440 | tf_op jit(solution)/shard_map/ppermute | solution.py:44
  276.2 15.4 %collective-permute-start.49 = (bf16[2,128,512]{2,1,0:T(8,128)(2,1)S(1)}, bf16[2,128,512]{2,1,0:T(8,128)(2,1)S(1)}, u32[]{:S(2)}, u32[]{:S(2)}) collective-permute-start(bf16[2,128,512]{2,1,0:T(8,128)(2,1)S(1)} %join.12.refs_0_), channel_id=1, source_target_pairs={{0,1},{1,0},{2,3},{3,2},{4,5},{5,4},{6,7},{7,6},{8,9},{9,8},{10,11... | collective-permute-start | bytes 786440 | tf_op jit(solution)/shard_map/ppermute | solution.py:44
  278.9 12.1 %collective-permute-start.38 = (bf16[2,128,256]{2,1,0:T(8,128)(2,1)S(1)}, bf16[2,128,256]{2,1,0:T(8,128)(2,1)S(1)}, u32[]{:S(2)}, u32[]{:S(2)}) collective-permute-start(bf16[2,128,256]{2,1,0:T(8,128)(2,1)S(1)} %get-tuple-element.179), channel_id=1, source_target_pairs={{0,1},{1,0},{2,3},{3,2},{4,5},{5,4},{6,7},{7,6},{8,9},{9,8},{10,11... | collective-permute-start | bytes 393224 | tf_op jit(solution)/shard_map/ppermute | solution.py:44
  291.7 27.2 %collective-permute-start.50 = (bf16[4,128,512]{2,1,0:T(8,128)(2,1)S(1)}, bf16[4,128,512]{2,1,0:T(8,128)(2,1)S(1)}, u32[]{:S(2)}, u32[]{:S(2)}) collective-permute-start(bf16[4,128,512]{2,1,0:T(8,128)(2,1)S(1)} %join.13.own_ref), channel_id=1, source_target_pairs={{0,16},{16,0},{1,17},{17,1},{2,18},{18,2},{3,19},{19,3},{4,20},{20... | collective-permute-start | bytes 1572872 | tf_op jit(solution)/shard_map/ppermute | solution.py:44
  302.8 13.3 %collective-permute-start.36 = (bf16[4,168,256]{2,1,0:T(8,128)(2,1)S(1)}, bf16[4,168,256]{2,1,0:T(8,128)(2,1)S(1)}, u32[]{:S(2)}, u32[]{:S(2)}) collective-permute-start(bf16[4,168,256]{2,1,0:T(8,128)(2,1)S(1)} %join.8.refs_0_), channel_id=1, source_target_pairs={{0,16},{16,0},{1,17},{17,1},{2,18},{18,2},{3,19},{19,3},{4,20},{20... | collective-permute-start | bytes 1032200 | tf_op jit(solution)/shard_map/ppermute | solution.py:44
  (68 other events, 657.7 us)

commit v4 on v3

--- a/solution.py
+++ b/solution.py
@@ -10,8 +10,8 @@
 EPSILON = 1e-05
 F32, BF16 = jnp.float32, jnp.bfloat16
 REDUCE_AXES = ("height", "batch")
-REDUCE_CHUNKS, EXPAND_CHUNKS, BACK_CHUNKS = (12, 4), (8, 8), (4, 8, 4)
-OWN_COUNT, TOTAL_COUNT, HEIGHT_AT, CHAN_AT, EDGE_ROW, BATCH_AT = range(6)
+REDUCE_CHUNKS, EXPAND_CHUNKS, BACK_CHUNKS = (8, 8), (8, 8), (8, 8)
+OWN_COUNT, TOTAL_COUNT, HEIGHT_AT, CHAN_AT, EDGE_ROW, NEAR_AT, FAR_AT = range(7)
 VMEM = pl.BlockSpec(memory_space=pltpu.VMEM)
 SMEM = pl.BlockSpec(memory_space=pltpu.SMEM)
 
@@ -20,8 +20,7 @@
     return lax.dot_general(a, b, (((left,), (right,)), ((), ())), preferred_element_type=F32)
 
 
-def kernel_call(body, name, ins, outs, scratch=(), alias=None, flops=0, heavy=0, room=16):
-    moved = sum(a.size * a.dtype.itemsize for a in ins)
+def kernel_call(body, name, ins, outs, scratch=(), alias=None, flops=0, room=16):
     return pl.pallas_call(
         body,
         in_specs=[SMEM if a.dtype == jnp.int32 else VMEM for a in ins],
@@ -30,7 +29,7 @@
         scratch_shapes=list(scratch),
         input_output_aliases=alias or {},
         compiler_params=pltpu.CompilerParams(vmem_limit_bytes=room << 20),
-        cost_estimate=pl.CostEstimate(flops=flops, bytes_accessed=moved, transcendentals=heavy),
+        cost_estimate=pl.CostEstimate(flops=flops, bytes_accessed=0, transcendentals=0),
         name=name,
     )(*ins)
 
@@ -50,6 +49,26 @@
 
 def spread_sums(sent):
     return lax.all_to_all(sent, REDUCE_AXES, 0, 0)
+
+
+def staged_sums(partial, *waits):
+    chans = partial.shape[2]
+    both = kernel_call(
+        add_rows_kernel, "add_rows", [after(partial, *waits), permute(partial, "height", 1)], [((2, chans), F32)]
+    )[0]
+    others = [permute(both, "batch", k) for k in range(1, lax.axis_size("batch"))]
+    return kernel_call(add_sums_kernel, "add_sums", [both] + others, [((1, 2, chans), F32)])[0]
+
+
+def add_rows_kernel(own_ref, other_ref, out_ref):
+    out_ref[...] = jnp.sum(own_ref[...] + other_ref[...], 1)
+
+
+def add_sums_kernel(*refs):
+    total = refs[0][...]
+    for ref in refs[1:-1]:
+        total = total + ref[...]
+    refs[-1][0] = total
 
 
 def norm_of(sums_ref, total):
@@ -155,14 +174,14 @@
     put_sums(sums_ref, one, two)
 
 
-def reduce_chunk(info, pieces, chunk, w_reduce, before, images, plan):
+def reduce_chunk(info, pieces, chunk, w_reduce, before, images, plan, staged):
     pixels, cols = plan
     first, share = chunk
     count, mid = len(pieces), w_reduce.shape[1]
     ins = [info] + list(pieces) + [w_reduce] + ([] if before is None else [before])
     return kernel_call(
         functools.partial(reduce_kernel, first, plan, count), "reduce", ins,
-        [((share, pixels, mid), F32), ((share, cols, mid), BF16), sums_out(first + share == images, mid)],
+        [((share, pixels, mid), F32), ((share, cols, mid), BF16), sums_out(first + share == images and not staged, mid)],
         flops=2 * pieces[0].size * count * mid,
     )
 
@@ -243,7 +262,6 @@
         [info, *reduced, *edges, sums_one, params, matrices],
         [(shape, BF16), (shape, F32), ((images, cols, chans), BF16), sums_out(True, chans)],
         [pltpu.VMEM((images, pixels + 2 * cols, 3 * chans), BF16)],
-        flops=18 * images * pixels * chans * chans, heavy=images * pixels * chans,
     )
 
 
@@ -264,7 +282,7 @@
     shape = (chunk[1] * pixels, grouped.shape[2])
     return kernel_call(
         functools.partial(act_two_kernel, chunk, plan, per_image), "act_two",
-        [info, grouped, sums_two, params], [(shape, BF16)], heavy=shape[0] * shape[1],
+        [info, grouped, sums_two, params], [(shape, BF16)],
     )[0]
 
 
@@ -279,7 +297,7 @@
     for start in range(0, images, step):
         total = None
         for a_ref, w_ref in zip(acts, weights):
-            term = dot(a_ref[start * pixels : (start + step) * pixels, :], w_ref[0:mid, :], 1, 0)
+            term = dot(a_ref[start * pixels : (start + step) * pixels, :], w_ref[...], 1, 0)
             total = term if total is None else total + term
         out_ref[start : start + step] = total.reshape(step, pixels, total.shape[1])
         for i in range(step):
@@ -297,7 +315,6 @@
     return kernel_call(
         functools.partial(expand_kernel, first, plan, count, mid), "expand", ins,
         [((share, pixels, out), F32), sums_out(first + share == images, out)],
-        flops=2 * acts[0].size * count * out,
     )
 
 
@@ -328,7 +345,6 @@
         functools.partial(output_kernel, per_image, len(expanded)), "output",
         [info, *expanded, field, grad_output, sums_three, params],
         [(field.shape, BF16), (field.shape, F32), sums_out(True, field.shape[2])],
-        heavy=field.size,
     )
 
 
@@ -356,7 +372,7 @@
         value = value * (scale * (image < info_ref[OWN_COUNT]).astype(F32))
         out_ref[i * pixels : (i + 1) * pixels, :] = value.astype(BF16)
     for k in range(count):
-        term = dot(out_ref[...], weights[k][0:mid, :], 1, 1)
+        term = dot(out_ref[...], weights[k][...], 1, 1)
         to = slice((k // 2) * mid, (k // 2 + 1) * mid)
         if k % 2 == 0:
             near_ref[:, to] = term
@@ -376,17 +392,17 @@
     )
 
 
-def pair_sum_kernel(near_ref, far_ref, own_ref, *send_refs):
+def pair_sum_kernel(info_ref, near_ref, far_ref, own_ref, *send_refs):
     mid = own_ref.shape[1]
     for k, ref in enumerate((own_ref,) + send_refs):
         at = slice(k * mid, (k + 1) * mid)
         ref[...] = (near_ref[:, at] + far_ref[:, at].astype(F32)).astype(ref.dtype)
 
 
-def pair_sum(near, far, mid):
+def pair_sum(info, near, far, mid):
     rows, half = near.shape
     return kernel_call(
-        pair_sum_kernel, "pair_sum", [near, far],
+        pair_sum_kernel, "pair_sum", [info, near, far],
         [((rows, mid), F32 if k == 0 else BF16) for k in range(half // mid)],
     )
 
@@ -415,15 +431,14 @@
     put_sums(sums_ref, one, two)
 
 
-def slope_two_chunk(info, own, arrived, grouped, sums_two, params, chunk, before, plan, per_image):
+def slope_two_chunk(info, own, arrived, grouped, sums_two, params, chunk, before, plan, per_image, staged):
     pixels, cols = plan
     first, share = chunk
     images, mid = grouped.shape[0], grouped.shape[2]
     ins = [info, own] + list(arrived) + [grouped, sums_two, params] + ([] if before is None else [before])
     return kernel_call(
         functools.partial(slope_two_kernel, first, plan, len(arrived), per_image), "slope_two", ins,
-        [((share, pixels, mid), F32), ((share, cols, mid), BF16), sums_out(first + share == images, mid)],
-        heavy=own.size,
+        [((share, pixels, mid), F32), ((share, cols, mid), BF16), sums_out(first + share == images and not staged, mid)],
     )
 
 
@@ -503,7 +518,6 @@
             pltpu.VMEM((images, pixels + 2 * cols, 3 * chans), BF16),
             pltpu.VMEM((chans, images * pixels), BF16),
         ],
-        flops=36 * images * pixels * chans * chans, heavy=images * pixels * chans,
     )
 
 
@@ -534,7 +548,7 @@
     )[0]
 
 
-def input_grad_kernel(count, mid, grad_ref, *refs):
+def input_grad_kernel(count, info_ref, grad_ref, *refs):
     pieces, weights, out_ref = refs[:count], refs[count : 2 * count], refs[-1]
     rows = 512
 
@@ -542,37 +556,40 @@
         at = pl.ds(pl.multiple_of(step * rows, rows), rows)
         total = grad_ref[at, :]
         for p_ref, w_ref in zip(pieces, weights):
-            total = total + dot(p_ref[at, :], w_ref[mid : 2 * mid, :], 1, 0)
+            total = total + dot(p_ref[at, :], w_ref[...], 1, 1)
         out_ref[at, :] = total.astype(BF16)
         return nothing
 
     lax.fori_loop(0, grad_ref.shape[0] // rows, body, 0)
 
 
-def input_grad(grad_summed, pieces, weights):
-    count, mid = len(pieces), pieces[0].shape[1]
-    return kernel_call(
-        functools.partial(input_grad_kernel, count, mid), "input_grad", [grad_summed] + list(pieces) + list(weights),
-        [(grad_summed.shape, BF16)], flops=2 * pieces[0].size * count * grad_summed.shape[1],
+def input_grad(info, grad_summed, pieces, weights):
+    return kernel_call(
+        functools.partial(input_grad_kernel, len(pieces)), "input_grad", [info, grad_summed] + list(pieces) + list(weights),
+        [(grad_summed.shape, BF16)],
     )[0]
 
 
-def cut_weights_kernel(count, info_ref, reduce_ref, expand_ref, *refs):
-    me = info_ref[CHAN_AT]
-    mid = expand_ref.shape[0]
+def cut_columns_kernel(info_ref, in_ref, *refs):
     for k, ref in enumerate(refs):
         part = ref.shape[1]
-        at = pl.ds(pl.multiple_of((me ^ k) * part, part), part)
-        ref[0:mid, :] = expand_ref[:, at]
-        ref[mid : 2 * mid, :] = reduce_ref[at, :].T
-
-
-def cut_weights(info, w_reduce, w_expand, count):
-    part, mid = w_reduce.shape[0] // count, w_reduce.shape[1]
-    return kernel_call(
-        functools.partial(cut_weights_kernel, count), "cut_weights", [info, w_reduce, w_expand],
-        [((2 * mid, part), BF16)] * count,
-    )
+        ref[...] = in_ref[:, pl.ds(pl.multiple_of((info_ref[CHAN_AT] ^ k) * part, part), part)]
+
+
+def cut_columns(info, value, count):
+    rows, part = value.shape[0], value.shape[1] // count
+    return kernel_call(cut_columns_kernel, "cut_columns", [info, value], [((rows, part), BF16)] * count)
+
+
+def cut_rows_kernel(info_ref, in_ref, *refs):
+    for k, ref in enumerate(refs):
+        part = ref.shape[0]
+        ref[...] = in_ref[pl.ds(pl.multiple_of((info_ref[CHAN_AT] ^ k) * part, part), part), :]
+
+
+def cut_rows(info, value, count):
+    part, cols = value.shape[0] // count, value.shape[1]
+    return kernel_call(cut_rows_kernel, "cut_rows", [info, value], [((part, cols), BF16)] * count)
 
 
 def sum_vectors_kernel(*refs):
@@ -586,6 +603,21 @@
 def sum_vectors(values):
     outs = [((1, v.shape[2]), F32) for v in values for _ in range(2)]
     return [v.reshape(-1) for v in kernel_call(sum_vectors_kernel, "sum_vectors", list(values), outs)]
+
+
+REDUCE_STEPS = (("height", 1, HEIGHT_AT), ("batch", 1, NEAR_AT), ("batch", 2, FAR_AT))
+EXPAND_STEPS = (("height", 1, HEIGHT_AT), ("batch", 1, NEAR_AT), ("batch", 2, FAR_AT))
+
+
+def part_of(info_ref, steps):
+    number = 0
+    for _, _, field in steps:
+        number = number * 2 + info_ref[field]
+    return number
+
+
+def send_half(pair, step):
+    return pair[0], permute(pair[1], step[0], step[1])
 
 
 def split(at, keep_ref, send_ref, all_ref, arrived_ref):
@@ -597,73 +629,52 @@
         ref[...] = value.astype(ref.dtype)
 
 
-def split_first_kernel(make, info_ref, *refs):
+def split_first_kernel(make, field, info_ref, *refs):
     keep_ref, send_ref, all_ref = refs[-3:]
     make(refs[:-3], all_ref)
-    split(info_ref[HEIGHT_AT], keep_ref, send_ref, all_ref, None)
-
-
-def split_first(info, make, name, ins, shape, flops):
+    split(info_ref[field], keep_ref, send_ref, all_ref, None)
+
+
+def split_first(info, make, step, name, ins, shape):
     half = (shape[0] // 2,) + shape[1:]
     return kernel_call(
-        functools.partial(split_first_kernel, make), name, [info] + ins, [(half, F32), (half, BF16)],
-        [pltpu.VMEM(shape, F32)], flops=flops,
-    )
-
-
-def split_next_kernel(bit, info_ref, keep_ref, arrived_ref, out_ref, send_ref):
-    split((info_ref[BATCH_AT] >> bit) & 1, out_ref, send_ref, keep_ref, arrived_ref)
-
-
-def split_next(info, bit, keep, arrived):
-    half = (keep.shape[0] // 2,) + keep.shape[1:]
-    return kernel_call(
-        functools.partial(split_next_kernel, bit), "split_next", [info, keep, arrived], [(half, F32), (half, BF16)]
-    )
-
-
-def add_kernel(first_ref, second_ref, out_ref):
+        functools.partial(split_first_kernel, make, step[2]), name, [info] + ins, [(half, F32), (half, BF16)],
+        [pltpu.VMEM(shape, F32)],
+    )
+
+
+def split_next_kernel(field, info_ref, keep_ref, arrived_ref, out_ref, send_ref):
+    split(info_ref[field], out_ref, send_ref, keep_ref, arrived_ref)
+
+
+def split_next(info, pair, step):
+    half = (pair[0].shape[0] // 2,) + pair[0].shape[1:]
+    return kernel_call(
+        functools.partial(split_next_kernel, step[2]), "split_next", [info, *pair], [(half, F32), (half, BF16)]
+    )
+
+
+def add_kernel(info_ref, first_ref, second_ref, out_ref):
     out_ref[...] = (first_ref[...] + second_ref[...].astype(F32)).astype(BF16)
 
 
-def add_last(keep, arrived):
-    return kernel_call(add_kernel, "add_last", [keep, arrived], [(keep.shape, BF16)])[0]
-
-
-def join_kernel(*refs):
+def add_last(info, pair):
+    return kernel_call(add_kernel, "add_last", [info, *pair], [(pair[0].shape, BF16)])[0]
+
+
+def join_kernel(info_ref, *refs):
     size = refs[0].shape[0]
     for k, ref in enumerate(refs[:-1]):
         refs[-1][k * size : (k + 1) * size] = ref[...]
 
 
-def join(*values):
+def join(info, *values):
     shape = (values[0].shape[0] * len(values),) + values[0].shape[1:]
-    return kernel_call(join_kernel, "join", list(values), [(shape, BF16)])[0]
-
-
-def batch_distance(bit):
-    return lax.axis_size("batch") >> (bit + 1)
-
-
-def scatter_height(pair):
-    return pair[0], permute(pair[1], "height", 1)
-
-
-def scatter_batch(info, pair):
-    for bit in reversed(range(lax.axis_size("batch").bit_length() - 1)):
-        keep, send = split_next(info, bit, *pair)
-        pair = keep, permute(send, "batch", batch_distance(bit))
-    return add_last(*pair)
-
-
-def gather_batch(value):
-    for bit in range(lax.axis_size("batch").bit_length() - 1):
-        value = join(value, permute(value, "batch", batch_distance(bit)))
-    return value
-
-
-def gather_height(value):
-    return value, permute(value, "height", 1)
+    return kernel_call(join_kernel, "join", [info, *values], [(shape, BF16)])[0]
+
+
+def send_back(value, step):
+    return value, permute(value, step[0], step[1])
 
 
 def reduce_grad_make(places, spans, extra, refs, all_ref):
@@ -691,8 +702,8 @@
     extra = 0 if more is None else -(-more.shape[0] * more.shape[1] // (8 * parts)) * 8
     ins = [v for piece in inputs for v in piece] + [grad] + ([] if more is None else [more])
     return split_first(
-        info, functools.partial(reduce_grad_make, len(inputs), tuple(spans), extra), "reduce_grad", ins,
-        (parts, rows // parts + extra, mid), 2 * grad.size * rows,
+        info, functools.partial(reduce_grad_make, len(inputs), tuple(spans), extra), REDUCE_STEPS[0], "reduce_grad", ins,
+        (parts, rows // parts + extra, mid),
     )
 
 
@@ -723,30 +734,26 @@
 def expand_grad(info, acts, grads, parts):
     count, mid, out = len(acts), acts[0][0].shape[1], grads[0].shape[1]
     return split_first(
-        info, functools.partial(expand_grad_make, count, len(acts[0])), "expand_grad",
-        [a for piece in acts for a in piece] + list(grads),
-        (parts, count * mid // parts, out), 2 * sum(g.size for g in grads) * mid * count,
-    )
-
-
-def cut_places_kernel(in_ref, *refs):
+        info, functools.partial(expand_grad_make, count, len(acts[0])), EXPAND_STEPS[0], "expand_grad",
+        [a for piece in acts for a in piece] + list(grads), (parts, count * mid // parts, out),
+    )
+
+
+def cut_places_kernel(info_ref, keep_ref, arrived_ref, *refs):
     size = refs[0].shape[0]
+    total = (keep_ref[0] + arrived_ref[0].astype(F32)).astype(BF16)
     for k, ref in enumerate(refs):
-        ref[...] = in_ref[0, k * size : (k + 1) * size, :]
-
-
-def cut_places(value, count):
-    rows, out = value.shape[1:]
-    return kernel_call(cut_places_kernel, "cut_places", [value], [((rows // count, out), BF16)] * count)
-
-
-def part_rows(info_ref, other, k, batches):
-    return (info_ref[HEIGHT_AT] ^ other) * batches + (info_ref[BATCH_AT] ^ k)
+        ref[...] = total[k * size : (k + 1) * size, :]
+
+
+def cut_places(info, pair, count):
+    rows, out = pair[0].shape[1:]
+    return kernel_call(cut_places_kernel, "cut_places", [info, *pair], [((rows // count, out), BF16)] * count)
 
 
 def place_reduce_kernel(count, info_ref, *refs):
-    out_ref, more_ref = refs[4:]
-    me = info_ref[CHAN_AT]
+    out_ref, group_ref, more_ref = refs[4:]
+    me, number = info_ref[CHAN_AT], part_of(info_ref, REDUCE_STEPS)
     part = out_ref.shape[0] // count
     batches = refs[0].shape[0]
     size = refs[2].shape[1]
@@ -755,30 +762,31 @@
         for other in range(2):
             ref = refs[2 * half + other]
             for k in range(batches):
-                at = part_rows(info_ref, other, k, batches)
+                at = number ^ (other * batches + k)
                 row = at * size
                 to = (me ^ (half * (count // 2) + row // part)) * part + row % part
                 out_ref[pl.ds(pl.multiple_of(to, size), size), :] = ref[k, 0:size, :].astype(F32)
                 if half == 0:
                     more_ref[pl.ds(pl.multiple_of(at * extra, 8), extra), :] = ref[k, size:, :].astype(F32)
-
-
-def place_reduce(info, halves, count, part):
+    group_ref[...] = more_ref[0 : group_ref.shape[0], :]
+
+
+def place_reduce(info, halves, count, part, group_rows):
     batches, rows, mid = halves[0][0].shape
     extra = rows - halves[1][0].shape[1]
     return kernel_call(
         functools.partial(place_reduce_kernel, count), "place_reduce", [info] + [v for pair in halves for v in pair],
-        [((part * count, mid), F32), ((2 * batches * extra, mid), F32)],
+        [((part * count, mid), F32), ((group_rows, mid), F32)], [pltpu.VMEM((2 * batches * extra, mid), F32)],
     )
 
 
 def place_expand_kernel(count, info_ref, own_ref, arrived_ref, out_ref):
-    me = info_ref[CHAN_AT]
+    me, number = info_ref[CHAN_AT], part_of(info_ref, EXPAND_STEPS)
     batches, rows, out = own_ref.shape
     size = rows // count
     for other, ref in enumerate((own_ref, arrived_ref)):
         for k in range(batches):
-            row = part_rows(info_ref, other, k, batches) * size
+            row = (number ^ (other * batches + k)) * size
             for place in range(count):
                 to = pl.ds(pl.multiple_of((me ^ place) * out, out), out)
                 out_ref[pl.ds(pl.multiple_of(row, size), size), to] = ref[k, place * size : (place + 1) * size, :].astype(F32)
@@ -821,127 +829,168 @@
     own_count = jnp.sum(
         jnp.where(jnp.arange(image_counts.shape[0]) == lax.axis_index("batch"), image_counts, 0)
     )
-    batch_at, bits = lax.axis_index("batch"), lax.axis_size("batch").bit_length() - 1
-    turned = sum(((batch_at >> bit) & 1) << (bits - 1 - bit) for bit in range(bits))
+    batch_at = lax.axis_index("batch")
     info = jnp.stack(
-        [own_count, jnp.sum(image_counts), height_at, me, jnp.where(height_at == 0, pixels - cols, 0), turned]
+        [
+            own_count, jnp.sum(image_counts), height_at, me, jnp.where(height_at == 0, pixels - cols, 0),
+            batch_at & 1, (batch_at >> 1) & 1,
+        ]
     ).astype(jnp.int32)
     parts = lax.axis_size(REDUCE_AXES)
-    staged = lax.axis_size("batch") == 4
+    staged = (lax.axis_size("height"), lax.axis_size("batch")) == (2, 4)
 
     def edge_swap(edge):
         return permute(edge, "height", 1)
 
-    def far_swaps(value, pieces):
+    def sums_of(sums, *waits):
+        return staged_sums(sums, *waits) if staged else spread_sums(sums)
+
+    def gather(value, *waits):
+        pieces = [value, swap(value, 1)]
         for k in distances:
-            pieces[k].append(swap(value, k))
-
-    def core_swaps(pieces, *waits):
-        for k in distances:
-            pieces[k + 1].append(swap(after(pieces[k][-1], *waits) if waits else pieces[k][-1], 1))
+            pieces.append(swap(value, k))
+            pieces.append(swap(after(pieces[k], *waits) if waits else pieces[k], 1))
+        return pieces
 
     field = block_input.reshape(images * pixels, out_part)
     matrices, matrices_back, mid_params, out_params = prepare(
         info, w_group, (gain_one, bias_one, gain_two, bias_two), (gain_three, bias_three)
     )
-    inputs = [[] for _ in range(chan_size)]
+    columns = cut_columns(info, w_expand, chan_size)
+    rows_back = cut_rows(info, w_reduce, chan_size)
+    weights = [columns[0], swap(columns[1], 1)]
+    reduce_back = [rows_back[0], swap(rows_back[1], 1)]
+    inputs = []
+    for first, share in cut_images(REDUCE_CHUNKS):
+        source = after(field, inputs[0][0], info) if first else field
+        piece = lax.slice_in_dim(source, first * pixels, (first + share) * pixels)
+        inputs.append(gather(piece, mid_params, weights[1], reduce_back[1]) if first else gather(piece))
     reduced, red_edges, sums = [], [], None
-    for first, share in cut_images(REDUCE_CHUNKS):
-        source = after(field, inputs[0][0]) if first else field
-        piece = lax.slice_in_dim(source, first * pixels, (first + share) * pixels)
-        inputs[0].append(piece)
-        far_swaps(piece, inputs)
-        inputs[1].append(swap(piece, 1))
-        core_swaps(inputs, *(() if sums is None else (sums,)))
-        red, edge, sums = reduce_chunk(info, [p[-1] for p in inputs], (first, share), w_reduce, sums, images, plan)
+    for pieces, (first, share) in zip(inputs, cut_images(REDUCE_CHUNKS)):
+        red, edge, sums = reduce_chunk(info, pieces, (first, share), w_reduce, sums, images, plan, False)
         reduced.append(red)
         red_edges.append(edge_swap(edge))
-    sums_one = spread_sums(sums)
-
-    w_expand, w_reduce = after((w_expand, w_reduce), sums)
-    weights = cut_weights(info, w_reduce, w_expand, chan_size)
-    weights = [v if k == 0 else swap(v, k) for k, v in enumerate(weights)]
+    inputs = [list(chunks) for chunks in zip(*inputs)]
+    weights += [swap(after(columns[k], inputs[2][-1]), k) for k in range(2, chan_size)]
+    sums_one = spread_sums(after(sums, *weights[2:]))
 
     acts_one, grouped, grp_edge, sums = conv_forward(
         info, reduced, red_edges, sums_one, mid_params, matrices, per_image
     )
     sums_two = spread_sums(sums)
 
-    acts = [[] for _ in range(chan_size)]
+    acts = []
     for chunk in cut_images(EXPAND_CHUNKS):
-        acts[0].append(act_two_chunk(info, grouped, sums_two, mid_params, chunk, plan, per_image))
-        far_swaps(acts[0][-1], acts)
+        acts.append(gather(act_two_chunk(info, grouped, sums_two, mid_params, chunk, plan, per_image)))
     expanded, sums = [], None
-    for c, chunk in enumerate(cut_images(EXPAND_CHUNKS)):
-        acts[1].append(swap(acts[0][c], 1))
-        for k in distances:
-            acts[k + 1].append(swap(acts[k][c] if sums is None else after(acts[k][c], sums), 1))
-        out, sums = expand_chunk(info, [piece[c] for piece in acts], weights, chunk, sums, images, plan)
+    for pieces, chunk in zip(acts, cut_images(EXPAND_CHUNKS)):
+        out, sums = expand_chunk(info, pieces, weights, chunk, sums, images, plan)
         expanded.append(out)
+    acts = [list(chunks) for chunks in zip(*acts)]
     sums_three = spread_sums(sums)
-    grp_edge = edge_swap(after(grp_edge, sums_three))
     output, grad_summed, sums = output_pass(
         info, expanded, field.reshape(images, pixels, out_part), grad_output.reshape(images, pixels, out_part), sums_three,
         out_params, per_image,
     )
     grads_three = spread_sums(sums)
 
-    own, sent = [], [[] for _ in range(chan_size)]
-    grad_expanded = []
+    grad_expanded, halves = [], []
     for chunk in cut_images(BACK_CHUNKS):
-        grad_here = after(grad_summed, own[-2]) if len(own) > 1 else grad_summed
         grad, near, far = back_expand_chunk(
-            info, grad_here, expanded, sums_three, grads_three, out_params, weights, chunk, mid_part, plan, per_image
+            info, grad_summed, expanded, sums_three, grads_three, out_params, weights, chunk, mid_part, plan, per_image
         )
         grad_expanded.append(grad)
-        summed = pair_sum(near, swap(far, 1), mid_part)
+        halves.append((near, swap(far, 1)))
+    own, sent = [], []
+    for near, far in halves:
+        summed = pair_sum(info, near, far, mid_part)
         own.append(summed[0])
-        for value, k in zip(summed[1:], distances):
-            sent[k].append(swap(value, k))
+        sent.append([swap(value, k) for value, k in zip(summed[1:], distances)])
+    grp_edge = edge_swap(after(grp_edge, own[0]))
     if staged:
-        expand_part = scatter_height(expand_grad(info, acts, after(grad_expanded, own[-1]), parts))
-    d_two, d_edges, sums = [], [], None
+        expand_pair = send_half(expand_grad(info, acts, grad_expanded, parts), EXPAND_STEPS[0])
+    d_two, d_edges, sums, turn = [], [], None, info
     for c, chunk in enumerate(cut_images(BACK_CHUNKS)):
+        if staged and c == 1:
+            pair = split_next(after(info, d_two[0]), expand_pair, EXPAND_STEPS[1])
+            turn = after(info, pair[0])
+            expand_pair = send_half(pair, EXPAND_STEPS[1])
         grad, edge, sums = slope_two_chunk(
-            info, own[c], [sent[k][c] for k in distances], grouped, sums_two, mid_params, chunk, sums, plan, per_image
+            turn, own[c], sent[c], grouped, sums_two, mid_params, chunk, sums, plan, per_image, staged
         )
         d_two.append(grad)
-        d_edges.append(edge)
+        d_edges.append(edge_swap(edge))
+    grads_two = sums_of(sums, grp_edge, *d_edges)
+    turn = info
     if staged:
-        sums = after(sums, expand_part[1])
-    grads_two = spread_sums(sums)
-    d_edges = [edge_swap(edge) for edge in d_edges]
+        pair = split_next(after(info, grads_two), expand_pair, EXPAND_STEPS[2])
+        turn = after(info, pair[0])
+        expand_pair = send_half(pair, EXPAND_STEPS[2])
+
+    d_one, sums, grad_group = conv_backward(
+        turn, d_two, d_edges, grouped, grp_edge, reduced, acts_one, sums_two, grads_two, sums_one, mid_params,
+        matrices_back, group, per_image,
+    )
     if staged:
-        expand_part = scatter_batch(info, (expand_part[0], after(expand_part[1], grads_two)))
-
-    d_one, sums, grad_group = conv_backward(
-        info, d_two, d_edges, grouped, grp_edge, reduced, acts_one, sums_two, grads_two, sums_one, mid_params,
-        matrices_back, group, per_image,
-    )
+        places = cut_places(after(info, d_one), expand_pair, chan_size)
+        sums = after(sums, places[0])
     grads_one = spread_sums(sums)
 
-    grads = [[] for _ in range(chan_size)]
-    grads[0].append(grad_reduced(info, d_one, reduced, sums_one, grads_one, mid_params, per_image))
-    far_swaps(grads[0][0], grads)
-    grads[1].append(swap(grads[0][0], 1))
-    core_swaps(grads)
-    half = chan_size // 2
+    grad = grad_reduced(info, d_one, reduced, sums_one, grads_one, mid_params, per_image)
+    grad_field = grad_summed.reshape(images * pixels, out_part)
     if staged:
-        halves = [
-            scatter_height(reduce_grad(info, inputs[i * half : (i + 1) * half], grads[0][0], parts, None if i else grad_group))
-            for i in range(2)
-        ]
-        halves = [gather_height(gather_batch(scatter_batch(info, pair))) for pair in halves]
-        grad_reduce, grad_group = place_reduce(info, halves, chan_size, out_part)
-        grad_group = grad_group[: 9 * group]
-        places = cut_places(expand_part, chan_size)
-        places = [v if k == 0 else swap(v, k) for k, v in enumerate(places)]
-        expand_part = after(join(*places), grads_one)
-        expand_part = gather_height(gather_batch(expand_part.reshape((1,) + expand_part.shape)))
-        grad_expand = place_expand(info, expand_part, chan_size, mid_part)
+        half = chan_size // 2
+        pairs, turn = [], after(info, grad)
+
+        def in_turn(call, *args):
+            nonlocal turn
+            result = call(turn, *args)
+            turn = after(info, result[0] if isinstance(result, (list, tuple)) else result)
+            return result
+
+        def first_half(i):
+            own = inputs[i * half : (i + 1) * half]
+            pair = in_turn(reduce_grad, own, grad, parts, None if i else grad_group)
+            pairs.append(send_half(pair, REDUCE_STEPS[0]))
+
+        def next_half(i, step):
+            pairs[i] = send_half(in_turn(split_next, pairs[i], REDUCE_STEPS[step]), REDUCE_STEPS[step])
+
+        def last_half(i):
+            pairs[i] = send_back(in_turn(add_last, pairs[i]), REDUCE_STEPS[2])
+
+        def back_half(i, step):
+            pairs[i] = send_back(in_turn(join, *pairs[i]), REDUCE_STEPS[step])
+
+        first_half(0)
+        first_half(1)
+        places = [v if k == 0 else swap(after(v, turn), k) for k, v in enumerate(places)]
+        back = in_turn(join, *places)
+        back = send_back(back.reshape((1,) + back.shape), EXPAND_STEPS[2])
+        far_grads = [swap(after(grad, turn), k) for k in distances]
+        next_half(0, 1)
+        next_half(1, 1)
+        back = send_back(in_turn(join, *back), EXPAND_STEPS[1])
+        next_half(0, 2)
+        next_half(1, 2)
+        back = send_back(in_turn(join, *back), EXPAND_STEPS[0])
+        last_half(0)
+        last_half(1)
+        grads = [grad, swap(after(grad, turn), 1)]
+        for value in far_grads:
+            grads += [value, swap(after(value, turn), 1)]
+        reduce_back += [swap(after(rows_back[k], turn), k) for k in range(2, chan_size)]
+        back_half(0, 1)
+        grad_input = in_turn(input_grad, grad_field, grads, reduce_back)
+        back_half(1, 1)
+        back_half(0, 0)
+        grad_expand = in_turn(place_expand, back, chan_size, mid_part)
+        back_half(1, 0)
+        grad_reduce, grad_group = place_reduce(turn, pairs, chan_size, out_part, 9 * group)
     else:
-        grad_reduce, grad_expand, grad_group = plain_weight_grads(inputs, grads[0][0], acts, grad_expanded, grad_group)
-    grad_input = input_grad(grad_summed.reshape(images * pixels, out_part), [piece[0] for piece in grads], weights)
+        reduce_back += [swap(rows_back[k], k) for k in range(2, chan_size)]
+        grad_input = input_grad(info, grad_field, gather(grad), reduce_back)
+        grad_reduce, grad_expand, grad_group = plain_weight_grads(inputs, grad, acts, grad_expanded, grad_group)
     vectors = sum_vectors([grads_one, grads_two, grads_three])
     return (
         output.reshape(block_input.shape), grad_input.reshape(block_input.shape), grad_reduce,

time: 326 us -> 299 us (0.917)
  local copies, waits for them, and re-layouts: 22.5 us -> 4.18 us
  waiting for transfers between devices: 149 us -> 132 us
  blocking collectives: 36.4 us -> 50.8 us
  starting transfers between devices: 48.7 us -> 44.6 us
    unnamed x94 -> x24, local copies, waits for them, and re-layouts: 17.6 us -> 0.07 us
    all_to_all x4 -> x5, blocking collectives: 36.4 us -> 50.8 us  [spread_sums(): return lax.all_to_all(sent, REDUCE_AXES, 0, 0)]
    all_to_all x2 -> x0, waiting for transfers between devices: 9.96 us -> none  [spread_sums(): return lax.all_to_all(sent, REDUCE_AXES, 0, 0)]
    all_to_all x2 -> x0, starting transfers between devices: 8.21 us -> none  [spread_sums(): return lax.all_to_all(sent, REDUCE_AXES, 0, 0)]
    ppermute x51 -> x55, waiting for transfers between devices: 139 us -> 132 us  [permute(): return lax.ppermute(value, axis, [(i, i ^ distance) for i in range(count)])]
    ppermute x51 -> x55, starting transfers between devices: 40.5 us -> 44.6 us  [permute(): return lax.ppermute(value, axis, [(i, i ^ distance) for i in range(count)])]
    pallas_call x45 -> x44, Pallas kernels: 66.7 us -> 64.5 us  [kernel_call(): pl.pallas_call(body, in_specs=[SMEM if a.dtype == jnp.int32 else VMEM for...]
  transfers between devices with their start and end apart: 53 -> 55, of which waited for: 23 -> 30; matrix products, arithmetic and copies ran while one was open for 1% -> 1% of each run, Pallas kernels for 12% -> 14%
where the time goes in v4:
time: 299 us; the launch traced here: 298 us
  waiting for transfers between devices  132 us (44%)
  Pallas kernels  64.5 us (22%)
  blocking collectives  50.8 us (17%)
  starting transfers between devices  44.6 us (15%)
  local copies, waits for them, and re-layouts  4.18 us (1%)
    ppermute x55, waiting for transfers between devices, permute(): return lax.ppermute(value, axis, [(i, i ^ distance) for i in range(count)])  132 us
    pallas_call x44, Pallas kernels, kernel_call(): pl.pallas_call(body, in_specs=[SMEM if a.dtype == jnp.int32 else VMEM for...  64.5 us
    all_to_all x5, blocking collectives, spread_sums(): return lax.all_to_all(sent, REDUCE_AXES, 0, 0)  50.8 us
    ppermute x55, starting transfers between devices, permute(): return lax.ppermute(value, axis, [(i, i ^ distance) for i in range(count)])  44.6 us
  transfers between devices with their start and end apart: 55, of which 30 were waited for; matrix products, arithmetic and copies ran while one was open for 1% of the time, Pallas kernels for 14%

profile of v4, /device:TPU:0, one launch (start us, length us, event | category | flops | bytes accessed | tf_op | source)
XLA Modules:
  0.0 298.4 jit_solution(11722920148527196603)
XLA Ops:
  2.0 3.0 %collective-permute-start.1 = (bf16[1024,512]{1,0:T(8,128)(2,1)S(1)}, bf16[1024,512]{1,0:T(8,128)(2,1)S(1)}, u32[]{:S(2)}, u32[]{:S(2)}) collective-permute-start(bf16[1024,512]{1,0:T(8,128)(2,1)S(1)} %bitcast.24), channel_id=1, source_target_pairs={{0,8},{4,12},{8,0},{12,4},{1,9},{5,13},{9,1},{13,5},{2,10},{6,14},... | collective-permute-start | bytes 3145736 | tf_op jit(solution)/shard_map/ppermute | solution.py:43
  10.6 18.4 %collective-permute-done.1.refs_2_.refs_0_ = bf16[1024,512]{1,0:T(8,128)(2,1)S(1)} collective-permute-done((bf16[1024,512]{1,0:T(8,128)(2,1)S(1)}, bf16[1024,512]{1,0:T(8,128)(2,1)S(1)}, u32[]{:S(2)}, u32[]{:S(2)}) %collective-permute-start.1) | collective-permute-done | bytes 1048608 | tf_op jit(solution)/shard_map/ppermute | solution.py:43
  30.7 19.9 %collective-permute-done.4.refs_2_.refs_1_ = bf16[1024,512]{1,0:T(8,128)(2,1)S(1)} collective-permute-done((bf16[1024,512]{1,0:T(8,128)(2,1)S(1)}, bf16[1024,512]{1,0:T(8,128)(2,1)S(1)}, u32[]{:S(2)}, u32[]{:S(2)}) %collective-permute-start.4) | collective-permute-done | bytes 1048608 | tf_op jit(solution)/shard_map/ppermute | solution.py:43
  59.7 4.8 %collective-permute-done.11.refs_7_.refs_9_ = bf16[256,512]{1,0:T(8,128)(2,1)S(1)} collective-permute-done((bf16[256,512]{1,0:T(8,128)(2,1)S(1)}, bf16[256,512]{1,0:T(8,128)(2,1)S(1)}, u32[]{:S(2)}, u32[]{:S(2)}) %collective-permute-start.11) | collective-permute-done | bytes 262176 | tf_op jit(solution)/shard_map/ppermute | solution.py:43
  64.6 12.5 %all_to_all.25.refs_4_.refs_11_.refs_3_ = f32[8,2,256]{2,1,0:T(2,128)S(1)} all-to-all(f32[8,2,256]{2,1,0:T(2,128)S(1)} %get-tuple-element.143), channel_id=1, replica_groups=mesh['height'=2,'chan'=4,'batch'=4] {'height','batch'}, dimensions={0} | all-to-all | bytes 32768 | tf_op jit(solution)/shard_map/all_to_all | solution.py:51
  77.1 5.2 %conv_forward.1 = (bf16[16,128,256]{2,1,0:T(8,128)(2,1)S(1)}, f32[16,128,256]{2,1,0:T(8,128)S(1)}, bf16[16,16,256]{2,1,0:T(8,128)(2,1)S(1)}, f32[8,2,256]{2,1,0:T(2,128)S(1)}) custom-call(s32[7]{0:T(128)S(1)} %stack.31.info_ref, f32[8,128,256]{2,1,0:T(8,128)S(1)} %get-tuple-element.128.refs_0_.refs_4_, ...), custom_call_target="tpu_custom_call" | custom-call | tf_op jit(solution)/shard_map/conv_forward/pallas_call | solution.py:24
  82.2 9.0 %all_to_all.26.sums_ref.refs_2_.refs_9_ = f32[8,2,256]{2,1,0:T(2,128)S(1)} all-to-all(f32[8,2,256]{2,1,0:T(2,128)S(1)} %get-tuple-element.146), channel_id=1, replica_groups=mesh['height'=2,'chan'=4,'batch'=4] {'height','batch'}, dimensions={0} | all-to-all | bytes 32768 | tf_op jit(solution)/shard_map/all_to_all | solution.py:51
  95.2 11.9 %collective-permute-done.13.refs_2_.refs_4_ = bf16[1024,256]{1,0:T(8,128)(2,1)S(1)} collective-permute-done((bf16[1024,256]{1,0:T(8,128)(2,1)S(1)}, bf16[1024,256]{1,0:T(8,128)(2,1)S(1)}, u32[]{:S(2)}, u32[]{:S(2)}) %collective-permute-start.13) | collective-permute-done | bytes 524320 | tf_op jit(solution)/shard_map/ppermute | solution.py:43
  107.5 7.3 %collective-permute-done.16.refs_2_.refs_5_ = bf16[1024,256]{1,0:T(8,128)(2,1)S(1)} collective-permute-done((bf16[1024,256]{1,0:T(8,128)(2,1)S(1)}, bf16[1024,256]{1,0:T(8,128)(2,1)S(1)}, u32[]{:S(2)}, u32[]{:S(2)}) %collective-permute-start.16) | collective-permute-done | bytes 524320 | tf_op jit(solution)/shard_map/ppermute | solution.py:43
  118.6 9.1 %all_to_all.27.refs_4_.refs_3_ = f32[8,2,512]{2,1,0:T(2,128)S(1)} all-to-all(f32[8,2,512]{2,1,0:T(2,128)S(1)} %get-tuple-element.151), channel_id=1, replica_groups=mesh['height'=2,'chan'=4,'batch'=4] {'height','batch'}, dimensions={0} | all-to-all | bytes 65536 | tf_op jit(solution)/shard_map/all_to_all | solution.py:51
  127.7 5.1 %output.1 = (bf16[16,128,512]{2,1,0:T(8,128)(2,1)}, f32[16,128,512]{2,1,0:T(8,128)S(1)}, f32[8,2,512]{2,1,0:T(2,128)S(1)}) custom-call(s32[7]{0:T(128)S(1)} %stack.31.info_ref, f32[8,128,512]{2,1,0:T(8,128)S(1)} %get-tuple-element.148.refs_0_, f32[8,128,512]{2,1,0:T(8,128)S(1)} %get-tuple-element.150.refs_1_, bf16[16,128,512]{2,1,0:T(8,128)(2,1)S(1)} %bitcast.29, ...), custom_call_target="tpu_custom_call" | custom-call | tf_op jit(solution)/shard_map/output/pallas_call | solution.py:24
  132.8 9.1 %all_to_all.28.refs_4_.refs_2_ = f32[8,2,512]{2,1,0:T(2,128)S(1)} all-to-all(f32[8,2,512]{2,1,0:T(2,128)S(1)} %get-tuple-element.155), channel_id=1, replica_groups=mesh['height'=2,'chan'=4,'batch'=4] {'height','batch'}, dimensions={0} | all-to-all | bytes 65536 | tf_op jit(solution)/shard_map/all_to_all | solution.py:51
  148.8 3.0 %expand_grad.1 = (f32[4,128,512]{2,1,0:T(8,128)S(1)}, bf16[4,128,512]{2,1,0:T(8,128)(2,1)S(1)}) custom-call(s32[7]{0:T(128)S(1)} %stack.31.info_ref, bf16[1024,256]{1,0:T(8,128)(2,1)S(1)} %act_two.2.refs_0_, bf16[1024,256]{1,0:T(8,128)(2,1)S(1)} %act_two.3.refs_0_.refs_1_, bf16[1024,256]{1,0:T(8,128)(2,1)S(1)} %collective-permute-done.12.refs_1_.refs_2_, ...), custom_call_target="tpu_custom_call" | custom-call | tf_op jit(solution)/shard_map/expand_grad/pallas_call | solution.py:24
  153.8 8.3 %collective-permute-done.19.refs_0_ = bf16[1024,256]{1,0:T(8,128)(2,1)S(1)} collective-permute-done((bf16[1024,256]{1,0:T(8,128)(2,1)S(1)}, bf16[1024,256]{1,0:T(8,128)(2,1)S(1)}, u32[]{:S(2)}, u32[]{:S(2)}) %collective-permute-start.19) | collective-permute-done | bytes 524320 | tf_op jit(solution)/shard_map/ppermute | solution.py:43
  163.4 2.2 collective-permute-done.20.arrived_ref
  167.3 5.2 %collective-permute-done.22.refs_0_ = bf16[1024,256]{1,0:T(8,128)(2,1)S(1)} collective-permute-done((bf16[1024,256]{1,0:T(8,128)(2,1)S(1)}, bf16[1024,256]{1,0:T(8,128)(2,1)S(1)}, u32[]{:S(2)}, u32[]{:S(2)}) %collective-permute-start.22) | collective-permute-done | bytes 524320 | tf_op jit(solution)/shard_map/ppermute | solution.py:43
  180.9 3.3 %collective-permute-start.29 = (f32[2,256]{1,0:T(2,128)S(1)}, f32[2,256]{1,0:T(2,128)S(1)}, u32[]{:S(2)}, u32[]{:S(2)}) collective-permute-start(f32[2,256]{1,0:T(2,128)S(1)} %add_rows.1.refs_0_), channel_id=1, source_target_pairs={{0,3},{1,2},{2,1},{3,0},{4,7},{5,6},{6,5},{7,4},{8,11},{9,10},{10,... | collective-permute-start | bytes 6152 | tf_op jit(solution)/shard_map/ppermute | solution.py:43
  187.4 8.3 %conv_backward.1 = (f32[16,128,256]{2,1,0:T(8,128)S(1)}, f32[8,2,256]{2,1,0:T(2,128)S(1)}, f32[9,32,256]{2,1,0:T(8,128)S(1)}) custom-call(s32[7]{0:T(128)S(1)} %stack.31.info_ref, f32[8,128,256]{2,1,0:T(8,128)S(1)} %get-tuple-element.160.refs_0_, f32[8,128,256]{2,1,0:T(8,128)S(1)} %get-tuple-element.183.refs_1_, ...), custom_call_target="tpu_custom_call" | custom-call | tf_op jit(solution)/shard_map/conv_backward/pallas_call | solution.py:24
  196.4 11.2 %all_to_all.29.refs_4_.refs_0_ = f32[8,2,256]{2,1,0:T(2,128)S(1)} all-to-all(f32[8,2,256]{2,1,0:T(2,128)S(1)} %get-tuple-element.191), channel_id=1, replica_groups=mesh['height'=2,'chan'=4,'batch'=4] {'height','batch'}, dimensions={0} | all-to-all | bytes 32768 | tf_op jit(solution)/shard_map/all_to_all | solution.py:51
  208.6 1.9 reduce_grad.2
  221.1 8.5 %collective-permute-done.35.arrived_ref = bf16[4,168,256]{2,1,0:T(8,128)(2,1)S(1)} collective-permute-done((bf16[4,168,256]{2,1,0:T(8,128)(2,1)S(1)}, bf16[4,168,256]{2,1,0:T(8,128)(2,1)S(1)}, u32[]{:S(2)}, u32[]{:S(2)}) %collective-permute-start.35) | collective-permute-done | bytes 344096 | tf_op jit(solution)/shard_map/ppermute | solution.py:43
  230.2 3.6 %collective-permute-done.36.arrived_ref = bf16[4,128,256]{2,1,0:T(8,128)(2,1)S(1)} collective-permute-done((bf16[4,128,256]{2,1,0:T(8,128)(2,1)S(1)}, bf16[4,128,256]{2,1,0:T(8,128)(2,1)S(1)}, u32[]{:S(2)}, u32[]{:S(2)}) %collective-permute-start.36) | collective-permute-done | bytes 262176 | tf_op jit(solution)/shard_map/ppermute | solution.py:43
  237.6 9.4 %collective-permute-done.38.arrived_ref = bf16[2,168,256]{2,1,0:T(8,128)(2,1)S(1)} collective-permute-done((bf16[2,168,256]{2,1,0:T(8,128)(2,1)S(1)}, bf16[2,168,256]{2,1,0:T(8,128)(2,1)S(1)}, u32[]{:S(2)}, u32[]{:S(2)}) %collective-permute-start.38) | collective-permute-done | bytes 172064 | tf_op jit(solution)/shard_map/ppermute | solution.py:43
  251.8 2.1 collective-permute-done.41.second_ref
  259.6 3.9 %collective-permute-done.43.refs_1_ = bf16[1,168,256]{2,1,0:T(8,128)(2,1)S(1)} collective-permute-done((bf16[1,168,256]{2,1,0:T(8,128)(2,1)S(1)}, bf16[1,168,256]{2,1,0:T(8,128)(2,1)S(1)}, u32[]{:S(2)}, u32[]{:S(2)}) %collective-permute-start.43) | collective-permute-done | bytes 86048 | tf_op jit(solution)/shard_map/ppermute | solution.py:43
  265.9 2.9 collective-permute-start.50
  268.8 3.1 %collective-permute-done.48.refs_7_ = bf16[512,256]{1,0:T(8,128)(2,1)S(1)} collective-permute-done((bf16[512,256]{1,0:T(8,128)(2,1)S(1)}, bf16[512,256]{1,0:T(8,128)(2,1)S(1)}, u32[]{:S(2)}, u32[]{:S(2)}) %collective-permute-start.48) | collective-permute-done | bytes 262176 | tf_op jit(solution)/shard_map/ppermute | solution.py:43
  272.5 4.8 %input_grad.1 = bf16[2048,512]{1,0:T(8,128)(2,1)} custom-call(s32[7]{0:T(128)S(1)} %stack.31.info_ref, f32[2048,512]{1,0:T(8,128)S(1)} %bitcast.23, bf16[2048,256]{1,0:T(8,128)(2,1)S(1)} %grad_reduced.1.refs_4_.refs_0_, bf16[2048,256]{1,0:T(8,128)(2,1)S(1)} %collective-permute-done.44.refs_1_, bf16[2048,256]{1,0:T(8,128)(2,1)S(1)} %collective-permute-done.45.refs_2_, ...), custom_call_target="tpu_custom_call" | custom-call | tf_op jit(solution)/shard_map/input_grad/pallas_call | solution.py:24
  281.4 2.0 place_expand.1
  287.2 4.6 %collective-permute-done.53.refs_1_ = bf16[4,168,256]{2,1,0:T(8,128)(2,1)S(1)} collective-permute-done((bf16[4,168,256]{2,1,0:T(8,128)(2,1)S(1)}, bf16[4,168,256]{2,1,0:T(8,128)(2,1)S(1)}, u32[]{:S(2)}, u32[]{:S(2)}) %collective-permute-start.53) | collective-permute-done | bytes 344096 | tf_op jit(solution)/shard_map/ppermute | solution.py:43
  291.8 4.4 %collective-permute-done.54.refs_3_ = bf16[4,128,256]{2,1,0:T(8,128)(2,1)S(1)} collective-permute-done((bf16[4,128,256]{2,1,0:T(8,128)(2,1)S(1)}, bf16[4,128,256]{2,1,0:T(8,128)(2,1)S(1)}, u32[]{:S(2)}, u32[]{:S(2)}) %collective-permute-start.54) | collective-permute-done | bytes 262176 | tf_op jit(solution)/shard_map/ppermute | solution.py:43
  296.2 2.2 place_reduce.1
  (161 shorter events, 86.8 us)
Async XLA Ops:
  2.0 27.0 %collective-permute-start.1 = (bf16[1024,512]{1,0:T(8,128)(2,1)S(1)}, bf16[1024,512]{1,0:T(8,128)(2,1)S(1)}, u32[]{:S(2)}, u32[]{:S(2)}) collective-permute-start(bf16[1024,512]{1,0:T(8,128)(2,1)S(1)} %bitcast.24), channel_id=1, source_target_pairs={{0,8},{4,12},{8,0},{12,4},{1,9},{5,13},{9,1},{13,5},{2,10},{6,14},... | collective-permute-start | bytes 3145736 | tf_op jit(solution)/shard_map/ppermute | solution.py:43
  8.5 42.2 %collective-permute-start.4 = (bf16[1024,512]{1,0:T(8,128)(2,1)S(1)}, bf16[1024,512]{1,0:T(8,128)(2,1)S(1)}, u32[]{:S(2)}, u32[]{:S(2)}) collective-permute-start(bf16[1024,512]{1,0:T(8,128)(2,1)S(1)} %slice.11.refs_0_.refs_1_), channel_id=1, source_target_pairs={{0,8},{4,12},{8,0},{12,4},{1,9},{5,13},{9,1},{13,5},{2,10},{6,14},... | collective-permute-start | bytes 3145736 | tf_op jit(solution)/shard_map/ppermute | solution.py:43
  9.2 20.9 %collective-permute-start.5 = (bf16[256,512]{1,0:T(8,128)(2,1)S(1)}, bf16[256,512]{1,0:T(8,128)(2,1)S(1)}, u32[]{:S(2)}, u32[]{:S(2)}) collective-permute-start(bf16[256,512]{1,0:T(8,128)(2,1)S(1)} %get-tuple-element.131), channel_id=1, source_target_pairs={{0,4},{4,0},{8,12},{12,8},{1,5},{5,1},{9,13},{13,9},{2,6},{6,2},{1... | collective-permute-start | bytes 786440 | tf_op jit(solution)/shard_map/ppermute | solution.py:43
  9.9 20.8 %collective-permute-start.6 = (bf16[512,256]{1,0:T(8,128)(2,1)S(1)}, bf16[512,256]{1,0:T(8,128)(2,1)S(1)}, u32[]{:S(2)}, u32[]{:S(2)}) collective-permute-start(bf16[512,256]{1,0:T(8,128)(2,1)S(1)} %get-tuple-element.132), channel_id=1, source_target_pairs={{0,4},{4,0},{8,12},{12,8},{1,5},{5,1},{9,13},{13,9},{2,6},{6,2},{1... | collective-permute-start | bytes 786440 | tf_op jit(solution)/shard_map/ppermute | solution.py:43
  10.5 41.9 %collective-permute-start = (bf16[1024,512]{1,0:T(8,128)(2,1)S(1)}, bf16[1024,512]{1,0:T(8,128)(2,1)S(1)}, u32[]{:S(2)}, u32[]{:S(2)}) collective-permute-start(bf16[1024,512]{1,0:T(8,128)(2,1)S(1)} %bitcast.25), channel_id=1, source_target_pairs={{0,4},{4,0},{8,12},{12,8},{1,5},{5,1},{9,13},{13,9},{2,6},{6,2},{1... | collective-permute-start | bytes 3145736 | tf_op jit(solution)/shard_map/ppermute | solution.py:43
  29.0 23.5 %collective-permute-start.2 = (bf16[1024,512]{1,0:T(8,128)(2,1)S(1)}, bf16[1024,512]{1,0:T(8,128)(2,1)S(1)}, u32[]{:S(2)}, u32[]{:S(2)}) collective-permute-start(bf16[1024,512]{1,0:T(8,128)(2,1)S(1)} %collective-permute-done.1.refs_2_.refs_0_), channel_id=1, source_target_pairs={{0,4},{4,0},{8,12},{12,8},{1,5},{5,1},{9,13},{13,9},{2,6},{6,2},{1... | collective-permute-start | bytes 3145736 | tf_op jit(solution)/shard_map/ppermute | solution.py:43
  30.1 24.3 %collective-permute-start.3 = (bf16[1024,512]{1,0:T(8,128)(2,1)S(1)}, bf16[1024,512]{1,0:T(8,128)(2,1)S(1)}, u32[]{:S(2)}, u32[]{:S(2)}) collective-permute-start(bf16[1024,512]{1,0:T(8,128)(2,1)S(1)} %slice.11.refs_0_.refs_1_), channel_id=1, source_target_pairs={{0,4},{4,0},{8,12},{12,8},{1,5},{5,1},{9,13},{13,9},{2,6},{6,2},{1... | collective-permute-start | bytes 3145736 | tf_op jit(solution)/shard_map/ppermute | solution.py:43
  52.4 12.2 %collective-permute-start.11 = (bf16[256,512]{1,0:T(8,128)(2,1)S(1)}, bf16[256,512]{1,0:T(8,128)(2,1)S(1)}, u32[]{:S(2)}, u32[]{:S(2)}) collective-permute-start(bf16[256,512]{1,0:T(8,128)(2,1)S(1)} %get-tuple-element.142), channel_id=1, source_target_pairs={{0,12},{4,8},{8,4},{12,0},{1,13},{5,9},{9,5},{13,1},{2,14},{6,10},... | collective-permute-start | bytes 786440 | tf_op jit(solution)/shard_map/ppermute | solution.py:43
  56.3 20.8 %collective-permute-start.9 = (bf16[8,16,256]{2,1,0:T(8,128)(2,1)S(1)}, bf16[8,16,256]{2,1,0:T(8,128)(2,1)S(1)}, u32[]{:S(2)}, u32[]{:S(2)}) collective-permute-start(bf16[8,16,256]{2,1,0:T(8,128)(2,1)S(1)} %get-tuple-element.137), channel_id=1, source_target_pairs={{0,16},{16,0},{1,17},{17,1},{2,18},{18,2},{3,19},{19,3},{4,20},{20... | collective-permute-start | bytes 196616 | tf_op jit(solution)/shard_map/ppermute | solution.py:43
  58.1 19.0 %collective-permute-start.8 = (bf16[8,16,256]{2,1,0:T(8,128)(2,1)S(1)}, bf16[8,16,256]{2,1,0:T(8,128)(2,1)S(1)}, u32[]{:S(2)}, u32[]{:S(2)}) collective-permute-start(bf16[8,16,256]{2,1,0:T(8,128)(2,1)S(1)} %get-tuple-element.136), channel_id=1, source_target_pairs={{0,16},{16,0},{1,17},{17,1},{2,18},{18,2},{3,19},{19,3},{4,20},{20... | collective-permute-start | bytes 196616 | tf_op jit(solution)/shard_map/ppermute | solution.py:43
  92.1 14.9 %collective-permute-start.13 = (bf16[1024,256]{1,0:T(8,128)(2,1)S(1)}, bf16[1024,256]{1,0:T(8,128)(2,1)S(1)}, u32[]{:S(2)}, u32[]{:S(2)}) collective-permute-start(bf16[1024,256]{1,0:T(8,128)(2,1)S(1)} %act_two.2.refs_0_), channel_id=1, source_target_pairs={{0,8},{4,12},{8,0},{12,4},{1,9},{5,13},{9,1},{13,5},{2,10},{6,14},... | collective-permute-start | bytes 1572872 | tf_op jit(solution)/shard_map/ppermute | solution.py:43
  94.5 20.3 %collective-permute-start.16 = (bf16[1024,256]{1,0:T(8,128)(2,1)S(1)}, bf16[1024,256]{1,0:T(8,128)(2,1)S(1)}, u32[]{:S(2)}, u32[]{:S(2)}) collective-permute-start(bf16[1024,256]{1,0:T(8,128)(2,1)S(1)} %act_two.3.refs_0_.refs_1_), channel_id=1, source_target_pairs={{0,8},{4,12},{8,0},{12,4},{1,9},{5,13},{9,1},{13,5},{2,10},{6,14},... | collective-permute-start | bytes 1572872 | tf_op jit(solution)/shard_map/ppermute | solution.py:43
  95.1 19.7 %collective-permute-start.12 = (bf16[1024,256]{1,0:T(8,128)(2,1)S(1)}, bf16[1024,256]{1,0:T(8,128)(2,1)S(1)}, u32[]{:S(2)}, u32[]{:S(2)}) collective-permute-start(bf16[1024,256]{1,0:T(8,128)(2,1)S(1)} %act_two.2.refs_0_), channel_id=1, source_target_pairs={{0,4},{4,0},{8,12},{12,8},{1,5},{5,1},{9,13},{13,9},{2,6},{6,2},{1... | collective-permute-start | bytes 1572872 | tf_op jit(solution)/shard_map/ppermute | solution.py:43
  107.0 9.7 %collective-permute-start.15 = (bf16[1024,256]{1,0:T(8,128)(2,1)S(1)}, bf16[1024,256]{1,0:T(8,128)(2,1)S(1)}, u32[]{:S(2)}, u32[]{:S(2)}) collective-permute-start(bf16[1024,256]{1,0:T(8,128)(2,1)S(1)} %act_two.3.refs_0_.refs_1_), channel_id=1, source_target_pairs={{0,4},{4,0},{8,12},{12,8},{1,5},{5,1},{9,13},{13,9},{2,6},{6,2},{1... | collective-permute-start | bytes 1572872 | tf_op jit(solution)/shard_map/ppermute | solution.py:43
  147.3 14.8 %collective-permute-start.19 = (bf16[1024,256]{1,0:T(8,128)(2,1)S(1)}, bf16[1024,256]{1,0:T(8,128)(2,1)S(1)}, u32[]{:S(2)}, u32[]{:S(2)}) collective-permute-start(bf16[1024,256]{1,0:T(8,128)(2,1)S(1)} %get-tuple-element.159), channel_id=1, source_target_pairs={{0,8},{4,12},{8,0},{12,4},{1,9},{5,13},{9,1},{13,5},{2,10},{6,14},... | collective-permute-start | bytes 1572872 | tf_op jit(solution)/shard_map/ppermute | solution.py:43
  151.8 13.7 %collective-permute-start.20 = (bf16[4,128,512]{2,1,0:T(8,128)(2,1)S(1)}, bf16[4,128,512]{2,1,0:T(8,128)(2,1)S(1)}, u32[]{:S(2)}, u32[]{:S(2)}) collective-permute-start(bf16[4,128,512]{2,1,0:T(8,128)(2,1)S(1)} %get-tuple-element.165), channel_id=1, source_target_pairs={{0,16},{16,0},{1,17},{17,1},{2,18},{18,2},{3,19},{19,3},{4,20},{20... | collective-permute-start | bytes 1572872 | tf_op jit(solution)/shard_map/ppermute | solution.py:43
  153.2 19.3 %collective-permute-start.22 = (bf16[1024,256]{1,0:T(8,128)(2,1)S(1)}, bf16[1024,256]{1,0:T(8,128)(2,1)S(1)}, u32[]{:S(2)}, u32[]{:S(2)}) collective-permute-start(bf16[1024,256]{1,0:T(8,128)(2,1)S(1)} %get-tuple-element.171), channel_id=1, source_target_pairs={{0,8},{4,12},{8,0},{12,4},{1,9},{5,13},{9,1},{13,5},{2,10},{6,14},... | collective-permute-start | bytes 1572872 | tf_op jit(solution)/shard_map/ppermute | solution.py:43
  166.2 20.0 %collective-permute-start.30 = (bf16[2,128,512]{2,1,0:T(8,128)(2,1)S(1)}, bf16[2,128,512]{2,1,0:T(8,128)(2,1)S(1)}, u32[]{:S(2)}, u32[]{:S(2)}) collective-permute-start(bf16[2,128,512]{2,1,0:T(8,128)(2,1)S(1)} %get-tuple-element.180), channel_id=1, source_target_pairs={{0,1},{1,0},{2,3},{3,2},{4,5},{5,4},{6,7},{7,6},{8,9},{9,8},{10,11... | collective-permute-start | bytes 786440 | tf_op jit(solution)/shard_map/ppermute | solution.py:43
  166.8 9.7 %collective-permute-start.23 = (bf16[16,16,256]{2,1,0:T(8,128)(2,1)S(1)}, bf16[16,16,256]{2,1,0:T(8,128)(2,1)S(1)}, u32[]{:S(2)}, u32[]{:S(2)}) collective-permute-start(bf16[16,16,256]{2,1,0:T(8,128)(2,1)S(1)} %get-tuple-element.175), channel_id=1, source_target_pairs={{0,16},{16,0},{1,17},{17,1},{2,18},{18,2},{3,19},{19,3},{4,20},{20... | collective-permute-start | bytes 393224 | tf_op jit(solution)/shard_map/ppermute | solution.py:43
  217.1 39.4 %collective-permute-start.45 = (bf16[2048,256]{1,0:T(8,128)(2,1)S(1)}, bf16[2048,256]{1,0:T(8,128)(2,1)S(1)}, u32[]{:S(2)}, u32[]{:S(2)}) collective-permute-start(bf16[2048,256]{1,0:T(8,128)(2,1)S(1)} %grad_reduced.1.refs_4_.refs_0_), channel_id=1, source_target_pairs={{0,8},{4,12},{8,0},{12,4},{1,9},{5,13},{9,1},{13,5},{2,10},{6,14},... | collective-permute-start | bytes 3145736 | tf_op jit(solution)/shard_map/ppermute | solution.py:43
  218.6 11.0 %collective-permute-start.35 = (bf16[4,168,256]{2,1,0:T(8,128)(2,1)S(1)}, bf16[4,168,256]{2,1,0:T(8,128)(2,1)S(1)}, u32[]{:S(2)}, u32[]{:S(2)}) collective-permute-start(bf16[4,168,256]{2,1,0:T(8,128)(2,1)S(1)} %get-tuple-element.205), channel_id=1, source_target_pairs={{0,16},{16,0},{1,17},{17,1},{2,18},{18,2},{3,19},{19,3},{4,20},{20... | collective-permute-start | bytes 1032200 | tf_op jit(solution)/shard_map/ppermute | solution.py:43
  219.2 14.6 %collective-permute-start.36 = (bf16[4,128,256]{2,1,0:T(8,128)(2,1)S(1)}, bf16[4,128,256]{2,1,0:T(8,128)(2,1)S(1)}, u32[]{:S(2)}, u32[]{:S(2)}) collective-permute-start(bf16[4,128,256]{2,1,0:T(8,128)(2,1)S(1)} %get-tuple-element.208), channel_id=1, source_target_pairs={{0,16},{16,0},{1,17},{17,1},{2,18},{18,2},{3,19},{19,3},{4,20},{20... | collective-permute-start | bytes 786440 | tf_op jit(solution)/shard_map/ppermute | solution.py:43
  220.6 13.7 %collective-permute-start.37 = (bf16[1,128,512]{2,1,0:T(8,128)(2,1)S(1)}, bf16[1,128,512]{2,1,0:T(8,128)(2,1)S(1)}, u32[]{:S(2)}, u32[]{:S(2)}) collective-permute-start(bf16[1,128,512]{2,1,0:T(8,128)(2,1)S(1)} %bitcast.31), channel_id=1, source_target_pairs={{0,2},{1,3},{2,0},{3,1},{4,6},{5,7},{6,4},{7,5},{8,10},{9,11},{10,... | collective-permute-start | bytes 393224 | tf_op jit(solution)/shard_map/ppermute | solution.py:43
  234.9 16.3 %collective-permute-start.40 = (bf16[2,128,512]{2,1,0:T(8,128)(2,1)S(1)}, bf16[2,128,512]{2,1,0:T(8,128)(2,1)S(1)}, u32[]{:S(2)}, u32[]{:S(2)}) collective-permute-start(bf16[2,128,512]{2,1,0:T(8,128)(2,1)S(1)} %join.8.refs_0_), channel_id=1, source_target_pairs={{0,1},{1,0},{2,3},{3,2},{4,5},{5,4},{6,7},{7,6},{8,9},{9,8},{10,11... | collective-permute-start | bytes 786440 | tf_op jit(solution)/shard_map/ppermute | solution.py:43
  235.5 11.5 %collective-permute-start.38 = (bf16[2,168,256]{2,1,0:T(8,128)(2,1)S(1)}, bf16[2,168,256]{2,1,0:T(8,128)(2,1)S(1)}, u32[]{:S(2)}, u32[]{:S(2)}) collective-permute-start(bf16[2,168,256]{2,1,0:T(8,128)(2,1)S(1)} %get-tuple-element.212), channel_id=1, source_target_pairs={{0,1},{1,0},{2,3},{3,2},{4,5},{5,4},{6,7},{7,6},{8,9},{9,8},{10,11... | collective-permute-start | bytes 516104 | tf_op jit(solution)/shard_map/ppermute | solution.py:43
  237.0 12.3 %collective-permute-start.39 = (bf16[2,128,256]{2,1,0:T(8,128)(2,1)S(1)}, bf16[2,128,256]{2,1,0:T(8,128)(2,1)S(1)}, u32[]{:S(2)}, u32[]{:S(2)}) collective-permute-start(bf16[2,128,256]{2,1,0:T(8,128)(2,1)S(1)} %get-tuple-element.215), channel_id=1, source_target_pairs={{0,1},{1,0},{2,3},{3,2},{4,5},{5,4},{6,7},{7,6},{8,9},{9,8},{10,11... | collective-permute-start | bytes 393224 | tf_op jit(solution)/shard_map/ppermute | solution.py:43
  256.3 16.1 %collective-permute-start.44 = (bf16[2048,256]{1,0:T(8,128)(2,1)S(1)}, bf16[2048,256]{1,0:T(8,128)(2,1)S(1)}, u32[]{:S(2)}, u32[]{:S(2)}) collective-permute-start(bf16[2048,256]{1,0:T(8,128)(2,1)S(1)} %grad_reduced.1.refs_4_.refs_0_), channel_id=1, source_target_pairs={{0,4},{4,0},{8,12},{12,8},{1,5},{5,1},{9,13},{13,9},{2,6},{6,2},{1... | collective-permute-start | bytes 3145736 | tf_op jit(solution)/shard_map/ppermute | solution.py:43
  256.4 16.0 %collective-permute-start.46 = (bf16[2048,256]{1,0:T(8,128)(2,1)S(1)}, bf16[2048,256]{1,0:T(8,128)(2,1)S(1)}, u32[]{:S(2)}, u32[]{:S(2)}) collective-permute-start(bf16[2048,256]{1,0:T(8,128)(2,1)S(1)} %collective-permute-done.45.refs_2_), channel_id=1, source_target_pairs={{0,4},{4,0},{8,12},{12,8},{1,5},{5,1},{9,13},{13,9},{2,6},{6,2},{1... | collective-permute-start | bytes 3145736 | tf_op jit(solution)/shard_map/ppermute | solution.py:43
  257.6 23.8 %collective-permute-start.51 = (bf16[4,128,512]{2,1,0:T(8,128)(2,1)S(1)}, bf16[4,128,512]{2,1,0:T(8,128)(2,1)S(1)}, u32[]{:S(2)}, u32[]{:S(2)}) collective-permute-start(bf16[4,128,512]{2,1,0:T(8,128)(2,1)S(1)} %join.9.own_ref), channel_id=1, source_target_pairs={{0,16},{16,0},{1,17},{17,1},{2,18},{18,2},{3,19},{19,3},{4,20},{20... | collective-permute-start | bytes 1572872 | tf_op jit(solution)/shard_map/ppermute | solution.py:43
  265.9 14.3 %collective-permute-start.50 = (bf16[2,168,256]{2,1,0:T(8,128)(2,1)S(1)}, bf16[2,168,256]{2,1,0:T(8,128)(2,1)S(1)}, u32[]{:S(2)}, u32[]{:S(2)}) collective-permute-start(bf16[2,168,256]{2,1,0:T(8,128)(2,1)S(1)} %join.10.refs_0_), channel_id=1, source_target_pairs={{0,1},{1,0},{2,3},{3,2},{4,5},{5,4},{6,7},{7,6},{8,9},{9,8},{10,11... | collective-permute-start | bytes 516104 | tf_op jit(solution)/shard_map/ppermute | solution.py:43
  280.8 11.0 %collective-permute-start.53 = (bf16[4,168,256]{2,1,0:T(8,128)(2,1)S(1)}, bf16[4,168,256]{2,1,0:T(8,128)(2,1)S(1)}, u32[]{:S(2)}, u32[]{:S(2)}) collective-permute-start(bf16[4,168,256]{2,1,0:T(8,128)(2,1)S(1)} %join.12.refs_0_), channel_id=1, source_target_pairs={{0,16},{16,0},{1,17},{17,1},{2,18},{18,2},{3,19},{19,3},{4,20},{20... | collective-permute-start | bytes 1032200 | tf_op jit(solution)/shard_map/ppermute | solution.py:43
  285.2 11.0 %collective-permute-start.54 = (bf16[4,128,256]{2,1,0:T(8,128)(2,1)S(1)}, bf16[4,128,256]{2,1,0:T(8,128)(2,1)S(1)}, u32[]{:S(2)}, u32[]{:S(2)}) collective-permute-start(bf16[4,128,256]{2,1,0:T(8,128)(2,1)S(1)} %join.13.refs_2_), channel_id=1, source_target_pairs={{0,16},{16,0},{1,17},{17,1},{2,18},{18,2},{3,19},{19,3},{4,20},{20... | collective-permute-start | bytes 786440 | tf_op jit(solution)/shard_map/ppermute | solution.py:43
  (35 other events, 316.3 us)

commit v5 on v4

--- a/solution.py
+++ b/solution.py
@@ -932,7 +932,8 @@
         matrices_back, group, per_image,
     )
     if staged:
-        places = cut_places(after(info, d_one), expand_pair, chan_size)
+        reduce_back.append(swap(after(rows_back[2], d_two[-1]), 2))
+        places = cut_places(after(info, d_one, reduce_back[2]), expand_pair, chan_size)
         sums = after(sums, places[0])
     grads_one = spread_sums(sums)
 
@@ -965,27 +966,28 @@
         first_half(0)
         first_half(1)
         places = [v if k == 0 else swap(after(v, turn), k) for k, v in enumerate(places)]
+        next_half(0, 1)
+        next_half(1, 1)
         back = in_turn(join, *places)
         back = send_back(back.reshape((1,) + back.shape), EXPAND_STEPS[2])
         far_grads = [swap(after(grad, turn), k) for k in distances]
-        next_half(0, 1)
-        next_half(1, 1)
-        back = send_back(in_turn(join, *back), EXPAND_STEPS[1])
         next_half(0, 2)
         next_half(1, 2)
+        back = send_back(in_turn(join, *back), EXPAND_STEPS[1])
+        grads = [grad, swap(after(grad, turn), 1)]
+        reduce_back += [swap(after(rows_back[k], *far_grads), k) for k in range(3, chan_size)]
+        last_half(0)
         back = send_back(in_turn(join, *back), EXPAND_STEPS[0])
-        last_half(0)
         last_half(1)
-        grads = [grad, swap(after(grad, turn), 1)]
+        back_half(0, 1)
         for value in far_grads:
             grads += [value, swap(after(value, turn), 1)]
-        reduce_back += [swap(after(rows_back[k], turn), k) for k in range(2, chan_size)]
-        back_half(0, 1)
-        grad_input = in_turn(input_grad, grad_field, grads, reduce_back)
         back_half(1, 1)
         back_half(0, 0)
+        turn = after(turn, reduce_back[3])
         grad_expand = in_turn(place_expand, back, chan_size, mid_part)
         back_half(1, 0)
+        grad_input = in_turn(input_grad, grad_field, grads, reduce_back)
         grad_reduce, grad_group = place_reduce(turn, pairs, chan_size, out_part, 9 * group)
     else:
         reduce_back += [swap(rows_back[k], k) for k in range(2, chan_size)]

time: 299 us -> 281 us (0.940)
  waiting for transfers between devices: 132 us -> 115 us
    ppermute x55, waiting for transfers between devices: 132 us -> 115 us  [permute(): return lax.ppermute(value, axis, [(i, i ^ distance) for i in range(count)])]
  transfers between devices with their start and end apart: 55 -> 55, of which waited for: 30 -> 25; matrix products, arithmetic and copies ran while one was open for 1% -> 1% of each run, Pallas kernels for 14% -> 15%
where the time goes in v5:
time: 281 us
  waiting for transfers between devices  115 us (41%)
  Pallas kernels  64.5 us (23%)
  blocking collectives  50.8 us (18%)
  starting transfers between devices  44.2 us (16%)
  local copies, waits for them, and re-layouts  4.18 us (1%)
    ppermute x55, waiting for transfers between devices, permute(): return lax.ppermute(value, axis, [(i, i ^ distance) for i in range(count)])  115 us
    pallas_call x44, Pallas kernels, kernel_call(): pl.pallas_call(body, in_specs=[SMEM if a.dtype == jnp.int32 else VMEM for...  64.5 us
    all_to_all x5, blocking collectives, spread_sums(): return lax.all_to_all(sent, REDUCE_AXES, 0, 0)  50.8 us
    ppermute x55, starting transfers between devices, permute(): return lax.ppermute(value, axis, [(i, i ^ distance) for i in range(count)])  44.2 us
  transfers between devices with their start and end apart: 55, of which 25 were waited for; matrix products, arithmetic and copies ran while one was open for 1% of the time, Pallas kernels for 15%

profile of v5, /device:TPU:0, one launch (start us, length us, event | category | flops | bytes accessed | tf_op | source)
XLA Modules:
  0.0 281.0 jit_solution(11654238810338455338)
XLA Ops:
  2.0 3.0 %collective-permute-start.1 = (bf16[1024,512]{1,0:T(8,128)(2,1)S(1)}, bf16[1024,512]{1,0:T(8,128)(2,1)S(1)}, u32[]{:S(2)}, u32[]{:S(2)}) collective-permute-start(bf16[1024,512]{1,0:T(8,128)(2,1)S(1)} %bitcast.24), channel_id=1, source_target_pairs={{0,8},{4,12},{8,0},{12,4},{1,9},{5,13},{9,1},{13,5},{2,10},{6,14},... | collective-permute-start | bytes 3145736 | tf_op jit(solution)/shard_map/ppermute | solution.py:43
  10.6 18.4 %collective-permute-done.1.refs_2_.refs_0_ = bf16[1024,512]{1,0:T(8,128)(2,1)S(1)} collective-permute-done((bf16[1024,512]{1,0:T(8,128)(2,1)S(1)}, bf16[1024,512]{1,0:T(8,128)(2,1)S(1)}, u32[]{:S(2)}, u32[]{:S(2)}) %collective-permute-start.1) | collective-permute-done | bytes 1048608 | tf_op jit(solution)/shard_map/ppermute | solution.py:43
  30.7 19.9 %collective-permute-done.4.refs_2_.refs_1_ = bf16[1024,512]{1,0:T(8,128)(2,1)S(1)} collective-permute-done((bf16[1024,512]{1,0:T(8,128)(2,1)S(1)}, bf16[1024,512]{1,0:T(8,128)(2,1)S(1)}, u32[]{:S(2)}, u32[]{:S(2)}) %collective-permute-start.4) | collective-permute-done | bytes 1048608 | tf_op jit(solution)/shard_map/ppermute | solution.py:43
  59.7 4.8 %collective-permute-done.11.refs_7_.refs_9_ = bf16[256,512]{1,0:T(8,128)(2,1)S(1)} collective-permute-done((bf16[256,512]{1,0:T(8,128)(2,1)S(1)}, bf16[256,512]{1,0:T(8,128)(2,1)S(1)}, u32[]{:S(2)}, u32[]{:S(2)}) %collective-permute-start.11) | collective-permute-done | bytes 262176 | tf_op jit(solution)/shard_map/ppermute | solution.py:43
  64.6 12.5 %all_to_all.25.refs_4_.refs_11_.refs_3_ = f32[8,2,256]{2,1,0:T(2,128)S(1)} all-to-all(f32[8,2,256]{2,1,0:T(2,128)S(1)} %get-tuple-element.144), channel_id=1, replica_groups=mesh['height'=2,'chan'=4,'batch'=4] {'height','batch'}, dimensions={0} | all-to-all | bytes 32768 | tf_op jit(solution)/shard_map/all_to_all | solution.py:51
  77.1 5.2 %conv_forward.1 = (bf16[16,128,256]{2,1,0:T(8,128)(2,1)S(1)}, f32[16,128,256]{2,1,0:T(8,128)S(1)}, bf16[16,16,256]{2,1,0:T(8,128)(2,1)S(1)}, f32[8,2,256]{2,1,0:T(2,128)S(1)}) custom-call(s32[7]{0:T(128)S(1)} %stack.31.info_ref, f32[8,128,256]{2,1,0:T(8,128)S(1)} %get-tuple-element.129.refs_0_.refs_4_, ...), custom_call_target="tpu_custom_call" | custom-call | tf_op jit(solution)/shard_map/conv_forward/pallas_call | solution.py:24
  82.2 9.0 %all_to_all.26.sums_ref.refs_2_.refs_9_ = f32[8,2,256]{2,1,0:T(2,128)S(1)} all-to-all(f32[8,2,256]{2,1,0:T(2,128)S(1)} %get-tuple-element.147), channel_id=1, replica_groups=mesh['height'=2,'chan'=4,'batch'=4] {'height','batch'}, dimensions={0} | all-to-all | bytes 32768 | tf_op jit(solution)/shard_map/all_to_all | solution.py:51
  95.2 11.9 %collective-permute-done.13.refs_2_.refs_4_ = bf16[1024,256]{1,0:T(8,128)(2,1)S(1)} collective-permute-done((bf16[1024,256]{1,0:T(8,128)(2,1)S(1)}, bf16[1024,256]{1,0:T(8,128)(2,1)S(1)}, u32[]{:S(2)}, u32[]{:S(2)}) %collective-permute-start.13) | collective-permute-done | bytes 524320 | tf_op jit(solution)/shard_map/ppermute | solution.py:43
  107.5 7.3 %collective-permute-done.16.refs_2_.refs_5_ = bf16[1024,256]{1,0:T(8,128)(2,1)S(1)} collective-permute-done((bf16[1024,256]{1,0:T(8,128)(2,1)S(1)}, bf16[1024,256]{1,0:T(8,128)(2,1)S(1)}, u32[]{:S(2)}, u32[]{:S(2)}) %collective-permute-start.16) | collective-permute-done | bytes 524320 | tf_op jit(solution)/shard_map/ppermute | solution.py:43
  118.6 9.1 %all_to_all.27.refs_4_.refs_3_ = f32[8,2,512]{2,1,0:T(2,128)S(1)} all-to-all(f32[8,2,512]{2,1,0:T(2,128)S(1)} %get-tuple-element.152), channel_id=1, replica_groups=mesh['height'=2,'chan'=4,'batch'=4] {'height','batch'}, dimensions={0} | all-to-all | bytes 65536 | tf_op jit(solution)/shard_map/all_to_all | solution.py:51
  127.7 5.1 %output.1 = (bf16[16,128,512]{2,1,0:T(8,128)(2,1)}, f32[16,128,512]{2,1,0:T(8,128)S(1)}, f32[8,2,512]{2,1,0:T(2,128)S(1)}) custom-call(s32[7]{0:T(128)S(1)} %stack.31.info_ref, f32[8,128,512]{2,1,0:T(8,128)S(1)} %get-tuple-element.149.refs_0_, f32[8,128,512]{2,1,0:T(8,128)S(1)} %get-tuple-element.151.refs_1_, bf16[16,128,512]{2,1,0:T(8,128)(2,1)S(1)} %bitcast.29, ...), custom_call_target="tpu_custom_call" | custom-call | tf_op jit(solution)/shard_map/output/pallas_call | solution.py:24
  132.8 9.1 %all_to_all.28.refs_4_.refs_2_ = f32[8,2,512]{2,1,0:T(2,128)S(1)} all-to-all(f32[8,2,512]{2,1,0:T(2,128)S(1)} %get-tuple-element.156), channel_id=1, replica_groups=mesh['height'=2,'chan'=4,'batch'=4] {'height','batch'}, dimensions={0} | all-to-all | bytes 65536 | tf_op jit(solution)/shard_map/all_to_all | solution.py:51
  148.8 3.0 %expand_grad.1 = (f32[4,128,512]{2,1,0:T(8,128)S(1)}, bf16[4,128,512]{2,1,0:T(8,128)(2,1)S(1)}) custom-call(s32[7]{0:T(128)S(1)} %stack.31.info_ref, bf16[1024,256]{1,0:T(8,128)(2,1)S(1)} %act_two.2.refs_0_, bf16[1024,256]{1,0:T(8,128)(2,1)S(1)} %act_two.3.refs_0_.refs_1_, bf16[1024,256]{1,0:T(8,128)(2,1)S(1)} %collective-permute-done.12.refs_1_.refs_2_, ...), custom_call_target="tpu_custom_call" | custom-call | tf_op jit(solution)/shard_map/expand_grad/pallas_call | solution.py:24
  153.8 8.3 %collective-permute-done.19.refs_0_ = bf16[1024,256]{1,0:T(8,128)(2,1)S(1)} collective-permute-done((bf16[1024,256]{1,0:T(8,128)(2,1)S(1)}, bf16[1024,256]{1,0:T(8,128)(2,1)S(1)}, u32[]{:S(2)}, u32[]{:S(2)}) %collective-permute-start.19) | collective-permute-done | bytes 524320 | tf_op jit(solution)/shard_map/ppermute | solution.py:43
  163.4 2.2 collective-permute-done.20.arrived_ref
  167.3 5.2 %collective-permute-done.22.refs_0_ = bf16[1024,256]{1,0:T(8,128)(2,1)S(1)} collective-permute-done((bf16[1024,256]{1,0:T(8,128)(2,1)S(1)}, bf16[1024,256]{1,0:T(8,128)(2,1)S(1)}, u32[]{:S(2)}, u32[]{:S(2)}) %collective-permute-start.22) | collective-permute-done | bytes 524320 | tf_op jit(solution)/shard_map/ppermute | solution.py:43
  182.3 3.3 %collective-permute-start.29 = (f32[2,256]{1,0:T(2,128)S(1)}, f32[2,256]{1,0:T(2,128)S(1)}, u32[]{:S(2)}, u32[]{:S(2)}) collective-permute-start(f32[2,256]{1,0:T(2,128)S(1)} %add_rows.1.refs_0_), channel_id=1, source_target_pairs={{0,3},{1,2},{2,1},{3,0},{4,7},{5,6},{6,5},{7,4},{8,11},{9,10},{10,... | collective-permute-start | bytes 6152 | tf_op jit(solution)/shard_map/ppermute | solution.py:43
  188.9 8.3 %conv_backward.1 = (f32[16,128,256]{2,1,0:T(8,128)S(1)}, f32[8,2,256]{2,1,0:T(2,128)S(1)}, f32[9,32,256]{2,1,0:T(8,128)S(1)}) custom-call(s32[7]{0:T(128)S(1)} %stack.31.info_ref, f32[8,128,256]{2,1,0:T(8,128)S(1)} %get-tuple-element.161.refs_0_, f32[8,128,256]{2,1,0:T(8,128)S(1)} %get-tuple-element.184.refs_1_, ...), custom_call_target="tpu_custom_call" | custom-call | tf_op jit(solution)/shard_map/conv_backward/pallas_call | solution.py:24
  197.9 11.2 %all_to_all.29.refs_4_.refs_0_ = f32[8,2,256]{2,1,0:T(2,128)S(1)} all-to-all(f32[8,2,256]{2,1,0:T(2,128)S(1)} %get-tuple-element.194), channel_id=1, replica_groups=mesh['height'=2,'chan'=4,'batch'=4] {'height','batch'}, dimensions={0} | all-to-all | bytes 32768 | tf_op jit(solution)/shard_map/all_to_all | solution.py:51
  210.1 1.9 reduce_grad.2
  220.1 2.2 collective-permute-done.34.arrived_ref
  226.6 5.6 %collective-permute-done.38.arrived_ref = bf16[2,168,256]{2,1,0:T(8,128)(2,1)S(1)} collective-permute-done((bf16[2,168,256]{2,1,0:T(8,128)(2,1)S(1)}, bf16[2,168,256]{2,1,0:T(8,128)(2,1)S(1)}, u32[]{:S(2)}, u32[]{:S(2)}) %collective-permute-start.38) | collective-permute-done | bytes 172064 | tf_op jit(solution)/shard_map/ppermute | solution.py:43
  235.9 4.7 %collective-permute-done.41.second_ref = bf16[1,168,256]{2,1,0:T(8,128)(2,1)S(1)} collective-permute-done((bf16[1,168,256]{2,1,0:T(8,128)(2,1)S(1)}, bf16[1,168,256]{2,1,0:T(8,128)(2,1)S(1)}, u32[]{:S(2)}, u32[]{:S(2)}) %collective-permute-start.41) | collective-permute-done | bytes 86048 | tf_op jit(solution)/shard_map/ppermute | solution.py:43
  241.2 2.8 collective-permute-start.44
  244.7 5.3 %collective-permute-done.43.second_ref = bf16[1,128,256]{2,1,0:T(8,128)(2,1)S(1)} collective-permute-done((bf16[1,128,256]{2,1,0:T(8,128)(2,1)S(1)}, bf16[1,128,256]{2,1,0:T(8,128)(2,1)S(1)}, u32[]{:S(2)}, u32[]{:S(2)}) %collective-permute-start.43) | collective-permute-done | bytes 65568 | tf_op jit(solution)/shard_map/ppermute | solution.py:43
  253.1 3.9 %collective-permute-done.45.refs_1_ = bf16[1,128,256]{2,1,0:T(8,128)(2,1)S(1)} collective-permute-done((bf16[1,128,256]{2,1,0:T(8,128)(2,1)S(1)}, bf16[1,128,256]{2,1,0:T(8,128)(2,1)S(1)}, u32[]{:S(2)}, u32[]{:S(2)}) %collective-permute-start.45) | collective-permute-done | bytes 65568 | tf_op jit(solution)/shard_map/ppermute | solution.py:43
  257.0 2.3 collective-permute-start.46
  259.9 3.0 %collective-permute-done.46.refs_1_ = bf16[2,168,256]{2,1,0:T(8,128)(2,1)S(1)} collective-permute-done((bf16[2,168,256]{2,1,0:T(8,128)(2,1)S(1)}, bf16[2,168,256]{2,1,0:T(8,128)(2,1)S(1)}, u32[]{:S(2)}, u32[]{:S(2)}) %collective-permute-start.46) | collective-permute-done | bytes 172064 | tf_op jit(solution)/shard_map/ppermute | solution.py:43
  266.8 2.0 place_expand.1
  270.6 4.8 %input_grad.1 = bf16[2048,512]{1,0:T(8,128)(2,1)} custom-call(s32[7]{0:T(128)S(1)} %stack.31.info_ref, f32[2048,512]{1,0:T(8,128)S(1)} %bitcast.23, bf16[2048,256]{1,0:T(8,128)(2,1)S(1)} %grad_reduced.1.refs_4_.refs_0_, bf16[2048,256]{1,0:T(8,128)(2,1)S(1)} %collective-permute-done.51.refs_1_, bf16[2048,256]{1,0:T(8,128)(2,1)S(1)} %collective-permute-done.47.refs_2_, ...), custom_call_target="tpu_custom_call" | custom-call | tf_op jit(solution)/shard_map/input_grad/pallas_call | solution.py:24
  275.9 3.0 %collective-permute-done.54.refs_3_ = bf16[4,128,256]{2,1,0:T(8,128)(2,1)S(1)} collective-permute-done((bf16[4,128,256]{2,1,0:T(8,128)(2,1)S(1)}, bf16[4,128,256]{2,1,0:T(8,128)(2,1)S(1)}, u32[]{:S(2)}, u32[]{:S(2)}) %collective-permute-start.54) | collective-permute-done | bytes 262176 | tf_op jit(solution)/shard_map/ppermute | solution.py:43
  278.8 2.2 place_reduce.1
  (161 shorter events, 79.3 us)
Async XLA Ops:
  2.0 27.0 %collective-permute-start.1 = (bf16[1024,512]{1,0:T(8,128)(2,1)S(1)}, bf16[1024,512]{1,0:T(8,128)(2,1)S(1)}, u32[]{:S(2)}, u32[]{:S(2)}) collective-permute-start(bf16[1024,512]{1,0:T(8,128)(2,1)S(1)} %bitcast.24), channel_id=1, source_target_pairs={{0,8},{4,12},{8,0},{12,4},{1,9},{5,13},{9,1},{13,5},{2,10},{6,14},... | collective-permute-start | bytes 3145736 | tf_op jit(solution)/shard_map/ppermute | solution.py:43
  8.5 42.2 %collective-permute-start.4 = (bf16[1024,512]{1,0:T(8,128)(2,1)S(1)}, bf16[1024,512]{1,0:T(8,128)(2,1)S(1)}, u32[]{:S(2)}, u32[]{:S(2)}) collective-permute-start(bf16[1024,512]{1,0:T(8,128)(2,1)S(1)} %slice.11.refs_0_.refs_1_), channel_id=1, source_target_pairs={{0,8},{4,12},{8,0},{12,4},{1,9},{5,13},{9,1},{13,5},{2,10},{6,14},... | collective-permute-start | bytes 3145736 | tf_op jit(solution)/shard_map/ppermute | solution.py:43
  9.2 20.9 %collective-permute-start.5 = (bf16[256,512]{1,0:T(8,128)(2,1)S(1)}, bf16[256,512]{1,0:T(8,128)(2,1)S(1)}, u32[]{:S(2)}, u32[]{:S(2)}) collective-permute-start(bf16[256,512]{1,0:T(8,128)(2,1)S(1)} %get-tuple-element.132), channel_id=1, source_target_pairs={{0,4},{4,0},{8,12},{12,8},{1,5},{5,1},{9,13},{13,9},{2,6},{6,2},{1... | collective-permute-start | bytes 786440 | tf_op jit(solution)/shard_map/ppermute | solution.py:43
  9.9 20.8 %collective-permute-start.6 = (bf16[512,256]{1,0:T(8,128)(2,1)S(1)}, bf16[512,256]{1,0:T(8,128)(2,1)S(1)}, u32[]{:S(2)}, u32[]{:S(2)}) collective-permute-start(bf16[512,256]{1,0:T(8,128)(2,1)S(1)} %get-tuple-element.133), channel_id=1, source_target_pairs={{0,4},{4,0},{8,12},{12,8},{1,5},{5,1},{9,13},{13,9},{2,6},{6,2},{1... | collective-permute-start | bytes 786440 | tf_op jit(solution)/shard_map/ppermute | solution.py:43
  10.5 41.9 %collective-permute-start = (bf16[1024,512]{1,0:T(8,128)(2,1)S(1)}, bf16[1024,512]{1,0:T(8,128)(2,1)S(1)}, u32[]{:S(2)}, u32[]{:S(2)}) collective-permute-start(bf16[1024,512]{1,0:T(8,128)(2,1)S(1)} %bitcast.25), channel_id=1, source_target_pairs={{0,4},{4,0},{8,12},{12,8},{1,5},{5,1},{9,13},{13,9},{2,6},{6,2},{1... | collective-permute-start | bytes 3145736 | tf_op jit(solution)/shard_map/ppermute | solution.py:43
  29.0 23.5 %collective-permute-start.2 = (bf16[1024,512]{1,0:T(8,128)(2,1)S(1)}, bf16[1024,512]{1,0:T(8,128)(2,1)S(1)}, u32[]{:S(2)}, u32[]{:S(2)}) collective-permute-start(bf16[1024,512]{1,0:T(8,128)(2,1)S(1)} %collective-permute-done.1.refs_2_.refs_0_), channel_id=1, source_target_pairs={{0,4},{4,0},{8,12},{12,8},{1,5},{5,1},{9,13},{13,9},{2,6},{6,2},{1... | collective-permute-start | bytes 3145736 | tf_op jit(solution)/shard_map/ppermute | solution.py:43
  30.1 24.3 %collective-permute-start.3 = (bf16[1024,512]{1,0:T(8,128)(2,1)S(1)}, bf16[1024,512]{1,0:T(8,128)(2,1)S(1)}, u32[]{:S(2)}, u32[]{:S(2)}) collective-permute-start(bf16[1024,512]{1,0:T(8,128)(2,1)S(1)} %slice.11.refs_0_.refs_1_), channel_id=1, source_target_pairs={{0,4},{4,0},{8,12},{12,8},{1,5},{5,1},{9,13},{13,9},{2,6},{6,2},{1... | collective-permute-start | bytes 3145736 | tf_op jit(solution)/shard_map/ppermute | solution.py:43
  50.6 9.1 %collective-permute-start.10 = (bf16[256,512]{1,0:T(8,128)(2,1)S(1)}, bf16[256,512]{1,0:T(8,128)(2,1)S(1)}, u32[]{:S(2)}, u32[]{:S(2)}) collective-permute-start(bf16[256,512]{1,0:T(8,128)(2,1)S(1)} %get-tuple-element.141), channel_id=1, source_target_pairs={{0,8},{4,12},{8,0},{12,4},{1,9},{5,13},{9,1},{13,5},{2,10},{6,14},... | collective-permute-start | bytes 786440 | tf_op jit(solution)/shard_map/ppermute | solution.py:43
  52.4 12.2 %collective-permute-start.11 = (bf16[256,512]{1,0:T(8,128)(2,1)S(1)}, bf16[256,512]{1,0:T(8,128)(2,1)S(1)}, u32[]{:S(2)}, u32[]{:S(2)}) collective-permute-start(bf16[256,512]{1,0:T(8,128)(2,1)S(1)} %get-tuple-element.143), channel_id=1, source_target_pairs={{0,12},{4,8},{8,4},{12,0},{1,13},{5,9},{9,5},{13,1},{2,14},{6,10},... | collective-permute-start | bytes 786440 | tf_op jit(solution)/shard_map/ppermute | solution.py:43
  56.3 20.8 %collective-permute-start.9 = (bf16[8,16,256]{2,1,0:T(8,128)(2,1)S(1)}, bf16[8,16,256]{2,1,0:T(8,128)(2,1)S(1)}, u32[]{:S(2)}, u32[]{:S(2)}) collective-permute-start(bf16[8,16,256]{2,1,0:T(8,128)(2,1)S(1)} %get-tuple-element.138), channel_id=1, source_target_pairs={{0,16},{16,0},{1,17},{17,1},{2,18},{18,2},{3,19},{19,3},{4,20},{20... | collective-permute-start | bytes 196616 | tf_op jit(solution)/shard_map/ppermute | solution.py:43
  58.1 19.0 %collective-permute-start.8 = (bf16[8,16,256]{2,1,0:T(8,128)(2,1)S(1)}, bf16[8,16,256]{2,1,0:T(8,128)(2,1)S(1)}, u32[]{:S(2)}, u32[]{:S(2)}) collective-permute-start(bf16[8,16,256]{2,1,0:T(8,128)(2,1)S(1)} %get-tuple-element.137), channel_id=1, source_target_pairs={{0,16},{16,0},{1,17},{17,1},{2,18},{18,2},{3,19},{19,3},{4,20},{20... | collective-permute-start | bytes 196616 | tf_op jit(solution)/shard_map/ppermute | solution.py:43
  92.1 14.9 %collective-permute-start.13 = (bf16[1024,256]{1,0:T(8,128)(2,1)S(1)}, bf16[1024,256]{1,0:T(8,128)(2,1)S(1)}, u32[]{:S(2)}, u32[]{:S(2)}) collective-permute-start(bf16[1024,256]{1,0:T(8,128)(2,1)S(1)} %act_two.2.refs_0_), channel_id=1, source_target_pairs={{0,8},{4,12},{8,0},{12,4},{1,9},{5,13},{9,1},{13,5},{2,10},{6,14},... | collective-permute-start | bytes 1572872 | tf_op jit(solution)/shard_map/ppermute | solution.py:43
  94.5 20.3 %collective-permute-start.16 = (bf16[1024,256]{1,0:T(8,128)(2,1)S(1)}, bf16[1024,256]{1,0:T(8,128)(2,1)S(1)}, u32[]{:S(2)}, u32[]{:S(2)}) collective-permute-start(bf16[1024,256]{1,0:T(8,128)(2,1)S(1)} %act_two.3.refs_0_.refs_1_), channel_id=1, source_target_pairs={{0,8},{4,12},{8,0},{12,4},{1,9},{5,13},{9,1},{13,5},{2,10},{6,14},... | collective-permute-start | bytes 1572872 | tf_op jit(solution)/shard_map/ppermute | solution.py:43
  95.1 19.7 %collective-permute-start.12 = (bf16[1024,256]{1,0:T(8,128)(2,1)S(1)}, bf16[1024,256]{1,0:T(8,128)(2,1)S(1)}, u32[]{:S(2)}, u32[]{:S(2)}) collective-permute-start(bf16[1024,256]{1,0:T(8,128)(2,1)S(1)} %act_two.2.refs_0_), channel_id=1, source_target_pairs={{0,4},{4,0},{8,12},{12,8},{1,5},{5,1},{9,13},{13,9},{2,6},{6,2},{1... | collective-permute-start | bytes 1572872 | tf_op jit(solution)/shard_map/ppermute | solution.py:43
  107.0 9.7 %collective-permute-start.15 = (bf16[1024,256]{1,0:T(8,128)(2,1)S(1)}, bf16[1024,256]{1,0:T(8,128)(2,1)S(1)}, u32[]{:S(2)}, u32[]{:S(2)}) collective-permute-start(bf16[1024,256]{1,0:T(8,128)(2,1)S(1)} %act_two.3.refs_0_.refs_1_), channel_id=1, source_target_pairs={{0,4},{4,0},{8,12},{12,8},{1,5},{5,1},{9,13},{13,9},{2,6},{6,2},{1... | collective-permute-start | bytes 1572872 | tf_op jit(solution)/shard_map/ppermute | solution.py:43
  147.3 14.8 %collective-permute-start.19 = (bf16[1024,256]{1,0:T(8,128)(2,1)S(1)}, bf16[1024,256]{1,0:T(8,128)(2,1)S(1)}, u32[]{:S(2)}, u32[]{:S(2)}) collective-permute-start(bf16[1024,256]{1,0:T(8,128)(2,1)S(1)} %get-tuple-element.160), channel_id=1, source_target_pairs={{0,8},{4,12},{8,0},{12,4},{1,9},{5,13},{9,1},{13,5},{2,10},{6,14},... | collective-permute-start | bytes 1572872 | tf_op jit(solution)/shard_map/ppermute | solution.py:43
  151.8 13.7 %collective-permute-start.20 = (bf16[4,128,512]{2,1,0:T(8,128)(2,1)S(1)}, bf16[4,128,512]{2,1,0:T(8,128)(2,1)S(1)}, u32[]{:S(2)}, u32[]{:S(2)}) collective-permute-start(bf16[4,128,512]{2,1,0:T(8,128)(2,1)S(1)} %get-tuple-element.166), channel_id=1, source_target_pairs={{0,16},{16,0},{1,17},{17,1},{2,18},{18,2},{3,19},{19,3},{4,20},{20... | collective-permute-start | bytes 1572872 | tf_op jit(solution)/shard_map/ppermute | solution.py:43
  153.2 19.3 %collective-permute-start.22 = (bf16[1024,256]{1,0:T(8,128)(2,1)S(1)}, bf16[1024,256]{1,0:T(8,128)(2,1)S(1)}, u32[]{:S(2)}, u32[]{:S(2)}) collective-permute-start(bf16[1024,256]{1,0:T(8,128)(2,1)S(1)} %get-tuple-element.172), channel_id=1, source_target_pairs={{0,8},{4,12},{8,0},{12,4},{1,9},{5,13},{9,1},{13,5},{2,10},{6,14},... | collective-permute-start | bytes 1572872 | tf_op jit(solution)/shard_map/ppermute | solution.py:43
  166.2 21.5 %collective-permute-start.30 = (bf16[2,128,512]{2,1,0:T(8,128)(2,1)S(1)}, bf16[2,128,512]{2,1,0:T(8,128)(2,1)S(1)}, u32[]{:S(2)}, u32[]{:S(2)}) collective-permute-start(bf16[2,128,512]{2,1,0:T(8,128)(2,1)S(1)} %get-tuple-element.181), channel_id=1, source_target_pairs={{0,1},{1,0},{2,3},{3,2},{4,5},{5,4},{6,7},{7,6},{8,9},{9,8},{10,11... | collective-permute-start | bytes 786440 | tf_op jit(solution)/shard_map/ppermute | solution.py:43
  166.8 10.7 %collective-permute-start.23 = (bf16[16,16,256]{2,1,0:T(8,128)(2,1)S(1)}, bf16[16,16,256]{2,1,0:T(8,128)(2,1)S(1)}, u32[]{:S(2)}, u32[]{:S(2)}) collective-permute-start(bf16[16,16,256]{2,1,0:T(8,128)(2,1)S(1)} %get-tuple-element.176), channel_id=1, source_target_pairs={{0,16},{16,0},{1,17},{17,1},{2,18},{18,2},{3,19},{19,3},{4,20},{20... | collective-permute-start | bytes 393224 | tf_op jit(solution)/shard_map/ppermute | solution.py:43
  173.9 23.4 %collective-permute-start.31 = (bf16[512,256]{1,0:T(8,128)(2,1)S(1)}, bf16[512,256]{1,0:T(8,128)(2,1)S(1)}, u32[]{:S(2)}, u32[]{:S(2)}) collective-permute-start(bf16[512,256]{1,0:T(8,128)(2,1)S(1)} %get-tuple-element.190), channel_id=1, source_target_pairs={{0,8},{4,12},{8,0},{12,4},{1,9},{5,13},{9,1},{13,5},{2,10},{6,14},... | collective-permute-start | bytes 786440 | tf_op jit(solution)/shard_map/ppermute | solution.py:43
  188.3 9.0 %collective-permute-start.32 = (bf16[1,128,512]{2,1,0:T(8,128)(2,1)S(1)}, bf16[1,128,512]{2,1,0:T(8,128)(2,1)S(1)}, u32[]{:S(2)}, u32[]{:S(2)}) collective-permute-start(bf16[1,128,512]{2,1,0:T(8,128)(2,1)S(1)} %get-tuple-element.192), channel_id=1, source_target_pairs={{0,2},{1,3},{2,0},{3,1},{4,6},{5,7},{6,4},{7,5},{8,10},{9,11},{10,... | collective-permute-start | bytes 393224 | tf_op jit(solution)/shard_map/ppermute | solution.py:43
  223.5 27.7 %collective-permute-start.47 = (bf16[2048,256]{1,0:T(8,128)(2,1)S(1)}, bf16[2048,256]{1,0:T(8,128)(2,1)S(1)}, u32[]{:S(2)}, u32[]{:S(2)}) collective-permute-start(bf16[2048,256]{1,0:T(8,128)(2,1)S(1)} %grad_reduced.1.refs_4_.refs_0_), channel_id=1, source_target_pairs={{0,8},{4,12},{8,0},{12,4},{1,9},{5,13},{9,1},{13,5},{2,10},{6,14},... | collective-permute-start | bytes 3145736 | tf_op jit(solution)/shard_map/ppermute | solution.py:43
  224.6 8.9 %collective-permute-start.39 = (bf16[2,128,256]{2,1,0:T(8,128)(2,1)S(1)}, bf16[2,128,256]{2,1,0:T(8,128)(2,1)S(1)}, u32[]{:S(2)}, u32[]{:S(2)}) collective-permute-start(bf16[2,128,256]{2,1,0:T(8,128)(2,1)S(1)} %get-tuple-element.217), channel_id=1, source_target_pairs={{0,1},{1,0},{2,3},{3,2},{4,5},{5,4},{6,7},{7,6},{8,9},{9,8},{10,11... | collective-permute-start | bytes 393224 | tf_op jit(solution)/shard_map/ppermute | solution.py:43
  234.7 9.5 %collective-permute-start.42 = (bf16[2,128,512]{2,1,0:T(8,128)(2,1)S(1)}, bf16[2,128,512]{2,1,0:T(8,128)(2,1)S(1)}, u32[]{:S(2)}, u32[]{:S(2)}) collective-permute-start(bf16[2,128,512]{2,1,0:T(8,128)(2,1)S(1)} %join.8.refs_0_), channel_id=1, source_target_pairs={{0,1},{1,0},{2,3},{3,2},{4,5},{5,4},{6,7},{7,6},{8,9},{9,8},{10,11... | collective-permute-start | bytes 786440 | tf_op jit(solution)/shard_map/ppermute | solution.py:43
  241.2 9.4 %collective-permute-start.44 = (bf16[1,168,256]{2,1,0:T(8,128)(2,1)S(1)}, bf16[1,168,256]{2,1,0:T(8,128)(2,1)S(1)}, u32[]{:S(2)}, u32[]{:S(2)}) collective-permute-start(bf16[1,168,256]{2,1,0:T(8,128)(2,1)S(1)} %add_last.2.refs_0_), channel_id=1, source_target_pairs={{0,2},{1,3},{2,0},{3,1},{4,6},{5,7},{6,4},{7,5},{8,10},{9,11},{10,... | collective-permute-start | bytes 258056 | tf_op jit(solution)/shard_map/ppermute | solution.py:43
  244.2 26.5 %collective-permute-start.51 = (bf16[2048,256]{1,0:T(8,128)(2,1)S(1)}, bf16[2048,256]{1,0:T(8,128)(2,1)S(1)}, u32[]{:S(2)}, u32[]{:S(2)}) collective-permute-start(bf16[2048,256]{1,0:T(8,128)(2,1)S(1)} %grad_reduced.1.refs_4_.refs_0_), channel_id=1, source_target_pairs={{0,4},{4,0},{8,12},{12,8},{1,5},{5,1},{9,13},{13,9},{2,6},{6,2},{1... | collective-permute-start | bytes 3145736 | tf_op jit(solution)/shard_map/ppermute | solution.py:43
  251.2 19.5 %collective-permute-start.52 = (bf16[2048,256]{1,0:T(8,128)(2,1)S(1)}, bf16[2048,256]{1,0:T(8,128)(2,1)S(1)}, u32[]{:S(2)}, u32[]{:S(2)}) collective-permute-start(bf16[2048,256]{1,0:T(8,128)(2,1)S(1)} %collective-permute-done.47.refs_2_), channel_id=1, source_target_pairs={{0,4},{4,0},{8,12},{12,8},{1,5},{5,1},{9,13},{13,9},{2,6},{6,2},{1... | collective-permute-start | bytes 3145736 | tf_op jit(solution)/shard_map/ppermute | solution.py:43
  251.3 15.6 %collective-permute-start.49 = (bf16[4,128,512]{2,1,0:T(8,128)(2,1)S(1)}, bf16[4,128,512]{2,1,0:T(8,128)(2,1)S(1)}, u32[]{:S(2)}, u32[]{:S(2)}) collective-permute-start(bf16[4,128,512]{2,1,0:T(8,128)(2,1)S(1)} %join.9.own_ref), channel_id=1, source_target_pairs={{0,16},{16,0},{1,17},{17,1},{2,18},{18,2},{3,19},{19,3},{4,20},{20... | collective-permute-start | bytes 1572872 | tf_op jit(solution)/shard_map/ppermute | solution.py:43
  251.9 13.4 %collective-permute-start.48 = (bf16[512,256]{1,0:T(8,128)(2,1)S(1)}, bf16[512,256]{1,0:T(8,128)(2,1)S(1)}, u32[]{:S(2)}, u32[]{:S(2)}) collective-permute-start(bf16[512,256]{1,0:T(8,128)(2,1)S(1)} %get-tuple-element.231), channel_id=1, source_target_pairs={{0,12},{4,8},{8,4},{12,0},{1,13},{5,9},{9,5},{13,1},{2,14},{6,10},... | collective-permute-start | bytes 786440 | tf_op jit(solution)/shard_map/ppermute | solution.py:43
  265.3 10.6 %collective-permute-start.53 = (bf16[4,168,256]{2,1,0:T(8,128)(2,1)S(1)}, bf16[4,168,256]{2,1,0:T(8,128)(2,1)S(1)}, u32[]{:S(2)}, u32[]{:S(2)}) collective-permute-start(bf16[4,168,256]{2,1,0:T(8,128)(2,1)S(1)} %join.12.refs_0_), channel_id=1, source_target_pairs={{0,16},{16,0},{1,17},{17,1},{2,18},{18,2},{3,19},{19,3},{4,20},{20... | collective-permute-start | bytes 1032200 | tf_op jit(solution)/shard_map/ppermute | solution.py:43
  269.4 9.4 %collective-permute-start.54 = (bf16[4,128,256]{2,1,0:T(8,128)(2,1)S(1)}, bf16[4,128,256]{2,1,0:T(8,128)(2,1)S(1)}, u32[]{:S(2)}, u32[]{:S(2)}) collective-permute-start(bf16[4,128,256]{2,1,0:T(8,128)(2,1)S(1)} %join.13.refs_2_), channel_id=1, source_target_pairs={{0,16},{16,0},{1,17},{17,1},{2,18},{18,2},{3,19},{19,3},{4,20},{20... | collective-permute-start | bytes 786440 | tf_op jit(solution)/shard_map/ppermute | solution.py:43
  (35 other events, 320.6 us)

commit v6 on v4

--- a/solution.py
+++ b/solution.py
@@ -8,6 +8,11 @@
 from jax.sharding import PartitionSpec as P
 
 EPSILON = 1e-05
+STAGE_COST = 1_500_000_000
+LAST_PHASE = (
+    "wz", "wr", "a0", "t", "b0", "c", "a1", "b1", "e0", "x", "a2", "b2", "e1", "o", "a3", "e2", "b3", "a4",
+    "d", "b4", "we", "a5", "wa", "b5", "i", "p",
+)
 F32, BF16 = jnp.float32, jnp.bfloat16
 REDUCE_AXES = ("height", "batch")
 REDUCE_CHUNKS, EXPAND_CHUNKS, BACK_CHUNKS = (8, 8), (8, 8), (8, 8)
@@ -227,29 +232,32 @@
         pre = (v - average) * scale + bias
         return pre * sigmoid(pre) * keep
 
-    def fill(refs, at, image, nothing):
+    def fill(image):
         keep = (image < info_ref[OWN_COUNT]).astype(F32)
-        own = activate(refs[0][at], keep)
-        edge = activate(refs[1][at].astype(F32), keep)
+        own = activate(at_image([f[0] for f in fields], image), keep)
+        edge = activate(at_image([f[1] for f in fields], image).astype(F32), keep)
         act_ref[image] = own.astype(BF16)
         fill_windows(window_ref, image, with_edges(info_ref, own, edge), cols)
-        return nothing
-
-    def convolve(step, sums):
-        first = step * group_images
+
+    def convolve(first):
         total = None
         for i in range(3):
-            piece = window_ref[pl.ds(first, group_images), i * cols : i * cols + pixels, :]
+            piece = window_ref[first : first + group_images, i * cols : i * cols + pixels, :]
             term = dot(piece.reshape(group_images * pixels, 3 * chans), mat_ref[i], 1, 0)
             total = term if total is None else total + term
-        out_ref[pl.ds(first, group_images)] = total.reshape(group_images, pixels, chans)
-        for i in range(group_images):
-            out_edge_ref[first + i] = edge_rows(info_ref, out_ref, first + i, cols).astype(BF16)
-        return sums[0] + fold(total), sums[1] + fold(total * total)
-
-    each_image(fields, fill, 0)
-    zero = jnp.zeros((8, chans), F32)
-    put_sums(sums_ref, *lax.fori_loop(0, images // group_images, convolve, (zero, zero)))
+        out_ref[first : first + group_images] = total.reshape(group_images, pixels, chans)
+        return fold(total), fold(total * total)
+
+    one = two = jnp.zeros((8, chans), F32)
+    for first in range(0, images + group_images, group_images):
+        for image in range(first, min(first + group_images, images)):
+            fill(image)
+        if first:
+            more = convolve(first - group_images)
+            one, two = one + more[0], two + more[1]
+    for image in range(images):
+        out_edge_ref[image] = edge_rows(info_ref, out_ref, image, cols).astype(BF16)
+    put_sums(sums_ref, one, two)
 
 
 def conv_forward(info, reduced, edges, sums_one, params, matrices, per_image):
@@ -443,13 +451,13 @@
 
 
 def conv_backward_kernel(
-    per_image, group_images, group, d_count, red_count, info_ref, *refs
+    per_image, group_images, d_count, red_count, info_ref, *refs
 ):
     d_fields, refs = list(zip(refs[:d_count], refs[d_count : 2 * d_count])), refs[2 * d_count :]
-    reduced, refs = [[v] for v in refs[:red_count]], refs[red_count:]
-    grp_ref, g_edge_ref, act_ref, sums_two_ref, grads_two_ref, sums_one_ref, par_ref, mat_ref = refs[:8]
-    out_ref, sums_ref, kernel_ref, window_ref, turned_ref = refs[8:]
-    images, pixels, chans = act_ref.shape
+    reduced, refs = refs[:red_count], refs[red_count:]
+    grp_ref, g_edge_ref, sums_two_ref, grads_two_ref, sums_one_ref, par_ref, mat_ref = refs[:7]
+    out_ref, sums_ref, window_ref = refs[7:]
+    images, pixels, chans = grp_ref.shape
     cols = g_edge_ref.shape[1]
     total_pixels = pixel_count(info_ref, per_image)
     avg_two, inv_two = norm_of(sums_two_ref, total_pixels)
@@ -462,62 +470,73 @@
     def input_grad(d, grouped, keep):
         return (d - (bias_part + (grouped - avg_two) * gain_part)) * (scale_two * keep)
 
-    def fill(refs, at, image, nothing):
+    def fill(image):
         keep = (image < info_ref[OWN_COUNT]).astype(F32)
-        own = input_grad(refs[0][at], grp_ref[image], keep)
-        edge = input_grad(refs[1][at].astype(F32), g_edge_ref[image].astype(F32), keep)
+        own = input_grad(at_image([f[0] for f in d_fields], image), grp_ref[image], keep)
+        edge = at_image([f[1] for f in d_fields], image).astype(F32)
+        edge = input_grad(edge, g_edge_ref[image].astype(F32), keep)
         fill_windows(window_ref, image, with_edges(info_ref, own, edge), cols)
-        turned_ref[:, pl.ds(pl.multiple_of(image * pixels, pixels), pixels)] = act_ref[image].T
-        return nothing
-
-    def convolve(refs, at, first, sums):
+
+    def convolve(first, one, two):
         grad = None
         for i in range(3):
-            piece = window_ref[pl.ds(first, group_images), i * cols : i * cols + pixels, :]
+            piece = window_ref[first : first + group_images, i * cols : i * cols + pixels, :]
             term = dot(piece.reshape(group_images * pixels, 3 * chans), mat_ref[i], 1, 0)
             grad = term if grad is None else grad + term
-        one, two = sums
         for i in range(group_images):
             image = first + i
             keep = (image < info_ref[OWN_COUNT]).astype(F32)
-            normalized = (refs[0][at + i] - avg_one) * inv_one
+            normalized = (at_image(reduced, image) - avg_one) * inv_one
             slope = silu_slope(normalized * gain_one + bias_one)
             d_one = grad[i * pixels : (i + 1) * pixels] * (slope * keep)
             out_ref[image] = d_one
             one, two = one + fold(d_one), two + fold(d_one * normalized)
         return one, two
 
-    each_image(d_fields, fill, 0)
-    zero = jnp.zeros((8, chans), F32)
-    put_sums(sums_ref, *each_image(reduced, convolve, (zero, zero), group_images))
+    one = two = jnp.zeros((8, chans), F32)
+    for first in range(0, images + group_images, group_images):
+        for image in range(first, min(first + group_images, images)):
+            fill(image)
+        if first:
+            one, two = convolve(first - group_images, one, two)
+    put_sums(sums_ref, one, two)
+
+
+def tap_grads_kernel(group, cols, step, info_ref, act_ref, window_ref, out_ref, turned_ref):
+    images, pixels, chans = act_ref.shape
+    for image in range(images):
+        turned_ref[:, image * pixels : (image + 1) * pixels] = act_ref[image].T
     same = (
         lax.broadcasted_iota(jnp.int32, (chans, 3 * chans), 0) // group
         == lax.broadcasted_iota(jnp.int32, (chans, 3 * chans), 1) % chans // group
     )
     for i in range(3):
         total = None
-        for first in range(0, images, group_images):
-            piece = window_ref[first : first + group_images, i * cols : i * cols + pixels, :]
-            turned = turned_ref[:, first * pixels : (first + group_images) * pixels]
-            term = dot(turned, piece.reshape(group_images * pixels, 3 * chans), 1, 0)
+        for first in range(0, images, step):
+            piece = window_ref[first : first + step, i * cols : i * cols + pixels, :]
+            turned = turned_ref[:, first * pixels : (first + step) * pixels]
+            term = dot(turned, piece.reshape(step * pixels, 3 * chans), 1, 0)
             total = term if total is None else total + term
         total = jnp.sum(jnp.where(same, total, 0.0).reshape(chans // group, group, 3 * chans), 0)
         for j in range(3):
-            kernel_ref[3 * (2 - i) + 2 - j] = total[:, j * chans : (j + 1) * chans].astype(kernel_ref.dtype)
-
-
-def conv_backward(info, d_two, d_edges, grouped, g_edge, reduced, acts, sums_two, grads_two, sums_one, params, matrices,
-                  group, per_image):
+            out_ref[3 * (2 - i) + 2 - j] = total[:, j * chans : (j + 1) * chans]
+
+
+def tap_grads(info, acts, windows, group, cols):
+    images, pixels, chans = acts.shape
+    return kernel_call(
+        functools.partial(tap_grads_kernel, group, cols, 4), "tap_grads", [info, acts, windows], [((9, group, chans), F32)],
+        [pltpu.VMEM((chans, images * pixels), BF16)],
+    )[0]
+
+
+def conv_backward(info, d_two, d_edges, grouped, g_edge, reduced, sums_two, grads_two, sums_one, params, matrices, per_image):
     images, pixels, chans = grouped.shape
     cols = g_edge.shape[1]
     return kernel_call(
-        functools.partial(conv_backward_kernel, per_image, 4, group, len(d_two), len(reduced)), "conv_backward",
-        [info, *d_two, *d_edges, *reduced, grouped, g_edge, acts, sums_two, grads_two, sums_one, params, matrices],
-        [(grouped.shape, F32), sums_out(True, chans), ((9, group, chans), F32)],
-        [
-            pltpu.VMEM((images, pixels + 2 * cols, 3 * chans), BF16),
-            pltpu.VMEM((chans, images * pixels), BF16),
-        ],
+        functools.partial(conv_backward_kernel, per_image, 4, len(d_two), len(reduced)), "conv_backward",
+        [info, *d_two, *d_edges, *reduced, grouped, g_edge, sums_two, grads_two, sums_one, params, matrices],
+        [(grouped.shape, F32), sums_out(True, chans), ((images, pixels + 2 * cols, 3 * chans), BF16)],
     )
 
 
@@ -650,7 +669,7 @@
 def split_next(info, pair, step):
     half = (pair[0].shape[0] // 2,) + pair[0].shape[1:]
     return kernel_call(
-        functools.partial(split_next_kernel, step[2]), "split_next", [info, *pair], [(half, F32), (half, BF16)]
+        functools.partial(split_next_kernel, step[2]), "split_next", [info, *pair], [(half, F32), (half, BF16)], flops=STAGE_COST
     )
 
 
@@ -659,7 +678,7 @@
 
 
 def add_last(info, pair):
-    return kernel_call(add_kernel, "add_last", [info, *pair], [(pair[0].shape, BF16)])[0]
+    return kernel_call(add_kernel, "add_last", [info, *pair], [(pair[0].shape, BF16)], flops=STAGE_COST)[0]
 
 
 def join_kernel(info_ref, *refs):
@@ -670,7 +689,7 @@
 
 def join(info, *values):
     shape = (values[0].shape[0] * len(values),) + values[0].shape[1:]
-    return kernel_call(join_kernel, "join", [info, *values], [(shape, BF16)])[0]
+    return kernel_call(join_kernel, "join", [info, *values], [(shape, BF16)], flops=STAGE_COST)[0]
 
 
 def send_back(value, step):
@@ -756,8 +775,8 @@
     me, number = info_ref[CHAN_AT], part_of(info_ref, REDUCE_STEPS)
     part = out_ref.shape[0] // count
     batches = refs[0].shape[0]
-    size = refs[2].shape[1]
-    extra = refs[0].shape[1] - size
+    size = refs[0].shape[1]
+    extra = refs[2].shape[1] - size
     for half in range(2):
         for other in range(2):
             ref = refs[2 * half + other]
@@ -766,14 +785,14 @@
                 row = at * size
                 to = (me ^ (half * (count // 2) + row // part)) * part + row % part
                 out_ref[pl.ds(pl.multiple_of(to, size), size), :] = ref[k, 0:size, :].astype(F32)
-                if half == 0:
+                if half == 1:
                     more_ref[pl.ds(pl.multiple_of(at * extra, 8), extra), :] = ref[k, size:, :].astype(F32)
     group_ref[...] = more_ref[0 : group_ref.shape[0], :]
 
 
 def place_reduce(info, halves, count, part, group_rows):
-    batches, rows, mid = halves[0][0].shape
-    extra = rows - halves[1][0].shape[1]
+    batches, rows, mid = halves[1][0].shape
+    extra = rows - halves[0][0].shape[1]
     return kernel_call(
         functools.partial(place_reduce_kernel, count), "place_reduce", [info] + [v for pair in halves for v in pair],
         [((part * count, mid), F32), ((group_rows, mid), F32)], [pltpu.VMEM((2 * batches * extra, mid), F32)],
@@ -872,12 +891,13 @@
         red_edges.append(edge_swap(edge))
     inputs = [list(chunks) for chunks in zip(*inputs)]
     weights += [swap(after(columns[k], inputs[2][-1]), k) for k in range(2, chan_size)]
-    sums_one = spread_sums(after(sums, *weights[2:]))
+    late_back = [swap(after(rows_back[k], inputs[2][-1]), k) for k in range(3, chan_size)]
+    sums_one = spread_sums(sums)
 
     acts_one, grouped, grp_edge, sums = conv_forward(
         info, reduced, red_edges, sums_one, mid_params, matrices, per_image
     )
-    sums_two = spread_sums(sums)
+    sums_two = spread_sums(after(sums, *weights[2:], *late_back))
 
     acts = []
     for chunk in cut_images(EXPAND_CHUNKS):
@@ -920,20 +940,20 @@
         )
         d_two.append(grad)
         d_edges.append(edge_swap(edge))
-    grads_two = sums_of(sums, grp_edge, *d_edges)
+    if staged:
+        sums = after(sums, expand_pair[1], grp_edge, d_edges[0])
+    grads_two = sums_of(sums, d_edges[-1])
     turn = info
     if staged:
         pair = split_next(after(info, grads_two), expand_pair, EXPAND_STEPS[2])
         turn = after(info, pair[0])
         expand_pair = send_half(pair, EXPAND_STEPS[2])
 
-    d_one, sums, grad_group = conv_backward(
-        turn, d_two, d_edges, grouped, grp_edge, reduced, acts_one, sums_two, grads_two, sums_one, mid_params,
-        matrices_back, group, per_image,
+    d_one, sums, windows = conv_backward(
+        turn, d_two, d_edges, grouped, grp_edge, reduced, sums_two, grads_two, sums_one, mid_params, matrices_back, per_image
     )
     if staged:
-        places = cut_places(after(info, d_one), expand_pair, chan_size)
-        sums = after(sums, places[0])
+        reduce_back.append(swap(after(rows_back[2], grads_two), 2))
     grads_one = spread_sums(sums)
 
     grad = grad_reduced(info, d_one, reduced, sums_one, grads_one, mid_params, per_image)
@@ -950,8 +970,7 @@
 
         def first_half(i):
             own = inputs[i * half : (i + 1) * half]
-            pair = in_turn(reduce_grad, own, grad, parts, None if i else grad_group)
-            pairs.append(send_half(pair, REDUCE_STEPS[0]))
+            pairs.append(send_half(in_turn(reduce_grad, own, grad, parts, taps if i else None), REDUCE_STEPS[0]))
 
         def next_half(i, step):
             pairs[i] = send_half(in_turn(split_next, pairs[i], REDUCE_STEPS[step]), REDUCE_STEPS[step])
@@ -962,34 +981,59 @@
         def back_half(i, step):
             pairs[i] = send_back(in_turn(join, *pairs[i]), REDUCE_STEPS[step])
 
-        first_half(0)
-        first_half(1)
-        places = [v if k == 0 else swap(after(v, turn), k) for k, v in enumerate(places)]
-        back = in_turn(join, *places)
-        back = send_back(back.reshape((1,) + back.shape), EXPAND_STEPS[2])
-        far_grads = [swap(after(grad, turn), k) for k in distances]
-        next_half(0, 1)
-        next_half(1, 1)
-        back = send_back(in_turn(join, *back), EXPAND_STEPS[1])
-        next_half(0, 2)
-        next_half(1, 2)
-        back = send_back(in_turn(join, *back), EXPAND_STEPS[0])
-        last_half(0)
-        last_half(1)
-        grads = [grad, swap(after(grad, turn), 1)]
-        for value in far_grads:
-            grads += [value, swap(after(value, turn), 1)]
-        reduce_back += [swap(after(rows_back[k], turn), k) for k in range(2, chan_size)]
-        back_half(0, 1)
-        grad_input = in_turn(input_grad, grad_field, grads, reduce_back)
-        back_half(1, 1)
-        back_half(0, 0)
-        grad_expand = in_turn(place_expand, back, chan_size, mid_part)
-        back_half(1, 0)
+        reduce_back += late_back
+        for word in LAST_PHASE:
+            kind, place = word[0], word[1:]
+            if kind in "ab":
+                i = "ab".index(kind)
+                if place == "0":
+                    first_half(i)
+                elif place in ("1", "2"):
+                    next_half(i, int(place))
+                elif place == "3":
+                    last_half(i)
+                else:
+                    back_half(i, 5 - int(place))
+            elif word == "t":
+                taps = in_turn(tap_grads, acts_one, windows, group, cols)
+            elif word == "c":
+                places = in_turn(cut_places, expand_pair, chan_size)
+                places = [v if k == 0 else swap(v, k) for k, v in enumerate(places)]
+            elif word == "e0":
+                back = in_turn(join, *places)
+                back = send_back(back.reshape((1,) + back.shape), EXPAND_STEPS[2])
+            elif kind == "e":
+                back = send_back(in_turn(join, *back), EXPAND_STEPS[2 - int(place)])
+            elif word == "x":
+                far_grads = [swap(after(grad, turn), k) for k in distances]
+            elif word == "o":
+                grads = [grad, swap(after(grad, turn), 1)]
+            elif word == "d":
+                for value in far_grads:
+                    grads += [value, swap(after(value, turn), 1)]
+            elif word == "p":
+                grad_expand = in_turn(place_expand, back, chan_size, mid_part)
+            elif word == "i":
+                grad_input = in_turn(input_grad, grad_field, grads, reduce_back)
+            elif word == "wo":
+                turn = after(turn, grads[1])
+            elif word == "wd":
+                turn = after(turn, *grads[2:])
+            elif word == "wz":
+                turn = after(turn, expand_pair[1])
+            elif word == "wr":
+                turn = after(turn, *reduce_back[2:])
+            elif word == "wa":
+                turn = after(turn, pairs[0][1])
+            elif word == "wb":
+                turn = after(turn, pairs[1][1])
+            elif word == "we":
+                turn = after(turn, back[1])
         grad_reduce, grad_group = place_reduce(turn, pairs, chan_size, out_part, 9 * group)
     else:
-        reduce_back += [swap(rows_back[k], k) for k in range(2, chan_size)]
+        reduce_back += [swap(rows_back[2], 2)] + late_back
         grad_input = input_grad(info, grad_field, gather(grad), reduce_back)
+        grad_group = tap_grads(info, acts_one, windows, group, cols)
         grad_reduce, grad_expand, grad_group = plain_weight_grads(inputs, grad, acts, grad_expanded, grad_group)
     vectors = sum_vectors([grads_one, grads_two, grads_three])
     return (

time: 299 us -> 268 us (0.90)
  waiting for transfers between devices: 132 us -> 101 us
    ppermute x55, waiting for transfers between devices: 132 us -> 101 us  [permute(): return lax.ppermute(value, axis, [(i, i ^ distance) for i in range(count)])]
    pallas_call x44 -> x45, Pallas kernels: 64.5 us -> 62.9 us  [kernel_call(): pl.pallas_call(body, in_specs=[SMEM if a.dtype == jnp.int32 else VMEM for...]
  transfers between devices with their start and end apart: 55 -> 55, of which waited for: 30 -> 23; matrix products, arithmetic and copies ran while one was open for 1% -> 1% of each run, Pallas kernels for 14% -> 18%
where the time goes in v6:
time: 268 us
  waiting for transfers between devices  101 us (38%)
  Pallas kernels  62.9 us (23%)
  blocking collectives  51.3 us (19%)
  starting transfers between devices  46.8 us (17%)
  local copies, waits for them, and re-layouts  4.18 us (2%)
    ppermute x55, waiting for transfers between devices, permute(): return lax.ppermute(value, axis, [(i, i ^ distance) for i in range(count)])  101 us
    pallas_call x45, Pallas kernels, kernel_call(): pl.pallas_call(body, in_specs=[SMEM if a.dtype == jnp.int32 else VMEM for...  62.9 us
    all_to_all x5, blocking collectives, spread_sums(): return lax.all_to_all(sent, REDUCE_AXES, 0, 0)  51.3 us
    ppermute x55, starting transfers between devices, permute(): return lax.ppermute(value, axis, [(i, i ^ distance) for i in range(count)])  46.8 us
  transfers between devices with their start and end apart: 55, of which 23 were waited for; matrix products, arithmetic and copies ran while one was open for 1% of the time, Pallas kernels for 18%

profile of v6, /device:TPU:0, one launch (start us, length us, event | category | flops | bytes accessed | tf_op | source)
XLA Modules:
  0.0 267.9 jit_solution(8876001613650611189)
XLA Ops:
  2.0 3.0 %collective-permute-start.1 = (bf16[1024,512]{1,0:T(8,128)(2,1)S(1)}, bf16[1024,512]{1,0:T(8,128)(2,1)S(1)}, u32[]{:S(2)}, u32[]{:S(2)}) collective-permute-start(bf16[1024,512]{1,0:T(8,128)(2,1)S(1)} %bitcast.24), channel_id=1, source_target_pairs={{0,8},{4,12},{8,0},{12,4},{1,9},{5,13},{9,1},{13,5},{2,10},{6,14},... | collective-permute-start | bytes 3145736 | tf_op jit(solution)/shard_map/ppermute | solution.py:48
  10.6 18.4 %collective-permute-done.1.refs_2_.refs_0_ = bf16[1024,512]{1,0:T(8,128)(2,1)S(1)} collective-permute-done((bf16[1024,512]{1,0:T(8,128)(2,1)S(1)}, bf16[1024,512]{1,0:T(8,128)(2,1)S(1)}, u32[]{:S(2)}, u32[]{:S(2)}) %collective-permute-start.1) | collective-permute-done | bytes 1048608 | tf_op jit(solution)/shard_map/ppermute | solution.py:48
  30.7 19.9 %collective-permute-done.4.refs_2_.refs_1_ = bf16[1024,512]{1,0:T(8,128)(2,1)S(1)} collective-permute-done((bf16[1024,512]{1,0:T(8,128)(2,1)S(1)}, bf16[1024,512]{1,0:T(8,128)(2,1)S(1)}, u32[]{:S(2)}, u32[]{:S(2)}) %collective-permute-start.4) | collective-permute-done | bytes 1048608 | tf_op jit(solution)/shard_map/ppermute | solution.py:48
  60.0 12.2 %all_to_all.25.refs_4_.refs_10_.refs_3_ = f32[8,2,256]{2,1,0:T(2,128)S(1)} all-to-all(f32[8,2,256]{2,1,0:T(2,128)S(1)} %get-tuple-element.140), channel_id=1, replica_groups=mesh['height'=2,'chan'=4,'batch'=4] {'height','batch'}, dimensions={0} | all-to-all | bytes 32768 | tf_op jit(solution)/shard_map/all_to_all | solution.py:56
  72.2 3.9 %conv_forward.1 = (bf16[16,128,256]{2,1,0:T(8,128)(2,1)S(1)}, f32[16,128,256]{2,1,0:T(8,128)S(1)}, bf16[16,16,256]{2,1,0:T(8,128)(2,1)S(1)}, f32[8,2,256]{2,1,0:T(2,128)S(1)}) custom-call(s32[7]{0:T(128)S(1)} %stack.31.info_ref, f32[8,128,256]{2,1,0:T(8,128)S(1)} %get-tuple-element.130.refs_0_.refs_4_, ...), custom_call_target="tpu_custom_call" | custom-call | tf_op jit(solution)/shard_map/conv_forward/pallas_call | solution.py:29
  76.1 9.0 %all_to_all.26.sums_ref.refs_2_.refs_8_ = f32[8,2,256]{2,1,0:T(2,128)S(1)} all-to-all(f32[8,2,256]{2,1,0:T(2,128)S(1)} %get-tuple-element.150), channel_id=1, replica_groups=mesh['height'=2,'chan'=4,'batch'=4] {'height','batch'}, dimensions={0} | all-to-all | bytes 32768 | tf_op jit(solution)/shard_map/all_to_all | solution.py:56
  89.0 11.9 %collective-permute-done.14.refs_2_.refs_4_ = bf16[1024,256]{1,0:T(8,128)(2,1)S(1)} collective-permute-done((bf16[1024,256]{1,0:T(8,128)(2,1)S(1)}, bf16[1024,256]{1,0:T(8,128)(2,1)S(1)}, u32[]{:S(2)}, u32[]{:S(2)}) %collective-permute-start.14) | collective-permute-done | bytes 524320 | tf_op jit(solution)/shard_map/ppermute | solution.py:48
  101.4 6.8 %collective-permute-done.17.refs_2_.refs_5_ = bf16[1024,256]{1,0:T(8,128)(2,1)S(1)} collective-permute-done((bf16[1024,256]{1,0:T(8,128)(2,1)S(1)}, bf16[1024,256]{1,0:T(8,128)(2,1)S(1)}, u32[]{:S(2)}, u32[]{:S(2)}) %collective-permute-start.17) | collective-permute-done | bytes 524320 | tf_op jit(solution)/shard_map/ppermute | solution.py:48
  111.9 9.1 %all_to_all.27.refs_4_.refs_3_ = f32[8,2,512]{2,1,0:T(2,128)S(1)} all-to-all(f32[8,2,512]{2,1,0:T(2,128)S(1)} %get-tuple-element.155), channel_id=1, replica_groups=mesh['height'=2,'chan'=4,'batch'=4] {'height','batch'}, dimensions={0} | all-to-all | bytes 65536 | tf_op jit(solution)/shard_map/all_to_all | solution.py:56
  121.0 5.1 %output.1 = (bf16[16,128,512]{2,1,0:T(8,128)(2,1)}, f32[16,128,512]{2,1,0:T(8,128)S(1)}, f32[8,2,512]{2,1,0:T(2,128)S(1)}) custom-call(s32[7]{0:T(128)S(1)} %stack.31.info_ref, f32[8,128,512]{2,1,0:T(8,128)S(1)} %get-tuple-element.152.refs_0_, f32[8,128,512]{2,1,0:T(8,128)S(1)} %get-tuple-element.154.refs_1_, bf16[16,128,512]{2,1,0:T(8,128)(2,1)S(1)} %bitcast.29, ...), custom_call_target="tpu_custom_call" | custom-call | tf_op jit(solution)/shard_map/output/pallas_call | solution.py:29
  126.1 9.1 %all_to_all.28.refs_4_.refs_2_ = f32[8,2,512]{2,1,0:T(2,128)S(1)} all-to-all(f32[8,2,512]{2,1,0:T(2,128)S(1)} %get-tuple-element.159), channel_id=1, replica_groups=mesh['height'=2,'chan'=4,'batch'=4] {'height','batch'}, dimensions={0} | all-to-all | bytes 65536 | tf_op jit(solution)/shard_map/all_to_all | solution.py:56
  135.2 1.9 back_expand.2
  141.4 3.0 %expand_grad.1 = (f32[4,128,512]{2,1,0:T(8,128)S(1)}, bf16[4,128,512]{2,1,0:T(8,128)(2,1)S(1)}) custom-call(s32[7]{0:T(128)S(1)} %stack.31.info_ref, bf16[1024,256]{1,0:T(8,128)(2,1)S(1)} %act_two.2.refs_0_, bf16[1024,256]{1,0:T(8,128)(2,1)S(1)} %act_two.3.refs_0_.refs_1_, bf16[1024,256]{1,0:T(8,128)(2,1)S(1)} %collective-permute-done.13.refs_1_.refs_2_, ...), custom_call_target="tpu_custom_call" | custom-call | tf_op jit(solution)/shard_map/expand_grad/pallas_call | solution.py:29
  147.2 8.2 %collective-permute-done.20.refs_0_ = bf16[1024,256]{1,0:T(8,128)(2,1)S(1)} collective-permute-done((bf16[1024,256]{1,0:T(8,128)(2,1)S(1)}, bf16[1024,256]{1,0:T(8,128)(2,1)S(1)}, u32[]{:S(2)}, u32[]{:S(2)}) %collective-permute-start.20) | collective-permute-done | bytes 524320 | tf_op jit(solution)/shard_map/ppermute | solution.py:48
  161.4 4.4 %collective-permute-done.23.refs_0_ = bf16[1024,256]{1,0:T(8,128)(2,1)S(1)} collective-permute-done((bf16[1024,256]{1,0:T(8,128)(2,1)S(1)}, bf16[1024,256]{1,0:T(8,128)(2,1)S(1)}, u32[]{:S(2)}, u32[]{:S(2)}) %collective-permute-start.23) | collective-permute-done | bytes 524320 | tf_op jit(solution)/shard_map/ppermute | solution.py:48
  169.4 2.2 collective-permute-done.27.refs_3_
  172.8 3.3 %collective-permute-start.31 = (f32[2,256]{1,0:T(2,128)S(1)}, f32[2,256]{1,0:T(2,128)S(1)}, u32[]{:S(2)}, u32[]{:S(2)}) collective-permute-start(f32[2,256]{1,0:T(2,128)S(1)} %add_rows.1.refs_0_), channel_id=1, source_target_pairs={{0,3},{1,2},{2,1},{3,0},{4,7},{5,6},{6,5},{7,4},{8,11},{9,10},{10,... | collective-permute-start | bytes 6152 | tf_op jit(solution)/shard_map/ppermute | solution.py:48
  180.2 4.7 %conv_backward.1 = (f32[16,128,256]{2,1,0:T(8,128)S(1)}, f32[8,2,256]{2,1,0:T(2,128)S(1)}, bf16[16,160,768]{2,1,0:T(8,128)(2,1)S(1)}) custom-call(s32[7]{0:T(128)S(1)} %stack.31.info_ref, f32[8,128,256]{2,1,0:T(8,128)S(1)} %get-tuple-element.164.refs_0_, f32[8,128,256]{2,1,0:T(8,128)S(1)} %get-tuple-element.188.refs_1_, ...), custom_call_target="tpu_custom_call" | custom-call | tf_op jit(solution)/shard_map/conv_backward/pallas_call | solution.py:29
  184.9 12.0 %all_to_all.29.refs_4_.refs_0_ = f32[8,2,256]{2,1,0:T(2,128)S(1)} all-to-all(f32[8,2,256]{2,1,0:T(2,128)S(1)} %get-tuple-element.191), channel_id=1, replica_groups=mesh['height'=2,'chan'=4,'batch'=4] {'height','batch'}, dimensions={0} | all-to-all | bytes 32768 | tf_op jit(solution)/shard_map/all_to_all | solution.py:56
  198.0 1.9 reduce_grad.2
  200.5 3.2 %tap_grads.1.refs_5_ = f32[9,32,256]{2,1,0:T(8,128)S(1)} custom-call(s32[7]{0:T(128)S(1)} %stack.31.info_ref, bf16[16,128,256]{2,1,0:T(8,128)(2,1)S(1)} %get-tuple-element.200.act_ref, bf16[16,160,768]{2,1,0:T(8,128)(2,1)S(1)} %get-tuple-element.201.window_ref), custom_call_target="tpu_custom_call" | custom-call | tf_op jit(solution)/shard_map/tap_grads/pallas_call | solution.py:29
  203.8 1.9 reduce_grad.3
  210.9 2.1 collective-permute-done.35.arrived_ref
  217.3 4.5 %collective-permute-done.40.arrived_ref = bf16[2,168,256]{2,1,0:T(8,128)(2,1)S(1)} collective-permute-done((bf16[2,168,256]{2,1,0:T(8,128)(2,1)S(1)}, bf16[2,168,256]{2,1,0:T(8,128)(2,1)S(1)}, u32[]{:S(2)}, u32[]{:S(2)}) %collective-permute-start.40) | collective-permute-done | bytes 172064 | tf_op jit(solution)/shard_map/ppermute | solution.py:48
  224.4 2.5 collective-permute-start.42
  226.9 3.4 %collective-permute-done.42.second_ref = bf16[1,128,256]{2,1,0:T(8,128)(2,1)S(1)} collective-permute-done((bf16[1,128,256]{2,1,0:T(8,128)(2,1)S(1)}, bf16[1,128,256]{2,1,0:T(8,128)(2,1)S(1)}, u32[]{:S(2)}, u32[]{:S(2)}) %collective-permute-start.42) | collective-permute-done | bytes 65568 | tf_op jit(solution)/shard_map/ppermute | solution.py:48
  230.9 2.6 collective-permute-start.44
  244.2 3.1 %collective-permute-done.48.refs_1_ = bf16[2,128,256]{2,1,0:T(8,128)(2,1)S(1)} collective-permute-done((bf16[2,128,256]{2,1,0:T(8,128)(2,1)S(1)}, bf16[2,128,256]{2,1,0:T(8,128)(2,1)S(1)}, u32[]{:S(2)}, u32[]{:S(2)}) %collective-permute-start.48) | collective-permute-done | bytes 131104 | tf_op jit(solution)/shard_map/ppermute | solution.py:48
  250.0 6.0 %collective-permute-done.49.refs_1_ = bf16[4,128,256]{2,1,0:T(8,128)(2,1)S(1)} collective-permute-done((bf16[4,128,256]{2,1,0:T(8,128)(2,1)S(1)}, bf16[4,128,256]{2,1,0:T(8,128)(2,1)S(1)}, u32[]{:S(2)}, u32[]{:S(2)}) %collective-permute-start.49) | collective-permute-done | bytes 262176 | tf_op jit(solution)/shard_map/ppermute | solution.py:48
  258.9 4.8 %input_grad.1 = bf16[2048,512]{1,0:T(8,128)(2,1)} custom-call(s32[7]{0:T(128)S(1)} %stack.31.info_ref, f32[2048,512]{1,0:T(8,128)S(1)} %bitcast.23, bf16[2048,256]{1,0:T(8,128)(2,1)S(1)} %grad_reduced.1.refs_4_.refs_0_, bf16[2048,256]{1,0:T(8,128)(2,1)S(1)} %collective-permute-done.51.refs_1_, bf16[2048,256]{1,0:T(8,128)(2,1)S(1)} %collective-permute-done.52.refs_2_, ...), custom_call_target="tpu_custom_call" | custom-call | tf_op jit(solution)/shard_map/input_grad/pallas_call | solution.py:29
  263.8 2.0 place_expand.1
  265.8 2.1 place_reduce.1
  (162 shorter events, 78.6 us)
Async XLA Ops:
  2.0 27.0 %collective-permute-start.1 = (bf16[1024,512]{1,0:T(8,128)(2,1)S(1)}, bf16[1024,512]{1,0:T(8,128)(2,1)S(1)}, u32[]{:S(2)}, u32[]{:S(2)}) collective-permute-start(bf16[1024,512]{1,0:T(8,128)(2,1)S(1)} %bitcast.24), channel_id=1, source_target_pairs={{0,8},{4,12},{8,0},{12,4},{1,9},{5,13},{9,1},{13,5},{2,10},{6,14},... | collective-permute-start | bytes 3145736 | tf_op jit(solution)/shard_map/ppermute | solution.py:48
  8.5 42.2 %collective-permute-start.4 = (bf16[1024,512]{1,0:T(8,128)(2,1)S(1)}, bf16[1024,512]{1,0:T(8,128)(2,1)S(1)}, u32[]{:S(2)}, u32[]{:S(2)}) collective-permute-start(bf16[1024,512]{1,0:T(8,128)(2,1)S(1)} %slice.11.refs_0_.refs_1_), channel_id=1, source_target_pairs={{0,8},{4,12},{8,0},{12,4},{1,9},{5,13},{9,1},{13,5},{2,10},{6,14},... | collective-permute-start | bytes 3145736 | tf_op jit(solution)/shard_map/ppermute | solution.py:48
  9.2 20.9 %collective-permute-start.5 = (bf16[256,512]{1,0:T(8,128)(2,1)S(1)}, bf16[256,512]{1,0:T(8,128)(2,1)S(1)}, u32[]{:S(2)}, u32[]{:S(2)}) collective-permute-start(bf16[256,512]{1,0:T(8,128)(2,1)S(1)} %get-tuple-element.133), channel_id=1, source_target_pairs={{0,4},{4,0},{8,12},{12,8},{1,5},{5,1},{9,13},{13,9},{2,6},{6,2},{1... | collective-permute-start | bytes 786440 | tf_op jit(solution)/shard_map/ppermute | solution.py:48
  9.9 20.8 %collective-permute-start.6 = (bf16[512,256]{1,0:T(8,128)(2,1)S(1)}, bf16[512,256]{1,0:T(8,128)(2,1)S(1)}, u32[]{:S(2)}, u32[]{:S(2)}) collective-permute-start(bf16[512,256]{1,0:T(8,128)(2,1)S(1)} %get-tuple-element.134), channel_id=1, source_target_pairs={{0,4},{4,0},{8,12},{12,8},{1,5},{5,1},{9,13},{13,9},{2,6},{6,2},{1... | collective-permute-start | bytes 786440 | tf_op jit(solution)/shard_map/ppermute | solution.py:48
  10.5 41.9 %collective-permute-start = (bf16[1024,512]{1,0:T(8,128)(2,1)S(1)}, bf16[1024,512]{1,0:T(8,128)(2,1)S(1)}, u32[]{:S(2)}, u32[]{:S(2)}) collective-permute-start(bf16[1024,512]{1,0:T(8,128)(2,1)S(1)} %bitcast.25), channel_id=1, source_target_pairs={{0,4},{4,0},{8,12},{12,8},{1,5},{5,1},{9,13},{13,9},{2,6},{6,2},{1... | collective-permute-start | bytes 3145736 | tf_op jit(solution)/shard_map/ppermute | solution.py:48
  29.0 23.5 %collective-permute-start.2 = (bf16[1024,512]{1,0:T(8,128)(2,1)S(1)}, bf16[1024,512]{1,0:T(8,128)(2,1)S(1)}, u32[]{:S(2)}, u32[]{:S(2)}) collective-permute-start(bf16[1024,512]{1,0:T(8,128)(2,1)S(1)} %collective-permute-done.1.refs_2_.refs_0_), channel_id=1, source_target_pairs={{0,4},{4,0},{8,12},{12,8},{1,5},{5,1},{9,13},{13,9},{2,6},{6,2},{1... | collective-permute-start | bytes 3145736 | tf_op jit(solution)/shard_map/ppermute | solution.py:48
  30.1 25.9 %collective-permute-start.3 = (bf16[1024,512]{1,0:T(8,128)(2,1)S(1)}, bf16[1024,512]{1,0:T(8,128)(2,1)S(1)}, u32[]{:S(2)}, u32[]{:S(2)}) collective-permute-start(bf16[1024,512]{1,0:T(8,128)(2,1)S(1)} %slice.11.refs_0_.refs_1_), channel_id=1, source_target_pairs={{0,4},{4,0},{8,12},{12,8},{1,5},{5,1},{9,13},{13,9},{2,6},{6,2},{1... | collective-permute-start | bytes 3145736 | tf_op jit(solution)/shard_map/ppermute | solution.py:48
  50.6 25.4 %collective-permute-start.10 = (bf16[256,512]{1,0:T(8,128)(2,1)S(1)}, bf16[256,512]{1,0:T(8,128)(2,1)S(1)}, u32[]{:S(2)}, u32[]{:S(2)}) collective-permute-start(bf16[256,512]{1,0:T(8,128)(2,1)S(1)} %get-tuple-element.145), channel_id=1, source_target_pairs={{0,8},{4,12},{8,0},{12,4},{1,9},{5,13},{9,1},{13,5},{2,10},{6,14},... | collective-permute-start | bytes 786440 | tf_op jit(solution)/shard_map/ppermute | solution.py:48
  52.4 23.7 %collective-permute-start.11 = (bf16[256,512]{1,0:T(8,128)(2,1)S(1)}, bf16[256,512]{1,0:T(8,128)(2,1)S(1)}, u32[]{:S(2)}, u32[]{:S(2)}) collective-permute-start(bf16[256,512]{1,0:T(8,128)(2,1)S(1)} %get-tuple-element.147), channel_id=1, source_target_pairs={{0,12},{4,8},{8,4},{12,0},{1,13},{5,9},{9,5},{13,1},{2,14},{6,10},... | collective-permute-start | bytes 786440 | tf_op jit(solution)/shard_map/ppermute | solution.py:48
  52.5 23.6 %collective-permute-start.12 = (bf16[512,256]{1,0:T(8,128)(2,1)S(1)}, bf16[512,256]{1,0:T(8,128)(2,1)S(1)}, u32[]{:S(2)}, u32[]{:S(2)}) collective-permute-start(bf16[512,256]{1,0:T(8,128)(2,1)S(1)} %get-tuple-element.149), channel_id=1, source_target_pairs={{0,12},{4,8},{8,4},{12,0},{1,13},{5,9},{9,5},{13,1},{2,14},{6,10},... | collective-permute-start | bytes 786440 | tf_op jit(solution)/shard_map/ppermute | solution.py:48
  57.9 14.3 %collective-permute-start.9 = (bf16[8,16,256]{2,1,0:T(8,128)(2,1)S(1)}, bf16[8,16,256]{2,1,0:T(8,128)(2,1)S(1)}, u32[]{:S(2)}, u32[]{:S(2)}) collective-permute-start(bf16[8,16,256]{2,1,0:T(8,128)(2,1)S(1)} %get-tuple-element.139), channel_id=1, source_target_pairs={{0,16},{16,0},{1,17},{17,1},{2,18},{18,2},{3,19},{19,3},{4,20},{20... | collective-permute-start | bytes 196616 | tf_op jit(solution)/shard_map/ppermute | solution.py:48
  59.4 12.7 %collective-permute-start.8 = (bf16[8,16,256]{2,1,0:T(8,128)(2,1)S(1)}, bf16[8,16,256]{2,1,0:T(8,128)(2,1)S(1)}, u32[]{:S(2)}, u32[]{:S(2)}) collective-permute-start(bf16[8,16,256]{2,1,0:T(8,128)(2,1)S(1)} %get-tuple-element.138), channel_id=1, source_target_pairs={{0,16},{16,0},{1,17},{17,1},{2,18},{18,2},{3,19},{19,3},{4,20},{20... | collective-permute-start | bytes 196616 | tf_op jit(solution)/shard_map/ppermute | solution.py:48
  86.0 14.9 %collective-permute-start.14 = (bf16[1024,256]{1,0:T(8,128)(2,1)S(1)}, bf16[1024,256]{1,0:T(8,128)(2,1)S(1)}, u32[]{:S(2)}, u32[]{:S(2)}) collective-permute-start(bf16[1024,256]{1,0:T(8,128)(2,1)S(1)} %act_two.2.refs_0_), channel_id=1, source_target_pairs={{0,8},{4,12},{8,0},{12,4},{1,9},{5,13},{9,1},{13,5},{2,10},{6,14},... | collective-permute-start | bytes 1572872 | tf_op jit(solution)/shard_map/ppermute | solution.py:48
  87.5 20.7 %collective-permute-start.17 = (bf16[1024,256]{1,0:T(8,128)(2,1)S(1)}, bf16[1024,256]{1,0:T(8,128)(2,1)S(1)}, u32[]{:S(2)}, u32[]{:S(2)}) collective-permute-start(bf16[1024,256]{1,0:T(8,128)(2,1)S(1)} %act_two.3.refs_0_.refs_1_), channel_id=1, source_target_pairs={{0,8},{4,12},{8,0},{12,4},{1,9},{5,13},{9,1},{13,5},{2,10},{6,14},... | collective-permute-start | bytes 1572872 | tf_op jit(solution)/shard_map/ppermute | solution.py:48
  89.0 19.2 %collective-permute-start.13 = (bf16[1024,256]{1,0:T(8,128)(2,1)S(1)}, bf16[1024,256]{1,0:T(8,128)(2,1)S(1)}, u32[]{:S(2)}, u32[]{:S(2)}) collective-permute-start(bf16[1024,256]{1,0:T(8,128)(2,1)S(1)} %act_two.2.refs_0_), channel_id=1, source_target_pairs={{0,4},{4,0},{8,12},{12,8},{1,5},{5,1},{9,13},{13,9},{2,6},{6,2},{1... | collective-permute-start | bytes 1572872 | tf_op jit(solution)/shard_map/ppermute | solution.py:48
  100.9 9.1 %collective-permute-start.16 = (bf16[1024,256]{1,0:T(8,128)(2,1)S(1)}, bf16[1024,256]{1,0:T(8,128)(2,1)S(1)}, u32[]{:S(2)}, u32[]{:S(2)}) collective-permute-start(bf16[1024,256]{1,0:T(8,128)(2,1)S(1)} %act_two.3.refs_0_.refs_1_), channel_id=1, source_target_pairs={{0,4},{4,0},{8,12},{12,8},{1,5},{5,1},{9,13},{13,9},{2,6},{6,2},{1... | collective-permute-start | bytes 1572872 | tf_op jit(solution)/shard_map/ppermute | solution.py:48
  140.6 14.8 %collective-permute-start.20 = (bf16[1024,256]{1,0:T(8,128)(2,1)S(1)}, bf16[1024,256]{1,0:T(8,128)(2,1)S(1)}, u32[]{:S(2)}, u32[]{:S(2)}) collective-permute-start(bf16[1024,256]{1,0:T(8,128)(2,1)S(1)} %get-tuple-element.163), channel_id=1, source_target_pairs={{0,8},{4,12},{8,0},{12,4},{1,9},{5,13},{9,1},{13,5},{2,10},{6,14},... | collective-permute-start | bytes 1572872 | tf_op jit(solution)/shard_map/ppermute | solution.py:48
  144.5 13.8 %collective-permute-start.21 = (bf16[4,128,512]{2,1,0:T(8,128)(2,1)S(1)}, bf16[4,128,512]{2,1,0:T(8,128)(2,1)S(1)}, u32[]{:S(2)}, u32[]{:S(2)}) collective-permute-start(bf16[4,128,512]{2,1,0:T(8,128)(2,1)S(1)} %get-tuple-element.169), channel_id=1, source_target_pairs={{0,16},{16,0},{1,17},{17,1},{2,18},{18,2},{3,19},{19,3},{4,20},{20... | collective-permute-start | bytes 1572872 | tf_op jit(solution)/shard_map/ppermute | solution.py:48
  145.9 20.0 %collective-permute-start.23 = (bf16[1024,256]{1,0:T(8,128)(2,1)S(1)}, bf16[1024,256]{1,0:T(8,128)(2,1)S(1)}, u32[]{:S(2)}, u32[]{:S(2)}) collective-permute-start(bf16[1024,256]{1,0:T(8,128)(2,1)S(1)} %get-tuple-element.175), channel_id=1, source_target_pairs={{0,8},{4,12},{8,0},{12,4},{1,9},{5,13},{9,1},{13,5},{2,10},{6,14},... | collective-permute-start | bytes 1572872 | tf_op jit(solution)/shard_map/ppermute | solution.py:48
  158.9 9.0 %collective-permute-start.24 = (bf16[2,128,512]{2,1,0:T(8,128)(2,1)S(1)}, bf16[2,128,512]{2,1,0:T(8,128)(2,1)S(1)}, u32[]{:S(2)}, u32[]{:S(2)}) collective-permute-start(bf16[2,128,512]{2,1,0:T(8,128)(2,1)S(1)} %get-tuple-element.178), channel_id=1, source_target_pairs={{0,1},{1,0},{2,3},{3,2},{4,5},{5,4},{6,7},{7,6},{8,9},{9,8},{10,11... | collective-permute-start | bytes 786440 | tf_op jit(solution)/shard_map/ppermute | solution.py:48
  159.4 8.4 %collective-permute-start.25 = (bf16[16,16,256]{2,1,0:T(8,128)(2,1)S(1)}, bf16[16,16,256]{2,1,0:T(8,128)(2,1)S(1)}, u32[]{:S(2)}, u32[]{:S(2)}) collective-permute-start(bf16[16,16,256]{2,1,0:T(8,128)(2,1)S(1)} %get-tuple-element.180), channel_id=1, source_target_pairs={{0,16},{16,0},{1,17},{17,1},{2,18},{18,2},{3,19},{19,3},{4,20},{20... | collective-permute-start | bytes 393224 | tf_op jit(solution)/shard_map/ppermute | solution.py:48
  178.2 19.7 %collective-permute-start.33 = (bf16[512,256]{1,0:T(8,128)(2,1)S(1)}, bf16[512,256]{1,0:T(8,128)(2,1)S(1)}, u32[]{:S(2)}, u32[]{:S(2)}) collective-permute-start(bf16[512,256]{1,0:T(8,128)(2,1)S(1)} %get-tuple-element.196), channel_id=1, source_target_pairs={{0,8},{4,12},{8,0},{12,4},{1,9},{5,13},{9,1},{13,5},{2,10},{6,14},... | collective-permute-start | bytes 786440 | tf_op jit(solution)/shard_map/ppermute | solution.py:48
  179.7 18.3 %collective-permute-start.32 = (bf16[1,128,512]{2,1,0:T(8,128)(2,1)S(1)}, bf16[1,128,512]{2,1,0:T(8,128)(2,1)S(1)}, u32[]{:S(2)}, u32[]{:S(2)}) collective-permute-start(bf16[1,128,512]{2,1,0:T(8,128)(2,1)S(1)} %get-tuple-element.193), channel_id=1, source_target_pairs={{0,2},{1,3},{2,0},{3,1},{4,6},{5,7},{6,4},{7,5},{8,10},{9,11},{10,... | collective-permute-start | bytes 393224 | tf_op jit(solution)/shard_map/ppermute | solution.py:48
  199.9 9.9 %collective-permute-start.34 = (bf16[4,128,256]{2,1,0:T(8,128)(2,1)S(1)}, bf16[4,128,256]{2,1,0:T(8,128)(2,1)S(1)}, u32[]{:S(2)}, u32[]{:S(2)}) collective-permute-start(bf16[4,128,256]{2,1,0:T(8,128)(2,1)S(1)} %get-tuple-element.207), channel_id=1, source_target_pairs={{0,16},{16,0},{1,17},{17,1},{2,18},{18,2},{3,19},{19,3},{4,20},{20... | collective-permute-start | bytes 786440 | tf_op jit(solution)/shard_map/ppermute | solution.py:48
  213.6 8.2 %collective-permute-start.40 = (bf16[2,168,256]{2,1,0:T(8,128)(2,1)S(1)}, bf16[2,168,256]{2,1,0:T(8,128)(2,1)S(1)}, u32[]{:S(2)}, u32[]{:S(2)}) collective-permute-start(bf16[2,168,256]{2,1,0:T(8,128)(2,1)S(1)} %get-tuple-element.220), channel_id=1, source_target_pairs={{0,1},{1,0},{2,3},{3,2},{4,5},{5,4},{6,7},{7,6},{8,9},{9,8},{10,11... | collective-permute-start | bytes 516104 | tf_op jit(solution)/shard_map/ppermute | solution.py:48
  214.8 26.6 %collective-permute-start.52 = (bf16[2048,256]{1,0:T(8,128)(2,1)S(1)}, bf16[2048,256]{1,0:T(8,128)(2,1)S(1)}, u32[]{:S(2)}, u32[]{:S(2)}) collective-permute-start(bf16[2048,256]{1,0:T(8,128)(2,1)S(1)} %grad_reduced.1.refs_4_.refs_0_), channel_id=1, source_target_pairs={{0,8},{4,12},{8,0},{12,4},{1,9},{5,13},{9,1},{13,5},{2,10},{6,14},... | collective-permute-start | bytes 3145736 | tf_op jit(solution)/shard_map/ppermute | solution.py:48
  224.4 9.1 %collective-permute-start.43 = (bf16[2,128,512]{2,1,0:T(8,128)(2,1)S(1)}, bf16[2,128,512]{2,1,0:T(8,128)(2,1)S(1)}, u32[]{:S(2)}, u32[]{:S(2)}) collective-permute-start(bf16[2,128,512]{2,1,0:T(8,128)(2,1)S(1)} %join.8.refs_0_), channel_id=1, source_target_pairs={{0,1},{1,0},{2,3},{3,2},{4,5},{5,4},{6,7},{7,6},{8,9},{9,8},{10,11... | collective-permute-start | bytes 786440 | tf_op jit(solution)/shard_map/ppermute | solution.py:48
  234.0 10.2 %collective-permute-start.47 = (bf16[4,128,512]{2,1,0:T(8,128)(2,1)S(1)}, bf16[4,128,512]{2,1,0:T(8,128)(2,1)S(1)}, u32[]{:S(2)}, u32[]{:S(2)}) collective-permute-start(bf16[4,128,512]{2,1,0:T(8,128)(2,1)S(1)} %join.9.own_ref), channel_id=1, source_target_pairs={{0,16},{16,0},{1,17},{17,1},{2,18},{18,2},{3,19},{19,3},{4,20},{20... | collective-permute-start | bytes 1572872 | tf_op jit(solution)/shard_map/ppermute | solution.py:48
  235.5 23.4 %collective-permute-start.51 = (bf16[2048,256]{1,0:T(8,128)(2,1)S(1)}, bf16[2048,256]{1,0:T(8,128)(2,1)S(1)}, u32[]{:S(2)}, u32[]{:S(2)}) collective-permute-start(bf16[2048,256]{1,0:T(8,128)(2,1)S(1)} %grad_reduced.1.refs_4_.refs_0_), channel_id=1, source_target_pairs={{0,4},{4,0},{8,12},{12,8},{1,5},{5,1},{9,13},{13,9},{2,6},{6,2},{1... | collective-permute-start | bytes 3145736 | tf_op jit(solution)/shard_map/ppermute | solution.py:48
  241.4 17.6 %collective-permute-start.53 = (bf16[2048,256]{1,0:T(8,128)(2,1)S(1)}, bf16[2048,256]{1,0:T(8,128)(2,1)S(1)}, u32[]{:S(2)}, u32[]{:S(2)}) collective-permute-start(bf16[2048,256]{1,0:T(8,128)(2,1)S(1)} %collective-permute-done.52.refs_2_), channel_id=1, source_target_pairs={{0,4},{4,0},{8,12},{12,8},{1,5},{5,1},{9,13},{13,9},{2,6},{6,2},{1... | collective-permute-start | bytes 3145736 | tf_op jit(solution)/shard_map/ppermute | solution.py:48
  247.9 8.0 %collective-permute-start.49 = (bf16[4,128,256]{2,1,0:T(8,128)(2,1)S(1)}, bf16[4,128,256]{2,1,0:T(8,128)(2,1)S(1)}, u32[]{:S(2)}, u32[]{:S(2)}) collective-permute-start(bf16[4,128,256]{2,1,0:T(8,128)(2,1)S(1)} %join.12.refs_0_), channel_id=1, source_target_pairs={{0,16},{16,0},{1,17},{17,1},{2,18},{18,2},{3,19},{19,3},{4,20},{20... | collective-permute-start | bytes 786440 | tf_op jit(solution)/shard_map/ppermute | solution.py:48
  256.5 9.3 %collective-permute-start.54 = (bf16[4,168,256]{2,1,0:T(8,128)(2,1)S(1)}, bf16[4,168,256]{2,1,0:T(8,128)(2,1)S(1)}, u32[]{:S(2)}, u32[]{:S(2)}) collective-permute-start(bf16[4,168,256]{2,1,0:T(8,128)(2,1)S(1)} %join.13.refs_2_), channel_id=1, source_target_pairs={{0,16},{16,0},{1,17},{17,1},{2,18},{18,2},{3,19},{19,3},{4,20},{20... | collective-permute-start | bytes 1032200 | tf_op jit(solution)/shard_map/ppermute | solution.py:48
  (35 other events, 319.5 us)

commit v7 on v6

--- a/solution.py
+++ b/solution.py
@@ -8,7 +8,7 @@
 from jax.sharding import PartitionSpec as P
 
 EPSILON = 1e-05
-STAGE_COST = 1_500_000_000
+STAGE_COST = 2_200_000_000
 LAST_PHASE = (
     "wz", "wr", "a0", "t", "b0", "c", "a1", "b1", "e0", "x", "a2", "b2", "e1", "o", "a3", "e2", "b3", "a4",
     "d", "b4", "we", "a5", "wa", "b5", "i", "p",
@@ -19,17 +19,18 @@
 OWN_COUNT, TOTAL_COUNT, HEIGHT_AT, CHAN_AT, EDGE_ROW, NEAR_AT, FAR_AT = range(7)
 VMEM = pl.BlockSpec(memory_space=pltpu.VMEM)
 SMEM = pl.BlockSpec(memory_space=pltpu.SMEM)
+FAR = pl.BlockSpec(memory_space=pl.ANY)
 
 
 def dot(a, b, left, right):
     return lax.dot_general(a, b, (((left,), (right,)), ((), ())), preferred_element_type=F32)
 
 
-def kernel_call(body, name, ins, outs, scratch=(), alias=None, flops=0, room=16):
+def kernel_call(body, name, ins, outs, scratch=(), alias=None, flops=0, room=16, far_outs=0):
     return pl.pallas_call(
         body,
         in_specs=[SMEM if a.dtype == jnp.int32 else VMEM for a in ins],
-        out_specs=[VMEM] * len(outs),
+        out_specs=[FAR] * far_outs + [VMEM] * (len(outs) - far_outs),
         out_shape=[jax.ShapeDtypeStruct(shape, dtype) for shape, dtype in outs],
         scratch_shapes=list(scratch),
         input_output_aliases=alias or {},
@@ -328,7 +329,7 @@
 
 def output_kernel(per_image, count, info_ref, *refs):
     expanded = [[v] for v in refs[:count]]
-    in_ref, go_ref, sums_three_ref, par_ref, out_ref, grad_ref, sums_ref = refs[count:]
+    in_ref, go_ref, sums_three_ref, par_ref, far_ref, grad_ref, sums_ref, out_ref, done_ref = refs[count:]
     average, inv_std = norm_of(sums_three_ref, pixel_count(info_ref, per_image))
     gain, bias = par_ref[0:1, :], par_ref[1:2, :]
     chans = out_ref.shape[2]
@@ -342,10 +343,13 @@
         slope = logistic * (1.0 + summed * (1.0 - logistic))
         grad = go_ref[image].astype(F32) * (slope * keep)
         grad_ref[image] = grad
+        pltpu.make_async_copy(out_ref.at[image], far_ref.at[image], done_ref.at[image]).start()
         return sums[0] + fold(grad), sums[1] + fold(grad * normalized)
 
     zero = jnp.zeros((8, chans), F32)
     put_sums(sums_ref, *each_image(expanded, body, (zero, zero)))
+    for image in range(out_ref.shape[0]):
+        pltpu.make_async_copy(out_ref.at[image], far_ref.at[image], done_ref.at[image]).wait()
 
 
 def output_pass(info, expanded, field, grad_output, sums_three, params, per_image):
@@ -353,6 +357,7 @@
         functools.partial(output_kernel, per_image, len(expanded)), "output",
         [info, *expanded, field, grad_output, sums_three, params],
         [(field.shape, BF16), (field.shape, F32), sums_out(True, field.shape[2])],
+        [pltpu.VMEM(field.shape, BF16), pltpu.SemaphoreType.DMA((field.shape[0],))], far_outs=1,
     )
 
 

time: 268 us -> 265 us (0.989)
  starting transfers between devices: 46.8 us -> 42.8 us
    ppermute x55, starting transfers between devices: 46.8 us -> 42.8 us  [permute(): return lax.ppermute(value, axis, [(i, i ^ distance) for i in range(count)])]
  transfers between devices with their start and end apart: 55 -> 55, of which waited for: 23 -> 21; matrix products, arithmetic and copies ran while one was open for 1% -> 1% of each run, Pallas kernels for 18% -> 19%
where the time goes in v7:
time: 265 us
  waiting for transfers between devices  102 us (38%)
  Pallas kernels  62.4 us (24%)
  blocking collectives  51.3 us (19%)
  starting transfers between devices  42.8 us (16%)
  local copies, waits for them, and re-layouts  4.18 us (2%)
    ppermute x55, waiting for transfers between devices, permute(): return lax.ppermute(value, axis, [(i, i ^ distance) for i in range(count)])  102 us
    pallas_call x45, Pallas kernels, kernel_call(): pl.pallas_call(body, in_specs=[SMEM if a.dtype == jnp.int32 else VMEM for...  62.4 us
    all_to_all x5, blocking collectives, spread_sums(): return lax.all_to_all(sent, REDUCE_AXES, 0, 0)  51.3 us
    ppermute x55, starting transfers between devices, permute(): return lax.ppermute(value, axis, [(i, i ^ distance) for i in range(count)])  42.8 us
  transfers between devices with their start and end apart: 55, of which 21 were waited for; matrix products, arithmetic and copies ran while one was open for 1% of the time, Pallas kernels for 19%

profile of v7, /device:TPU:0, one launch (start us, length us, event | category | flops | bytes accessed | tf_op | source)
XLA Modules:
  0.0 264.8 jit_solution(432329695151417529)
XLA Ops:
  2.0 3.0 %collective-permute-start.1 = (bf16[1024,512]{1,0:T(8,128)(2,1)S(1)}, bf16[1024,512]{1,0:T(8,128)(2,1)S(1)}, u32[]{:S(2)}, u32[]{:S(2)}) collective-permute-start(bf16[1024,512]{1,0:T(8,128)(2,1)S(1)} %bitcast.24), channel_id=1, source_target_pairs={{0,8},{4,12},{8,0},{12,4},{1,9},{5,13},{9,1},{13,5},{2,10},{6,14},... | collective-permute-start | bytes 3145736 | tf_op jit(solution)/shard_map/ppermute | solution.py:49
  10.6 18.4 %collective-permute-done.1.refs_2_.refs_0_ = bf16[1024,512]{1,0:T(8,128)(2,1)S(1)} collective-permute-done((bf16[1024,512]{1,0:T(8,128)(2,1)S(1)}, bf16[1024,512]{1,0:T(8,128)(2,1)S(1)}, u32[]{:S(2)}, u32[]{:S(2)}) %collective-permute-start.1) | collective-permute-done | bytes 1048608 | tf_op jit(solution)/shard_map/ppermute | solution.py:49
  30.7 19.9 %collective-permute-done.4.refs_2_.refs_1_ = bf16[1024,512]{1,0:T(8,128)(2,1)S(1)} collective-permute-done((bf16[1024,512]{1,0:T(8,128)(2,1)S(1)}, bf16[1024,512]{1,0:T(8,128)(2,1)S(1)}, u32[]{:S(2)}, u32[]{:S(2)}) %collective-permute-start.4) | collective-permute-done | bytes 1048608 | tf_op jit(solution)/shard_map/ppermute | solution.py:49
  60.0 12.2 %all_to_all.25.refs_4_.refs_10_.refs_3_ = f32[8,2,256]{2,1,0:T(2,128)S(1)} all-to-all(f32[8,2,256]{2,1,0:T(2,128)S(1)} %get-tuple-element.140), channel_id=1, replica_groups=mesh['height'=2,'chan'=4,'batch'=4] {'height','batch'}, dimensions={0} | all-to-all | bytes 32768 | tf_op jit(solution)/shard_map/all_to_all | solution.py:57
  72.2 3.9 %conv_forward.1 = (bf16[16,128,256]{2,1,0:T(8,128)(2,1)S(1)}, f32[16,128,256]{2,1,0:T(8,128)S(1)}, bf16[16,16,256]{2,1,0:T(8,128)(2,1)S(1)}, f32[8,2,256]{2,1,0:T(2,128)S(1)}) custom-call(s32[7]{0:T(128)S(1)} %stack.31.info_ref, f32[8,128,256]{2,1,0:T(8,128)S(1)} %get-tuple-element.130.refs_0_.refs_4_, ...), custom_call_target="tpu_custom_call" | custom-call | tf_op jit(solution)/shard_map/conv_forward/pallas_call | solution.py:30
  76.1 9.0 %all_to_all.26.sums_ref.refs_2_.refs_8_ = f32[8,2,256]{2,1,0:T(2,128)S(1)} all-to-all(f32[8,2,256]{2,1,0:T(2,128)S(1)} %get-tuple-element.150), channel_id=1, replica_groups=mesh['height'=2,'chan'=4,'batch'=4] {'height','batch'}, dimensions={0} | all-to-all | bytes 32768 | tf_op jit(solution)/shard_map/all_to_all | solution.py:57
  89.0 11.9 %collective-permute-done.14.refs_2_.refs_4_ = bf16[1024,256]{1,0:T(8,128)(2,1)S(1)} collective-permute-done((bf16[1024,256]{1,0:T(8,128)(2,1)S(1)}, bf16[1024,256]{1,0:T(8,128)(2,1)S(1)}, u32[]{:S(2)}, u32[]{:S(2)}) %collective-permute-start.14) | collective-permute-done | bytes 524320 | tf_op jit(solution)/shard_map/ppermute | solution.py:49
  101.4 6.8 %collective-permute-done.17.refs_2_.refs_5_ = bf16[1024,256]{1,0:T(8,128)(2,1)S(1)} collective-permute-done((bf16[1024,256]{1,0:T(8,128)(2,1)S(1)}, bf16[1024,256]{1,0:T(8,128)(2,1)S(1)}, u32[]{:S(2)}, u32[]{:S(2)}) %collective-permute-start.17) | collective-permute-done | bytes 524320 | tf_op jit(solution)/shard_map/ppermute | solution.py:49
  111.9 9.1 %all_to_all.27.refs_4_.refs_3_ = f32[8,2,512]{2,1,0:T(2,128)S(1)} all-to-all(f32[8,2,512]{2,1,0:T(2,128)S(1)} %get-tuple-element.155), channel_id=1, replica_groups=mesh['height'=2,'chan'=4,'batch'=4] {'height','batch'}, dimensions={0} | all-to-all | bytes 65536 | tf_op jit(solution)/shard_map/all_to_all | solution.py:57
  121.0 4.6 %output.1 = (bf16[16,128,512]{2,1,0:T(8,128)(2,1)}, f32[16,128,512]{2,1,0:T(8,128)S(1)}, f32[8,2,512]{2,1,0:T(2,128)S(1)}) custom-call(s32[7]{0:T(128)S(1)} %stack.31.info_ref, f32[8,128,512]{2,1,0:T(8,128)S(1)} %get-tuple-element.152.refs_0_, f32[8,128,512]{2,1,0:T(8,128)S(1)} %get-tuple-element.154.refs_1_, bf16[16,128,512]{2,1,0:T(8,128)(2,1)S(1)} %bitcast.29, ...), custom_call_target="tpu_custom_call" | custom-call | tf_op jit(solution)/shard_map/output/pallas_call | solution.py:30
  125.6 9.1 %all_to_all.28.refs_4_.refs_2_ = f32[8,2,512]{2,1,0:T(2,128)S(1)} all-to-all(f32[8,2,512]{2,1,0:T(2,128)S(1)} %get-tuple-element.159), channel_id=1, replica_groups=mesh['height'=2,'chan'=4,'batch'=4] {'height','batch'}, dimensions={0} | all-to-all | bytes 65536 | tf_op jit(solution)/shard_map/all_to_all | solution.py:57
  140.9 3.0 %expand_grad.1 = (f32[4,128,512]{2,1,0:T(8,128)S(1)}, bf16[4,128,512]{2,1,0:T(8,128)(2,1)S(1)}) custom-call(s32[7]{0:T(128)S(1)} %stack.31.info_ref, bf16[1024,256]{1,0:T(8,128)(2,1)S(1)} %act_two.2.refs_0_, bf16[1024,256]{1,0:T(8,128)(2,1)S(1)} %act_two.3.refs_0_.refs_1_, bf16[1024,256]{1,0:T(8,128)(2,1)S(1)} %collective-permute-done.13.refs_1_.refs_2_, ...), custom_call_target="tpu_custom_call" | custom-call | tf_op jit(solution)/shard_map/expand_grad/pallas_call | solution.py:30
  146.7 8.3 %collective-permute-done.20.refs_0_ = bf16[1024,256]{1,0:T(8,128)(2,1)S(1)} collective-permute-done((bf16[1024,256]{1,0:T(8,128)(2,1)S(1)}, bf16[1024,256]{1,0:T(8,128)(2,1)S(1)}, u32[]{:S(2)}, u32[]{:S(2)}) %collective-permute-start.20) | collective-permute-done | bytes 524320 | tf_op jit(solution)/shard_map/ppermute | solution.py:49
  160.9 4.4 %collective-permute-done.23.refs_0_ = bf16[1024,256]{1,0:T(8,128)(2,1)S(1)} collective-permute-done((bf16[1024,256]{1,0:T(8,128)(2,1)S(1)}, bf16[1024,256]{1,0:T(8,128)(2,1)S(1)}, u32[]{:S(2)}, u32[]{:S(2)}) %collective-permute-start.23) | collective-permute-done | bytes 524320 | tf_op jit(solution)/shard_map/ppermute | solution.py:49
  168.9 2.2 collective-permute-done.27.refs_3_
  172.3 3.3 %collective-permute-start.31 = (f32[2,256]{1,0:T(2,128)S(1)}, f32[2,256]{1,0:T(2,128)S(1)}, u32[]{:S(2)}, u32[]{:S(2)}) collective-permute-start(f32[2,256]{1,0:T(2,128)S(1)} %add_rows.1.refs_0_), channel_id=1, source_target_pairs={{0,3},{1,2},{2,1},{3,0},{4,7},{5,6},{6,5},{7,4},{8,11},{9,10},{10,... | collective-permute-start | bytes 6152 | tf_op jit(solution)/shard_map/ppermute | solution.py:49
  179.7 4.7 %conv_backward.1 = (f32[16,128,256]{2,1,0:T(8,128)S(1)}, f32[8,2,256]{2,1,0:T(2,128)S(1)}, bf16[16,160,768]{2,1,0:T(8,128)(2,1)S(1)}) custom-call(s32[7]{0:T(128)S(1)} %stack.31.info_ref, f32[8,128,256]{2,1,0:T(8,128)S(1)} %get-tuple-element.164.refs_0_, f32[8,128,256]{2,1,0:T(8,128)S(1)} %get-tuple-element.188.refs_1_, ...), custom_call_target="tpu_custom_call" | custom-call | tf_op jit(solution)/shard_map/conv_backward/pallas_call | solution.py:30
  184.4 12.0 %all_to_all.29.refs_4_.refs_0_ = f32[8,2,256]{2,1,0:T(2,128)S(1)} all-to-all(f32[8,2,256]{2,1,0:T(2,128)S(1)} %get-tuple-element.191), channel_id=1, replica_groups=mesh['height'=2,'chan'=4,'batch'=4] {'height','batch'}, dimensions={0} | all-to-all | bytes 32768 | tf_op jit(solution)/shard_map/all_to_all | solution.py:57
  200.0 3.2 %tap_grads.1.refs_5_ = f32[9,32,256]{2,1,0:T(8,128)S(1)} custom-call(s32[7]{0:T(128)S(1)} %stack.31.info_ref, bf16[16,128,256]{2,1,0:T(8,128)(2,1)S(1)} %get-tuple-element.200.act_ref, bf16[16,160,768]{2,1,0:T(8,128)(2,1)S(1)} %get-tuple-element.201.window_ref), custom_call_target="tpu_custom_call" | custom-call | tf_op jit(solution)/shard_map/tap_grads/pallas_call | solution.py:30
  203.3 1.9 reduce_grad.3
  210.4 2.1 collective-permute-done.35.arrived_ref
  216.7 2.5 collective-permute-start.42
  219.1 3.7 %collective-permute-done.40.arrived_ref = bf16[2,168,256]{2,1,0:T(8,128)(2,1)S(1)} collective-permute-done((bf16[2,168,256]{2,1,0:T(8,128)(2,1)S(1)}, bf16[2,168,256]{2,1,0:T(8,128)(2,1)S(1)}, u32[]{:S(2)}, u32[]{:S(2)}) %collective-permute-start.40) | collective-permute-done | bytes 172064 | tf_op jit(solution)/shard_map/ppermute | solution.py:49
  226.6 2.4 collective-permute-start.45
  229.6 4.3 %collective-permute-done.43.refs_1_ = bf16[2,128,512]{2,1,0:T(8,128)(2,1)S(1)} collective-permute-done((bf16[2,128,512]{2,1,0:T(8,128)(2,1)S(1)}, bf16[2,128,512]{2,1,0:T(8,128)(2,1)S(1)}, u32[]{:S(2)}, u32[]{:S(2)}) %collective-permute-start.43) | collective-permute-done | bytes 262176 | tf_op jit(solution)/shard_map/ppermute | solution.py:49
  236.3 2.5 collective-permute-start.48
  238.8 2.3 collective-permute-done.46.refs_1_
  241.7 4.3 %collective-permute-done.47.arrived_ref = bf16[4,128,512]{2,1,0:T(8,128)(2,1)S(1)} collective-permute-done((bf16[4,128,512]{2,1,0:T(8,128)(2,1)S(1)}, bf16[4,128,512]{2,1,0:T(8,128)(2,1)S(1)}, u32[]{:S(2)}, u32[]{:S(2)}) %collective-permute-start.47) | collective-permute-done | bytes 524320 | tf_op jit(solution)/shard_map/ppermute | solution.py:49
  247.4 7.2 %collective-permute-done.49.refs_1_ = bf16[4,128,256]{2,1,0:T(8,128)(2,1)S(1)} collective-permute-done((bf16[4,128,256]{2,1,0:T(8,128)(2,1)S(1)}, bf16[4,128,256]{2,1,0:T(8,128)(2,1)S(1)}, u32[]{:S(2)}, u32[]{:S(2)}) %collective-permute-start.49) | collective-permute-done | bytes 262176 | tf_op jit(solution)/shard_map/ppermute | solution.py:49
  255.9 4.8 %input_grad.1 = bf16[2048,512]{1,0:T(8,128)(2,1)} custom-call(s32[7]{0:T(128)S(1)} %stack.31.info_ref, f32[2048,512]{1,0:T(8,128)S(1)} %bitcast.23, bf16[2048,256]{1,0:T(8,128)(2,1)S(1)} %grad_reduced.1.refs_4_.refs_0_, bf16[2048,256]{1,0:T(8,128)(2,1)S(1)} %collective-permute-done.51.refs_1_, bf16[2048,256]{1,0:T(8,128)(2,1)S(1)} %collective-permute-done.52.refs_2_, ...), custom_call_target="tpu_custom_call" | custom-call | tf_op jit(solution)/shard_map/input_grad/pallas_call | solution.py:30
  260.7 2.0 place_expand.1
  262.7 2.1 place_reduce.1
  (162 shorter events, 72.4 us)
Async XLA Ops:
  2.0 27.0 %collective-permute-start.1 = (bf16[1024,512]{1,0:T(8,128)(2,1)S(1)}, bf16[1024,512]{1,0:T(8,128)(2,1)S(1)}, u32[]{:S(2)}, u32[]{:S(2)}) collective-permute-start(bf16[1024,512]{1,0:T(8,128)(2,1)S(1)} %bitcast.24), channel_id=1, source_target_pairs={{0,8},{4,12},{8,0},{12,4},{1,9},{5,13},{9,1},{13,5},{2,10},{6,14},... | collective-permute-start | bytes 3145736 | tf_op jit(solution)/shard_map/ppermute | solution.py:49
  8.5 42.2 %collective-permute-start.4 = (bf16[1024,512]{1,0:T(8,128)(2,1)S(1)}, bf16[1024,512]{1,0:T(8,128)(2,1)S(1)}, u32[]{:S(2)}, u32[]{:S(2)}) collective-permute-start(bf16[1024,512]{1,0:T(8,128)(2,1)S(1)} %slice.11.refs_0_.refs_1_), channel_id=1, source_target_pairs={{0,8},{4,12},{8,0},{12,4},{1,9},{5,13},{9,1},{13,5},{2,10},{6,14},... | collective-permute-start | bytes 3145736 | tf_op jit(solution)/shard_map/ppermute | solution.py:49
  9.2 20.9 %collective-permute-start.5 = (bf16[256,512]{1,0:T(8,128)(2,1)S(1)}, bf16[256,512]{1,0:T(8,128)(2,1)S(1)}, u32[]{:S(2)}, u32[]{:S(2)}) collective-permute-start(bf16[256,512]{1,0:T(8,128)(2,1)S(1)} %get-tuple-element.133), channel_id=1, source_target_pairs={{0,4},{4,0},{8,12},{12,8},{1,5},{5,1},{9,13},{13,9},{2,6},{6,2},{1... | collective-permute-start | bytes 786440 | tf_op jit(solution)/shard_map/ppermute | solution.py:49
  9.9 20.8 %collective-permute-start.6 = (bf16[512,256]{1,0:T(8,128)(2,1)S(1)}, bf16[512,256]{1,0:T(8,128)(2,1)S(1)}, u32[]{:S(2)}, u32[]{:S(2)}) collective-permute-start(bf16[512,256]{1,0:T(8,128)(2,1)S(1)} %get-tuple-element.134), channel_id=1, source_target_pairs={{0,4},{4,0},{8,12},{12,8},{1,5},{5,1},{9,13},{13,9},{2,6},{6,2},{1... | collective-permute-start | bytes 786440 | tf_op jit(solution)/shard_map/ppermute | solution.py:49
  10.5 41.9 %collective-permute-start = (bf16[1024,512]{1,0:T(8,128)(2,1)S(1)}, bf16[1024,512]{1,0:T(8,128)(2,1)S(1)}, u32[]{:S(2)}, u32[]{:S(2)}) collective-permute-start(bf16[1024,512]{1,0:T(8,128)(2,1)S(1)} %bitcast.25), channel_id=1, source_target_pairs={{0,4},{4,0},{8,12},{12,8},{1,5},{5,1},{9,13},{13,9},{2,6},{6,2},{1... | collective-permute-start | bytes 3145736 | tf_op jit(solution)/shard_map/ppermute | solution.py:49
  29.0 23.5 %collective-permute-start.2 = (bf16[1024,512]{1,0:T(8,128)(2,1)S(1)}, bf16[1024,512]{1,0:T(8,128)(2,1)S(1)}, u32[]{:S(2)}, u32[]{:S(2)}) collective-permute-start(bf16[1024,512]{1,0:T(8,128)(2,1)S(1)} %collective-permute-done.1.refs_2_.refs_0_), channel_id=1, source_target_pairs={{0,4},{4,0},{8,12},{12,8},{1,5},{5,1},{9,13},{13,9},{2,6},{6,2},{1... | collective-permute-start | bytes 3145736 | tf_op jit(solution)/shard_map/ppermute | solution.py:49
  30.1 25.9 %collective-permute-start.3 = (bf16[1024,512]{1,0:T(8,128)(2,1)S(1)}, bf16[1024,512]{1,0:T(8,128)(2,1)S(1)}, u32[]{:S(2)}, u32[]{:S(2)}) collective-permute-start(bf16[1024,512]{1,0:T(8,128)(2,1)S(1)} %slice.11.refs_0_.refs_1_), channel_id=1, source_target_pairs={{0,4},{4,0},{8,12},{12,8},{1,5},{5,1},{9,13},{13,9},{2,6},{6,2},{1... | collective-permute-start | bytes 3145736 | tf_op jit(solution)/shard_map/ppermute | solution.py:49
  50.6 25.4 %collective-permute-start.10 = (bf16[256,512]{1,0:T(8,128)(2,1)S(1)}, bf16[256,512]{1,0:T(8,128)(2,1)S(1)}, u32[]{:S(2)}, u32[]{:S(2)}) collective-permute-start(bf16[256,512]{1,0:T(8,128)(2,1)S(1)} %get-tuple-element.145), channel_id=1, source_target_pairs={{0,8},{4,12},{8,0},{12,4},{1,9},{5,13},{9,1},{13,5},{2,10},{6,14},... | collective-permute-start | bytes 786440 | tf_op jit(solution)/shard_map/ppermute | solution.py:49
  52.4 23.7 %collective-permute-start.11 = (bf16[256,512]{1,0:T(8,128)(2,1)S(1)}, bf16[256,512]{1,0:T(8,128)(2,1)S(1)}, u32[]{:S(2)}, u32[]{:S(2)}) collective-permute-start(bf16[256,512]{1,0:T(8,128)(2,1)S(1)} %get-tuple-element.147), channel_id=1, source_target_pairs={{0,12},{4,8},{8,4},{12,0},{1,13},{5,9},{9,5},{13,1},{2,14},{6,10},... | collective-permute-start | bytes 786440 | tf_op jit(solution)/shard_map/ppermute | solution.py:49
  52.5 23.6 %collective-permute-start.12 = (bf16[512,256]{1,0:T(8,128)(2,1)S(1)}, bf16[512,256]{1,0:T(8,128)(2,1)S(1)}, u32[]{:S(2)}, u32[]{:S(2)}) collective-permute-start(bf16[512,256]{1,0:T(8,128)(2,1)S(1)} %get-tuple-element.149), channel_id=1, source_target_pairs={{0,12},{4,8},{8,4},{12,0},{1,13},{5,9},{9,5},{13,1},{2,14},{6,10},... | collective-permute-start | bytes 786440 | tf_op jit(solution)/shard_map/ppermute | solution.py:49
  57.9 14.3 %collective-permute-start.9 = (bf16[8,16,256]{2,1,0:T(8,128)(2,1)S(1)}, bf16[8,16,256]{2,1,0:T(8,128)(2,1)S(1)}, u32[]{:S(2)}, u32[]{:S(2)}) collective-permute-start(bf16[8,16,256]{2,1,0:T(8,128)(2,1)S(1)} %get-tuple-element.139), channel_id=1, source_target_pairs={{0,16},{16,0},{1,17},{17,1},{2,18},{18,2},{3,19},{19,3},{4,20},{20... | collective-permute-start | bytes 196616 | tf_op jit(solution)/shard_map/ppermute | solution.py:49
  59.4 12.7 %collective-permute-start.8 = (bf16[8,16,256]{2,1,0:T(8,128)(2,1)S(1)}, bf16[8,16,256]{2,1,0:T(8,128)(2,1)S(1)}, u32[]{:S(2)}, u32[]{:S(2)}) collective-permute-start(bf16[8,16,256]{2,1,0:T(8,128)(2,1)S(1)} %get-tuple-element.138), channel_id=1, source_target_pairs={{0,16},{16,0},{1,17},{17,1},{2,18},{18,2},{3,19},{19,3},{4,20},{20... | collective-permute-start | bytes 196616 | tf_op jit(solution)/shard_map/ppermute | solution.py:49
  86.0 14.9 %collective-permute-start.14 = (bf16[1024,256]{1,0:T(8,128)(2,1)S(1)}, bf16[1024,256]{1,0:T(8,128)(2,1)S(1)}, u32[]{:S(2)}, u32[]{:S(2)}) collective-permute-start(bf16[1024,256]{1,0:T(8,128)(2,1)S(1)} %act_two.2.refs_0_), channel_id=1, source_target_pairs={{0,8},{4,12},{8,0},{12,4},{1,9},{5,13},{9,1},{13,5},{2,10},{6,14},... | collective-permute-start | bytes 1572872 | tf_op jit(solution)/shard_map/ppermute | solution.py:49
  87.5 20.7 %collective-permute-start.17 = (bf16[1024,256]{1,0:T(8,128)(2,1)S(1)}, bf16[1024,256]{1,0:T(8,128)(2,1)S(1)}, u32[]{:S(2)}, u32[]{:S(2)}) collective-permute-start(bf16[1024,256]{1,0:T(8,128)(2,1)S(1)} %act_two.3.refs_0_.refs_1_), channel_id=1, source_target_pairs={{0,8},{4,12},{8,0},{12,4},{1,9},{5,13},{9,1},{13,5},{2,10},{6,14},... | collective-permute-start | bytes 1572872 | tf_op jit(solution)/shard_map/ppermute | solution.py:49
  89.0 19.2 %collective-permute-start.13 = (bf16[1024,256]{1,0:T(8,128)(2,1)S(1)}, bf16[1024,256]{1,0:T(8,128)(2,1)S(1)}, u32[]{:S(2)}, u32[]{:S(2)}) collective-permute-start(bf16[1024,256]{1,0:T(8,128)(2,1)S(1)} %act_two.2.refs_0_), channel_id=1, source_target_pairs={{0,4},{4,0},{8,12},{12,8},{1,5},{5,1},{9,13},{13,9},{2,6},{6,2},{1... | collective-permute-start | bytes 1572872 | tf_op jit(solution)/shard_map/ppermute | solution.py:49
  100.9 9.1 %collective-permute-start.16 = (bf16[1024,256]{1,0:T(8,128)(2,1)S(1)}, bf16[1024,256]{1,0:T(8,128)(2,1)S(1)}, u32[]{:S(2)}, u32[]{:S(2)}) collective-permute-start(bf16[1024,256]{1,0:T(8,128)(2,1)S(1)} %act_two.3.refs_0_.refs_1_), channel_id=1, source_target_pairs={{0,4},{4,0},{8,12},{12,8},{1,5},{5,1},{9,13},{13,9},{2,6},{6,2},{1... | collective-permute-start | bytes 1572872 | tf_op jit(solution)/shard_map/ppermute | solution.py:49
  140.1 14.8 %collective-permute-start.20 = (bf16[1024,256]{1,0:T(8,128)(2,1)S(1)}, bf16[1024,256]{1,0:T(8,128)(2,1)S(1)}, u32[]{:S(2)}, u32[]{:S(2)}) collective-permute-start(bf16[1024,256]{1,0:T(8,128)(2,1)S(1)} %get-tuple-element.163), channel_id=1, source_target_pairs={{0,8},{4,12},{8,0},{12,4},{1,9},{5,13},{9,1},{13,5},{2,10},{6,14},... | collective-permute-start | bytes 1572872 | tf_op jit(solution)/shard_map/ppermute | solution.py:49
  144.0 13.7 %collective-permute-start.21 = (bf16[4,128,512]{2,1,0:T(8,128)(2,1)S(1)}, bf16[4,128,512]{2,1,0:T(8,128)(2,1)S(1)}, u32[]{:S(2)}, u32[]{:S(2)}) collective-permute-start(bf16[4,128,512]{2,1,0:T(8,128)(2,1)S(1)} %get-tuple-element.169), channel_id=1, source_target_pairs={{0,16},{16,0},{1,17},{17,1},{2,18},{18,2},{3,19},{19,3},{4,20},{20... | collective-permute-start | bytes 1572872 | tf_op jit(solution)/shard_map/ppermute | solution.py:49
  145.4 20.0 %collective-permute-start.23 = (bf16[1024,256]{1,0:T(8,128)(2,1)S(1)}, bf16[1024,256]{1,0:T(8,128)(2,1)S(1)}, u32[]{:S(2)}, u32[]{:S(2)}) collective-permute-start(bf16[1024,256]{1,0:T(8,128)(2,1)S(1)} %get-tuple-element.175), channel_id=1, source_target_pairs={{0,8},{4,12},{8,0},{12,4},{1,9},{5,13},{9,1},{13,5},{2,10},{6,14},... | collective-permute-start | bytes 1572872 | tf_op jit(solution)/shard_map/ppermute | solution.py:49
  158.4 8.9 %collective-permute-start.24 = (bf16[2,128,512]{2,1,0:T(8,128)(2,1)S(1)}, bf16[2,128,512]{2,1,0:T(8,128)(2,1)S(1)}, u32[]{:S(2)}, u32[]{:S(2)}) collective-permute-start(bf16[2,128,512]{2,1,0:T(8,128)(2,1)S(1)} %get-tuple-element.178), channel_id=1, source_target_pairs={{0,1},{1,0},{2,3},{3,2},{4,5},{5,4},{6,7},{7,6},{8,9},{9,8},{10,11... | collective-permute-start | bytes 786440 | tf_op jit(solution)/shard_map/ppermute | solution.py:49
  158.9 8.4 %collective-permute-start.25 = (bf16[16,16,256]{2,1,0:T(8,128)(2,1)S(1)}, bf16[16,16,256]{2,1,0:T(8,128)(2,1)S(1)}, u32[]{:S(2)}, u32[]{:S(2)}) collective-permute-start(bf16[16,16,256]{2,1,0:T(8,128)(2,1)S(1)} %get-tuple-element.180), channel_id=1, source_target_pairs={{0,16},{16,0},{1,17},{17,1},{2,18},{18,2},{3,19},{19,3},{4,20},{20... | collective-permute-start | bytes 393224 | tf_op jit(solution)/shard_map/ppermute | solution.py:49
  177.7 19.8 %collective-permute-start.33 = (bf16[512,256]{1,0:T(8,128)(2,1)S(1)}, bf16[512,256]{1,0:T(8,128)(2,1)S(1)}, u32[]{:S(2)}, u32[]{:S(2)}) collective-permute-start(bf16[512,256]{1,0:T(8,128)(2,1)S(1)} %get-tuple-element.196), channel_id=1, source_target_pairs={{0,8},{4,12},{8,0},{12,4},{1,9},{5,13},{9,1},{13,5},{2,10},{6,14},... | collective-permute-start | bytes 786440 | tf_op jit(solution)/shard_map/ppermute | solution.py:49
  179.2 18.3 %collective-permute-start.32 = (bf16[1,128,512]{2,1,0:T(8,128)(2,1)S(1)}, bf16[1,128,512]{2,1,0:T(8,128)(2,1)S(1)}, u32[]{:S(2)}, u32[]{:S(2)}) collective-permute-start(bf16[1,128,512]{2,1,0:T(8,128)(2,1)S(1)} %get-tuple-element.193), channel_id=1, source_target_pairs={{0,2},{1,3},{2,0},{3,1},{4,6},{5,7},{6,4},{7,5},{8,10},{9,11},{10,... | collective-permute-start | bytes 393224 | tf_op jit(solution)/shard_map/ppermute | solution.py:49
  199.4 9.9 %collective-permute-start.34 = (bf16[4,128,256]{2,1,0:T(8,128)(2,1)S(1)}, bf16[4,128,256]{2,1,0:T(8,128)(2,1)S(1)}, u32[]{:S(2)}, u32[]{:S(2)}) collective-permute-start(bf16[4,128,256]{2,1,0:T(8,128)(2,1)S(1)} %get-tuple-element.207), channel_id=1, source_target_pairs={{0,16},{16,0},{1,17},{17,1},{2,18},{18,2},{3,19},{19,3},{4,20},{20... | collective-permute-start | bytes 786440 | tf_op jit(solution)/shard_map/ppermute | solution.py:49
  213.7 25.1 %collective-permute-start.52 = (bf16[2048,256]{1,0:T(8,128)(2,1)S(1)}, bf16[2048,256]{1,0:T(8,128)(2,1)S(1)}, u32[]{:S(2)}, u32[]{:S(2)}) collective-permute-start(bf16[2048,256]{1,0:T(8,128)(2,1)S(1)} %grad_reduced.1.refs_4_.refs_0_), channel_id=1, source_target_pairs={{0,8},{4,12},{8,0},{12,4},{1,9},{5,13},{9,1},{13,5},{2,10},{6,14},... | collective-permute-start | bytes 3145736 | tf_op jit(solution)/shard_map/ppermute | solution.py:49
  215.6 9.7 %collective-permute-start.41 = (bf16[1,128,512]{2,1,0:T(8,128)(2,1)S(1)}, bf16[1,128,512]{2,1,0:T(8,128)(2,1)S(1)}, u32[]{:S(2)}, u32[]{:S(2)}) collective-permute-start(bf16[1,128,512]{2,1,0:T(8,128)(2,1)S(1)} %bitcast.32), channel_id=1, source_target_pairs={{0,2},{1,3},{2,0},{3,1},{4,6},{5,7},{6,4},{7,5},{8,10},{9,11},{10,... | collective-permute-start | bytes 393224 | tf_op jit(solution)/shard_map/ppermute | solution.py:49
  216.7 9.4 %collective-permute-start.42 = (bf16[1,128,256]{2,1,0:T(8,128)(2,1)S(1)}, bf16[1,128,256]{2,1,0:T(8,128)(2,1)S(1)}, u32[]{:S(2)}, u32[]{:S(2)}) collective-permute-start(bf16[1,128,256]{2,1,0:T(8,128)(2,1)S(1)} %get-tuple-element.224), channel_id=1, source_target_pairs={{0,2},{1,3},{2,0},{3,1},{4,6},{5,7},{6,4},{7,5},{8,10},{9,11},{10,... | collective-permute-start | bytes 196616 | tf_op jit(solution)/shard_map/ppermute | solution.py:49
  226.6 9.2 %collective-permute-start.45 = (bf16[1,128,256]{2,1,0:T(8,128)(2,1)S(1)}, bf16[1,128,256]{2,1,0:T(8,128)(2,1)S(1)}, u32[]{:S(2)}, u32[]{:S(2)}) collective-permute-start(bf16[1,128,256]{2,1,0:T(8,128)(2,1)S(1)} %add_last.2.refs_0_), channel_id=1, source_target_pairs={{0,2},{1,3},{2,0},{3,1},{4,6},{5,7},{6,4},{7,5},{8,10},{9,11},{10,... | collective-permute-start | bytes 196616 | tf_op jit(solution)/shard_map/ppermute | solution.py:49
  229.6 26.3 %collective-permute-start.51 = (bf16[2048,256]{1,0:T(8,128)(2,1)S(1)}, bf16[2048,256]{1,0:T(8,128)(2,1)S(1)}, u32[]{:S(2)}, u32[]{:S(2)}) collective-permute-start(bf16[2048,256]{1,0:T(8,128)(2,1)S(1)} %grad_reduced.1.refs_4_.refs_0_), channel_id=1, source_target_pairs={{0,4},{4,0},{8,12},{12,8},{1,5},{5,1},{9,13},{13,9},{2,6},{6,2},{1... | collective-permute-start | bytes 3145736 | tf_op jit(solution)/shard_map/ppermute | solution.py:49
  234.5 11.5 %collective-permute-start.47 = (bf16[4,128,512]{2,1,0:T(8,128)(2,1)S(1)}, bf16[4,128,512]{2,1,0:T(8,128)(2,1)S(1)}, u32[]{:S(2)}, u32[]{:S(2)}) collective-permute-start(bf16[4,128,512]{2,1,0:T(8,128)(2,1)S(1)} %join.9.own_ref), channel_id=1, source_target_pairs={{0,16},{16,0},{1,17},{17,1},{2,18},{18,2},{3,19},{19,3},{4,20},{20... | collective-permute-start | bytes 1572872 | tf_op jit(solution)/shard_map/ppermute | solution.py:49
  236.3 9.7 %collective-permute-start.48 = (bf16[2,128,256]{2,1,0:T(8,128)(2,1)S(1)}, bf16[2,128,256]{2,1,0:T(8,128)(2,1)S(1)}, u32[]{:S(2)}, u32[]{:S(2)}) collective-permute-start(bf16[2,128,256]{2,1,0:T(8,128)(2,1)S(1)} %join.10.refs_0_), channel_id=1, source_target_pairs={{0,1},{1,0},{2,3},{3,2},{4,5},{5,4},{6,7},{7,6},{8,9},{9,8},{10,11... | collective-permute-start | bytes 393224 | tf_op jit(solution)/shard_map/ppermute | solution.py:49
  238.8 17.1 %collective-permute-start.53 = (bf16[2048,256]{1,0:T(8,128)(2,1)S(1)}, bf16[2048,256]{1,0:T(8,128)(2,1)S(1)}, u32[]{:S(2)}, u32[]{:S(2)}) collective-permute-start(bf16[2048,256]{1,0:T(8,128)(2,1)S(1)} %collective-permute-done.52.refs_2_), channel_id=1, source_target_pairs={{0,4},{4,0},{8,12},{12,8},{1,5},{5,1},{9,13},{13,9},{2,6},{6,2},{1... | collective-permute-start | bytes 3145736 | tf_op jit(solution)/shard_map/ppermute | solution.py:49
  (35 other events, 325.4 us)

commit v8 on v7

--- a/solution.py
+++ b/solution.py
@@ -8,7 +8,7 @@
 from jax.sharding import PartitionSpec as P
 
 EPSILON = 1e-05
-STAGE_COST = 2_200_000_000
+SPLIT_COST, ADD_COST, STAGE_COST = 1_800_000_000, 3_000_000_000, 2_200_000_000
 LAST_PHASE = (
     "wz", "wr", "a0", "t", "b0", "c", "a1", "b1", "e0", "x", "a2", "b2", "e1", "o", "a3", "e2", "b3", "a4",
     "d", "b4", "we", "a5", "wa", "b5", "i", "p",
@@ -674,7 +674,7 @@
 def split_next(info, pair, step):
     half = (pair[0].shape[0] // 2,) + pair[0].shape[1:]
     return kernel_call(
-        functools.partial(split_next_kernel, step[2]), "split_next", [info, *pair], [(half, F32), (half, BF16)], flops=STAGE_COST
+        functools.partial(split_next_kernel, step[2]), "split_next", [info, *pair], [(half, F32), (half, BF16)], flops=SPLIT_COST
     )
 
 
@@ -683,7 +683,7 @@
 
 
 def add_last(info, pair):
-    return kernel_call(add_kernel, "add_last", [info, *pair], [(pair[0].shape, BF16)], flops=STAGE_COST)[0]
+    return kernel_call(add_kernel, "add_last", [info, *pair], [(pair[0].shape, BF16)], flops=ADD_COST)[0]
 
 
 def join_kernel(info_ref, *refs):

time: 265 us -> 264 us (level)
  waiting for transfers between devices: 102 us -> 98.3 us
  starting transfers between devices: 42.8 us -> 45.5 us
    ppermute x55, waiting for transfers between devices: 102 us -> 98.3 us  [permute(): return lax.ppermute(value, axis, [(i, i ^ distance) for i in range(count)])]
    ppermute x55, starting transfers between devices: 42.8 us -> 45.5 us  [permute(): return lax.ppermute(value, axis, [(i, i ^ distance) for i in range(count)])]
where the time goes in v8:
time: 264 us
  waiting for transfers between devices  98.3 us (37%)
  Pallas kernels  62.4 us (24%)
  blocking collectives  51.3 us (19%)
  starting transfers between devices  45.5 us (17%)
  local copies, waits for them, and re-layouts  4.18 us (2%)
    ppermute x55, waiting for transfers between devices, permute(): return lax.ppermute(value, axis, [(i, i ^ distance) for i in range(count)])  98.3 us
    pallas_call x45, Pallas kernels, kernel_call(): pl.pallas_call(body, in_specs=[SMEM if a.dtype == jnp.int32 else VMEM for...  62.4 us
    all_to_all x5, blocking collectives, spread_sums(): return lax.all_to_all(sent, REDUCE_AXES, 0, 0)  51.3 us
    ppermute x55, starting transfers between devices, permute(): return lax.ppermute(value, axis, [(i, i ^ distance) for i in range(count)])  45.5 us
  transfers between devices with their start and end apart: 55, of which 21 were waited for; matrix products, arithmetic and copies ran while one was open for 1% of the time, Pallas kernels for 19%

profile of v8, /device:TPU:0, one launch (start us, length us, event | category | flops | bytes accessed | tf_op | source)
XLA Modules:
  0.0 263.6 jit_solution(6604559315565213292)
XLA Ops:
  2.0 3.0 %collective-permute-start.1 = (bf16[1024,512]{1,0:T(8,128)(2,1)S(1)}, bf16[1024,512]{1,0:T(8,128)(2,1)S(1)}, u32[]{:S(2)}, u32[]{:S(2)}) collective-permute-start(bf16[1024,512]{1,0:T(8,128)(2,1)S(1)} %bitcast.24), channel_id=1, source_target_pairs={{0,8},{4,12},{8,0},{12,4},{1,9},{5,13},{9,1},{13,5},{2,10},{6,14},... | collective-permute-start | bytes 3145736 | tf_op jit(solution)/shard_map/ppermute | solution.py:49
  10.6 18.4 %collective-permute-done.1.refs_2_.refs_0_ = bf16[1024,512]{1,0:T(8,128)(2,1)S(1)} collective-permute-done((bf16[1024,512]{1,0:T(8,128)(2,1)S(1)}, bf16[1024,512]{1,0:T(8,128)(2,1)S(1)}, u32[]{:S(2)}, u32[]{:S(2)}) %collective-permute-start.1) | collective-permute-done | bytes 1048608 | tf_op jit(solution)/shard_map/ppermute | solution.py:49
  30.7 19.9 %collective-permute-done.4.refs_2_.refs_1_ = bf16[1024,512]{1,0:T(8,128)(2,1)S(1)} collective-permute-done((bf16[1024,512]{1,0:T(8,128)(2,1)S(1)}, bf16[1024,512]{1,0:T(8,128)(2,1)S(1)}, u32[]{:S(2)}, u32[]{:S(2)}) %collective-permute-start.4) | collective-permute-done | bytes 1048608 | tf_op jit(solution)/shard_map/ppermute | solution.py:49
  60.0 12.2 %all_to_all.25.refs_4_.refs_10_.refs_3_ = f32[8,2,256]{2,1,0:T(2,128)S(1)} all-to-all(f32[8,2,256]{2,1,0:T(2,128)S(1)} %get-tuple-element.140), channel_id=1, replica_groups=mesh['height'=2,'chan'=4,'batch'=4] {'height','batch'}, dimensions={0} | all-to-all | bytes 32768 | tf_op jit(solution)/shard_map/all_to_all | solution.py:57
  72.2 3.9 %conv_forward.1 = (bf16[16,128,256]{2,1,0:T(8,128)(2,1)S(1)}, f32[16,128,256]{2,1,0:T(8,128)S(1)}, bf16[16,16,256]{2,1,0:T(8,128)(2,1)S(1)}, f32[8,2,256]{2,1,0:T(2,128)S(1)}) custom-call(s32[7]{0:T(128)S(1)} %stack.31.info_ref, f32[8,128,256]{2,1,0:T(8,128)S(1)} %get-tuple-element.130.refs_0_.refs_4_, ...), custom_call_target="tpu_custom_call" | custom-call | tf_op jit(solution)/shard_map/conv_forward/pallas_call | solution.py:30
  76.1 9.0 %all_to_all.26.sums_ref.refs_2_.refs_8_ = f32[8,2,256]{2,1,0:T(2,128)S(1)} all-to-all(f32[8,2,256]{2,1,0:T(2,128)S(1)} %get-tuple-element.150), channel_id=1, replica_groups=mesh['height'=2,'chan'=4,'batch'=4] {'height','batch'}, dimensions={0} | all-to-all | bytes 32768 | tf_op jit(solution)/shard_map/all_to_all | solution.py:57
  89.0 11.9 %collective-permute-done.14.refs_2_.refs_4_ = bf16[1024,256]{1,0:T(8,128)(2,1)S(1)} collective-permute-done((bf16[1024,256]{1,0:T(8,128)(2,1)S(1)}, bf16[1024,256]{1,0:T(8,128)(2,1)S(1)}, u32[]{:S(2)}, u32[]{:S(2)}) %collective-permute-start.14) | collective-permute-done | bytes 524320 | tf_op jit(solution)/shard_map/ppermute | solution.py:49
  101.4 6.8 %collective-permute-done.17.refs_2_.refs_5_ = bf16[1024,256]{1,0:T(8,128)(2,1)S(1)} collective-permute-done((bf16[1024,256]{1,0:T(8,128)(2,1)S(1)}, bf16[1024,256]{1,0:T(8,128)(2,1)S(1)}, u32[]{:S(2)}, u32[]{:S(2)}) %collective-permute-start.17) | collective-permute-done | bytes 524320 | tf_op jit(solution)/shard_map/ppermute | solution.py:49
  111.9 9.1 %all_to_all.27.refs_4_.refs_3_ = f32[8,2,512]{2,1,0:T(2,128)S(1)} all-to-all(f32[8,2,512]{2,1,0:T(2,128)S(1)} %get-tuple-element.155), channel_id=1, replica_groups=mesh['height'=2,'chan'=4,'batch'=4] {'height','batch'}, dimensions={0} | all-to-all | bytes 65536 | tf_op jit(solution)/shard_map/all_to_all | solution.py:57
  121.0 4.6 %output.1 = (bf16[16,128,512]{2,1,0:T(8,128)(2,1)}, f32[16,128,512]{2,1,0:T(8,128)S(1)}, f32[8,2,512]{2,1,0:T(2,128)S(1)}) custom-call(s32[7]{0:T(128)S(1)} %stack.31.info_ref, f32[8,128,512]{2,1,0:T(8,128)S(1)} %get-tuple-element.152.refs_0_, f32[8,128,512]{2,1,0:T(8,128)S(1)} %get-tuple-element.154.refs_1_, bf16[16,128,512]{2,1,0:T(8,128)(2,1)S(1)} %bitcast.29, ...), custom_call_target="tpu_custom_call" | custom-call | tf_op jit(solution)/shard_map/output/pallas_call | solution.py:30
  125.6 9.1 %all_to_all.28.refs_4_.refs_2_ = f32[8,2,512]{2,1,0:T(2,128)S(1)} all-to-all(f32[8,2,512]{2,1,0:T(2,128)S(1)} %get-tuple-element.159), channel_id=1, replica_groups=mesh['height'=2,'chan'=4,'batch'=4] {'height','batch'}, dimensions={0} | all-to-all | bytes 65536 | tf_op jit(solution)/shard_map/all_to_all | solution.py:57
  140.9 3.0 %expand_grad.1 = (f32[4,128,512]{2,1,0:T(8,128)S(1)}, bf16[4,128,512]{2,1,0:T(8,128)(2,1)S(1)}) custom-call(s32[7]{0:T(128)S(1)} %stack.31.info_ref, bf16[1024,256]{1,0:T(8,128)(2,1)S(1)} %act_two.2.refs_0_, bf16[1024,256]{1,0:T(8,128)(2,1)S(1)} %act_two.3.refs_0_.refs_1_, bf16[1024,256]{1,0:T(8,128)(2,1)S(1)} %collective-permute-done.13.refs_1_.refs_2_, ...), custom_call_target="tpu_custom_call" | custom-call | tf_op jit(solution)/shard_map/expand_grad/pallas_call | solution.py:30
  146.7 8.3 %collective-permute-done.20.refs_0_ = bf16[1024,256]{1,0:T(8,128)(2,1)S(1)} collective-permute-done((bf16[1024,256]{1,0:T(8,128)(2,1)S(1)}, bf16[1024,256]{1,0:T(8,128)(2,1)S(1)}, u32[]{:S(2)}, u32[]{:S(2)}) %collective-permute-start.20) | collective-permute-done | bytes 524320 | tf_op jit(solution)/shard_map/ppermute | solution.py:49
  160.9 4.4 %collective-permute-done.23.refs_0_ = bf16[1024,256]{1,0:T(8,128)(2,1)S(1)} collective-permute-done((bf16[1024,256]{1,0:T(8,128)(2,1)S(1)}, bf16[1024,256]{1,0:T(8,128)(2,1)S(1)}, u32[]{:S(2)}, u32[]{:S(2)}) %collective-permute-start.23) | collective-permute-done | bytes 524320 | tf_op jit(solution)/shard_map/ppermute | solution.py:49
  168.9 2.2 collective-permute-done.27.refs_3_
  172.3 3.3 %collective-permute-start.31 = (f32[2,256]{1,0:T(2,128)S(1)}, f32[2,256]{1,0:T(2,128)S(1)}, u32[]{:S(2)}, u32[]{:S(2)}) collective-permute-start(f32[2,256]{1,0:T(2,128)S(1)} %add_rows.1.refs_0_), channel_id=1, source_target_pairs={{0,3},{1,2},{2,1},{3,0},{4,7},{5,6},{6,5},{7,4},{8,11},{9,10},{10,... | collective-permute-start | bytes 6152 | tf_op jit(solution)/shard_map/ppermute | solution.py:49
  179.7 4.7 %conv_backward.1 = (f32[16,128,256]{2,1,0:T(8,128)S(1)}, f32[8,2,256]{2,1,0:T(2,128)S(1)}, bf16[16,160,768]{2,1,0:T(8,128)(2,1)S(1)}) custom-call(s32[7]{0:T(128)S(1)} %stack.31.info_ref, f32[8,128,256]{2,1,0:T(8,128)S(1)} %get-tuple-element.164.refs_0_, f32[8,128,256]{2,1,0:T(8,128)S(1)} %get-tuple-element.188.refs_1_, ...), custom_call_target="tpu_custom_call" | custom-call | tf_op jit(solution)/shard_map/conv_backward/pallas_call | solution.py:30
  184.4 12.0 %all_to_all.29.refs_4_.refs_0_ = f32[8,2,256]{2,1,0:T(2,128)S(1)} all-to-all(f32[8,2,256]{2,1,0:T(2,128)S(1)} %get-tuple-element.191), channel_id=1, replica_groups=mesh['height'=2,'chan'=4,'batch'=4] {'height','batch'}, dimensions={0} | all-to-all | bytes 32768 | tf_op jit(solution)/shard_map/all_to_all | solution.py:57
  200.0 3.2 %tap_grads.1.refs_5_ = f32[9,32,256]{2,1,0:T(8,128)S(1)} custom-call(s32[7]{0:T(128)S(1)} %stack.31.info_ref, bf16[16,128,256]{2,1,0:T(8,128)(2,1)S(1)} %get-tuple-element.200.act_ref, bf16[16,160,768]{2,1,0:T(8,128)(2,1)S(1)} %get-tuple-element.201.window_ref), custom_call_target="tpu_custom_call" | custom-call | tf_op jit(solution)/shard_map/tap_grads/pallas_call | solution.py:30
  203.3 1.9 reduce_grad.3
  210.4 2.1 collective-permute-done.35.arrived_ref
  216.8 2.4 collective-permute-start.42
  219.2 2.0 collective-permute-done.40.arrived_ref
  221.8 3.5 %collective-permute-done.41.refs_1_ = bf16[1,128,512]{2,1,0:T(8,128)(2,1)S(1)} collective-permute-done((bf16[1,128,512]{2,1,0:T(8,128)(2,1)S(1)}, bf16[1,128,512]{2,1,0:T(8,128)(2,1)S(1)}, u32[]{:S(2)}, u32[]{:S(2)}) %collective-permute-start.41) | collective-permute-done | bytes 131104 | tf_op jit(solution)/shard_map/ppermute | solution.py:49
  226.6 2.3 collective-permute-start.45
  229.6 5.9 %collective-permute-done.43.refs_1_ = bf16[2,128,512]{2,1,0:T(8,128)(2,1)S(1)} collective-permute-done((bf16[2,128,512]{2,1,0:T(8,128)(2,1)S(1)}, bf16[2,128,512]{2,1,0:T(8,128)(2,1)S(1)}, u32[]{:S(2)}, u32[]{:S(2)}) %collective-permute-start.43) | collective-permute-done | bytes 262176 | tf_op jit(solution)/shard_map/ppermute | solution.py:49
  237.4 3.9 %collective-permute-start.48 = (bf16[2,128,256]{2,1,0:T(8,128)(2,1)S(1)}, bf16[2,128,256]{2,1,0:T(8,128)(2,1)S(1)}, u32[]{:S(2)}, u32[]{:S(2)}) collective-permute-start(bf16[2,128,256]{2,1,0:T(8,128)(2,1)S(1)} %join.10.refs_0_), channel_id=1, source_target_pairs={{0,1},{1,0},{2,3},{3,2},{4,5},{5,4},{6,7},{7,6},{8,9},{9,8},{10,11... | collective-permute-start | bytes 393224 | tf_op jit(solution)/shard_map/ppermute | solution.py:49
  245.9 1.9 collective-permute-start.50
  247.9 5.2 %collective-permute-done.49.refs_1_ = bf16[4,128,256]{2,1,0:T(8,128)(2,1)S(1)} collective-permute-done((bf16[4,128,256]{2,1,0:T(8,128)(2,1)S(1)}, bf16[4,128,256]{2,1,0:T(8,128)(2,1)S(1)}, u32[]{:S(2)}, u32[]{:S(2)}) %collective-permute-start.49) | collective-permute-done | bytes 262176 | tf_op jit(solution)/shard_map/ppermute | solution.py:49
  254.6 4.8 %input_grad.1 = bf16[2048,512]{1,0:T(8,128)(2,1)} custom-call(s32[7]{0:T(128)S(1)} %stack.31.info_ref, f32[2048,512]{1,0:T(8,128)S(1)} %bitcast.23, bf16[2048,256]{1,0:T(8,128)(2,1)S(1)} %grad_reduced.1.refs_4_.refs_0_, bf16[2048,256]{1,0:T(8,128)(2,1)S(1)} %collective-permute-done.51.refs_1_, bf16[2048,256]{1,0:T(8,128)(2,1)S(1)} %collective-permute-done.52.refs_2_, ...), custom_call_target="tpu_custom_call" | custom-call | tf_op jit(solution)/shard_map/input_grad/pallas_call | solution.py:30
  259.4 2.0 place_expand.1
  261.5 2.1 place_reduce.1
  (162 shorter events, 73.3 us)
Async XLA Ops:
  2.0 27.0 %collective-permute-start.1 = (bf16[1024,512]{1,0:T(8,128)(2,1)S(1)}, bf16[1024,512]{1,0:T(8,128)(2,1)S(1)}, u32[]{:S(2)}, u32[]{:S(2)}) collective-permute-start(bf16[1024,512]{1,0:T(8,128)(2,1)S(1)} %bitcast.24), channel_id=1, source_target_pairs={{0,8},{4,12},{8,0},{12,4},{1,9},{5,13},{9,1},{13,5},{2,10},{6,14},... | collective-permute-start | bytes 3145736 | tf_op jit(solution)/shard_map/ppermute | solution.py:49
  8.5 42.2 %collective-permute-start.4 = (bf16[1024,512]{1,0:T(8,128)(2,1)S(1)}, bf16[1024,512]{1,0:T(8,128)(2,1)S(1)}, u32[]{:S(2)}, u32[]{:S(2)}) collective-permute-start(bf16[1024,512]{1,0:T(8,128)(2,1)S(1)} %slice.11.refs_0_.refs_1_), channel_id=1, source_target_pairs={{0,8},{4,12},{8,0},{12,4},{1,9},{5,13},{9,1},{13,5},{2,10},{6,14},... | collective-permute-start | bytes 3145736 | tf_op jit(solution)/shard_map/ppermute | solution.py:49
  9.2 20.9 %collective-permute-start.5 = (bf16[256,512]{1,0:T(8,128)(2,1)S(1)}, bf16[256,512]{1,0:T(8,128)(2,1)S(1)}, u32[]{:S(2)}, u32[]{:S(2)}) collective-permute-start(bf16[256,512]{1,0:T(8,128)(2,1)S(1)} %get-tuple-element.133), channel_id=1, source_target_pairs={{0,4},{4,0},{8,12},{12,8},{1,5},{5,1},{9,13},{13,9},{2,6},{6,2},{1... | collective-permute-start | bytes 786440 | tf_op jit(solution)/shard_map/ppermute | solution.py:49
  9.9 20.8 %collective-permute-start.6 = (bf16[512,256]{1,0:T(8,128)(2,1)S(1)}, bf16[512,256]{1,0:T(8,128)(2,1)S(1)}, u32[]{:S(2)}, u32[]{:S(2)}) collective-permute-start(bf16[512,256]{1,0:T(8,128)(2,1)S(1)} %get-tuple-element.134), channel_id=1, source_target_pairs={{0,4},{4,0},{8,12},{12,8},{1,5},{5,1},{9,13},{13,9},{2,6},{6,2},{1... | collective-permute-start | bytes 786440 | tf_op jit(solution)/shard_map/ppermute | solution.py:49
  10.5 41.9 %collective-permute-start = (bf16[1024,512]{1,0:T(8,128)(2,1)S(1)}, bf16[1024,512]{1,0:T(8,128)(2,1)S(1)}, u32[]{:S(2)}, u32[]{:S(2)}) collective-permute-start(bf16[1024,512]{1,0:T(8,128)(2,1)S(1)} %bitcast.25), channel_id=1, source_target_pairs={{0,4},{4,0},{8,12},{12,8},{1,5},{5,1},{9,13},{13,9},{2,6},{6,2},{1... | collective-permute-start | bytes 3145736 | tf_op jit(solution)/shard_map/ppermute | solution.py:49
  29.0 23.5 %collective-permute-start.2 = (bf16[1024,512]{1,0:T(8,128)(2,1)S(1)}, bf16[1024,512]{1,0:T(8,128)(2,1)S(1)}, u32[]{:S(2)}, u32[]{:S(2)}) collective-permute-start(bf16[1024,512]{1,0:T(8,128)(2,1)S(1)} %collective-permute-done.1.refs_2_.refs_0_), channel_id=1, source_target_pairs={{0,4},{4,0},{8,12},{12,8},{1,5},{5,1},{9,13},{13,9},{2,6},{6,2},{1... | collective-permute-start | bytes 3145736 | tf_op jit(solution)/shard_map/ppermute | solution.py:49
  30.1 25.9 %collective-permute-start.3 = (bf16[1024,512]{1,0:T(8,128)(2,1)S(1)}, bf16[1024,512]{1,0:T(8,128)(2,1)S(1)}, u32[]{:S(2)}, u32[]{:S(2)}) collective-permute-start(bf16[1024,512]{1,0:T(8,128)(2,1)S(1)} %slice.11.refs_0_.refs_1_), channel_id=1, source_target_pairs={{0,4},{4,0},{8,12},{12,8},{1,5},{5,1},{9,13},{13,9},{2,6},{6,2},{1... | collective-permute-start | bytes 3145736 | tf_op jit(solution)/shard_map/ppermute | solution.py:49
  50.6 25.4 %collective-permute-start.10 = (bf16[256,512]{1,0:T(8,128)(2,1)S(1)}, bf16[256,512]{1,0:T(8,128)(2,1)S(1)}, u32[]{:S(2)}, u32[]{:S(2)}) collective-permute-start(bf16[256,512]{1,0:T(8,128)(2,1)S(1)} %get-tuple-element.145), channel_id=1, source_target_pairs={{0,8},{4,12},{8,0},{12,4},{1,9},{5,13},{9,1},{13,5},{2,10},{6,14},... | collective-permute-start | bytes 786440 | tf_op jit(solution)/shard_map/ppermute | solution.py:49
  52.4 23.7 %collective-permute-start.11 = (bf16[256,512]{1,0:T(8,128)(2,1)S(1)}, bf16[256,512]{1,0:T(8,128)(2,1)S(1)}, u32[]{:S(2)}, u32[]{:S(2)}) collective-permute-start(bf16[256,512]{1,0:T(8,128)(2,1)S(1)} %get-tuple-element.147), channel_id=1, source_target_pairs={{0,12},{4,8},{8,4},{12,0},{1,13},{5,9},{9,5},{13,1},{2,14},{6,10},... | collective-permute-start | bytes 786440 | tf_op jit(solution)/shard_map/ppermute | solution.py:49
  52.5 23.6 %collective-permute-start.12 = (bf16[512,256]{1,0:T(8,128)(2,1)S(1)}, bf16[512,256]{1,0:T(8,128)(2,1)S(1)}, u32[]{:S(2)}, u32[]{:S(2)}) collective-permute-start(bf16[512,256]{1,0:T(8,128)(2,1)S(1)} %get-tuple-element.149), channel_id=1, source_target_pairs={{0,12},{4,8},{8,4},{12,0},{1,13},{5,9},{9,5},{13,1},{2,14},{6,10},... | collective-permute-start | bytes 786440 | tf_op jit(solution)/shard_map/ppermute | solution.py:49
  57.9 14.3 %collective-permute-start.9 = (bf16[8,16,256]{2,1,0:T(8,128)(2,1)S(1)}, bf16[8,16,256]{2,1,0:T(8,128)(2,1)S(1)}, u32[]{:S(2)}, u32[]{:S(2)}) collective-permute-start(bf16[8,16,256]{2,1,0:T(8,128)(2,1)S(1)} %get-tuple-element.139), channel_id=1, source_target_pairs={{0,16},{16,0},{1,17},{17,1},{2,18},{18,2},{3,19},{19,3},{4,20},{20... | collective-permute-start | bytes 196616 | tf_op jit(solution)/shard_map/ppermute | solution.py:49
  59.4 12.7 %collective-permute-start.8 = (bf16[8,16,256]{2,1,0:T(8,128)(2,1)S(1)}, bf16[8,16,256]{2,1,0:T(8,128)(2,1)S(1)}, u32[]{:S(2)}, u32[]{:S(2)}) collective-permute-start(bf16[8,16,256]{2,1,0:T(8,128)(2,1)S(1)} %get-tuple-element.138), channel_id=1, source_target_pairs={{0,16},{16,0},{1,17},{17,1},{2,18},{18,2},{3,19},{19,3},{4,20},{20... | collective-permute-start | bytes 196616 | tf_op jit(solution)/shard_map/ppermute | solution.py:49
  86.0 14.9 %collective-permute-start.14 = (bf16[1024,256]{1,0:T(8,128)(2,1)S(1)}, bf16[1024,256]{1,0:T(8,128)(2,1)S(1)}, u32[]{:S(2)}, u32[]{:S(2)}) collective-permute-start(bf16[1024,256]{1,0:T(8,128)(2,1)S(1)} %act_two.2.refs_0_), channel_id=1, source_target_pairs={{0,8},{4,12},{8,0},{12,4},{1,9},{5,13},{9,1},{13,5},{2,10},{6,14},... | collective-permute-start | bytes 1572872 | tf_op jit(solution)/shard_map/ppermute | solution.py:49
  87.5 20.7 %collective-permute-start.17 = (bf16[1024,256]{1,0:T(8,128)(2,1)S(1)}, bf16[1024,256]{1,0:T(8,128)(2,1)S(1)}, u32[]{:S(2)}, u32[]{:S(2)}) collective-permute-start(bf16[1024,256]{1,0:T(8,128)(2,1)S(1)} %act_two.3.refs_0_.refs_1_), channel_id=1, source_target_pairs={{0,8},{4,12},{8,0},{12,4},{1,9},{5,13},{9,1},{13,5},{2,10},{6,14},... | collective-permute-start | bytes 1572872 | tf_op jit(solution)/shard_map/ppermute | solution.py:49
  89.0 19.2 %collective-permute-start.13 = (bf16[1024,256]{1,0:T(8,128)(2,1)S(1)}, bf16[1024,256]{1,0:T(8,128)(2,1)S(1)}, u32[]{:S(2)}, u32[]{:S(2)}) collective-permute-start(bf16[1024,256]{1,0:T(8,128)(2,1)S(1)} %act_two.2.refs_0_), channel_id=1, source_target_pairs={{0,4},{4,0},{8,12},{12,8},{1,5},{5,1},{9,13},{13,9},{2,6},{6,2},{1... | collective-permute-start | bytes 1572872 | tf_op jit(solution)/shard_map/ppermute | solution.py:49
  100.9 9.1 %collective-permute-start.16 = (bf16[1024,256]{1,0:T(8,128)(2,1)S(1)}, bf16[1024,256]{1,0:T(8,128)(2,1)S(1)}, u32[]{:S(2)}, u32[]{:S(2)}) collective-permute-start(bf16[1024,256]{1,0:T(8,128)(2,1)S(1)} %act_two.3.refs_0_.refs_1_), channel_id=1, source_target_pairs={{0,4},{4,0},{8,12},{12,8},{1,5},{5,1},{9,13},{13,9},{2,6},{6,2},{1... | collective-permute-start | bytes 1572872 | tf_op jit(solution)/shard_map/ppermute | solution.py:49
  140.1 14.8 %collective-permute-start.20 = (bf16[1024,256]{1,0:T(8,128)(2,1)S(1)}, bf16[1024,256]{1,0:T(8,128)(2,1)S(1)}, u32[]{:S(2)}, u32[]{:S(2)}) collective-permute-start(bf16[1024,256]{1,0:T(8,128)(2,1)S(1)} %get-tuple-element.163), channel_id=1, source_target_pairs={{0,8},{4,12},{8,0},{12,4},{1,9},{5,13},{9,1},{13,5},{2,10},{6,14},... | collective-permute-start | bytes 1572872 | tf_op jit(solution)/shard_map/ppermute | solution.py:49
  144.0 13.7 %collective-permute-start.21 = (bf16[4,128,512]{2,1,0:T(8,128)(2,1)S(1)}, bf16[4,128,512]{2,1,0:T(8,128)(2,1)S(1)}, u32[]{:S(2)}, u32[]{:S(2)}) collective-permute-start(bf16[4,128,512]{2,1,0:T(8,128)(2,1)S(1)} %get-tuple-element.169), channel_id=1, source_target_pairs={{0,16},{16,0},{1,17},{17,1},{2,18},{18,2},{3,19},{19,3},{4,20},{20... | collective-permute-start | bytes 1572872 | tf_op jit(solution)/shard_map/ppermute | solution.py:49
  145.4 20.0 %collective-permute-start.23 = (bf16[1024,256]{1,0:T(8,128)(2,1)S(1)}, bf16[1024,256]{1,0:T(8,128)(2,1)S(1)}, u32[]{:S(2)}, u32[]{:S(2)}) collective-permute-start(bf16[1024,256]{1,0:T(8,128)(2,1)S(1)} %get-tuple-element.175), channel_id=1, source_target_pairs={{0,8},{4,12},{8,0},{12,4},{1,9},{5,13},{9,1},{13,5},{2,10},{6,14},... | collective-permute-start | bytes 1572872 | tf_op jit(solution)/shard_map/ppermute | solution.py:49
  158.4 8.9 %collective-permute-start.24 = (bf16[2,128,512]{2,1,0:T(8,128)(2,1)S(1)}, bf16[2,128,512]{2,1,0:T(8,128)(2,1)S(1)}, u32[]{:S(2)}, u32[]{:S(2)}) collective-permute-start(bf16[2,128,512]{2,1,0:T(8,128)(2,1)S(1)} %get-tuple-element.178), channel_id=1, source_target_pairs={{0,1},{1,0},{2,3},{3,2},{4,5},{5,4},{6,7},{7,6},{8,9},{9,8},{10,11... | collective-permute-start | bytes 786440 | tf_op jit(solution)/shard_map/ppermute | solution.py:49
  158.9 8.4 %collective-permute-start.25 = (bf16[16,16,256]{2,1,0:T(8,128)(2,1)S(1)}, bf16[16,16,256]{2,1,0:T(8,128)(2,1)S(1)}, u32[]{:S(2)}, u32[]{:S(2)}) collective-permute-start(bf16[16,16,256]{2,1,0:T(8,128)(2,1)S(1)} %get-tuple-element.180), channel_id=1, source_target_pairs={{0,16},{16,0},{1,17},{17,1},{2,18},{18,2},{3,19},{19,3},{4,20},{20... | collective-permute-start | bytes 393224 | tf_op jit(solution)/shard_map/ppermute | solution.py:49
  177.7 19.8 %collective-permute-start.33 = (bf16[512,256]{1,0:T(8,128)(2,1)S(1)}, bf16[512,256]{1,0:T(8,128)(2,1)S(1)}, u32[]{:S(2)}, u32[]{:S(2)}) collective-permute-start(bf16[512,256]{1,0:T(8,128)(2,1)S(1)} %get-tuple-element.196), channel_id=1, source_target_pairs={{0,8},{4,12},{8,0},{12,4},{1,9},{5,13},{9,1},{13,5},{2,10},{6,14},... | collective-permute-start | bytes 786440 | tf_op jit(solution)/shard_map/ppermute | solution.py:49
  179.2 18.3 %collective-permute-start.32 = (bf16[1,128,512]{2,1,0:T(8,128)(2,1)S(1)}, bf16[1,128,512]{2,1,0:T(8,128)(2,1)S(1)}, u32[]{:S(2)}, u32[]{:S(2)}) collective-permute-start(bf16[1,128,512]{2,1,0:T(8,128)(2,1)S(1)} %get-tuple-element.193), channel_id=1, source_target_pairs={{0,2},{1,3},{2,0},{3,1},{4,6},{5,7},{6,4},{7,5},{8,10},{9,11},{10,... | collective-permute-start | bytes 393224 | tf_op jit(solution)/shard_map/ppermute | solution.py:49
  199.4 9.9 %collective-permute-start.34 = (bf16[4,128,256]{2,1,0:T(8,128)(2,1)S(1)}, bf16[4,128,256]{2,1,0:T(8,128)(2,1)S(1)}, u32[]{:S(2)}, u32[]{:S(2)}) collective-permute-start(bf16[4,128,256]{2,1,0:T(8,128)(2,1)S(1)} %get-tuple-element.207), channel_id=1, source_target_pairs={{0,16},{16,0},{1,17},{17,1},{2,18},{18,2},{3,19},{19,3},{4,20},{20... | collective-permute-start | bytes 786440 | tf_op jit(solution)/shard_map/ppermute | solution.py:49
  214.3 27.0 %collective-permute-start.52 = (bf16[2048,256]{1,0:T(8,128)(2,1)S(1)}, bf16[2048,256]{1,0:T(8,128)(2,1)S(1)}, u32[]{:S(2)}, u32[]{:S(2)}) collective-permute-start(bf16[2048,256]{1,0:T(8,128)(2,1)S(1)} %grad_reduced.1.refs_4_.refs_0_), channel_id=1, source_target_pairs={{0,8},{4,12},{8,0},{12,4},{1,9},{5,13},{9,1},{13,5},{2,10},{6,14},... | collective-permute-start | bytes 3145736 | tf_op jit(solution)/shard_map/ppermute | solution.py:49
  215.6 9.7 %collective-permute-start.41 = (bf16[1,128,512]{2,1,0:T(8,128)(2,1)S(1)}, bf16[1,128,512]{2,1,0:T(8,128)(2,1)S(1)}, u32[]{:S(2)}, u32[]{:S(2)}) collective-permute-start(bf16[1,128,512]{2,1,0:T(8,128)(2,1)S(1)} %bitcast.32), channel_id=1, source_target_pairs={{0,2},{1,3},{2,0},{3,1},{4,6},{5,7},{6,4},{7,5},{8,10},{9,11},{10,... | collective-permute-start | bytes 393224 | tf_op jit(solution)/shard_map/ppermute | solution.py:49
  216.8 9.2 %collective-permute-start.42 = (bf16[1,128,256]{2,1,0:T(8,128)(2,1)S(1)}, bf16[1,128,256]{2,1,0:T(8,128)(2,1)S(1)}, u32[]{:S(2)}, u32[]{:S(2)}) collective-permute-start(bf16[1,128,256]{2,1,0:T(8,128)(2,1)S(1)} %get-tuple-element.224), channel_id=1, source_target_pairs={{0,2},{1,3},{2,0},{3,1},{4,6},{5,7},{6,4},{7,5},{8,10},{9,11},{10,... | collective-permute-start | bytes 196616 | tf_op jit(solution)/shard_map/ppermute | solution.py:49
  225.9 9.6 %collective-permute-start.43 = (bf16[2,128,512]{2,1,0:T(8,128)(2,1)S(1)}, bf16[2,128,512]{2,1,0:T(8,128)(2,1)S(1)}, u32[]{:S(2)}, u32[]{:S(2)}) collective-permute-start(bf16[2,128,512]{2,1,0:T(8,128)(2,1)S(1)} %join.8.refs_0_), channel_id=1, source_target_pairs={{0,1},{1,0},{2,3},{3,2},{4,5},{5,4},{6,7},{7,6},{8,9},{9,8},{10,11... | collective-permute-start | bytes 786440 | tf_op jit(solution)/shard_map/ppermute | solution.py:49
  226.6 10.2 %collective-permute-start.45 = (bf16[1,128,256]{2,1,0:T(8,128)(2,1)S(1)}, bf16[1,128,256]{2,1,0:T(8,128)(2,1)S(1)}, u32[]{:S(2)}, u32[]{:S(2)}) collective-permute-start(bf16[1,128,256]{2,1,0:T(8,128)(2,1)S(1)} %add_last.2.refs_0_), channel_id=1, source_target_pairs={{0,2},{1,3},{2,0},{3,1},{4,6},{5,7},{6,4},{7,5},{8,10},{9,11},{10,... | collective-permute-start | bytes 196616 | tf_op jit(solution)/shard_map/ppermute | solution.py:49
  229.6 25.0 %collective-permute-start.51 = (bf16[2048,256]{1,0:T(8,128)(2,1)S(1)}, bf16[2048,256]{1,0:T(8,128)(2,1)S(1)}, u32[]{:S(2)}, u32[]{:S(2)}) collective-permute-start(bf16[2048,256]{1,0:T(8,128)(2,1)S(1)} %grad_reduced.1.refs_4_.refs_0_), channel_id=1, source_target_pairs={{0,4},{4,0},{8,12},{12,8},{1,5},{5,1},{9,13},{13,9},{2,6},{6,2},{1... | collective-permute-start | bytes 3145736 | tf_op jit(solution)/shard_map/ppermute | solution.py:49
  236.0 9.2 %collective-permute-start.47 = (bf16[4,128,512]{2,1,0:T(8,128)(2,1)S(1)}, bf16[4,128,512]{2,1,0:T(8,128)(2,1)S(1)}, u32[]{:S(2)}, u32[]{:S(2)}) collective-permute-start(bf16[4,128,512]{2,1,0:T(8,128)(2,1)S(1)} %join.9.own_ref), channel_id=1, source_target_pairs={{0,16},{16,0},{1,17},{17,1},{2,18},{18,2},{3,19},{19,3},{4,20},{20... | collective-permute-start | bytes 1572872 | tf_op jit(solution)/shard_map/ppermute | solution.py:49
  241.3 13.4 %collective-permute-start.53 = (bf16[2048,256]{1,0:T(8,128)(2,1)S(1)}, bf16[2048,256]{1,0:T(8,128)(2,1)S(1)}, u32[]{:S(2)}, u32[]{:S(2)}) collective-permute-start(bf16[2048,256]{1,0:T(8,128)(2,1)S(1)} %collective-permute-done.52.refs_2_), channel_id=1, source_target_pairs={{0,4},{4,0},{8,12},{12,8},{1,5},{5,1},{9,13},{13,9},{2,6},{6,2},{1... | collective-permute-start | bytes 3145736 | tf_op jit(solution)/shard_map/ppermute | solution.py:49
  (35 other events, 328.1 us)

commit v9 on v8

--- a/solution.py
+++ b/solution.py
@@ -10,7 +10,7 @@
 EPSILON = 1e-05
 SPLIT_COST, ADD_COST, STAGE_COST = 1_800_000_000, 3_000_000_000, 2_200_000_000
 LAST_PHASE = (
-    "wz", "wr", "a0", "t", "b0", "c", "a1", "b1", "e0", "x", "a2", "b2", "e1", "o", "a3", "e2", "b3", "a4",
+    "wz", "wr", "a0", "t", "b0", "c", "a1", "b1", "e0", "a2", "x", "b2", "e1", "o", "a3", "e2", "b3", "a4",
     "d", "b4", "we", "a5", "wa", "b5", "i", "p",
 )
 F32, BF16 = jnp.float32, jnp.bfloat16

time: 264 us -> 263 us (level)
  transfers between devices with their start and end apart: 55 -> 55, of which waited for: 21 -> 23; matrix products, arithmetic and copies ran while one was open for 1% -> 1% of each run, Pallas kernels for 19% -> 19%
where the time goes in v9:
time: 263 us
  waiting for transfers between devices  97.8 us (37%)
  Pallas kernels  62.4 us (24%)
  blocking collectives  51.3 us (20%)
  starting transfers between devices  45 us (17%)
  local copies, waits for them, and re-layouts  4.18 us (2%)
    ppermute x55, waiting for transfers between devices, permute(): return lax.ppermute(value, axis, [(i, i ^ distance) for i in range(count)])  97.8 us
    pallas_call x45, Pallas kernels, kernel_call(): pl.pallas_call(body, in_specs=[SMEM if a.dtype == jnp.int32 else VMEM for...  62.4 us
    all_to_all x5, blocking collectives, spread_sums(): return lax.all_to_all(sent, REDUCE_AXES, 0, 0)  51.3 us
    ppermute x55, starting transfers between devices, permute(): return lax.ppermute(value, axis, [(i, i ^ distance) for i in range(count)])  45 us
  transfers between devices with their start and end apart: 55, of which 23 were waited for; matrix products, arithmetic and copies ran while one was open for 1% of the time, Pallas kernels for 19%

profile of v9, /device:TPU:0, one launch (start us, length us, event | category | flops | bytes accessed | tf_op | source)
XLA Modules:
  0.0 262.6 jit_solution(10005805460111513425)
XLA Ops:
  2.0 3.0 %collective-permute-start.1 = (bf16[1024,512]{1,0:T(8,128)(2,1)S(1)}, bf16[1024,512]{1,0:T(8,128)(2,1)S(1)}, u32[]{:S(2)}, u32[]{:S(2)}) collective-permute-start(bf16[1024,512]{1,0:T(8,128)(2,1)S(1)} %bitcast.24), channel_id=1, source_target_pairs={{0,8},{4,12},{8,0},{12,4},{1,9},{5,13},{9,1},{13,5},{2,10},{6,14},... | collective-permute-start | bytes 3145736 | tf_op jit(solution)/shard_map/ppermute | solution.py:49
  10.6 18.4 %collective-permute-done.1.refs_2_.refs_0_ = bf16[1024,512]{1,0:T(8,128)(2,1)S(1)} collective-permute-done((bf16[1024,512]{1,0:T(8,128)(2,1)S(1)}, bf16[1024,512]{1,0:T(8,128)(2,1)S(1)}, u32[]{:S(2)}, u32[]{:S(2)}) %collective-permute-start.1) | collective-permute-done | bytes 1048608 | tf_op jit(solution)/shard_map/ppermute | solution.py:49
  30.7 19.9 %collective-permute-done.4.refs_2_.refs_1_ = bf16[1024,512]{1,0:T(8,128)(2,1)S(1)} collective-permute-done((bf16[1024,512]{1,0:T(8,128)(2,1)S(1)}, bf16[1024,512]{1,0:T(8,128)(2,1)S(1)}, u32[]{:S(2)}, u32[]{:S(2)}) %collective-permute-start.4) | collective-permute-done | bytes 1048608 | tf_op jit(solution)/shard_map/ppermute | solution.py:49
  60.0 12.2 %all_to_all.25.refs_4_.refs_10_.refs_3_ = f32[8,2,256]{2,1,0:T(2,128)S(1)} all-to-all(f32[8,2,256]{2,1,0:T(2,128)S(1)} %get-tuple-element.140), channel_id=1, replica_groups=mesh['height'=2,'chan'=4,'batch'=4] {'height','batch'}, dimensions={0} | all-to-all | bytes 32768 | tf_op jit(solution)/shard_map/all_to_all | solution.py:57
  72.2 3.9 %conv_forward.1 = (bf16[16,128,256]{2,1,0:T(8,128)(2,1)S(1)}, f32[16,128,256]{2,1,0:T(8,128)S(1)}, bf16[16,16,256]{2,1,0:T(8,128)(2,1)S(1)}, f32[8,2,256]{2,1,0:T(2,128)S(1)}) custom-call(s32[7]{0:T(128)S(1)} %stack.31.info_ref, f32[8,128,256]{2,1,0:T(8,128)S(1)} %get-tuple-element.130.refs_0_.refs_4_, ...), custom_call_target="tpu_custom_call" | custom-call | tf_op jit(solution)/shard_map/conv_forward/pallas_call | solution.py:30
  76.1 9.0 %all_to_all.26.sums_ref.refs_2_.refs_8_ = f32[8,2,256]{2,1,0:T(2,128)S(1)} all-to-all(f32[8,2,256]{2,1,0:T(2,128)S(1)} %get-tuple-element.150), channel_id=1, replica_groups=mesh['height'=2,'chan'=4,'batch'=4] {'height','batch'}, dimensions={0} | all-to-all | bytes 32768 | tf_op jit(solution)/shard_map/all_to_all | solution.py:57
  89.0 11.9 %collective-permute-done.14.refs_2_.refs_4_ = bf16[1024,256]{1,0:T(8,128)(2,1)S(1)} collective-permute-done((bf16[1024,256]{1,0:T(8,128)(2,1)S(1)}, bf16[1024,256]{1,0:T(8,128)(2,1)S(1)}, u32[]{:S(2)}, u32[]{:S(2)}) %collective-permute-start.14) | collective-permute-done | bytes 524320 | tf_op jit(solution)/shard_map/ppermute | solution.py:49
  101.4 6.8 %collective-permute-done.17.refs_2_.refs_5_ = bf16[1024,256]{1,0:T(8,128)(2,1)S(1)} collective-permute-done((bf16[1024,256]{1,0:T(8,128)(2,1)S(1)}, bf16[1024,256]{1,0:T(8,128)(2,1)S(1)}, u32[]{:S(2)}, u32[]{:S(2)}) %collective-permute-start.17) | collective-permute-done | bytes 524320 | tf_op jit(solution)/shard_map/ppermute | solution.py:49
  111.9 9.1 %all_to_all.27.refs_4_.refs_3_ = f32[8,2,512]{2,1,0:T(2,128)S(1)} all-to-all(f32[8,2,512]{2,1,0:T(2,128)S(1)} %get-tuple-element.155), channel_id=1, replica_groups=mesh['height'=2,'chan'=4,'batch'=4] {'height','batch'}, dimensions={0} | all-to-all | bytes 65536 | tf_op jit(solution)/shard_map/all_to_all | solution.py:57
  121.0 4.6 %output.1 = (bf16[16,128,512]{2,1,0:T(8,128)(2,1)}, f32[16,128,512]{2,1,0:T(8,128)S(1)}, f32[8,2,512]{2,1,0:T(2,128)S(1)}) custom-call(s32[7]{0:T(128)S(1)} %stack.31.info_ref, f32[8,128,512]{2,1,0:T(8,128)S(1)} %get-tuple-element.152.refs_0_, f32[8,128,512]{2,1,0:T(8,128)S(1)} %get-tuple-element.154.refs_1_, bf16[16,128,512]{2,1,0:T(8,128)(2,1)S(1)} %bitcast.29, ...), custom_call_target="tpu_custom_call" | custom-call | tf_op jit(solution)/shard_map/output/pallas_call | solution.py:30
  125.6 9.1 %all_to_all.28.refs_4_.refs_2_ = f32[8,2,512]{2,1,0:T(2,128)S(1)} all-to-all(f32[8,2,512]{2,1,0:T(2,128)S(1)} %get-tuple-element.159), channel_id=1, replica_groups=mesh['height'=2,'chan'=4,'batch'=4] {'height','batch'}, dimensions={0} | all-to-all | bytes 65536 | tf_op jit(solution)/shard_map/all_to_all | solution.py:57
  136.7 1.9 back_expand.3
  140.9 3.0 %expand_grad.1 = (f32[4,128,512]{2,1,0:T(8,128)S(1)}, bf16[4,128,512]{2,1,0:T(8,128)(2,1)S(1)}) custom-call(s32[7]{0:T(128)S(1)} %stack.31.info_ref, bf16[1024,256]{1,0:T(8,128)(2,1)S(1)} %act_two.2.refs_0_, bf16[1024,256]{1,0:T(8,128)(2,1)S(1)} %act_two.3.refs_0_.refs_1_, bf16[1024,256]{1,0:T(8,128)(2,1)S(1)} %collective-permute-done.13.refs_1_.refs_2_, ...), custom_call_target="tpu_custom_call" | custom-call | tf_op jit(solution)/shard_map/expand_grad/pallas_call | solution.py:30
  146.7 8.3 %collective-permute-done.20.refs_0_ = bf16[1024,256]{1,0:T(8,128)(2,1)S(1)} collective-permute-done((bf16[1024,256]{1,0:T(8,128)(2,1)S(1)}, bf16[1024,256]{1,0:T(8,128)(2,1)S(1)}, u32[]{:S(2)}, u32[]{:S(2)}) %collective-permute-start.20) | collective-permute-done | bytes 524320 | tf_op jit(solution)/shard_map/ppermute | solution.py:49
  160.9 4.4 %collective-permute-done.23.refs_0_ = bf16[1024,256]{1,0:T(8,128)(2,1)S(1)} collective-permute-done((bf16[1024,256]{1,0:T(8,128)(2,1)S(1)}, bf16[1024,256]{1,0:T(8,128)(2,1)S(1)}, u32[]{:S(2)}, u32[]{:S(2)}) %collective-permute-start.23) | collective-permute-done | bytes 524320 | tf_op jit(solution)/shard_map/ppermute | solution.py:49
  168.9 2.2 collective-permute-done.27.refs_3_
  172.3 3.3 %collective-permute-start.31 = (f32[2,256]{1,0:T(2,128)S(1)}, f32[2,256]{1,0:T(2,128)S(1)}, u32[]{:S(2)}, u32[]{:S(2)}) collective-permute-start(f32[2,256]{1,0:T(2,128)S(1)} %add_rows.1.refs_0_), channel_id=1, source_target_pairs={{0,3},{1,2},{2,1},{3,0},{4,7},{5,6},{6,5},{7,4},{8,11},{9,10},{10,... | collective-permute-start | bytes 6152 | tf_op jit(solution)/shard_map/ppermute | solution.py:49
  179.7 4.7 %conv_backward.1 = (f32[16,128,256]{2,1,0:T(8,128)S(1)}, f32[8,2,256]{2,1,0:T(2,128)S(1)}, bf16[16,160,768]{2,1,0:T(8,128)(2,1)S(1)}) custom-call(s32[7]{0:T(128)S(1)} %stack.31.info_ref, f32[8,128,256]{2,1,0:T(8,128)S(1)} %get-tuple-element.164.refs_0_, f32[8,128,256]{2,1,0:T(8,128)S(1)} %get-tuple-element.188.refs_1_, ...), custom_call_target="tpu_custom_call" | custom-call | tf_op jit(solution)/shard_map/conv_backward/pallas_call | solution.py:30
  184.4 12.0 %all_to_all.29.refs_4_.refs_0_ = f32[8,2,256]{2,1,0:T(2,128)S(1)} all-to-all(f32[8,2,256]{2,1,0:T(2,128)S(1)} %get-tuple-element.191), channel_id=1, replica_groups=mesh['height'=2,'chan'=4,'batch'=4] {'height','batch'}, dimensions={0} | all-to-all | bytes 32768 | tf_op jit(solution)/shard_map/all_to_all | solution.py:57
  197.5 1.9 reduce_grad.2
  200.0 3.2 %tap_grads.1.refs_5_ = f32[9,32,256]{2,1,0:T(8,128)S(1)} custom-call(s32[7]{0:T(128)S(1)} %stack.31.info_ref, bf16[16,128,256]{2,1,0:T(8,128)(2,1)S(1)} %get-tuple-element.200.act_ref, bf16[16,160,768]{2,1,0:T(8,128)(2,1)S(1)} %get-tuple-element.201.window_ref), custom_call_target="tpu_custom_call" | custom-call | tf_op jit(solution)/shard_map/tap_grads/pallas_call | solution.py:30
  203.3 1.9 reduce_grad.3
  210.4 2.1 collective-permute-done.35.arrived_ref
  219.2 2.5 collective-permute-done.40.arrived_ref
  222.2 2.4 collective-permute-done.41.refs_1_
  226.1 2.3 collective-permute-start.45
  229.1 5.0 %collective-permute-done.43.refs_1_ = bf16[2,128,512]{2,1,0:T(8,128)(2,1)S(1)} collective-permute-done((bf16[2,128,512]{2,1,0:T(8,128)(2,1)S(1)}, bf16[2,128,512]{2,1,0:T(8,128)(2,1)S(1)}, u32[]{:S(2)}, u32[]{:S(2)}) %collective-permute-start.43) | collective-permute-done | bytes 262176 | tf_op jit(solution)/shard_map/ppermute | solution.py:49
  237.2 2.0 collective-permute-start.48
  247.3 3.8 %collective-permute-done.49.refs_1_ = bf16[4,128,256]{2,1,0:T(8,128)(2,1)S(1)} collective-permute-done((bf16[4,128,256]{2,1,0:T(8,128)(2,1)S(1)}, bf16[4,128,256]{2,1,0:T(8,128)(2,1)S(1)}, u32[]{:S(2)}, u32[]{:S(2)}) %collective-permute-start.49) | collective-permute-done | bytes 262176 | tf_op jit(solution)/shard_map/ppermute | solution.py:49
  253.6 4.8 %input_grad.1 = bf16[2048,512]{1,0:T(8,128)(2,1)} custom-call(s32[7]{0:T(128)S(1)} %stack.31.info_ref, f32[2048,512]{1,0:T(8,128)S(1)} %bitcast.23, bf16[2048,256]{1,0:T(8,128)(2,1)S(1)} %grad_reduced.1.refs_4_.refs_0_, bf16[2048,256]{1,0:T(8,128)(2,1)S(1)} %collective-permute-done.51.refs_1_, bf16[2048,256]{1,0:T(8,128)(2,1)S(1)} %collective-permute-done.52.refs_2_, ...), custom_call_target="tpu_custom_call" | custom-call | tf_op jit(solution)/shard_map/input_grad/pallas_call | solution.py:30
  258.5 2.0 place_expand.1
  260.5 2.1 place_reduce.1
  (162 shorter events, 77.6 us)
Async XLA Ops:
  2.0 27.0 %collective-permute-start.1 = (bf16[1024,512]{1,0:T(8,128)(2,1)S(1)}, bf16[1024,512]{1,0:T(8,128)(2,1)S(1)}, u32[]{:S(2)}, u32[]{:S(2)}) collective-permute-start(bf16[1024,512]{1,0:T(8,128)(2,1)S(1)} %bitcast.24), channel_id=1, source_target_pairs={{0,8},{4,12},{8,0},{12,4},{1,9},{5,13},{9,1},{13,5},{2,10},{6,14},... | collective-permute-start | bytes 3145736 | tf_op jit(solution)/shard_map/ppermute | solution.py:49
  8.5 42.2 %collective-permute-start.4 = (bf16[1024,512]{1,0:T(8,128)(2,1)S(1)}, bf16[1024,512]{1,0:T(8,128)(2,1)S(1)}, u32[]{:S(2)}, u32[]{:S(2)}) collective-permute-start(bf16[1024,512]{1,0:T(8,128)(2,1)S(1)} %slice.11.refs_0_.refs_1_), channel_id=1, source_target_pairs={{0,8},{4,12},{8,0},{12,4},{1,9},{5,13},{9,1},{13,5},{2,10},{6,14},... | collective-permute-start | bytes 3145736 | tf_op jit(solution)/shard_map/ppermute | solution.py:49
  9.2 20.9 %collective-permute-start.5 = (bf16[256,512]{1,0:T(8,128)(2,1)S(1)}, bf16[256,512]{1,0:T(8,128)(2,1)S(1)}, u32[]{:S(2)}, u32[]{:S(2)}) collective-permute-start(bf16[256,512]{1,0:T(8,128)(2,1)S(1)} %get-tuple-element.133), channel_id=1, source_target_pairs={{0,4},{4,0},{8,12},{12,8},{1,5},{5,1},{9,13},{13,9},{2,6},{6,2},{1... | collective-permute-start | bytes 786440 | tf_op jit(solution)/shard_map/ppermute | solution.py:49
  9.9 20.8 %collective-permute-start.6 = (bf16[512,256]{1,0:T(8,128)(2,1)S(1)}, bf16[512,256]{1,0:T(8,128)(2,1)S(1)}, u32[]{:S(2)}, u32[]{:S(2)}) collective-permute-start(bf16[512,256]{1,0:T(8,128)(2,1)S(1)} %get-tuple-element.134), channel_id=1, source_target_pairs={{0,4},{4,0},{8,12},{12,8},{1,5},{5,1},{9,13},{13,9},{2,6},{6,2},{1... | collective-permute-start | bytes 786440 | tf_op jit(solution)/shard_map/ppermute | solution.py:49
  10.5 41.9 %collective-permute-start = (bf16[1024,512]{1,0:T(8,128)(2,1)S(1)}, bf16[1024,512]{1,0:T(8,128)(2,1)S(1)}, u32[]{:S(2)}, u32[]{:S(2)}) collective-permute-start(bf16[1024,512]{1,0:T(8,128)(2,1)S(1)} %bitcast.25), channel_id=1, source_target_pairs={{0,4},{4,0},{8,12},{12,8},{1,5},{5,1},{9,13},{13,9},{2,6},{6,2},{1... | collective-permute-start | bytes 3145736 | tf_op jit(solution)/shard_map/ppermute | solution.py:49
  29.0 23.5 %collective-permute-start.2 = (bf16[1024,512]{1,0:T(8,128)(2,1)S(1)}, bf16[1024,512]{1,0:T(8,128)(2,1)S(1)}, u32[]{:S(2)}, u32[]{:S(2)}) collective-permute-start(bf16[1024,512]{1,0:T(8,128)(2,1)S(1)} %collective-permute-done.1.refs_2_.refs_0_), channel_id=1, source_target_pairs={{0,4},{4,0},{8,12},{12,8},{1,5},{5,1},{9,13},{13,9},{2,6},{6,2},{1... | collective-permute-start | bytes 3145736 | tf_op jit(solution)/shard_map/ppermute | solution.py:49
  30.1 25.9 %collective-permute-start.3 = (bf16[1024,512]{1,0:T(8,128)(2,1)S(1)}, bf16[1024,512]{1,0:T(8,128)(2,1)S(1)}, u32[]{:S(2)}, u32[]{:S(2)}) collective-permute-start(bf16[1024,512]{1,0:T(8,128)(2,1)S(1)} %slice.11.refs_0_.refs_1_), channel_id=1, source_target_pairs={{0,4},{4,0},{8,12},{12,8},{1,5},{5,1},{9,13},{13,9},{2,6},{6,2},{1... | collective-permute-start | bytes 3145736 | tf_op jit(solution)/shard_map/ppermute | solution.py:49
  50.6 25.4 %collective-permute-start.10 = (bf16[256,512]{1,0:T(8,128)(2,1)S(1)}, bf16[256,512]{1,0:T(8,128)(2,1)S(1)}, u32[]{:S(2)}, u32[]{:S(2)}) collective-permute-start(bf16[256,512]{1,0:T(8,128)(2,1)S(1)} %get-tuple-element.145), channel_id=1, source_target_pairs={{0,8},{4,12},{8,0},{12,4},{1,9},{5,13},{9,1},{13,5},{2,10},{6,14},... | collective-permute-start | bytes 786440 | tf_op jit(solution)/shard_map/ppermute | solution.py:49
  52.4 23.7 %collective-permute-start.11 = (bf16[256,512]{1,0:T(8,128)(2,1)S(1)}, bf16[256,512]{1,0:T(8,128)(2,1)S(1)}, u32[]{:S(2)}, u32[]{:S(2)}) collective-permute-start(bf16[256,512]{1,0:T(8,128)(2,1)S(1)} %get-tuple-element.147), channel_id=1, source_target_pairs={{0,12},{4,8},{8,4},{12,0},{1,13},{5,9},{9,5},{13,1},{2,14},{6,10},... | collective-permute-start | bytes 786440 | tf_op jit(solution)/shard_map/ppermute | solution.py:49
  52.5 23.6 %collective-permute-start.12 = (bf16[512,256]{1,0:T(8,128)(2,1)S(1)}, bf16[512,256]{1,0:T(8,128)(2,1)S(1)}, u32[]{:S(2)}, u32[]{:S(2)}) collective-permute-start(bf16[512,256]{1,0:T(8,128)(2,1)S(1)} %get-tuple-element.149), channel_id=1, source_target_pairs={{0,12},{4,8},{8,4},{12,0},{1,13},{5,9},{9,5},{13,1},{2,14},{6,10},... | collective-permute-start | bytes 786440 | tf_op jit(solution)/shard_map/ppermute | solution.py:49
  57.9 14.3 %collective-permute-start.9 = (bf16[8,16,256]{2,1,0:T(8,128)(2,1)S(1)}, bf16[8,16,256]{2,1,0:T(8,128)(2,1)S(1)}, u32[]{:S(2)}, u32[]{:S(2)}) collective-permute-start(bf16[8,16,256]{2,1,0:T(8,128)(2,1)S(1)} %get-tuple-element.139), channel_id=1, source_target_pairs={{0,16},{16,0},{1,17},{17,1},{2,18},{18,2},{3,19},{19,3},{4,20},{20... | collective-permute-start | bytes 196616 | tf_op jit(solution)/shard_map/ppermute | solution.py:49
  59.4 12.7 %collective-permute-start.8 = (bf16[8,16,256]{2,1,0:T(8,128)(2,1)S(1)}, bf16[8,16,256]{2,1,0:T(8,128)(2,1)S(1)}, u32[]{:S(2)}, u32[]{:S(2)}) collective-permute-start(bf16[8,16,256]{2,1,0:T(8,128)(2,1)S(1)} %get-tuple-element.138), channel_id=1, source_target_pairs={{0,16},{16,0},{1,17},{17,1},{2,18},{18,2},{3,19},{19,3},{4,20},{20... | collective-permute-start | bytes 196616 | tf_op jit(solution)/shard_map/ppermute | solution.py:49
  86.0 14.9 %collective-permute-start.14 = (bf16[1024,256]{1,0:T(8,128)(2,1)S(1)}, bf16[1024,256]{1,0:T(8,128)(2,1)S(1)}, u32[]{:S(2)}, u32[]{:S(2)}) collective-permute-start(bf16[1024,256]{1,0:T(8,128)(2,1)S(1)} %act_two.2.refs_0_), channel_id=1, source_target_pairs={{0,8},{4,12},{8,0},{12,4},{1,9},{5,13},{9,1},{13,5},{2,10},{6,14},... | collective-permute-start | bytes 1572872 | tf_op jit(solution)/shard_map/ppermute | solution.py:49
  87.5 20.7 %collective-permute-start.17 = (bf16[1024,256]{1,0:T(8,128)(2,1)S(1)}, bf16[1024,256]{1,0:T(8,128)(2,1)S(1)}, u32[]{:S(2)}, u32[]{:S(2)}) collective-permute-start(bf16[1024,256]{1,0:T(8,128)(2,1)S(1)} %act_two.3.refs_0_.refs_1_), channel_id=1, source_target_pairs={{0,8},{4,12},{8,0},{12,4},{1,9},{5,13},{9,1},{13,5},{2,10},{6,14},... | collective-permute-start | bytes 1572872 | tf_op jit(solution)/shard_map/ppermute | solution.py:49
  89.0 19.2 %collective-permute-start.13 = (bf16[1024,256]{1,0:T(8,128)(2,1)S(1)}, bf16[1024,256]{1,0:T(8,128)(2,1)S(1)}, u32[]{:S(2)}, u32[]{:S(2)}) collective-permute-start(bf16[1024,256]{1,0:T(8,128)(2,1)S(1)} %act_two.2.refs_0_), channel_id=1, source_target_pairs={{0,4},{4,0},{8,12},{12,8},{1,5},{5,1},{9,13},{13,9},{2,6},{6,2},{1... | collective-permute-start | bytes 1572872 | tf_op jit(solution)/shard_map/ppermute | solution.py:49
  100.9 9.1 %collective-permute-start.16 = (bf16[1024,256]{1,0:T(8,128)(2,1)S(1)}, bf16[1024,256]{1,0:T(8,128)(2,1)S(1)}, u32[]{:S(2)}, u32[]{:S(2)}) collective-permute-start(bf16[1024,256]{1,0:T(8,128)(2,1)S(1)} %act_two.3.refs_0_.refs_1_), channel_id=1, source_target_pairs={{0,4},{4,0},{8,12},{12,8},{1,5},{5,1},{9,13},{13,9},{2,6},{6,2},{1... | collective-permute-start | bytes 1572872 | tf_op jit(solution)/shard_map/ppermute | solution.py:49
  140.1 14.8 %collective-permute-start.20 = (bf16[1024,256]{1,0:T(8,128)(2,1)S(1)}, bf16[1024,256]{1,0:T(8,128)(2,1)S(1)}, u32[]{:S(2)}, u32[]{:S(2)}) collective-permute-start(bf16[1024,256]{1,0:T(8,128)(2,1)S(1)} %get-tuple-element.163), channel_id=1, source_target_pairs={{0,8},{4,12},{8,0},{12,4},{1,9},{5,13},{9,1},{13,5},{2,10},{6,14},... | collective-permute-start | bytes 1572872 | tf_op jit(solution)/shard_map/ppermute | solution.py:49
  144.0 13.7 %collective-permute-start.21 = (bf16[4,128,512]{2,1,0:T(8,128)(2,1)S(1)}, bf16[4,128,512]{2,1,0:T(8,128)(2,1)S(1)}, u32[]{:S(2)}, u32[]{:S(2)}) collective-permute-start(bf16[4,128,512]{2,1,0:T(8,128)(2,1)S(1)} %get-tuple-element.169), channel_id=1, source_target_pairs={{0,16},{16,0},{1,17},{17,1},{2,18},{18,2},{3,19},{19,3},{4,20},{20... | collective-permute-start | bytes 1572872 | tf_op jit(solution)/shard_map/ppermute | solution.py:49
  145.4 20.0 %collective-permute-start.23 = (bf16[1024,256]{1,0:T(8,128)(2,1)S(1)}, bf16[1024,256]{1,0:T(8,128)(2,1)S(1)}, u32[]{:S(2)}, u32[]{:S(2)}) collective-permute-start(bf16[1024,256]{1,0:T(8,128)(2,1)S(1)} %get-tuple-element.175), channel_id=1, source_target_pairs={{0,8},{4,12},{8,0},{12,4},{1,9},{5,13},{9,1},{13,5},{2,10},{6,14},... | collective-permute-start | bytes 1572872 | tf_op jit(solution)/shard_map/ppermute | solution.py:49
  158.4 8.9 %collective-permute-start.24 = (bf16[2,128,512]{2,1,0:T(8,128)(2,1)S(1)}, bf16[2,128,512]{2,1,0:T(8,128)(2,1)S(1)}, u32[]{:S(2)}, u32[]{:S(2)}) collective-permute-start(bf16[2,128,512]{2,1,0:T(8,128)(2,1)S(1)} %get-tuple-element.178), channel_id=1, source_target_pairs={{0,1},{1,0},{2,3},{3,2},{4,5},{5,4},{6,7},{7,6},{8,9},{9,8},{10,11... | collective-permute-start | bytes 786440 | tf_op jit(solution)/shard_map/ppermute | solution.py:49
  177.7 19.8 %collective-permute-start.33 = (bf16[512,256]{1,0:T(8,128)(2,1)S(1)}, bf16[512,256]{1,0:T(8,128)(2,1)S(1)}, u32[]{:S(2)}, u32[]{:S(2)}) collective-permute-start(bf16[512,256]{1,0:T(8,128)(2,1)S(1)} %get-tuple-element.196), channel_id=1, source_target_pairs={{0,8},{4,12},{8,0},{12,4},{1,9},{5,13},{9,1},{13,5},{2,10},{6,14},... | collective-permute-start | bytes 786440 | tf_op jit(solution)/shard_map/ppermute | solution.py:49
  179.2 18.3 %collective-permute-start.32 = (bf16[1,128,512]{2,1,0:T(8,128)(2,1)S(1)}, bf16[1,128,512]{2,1,0:T(8,128)(2,1)S(1)}, u32[]{:S(2)}, u32[]{:S(2)}) collective-permute-start(bf16[1,128,512]{2,1,0:T(8,128)(2,1)S(1)} %get-tuple-element.193), channel_id=1, source_target_pairs={{0,2},{1,3},{2,0},{3,1},{4,6},{5,7},{6,4},{7,5},{8,10},{9,11},{10,... | collective-permute-start | bytes 393224 | tf_op jit(solution)/shard_map/ppermute | solution.py:49
  199.4 9.9 %collective-permute-start.34 = (bf16[4,128,256]{2,1,0:T(8,128)(2,1)S(1)}, bf16[4,128,256]{2,1,0:T(8,128)(2,1)S(1)}, u32[]{:S(2)}, u32[]{:S(2)}) collective-permute-start(bf16[4,128,256]{2,1,0:T(8,128)(2,1)S(1)} %get-tuple-element.207), channel_id=1, source_target_pairs={{0,16},{16,0},{1,17},{17,1},{2,18},{18,2},{3,19},{19,3},{4,20},{20... | collective-permute-start | bytes 786440 | tf_op jit(solution)/shard_map/ppermute | solution.py:49
  213.1 8.5 %collective-permute-start.40 = (bf16[2,168,256]{2,1,0:T(8,128)(2,1)S(1)}, bf16[2,168,256]{2,1,0:T(8,128)(2,1)S(1)}, u32[]{:S(2)}, u32[]{:S(2)}) collective-permute-start(bf16[2,168,256]{2,1,0:T(8,128)(2,1)S(1)} %get-tuple-element.220), channel_id=1, source_target_pairs={{0,1},{1,0},{2,3},{3,2},{4,5},{5,4},{6,7},{7,6},{8,9},{9,8},{10,11... | collective-permute-start | bytes 516104 | tf_op jit(solution)/shard_map/ppermute | solution.py:49
  214.3 10.4 %collective-permute-start.41 = (bf16[1,128,512]{2,1,0:T(8,128)(2,1)S(1)}, bf16[1,128,512]{2,1,0:T(8,128)(2,1)S(1)}, u32[]{:S(2)}, u32[]{:S(2)}) collective-permute-start(bf16[1,128,512]{2,1,0:T(8,128)(2,1)S(1)} %bitcast.32), channel_id=1, source_target_pairs={{0,2},{1,3},{2,0},{3,1},{4,6},{5,7},{6,4},{7,5},{8,10},{9,11},{10,... | collective-permute-start | bytes 393224 | tf_op jit(solution)/shard_map/ppermute | solution.py:49
  216.8 24.1 %collective-permute-start.52 = (bf16[2048,256]{1,0:T(8,128)(2,1)S(1)}, bf16[2048,256]{1,0:T(8,128)(2,1)S(1)}, u32[]{:S(2)}, u32[]{:S(2)}) collective-permute-start(bf16[2048,256]{1,0:T(8,128)(2,1)S(1)} %grad_reduced.1.refs_4_.refs_0_), channel_id=1, source_target_pairs={{0,8},{4,12},{8,0},{12,4},{1,9},{5,13},{9,1},{13,5},{2,10},{6,14},... | collective-permute-start | bytes 3145736 | tf_op jit(solution)/shard_map/ppermute | solution.py:49
  225.2 8.9 %collective-permute-start.43 = (bf16[2,128,512]{2,1,0:T(8,128)(2,1)S(1)}, bf16[2,128,512]{2,1,0:T(8,128)(2,1)S(1)}, u32[]{:S(2)}, u32[]{:S(2)}) collective-permute-start(bf16[2,128,512]{2,1,0:T(8,128)(2,1)S(1)} %join.8.refs_0_), channel_id=1, source_target_pairs={{0,1},{1,0},{2,3},{3,2},{4,5},{5,4},{6,7},{7,6},{8,9},{9,8},{10,11... | collective-permute-start | bytes 786440 | tf_op jit(solution)/shard_map/ppermute | solution.py:49
  226.1 10.5 %collective-permute-start.45 = (bf16[1,128,256]{2,1,0:T(8,128)(2,1)S(1)}, bf16[1,128,256]{2,1,0:T(8,128)(2,1)S(1)}, u32[]{:S(2)}, u32[]{:S(2)}) collective-permute-start(bf16[1,128,256]{2,1,0:T(8,128)(2,1)S(1)} %add_last.2.refs_0_), channel_id=1, source_target_pairs={{0,2},{1,3},{2,0},{3,1},{4,6},{5,7},{6,4},{7,5},{8,10},{9,11},{10,... | collective-permute-start | bytes 196616 | tf_op jit(solution)/shard_map/ppermute | solution.py:49
  229.1 24.5 %collective-permute-start.51 = (bf16[2048,256]{1,0:T(8,128)(2,1)S(1)}, bf16[2048,256]{1,0:T(8,128)(2,1)S(1)}, u32[]{:S(2)}, u32[]{:S(2)}) collective-permute-start(bf16[2048,256]{1,0:T(8,128)(2,1)S(1)} %grad_reduced.1.refs_4_.refs_0_), channel_id=1, source_target_pairs={{0,4},{4,0},{8,12},{12,8},{1,5},{5,1},{9,13},{13,9},{2,6},{6,2},{1... | collective-permute-start | bytes 3145736 | tf_op jit(solution)/shard_map/ppermute | solution.py:49
  234.7 9.4 %collective-permute-start.47 = (bf16[4,128,512]{2,1,0:T(8,128)(2,1)S(1)}, bf16[4,128,512]{2,1,0:T(8,128)(2,1)S(1)}, u32[]{:S(2)}, u32[]{:S(2)}) collective-permute-start(bf16[4,128,512]{2,1,0:T(8,128)(2,1)S(1)} %join.9.own_ref), channel_id=1, source_target_pairs={{0,16},{16,0},{1,17},{17,1},{2,18},{18,2},{3,19},{19,3},{4,20},{20... | collective-permute-start | bytes 1572872 | tf_op jit(solution)/shard_map/ppermute | solution.py:49
  240.9 12.7 %collective-permute-start.53 = (bf16[2048,256]{1,0:T(8,128)(2,1)S(1)}, bf16[2048,256]{1,0:T(8,128)(2,1)S(1)}, u32[]{:S(2)}, u32[]{:S(2)}) collective-permute-start(bf16[2048,256]{1,0:T(8,128)(2,1)S(1)} %collective-permute-done.52.refs_2_), channel_id=1, source_target_pairs={{0,4},{4,0},{8,12},{12,8},{1,5},{5,1},{9,13},{13,9},{2,6},{6,2},{1... | collective-permute-start | bytes 3145736 | tf_op jit(solution)/shard_map/ppermute | solution.py:49
  251.8 8.7 %collective-permute-start.54 = (bf16[4,168,256]{2,1,0:T(8,128)(2,1)S(1)}, bf16[4,168,256]{2,1,0:T(8,128)(2,1)S(1)}, u32[]{:S(2)}, u32[]{:S(2)}) collective-permute-start(bf16[4,168,256]{2,1,0:T(8,128)(2,1)S(1)} %join.13.refs_2_), channel_id=1, source_target_pairs={{0,16},{16,0},{1,17},{17,1},{2,18},{18,2},{3,19},{19,3},{4,20},{20... | collective-permute-start | bytes 1032200 | tf_op jit(solution)/shard_map/ppermute | solution.py:49
  (35 other events, 324.0 us)
